TPU v7x, 32 devices: a whole 2x2x4 slice. The times are simulated.
32 devices in a mesh: group: 4 (over x, core), dev: 8 (over z, y).
Axes of the slice: x: 2, y: 2, z: 4, core: 2. Of those that a mesh axis runs over, the one named last changes fastest.
Arguments:
- images: bfloat16 [4096, 1152], P(('group', 'dev')), may hold values from -1 to 1
- texts: bfloat16 [4096, 1152], P(('group', 'dev')), may hold values from -1 to 1
- lang_order: int32 [4096], P(('group', 'dev')), may hold values from 0 to 1023, as said below
- position: int32 [4096], P(('group', 'dev')), may hold values from 0 to 1023, as said below
- logit_scale: float32 [1], replicated, may hold values from 8 to 24
- logit_bias: float32 [1], replicated, may hold values from -4 to -1
Outputs:
- image_grad: float32 [4096, 1152], P(('group', 'dev'))
- text_grad: float32 [4096, 1152], P(('group', 'dev'))
- loss: float32 [1], replicated
Inputs may be any that keep to these rules, and one draw needn't show every extreme that they name: In each group of 1024 examples, lang_order is a permutation of the group-local indices; the 128 entries of one device name at most 16 examples held by any one device of the group, and exactly 16 for each device they name. position is the inverse of lang_order within each group.
All inputs are finite; a program needn't handle non-finite values.
Results may differ from a plain program's by a relative error of at most 0.00062.
Values may be sent and summed in bfloat16 or wider, within the bound.
No kernel may reach another device: no remote copies, remote signals or barrier semaphores. Data moves between devices by JAX's collectives and lax.ppermute only.
A program may use at most 64 MiB of HBM per device.

v0:
```python
import functools

import jax
import jax.numpy as jnp
from jax import lax
from jax.experimental import pallas as pl
from jax.experimental.pallas import tpu as pltpu
from jax.sharding import PartitionSpec as P

EPSILON = 1e-06
AXES = ("group", "dev")
VMEM = pl.BlockSpec(memory_space=pltpu.VMEM)
SMEM = pl.BlockSpec(memory_space=pltpu.SMEM)
PARAMS = pltpu.CompilerParams(vmem_limit_bytes=24 << 20)


def unit_of(values):
    wide = values.astype(jnp.float32)
    recip = lax.rsqrt(jnp.sum(wide * wide, axis=1, keepdims=True) + EPSILON)
    return wide * recip, recip


def normalize_kernel(images, texts, img_half, txt_half):
    txt_half[...] = unit_of(texts[...])[0].astype(jnp.bfloat16)
    img_half[...] = unit_of(images[...])[0].astype(jnp.bfloat16)


def normalize(images, texts):
    half = jax.ShapeDtypeStruct(images.shape, jnp.bfloat16)
    return pl.pallas_call(
        normalize_kernel,
        out_shape=(half, half),
        in_specs=[VMEM] * 2,
        out_specs=(VMEM, VMEM),
        compiler_params=PARAMS,
        name="normalize",
    )(images, texts)


def project_kernel(count, scale, values, *refs):
    parts, out = refs[:count], refs[count]
    unit, recip = unit_of(values[...])
    total = parts[0][...]
    for part in parts[1:]:
        total = total + part[...]
    grad = scale[0] * total
    out[...] = recip * (grad - unit * jnp.sum(unit * grad, axis=1, keepdims=True))


def project(values, scale, parts):
    return pl.pallas_call(
        functools.partial(project_kernel, len(parts)),
        out_shape=jax.ShapeDtypeStruct(values.shape, jnp.float32),
        in_specs=[SMEM] + [VMEM] * (1 + len(parts)),
        out_specs=VMEM,
        compiler_params=PARAMS,
    )(scale, values, *parts)


def terms_kernel(own_count, block_count, places, pairs, first, with_loss, scale, bias, bases, *refs):
    refs = list(refs)
    own = [refs.pop(0) for _ in range(own_count)]
    blocks = [refs.pop(0) for _ in range(block_count)]
    targets = [refs.pop(0) for _ in range(own_count)]
    carried = [] if first else [refs.pop(0) for _ in range(own_count + with_loss)]
    sums = [refs.pop(0) for _ in range(own_count)]
    losses = refs.pop(0) if with_loss else None
    rows = own[0].shape[0]
    columns = [
        jnp.transpose(jnp.broadcast_to(target[...], (rows, rows))) for target in targets
    ]
    own_all = jnp.concatenate([ref[...] for ref in own], axis=0)
    if first:
        totals = None
        loss = jnp.zeros((8, 128), jnp.float32)
    else:
        totals = jnp.concatenate([ref[...] for ref in carried[:own_count]], axis=0)
        loss = carried[own_count][...] if with_loss else None
    for start in range(0, block_count, 2):
        some = range(start, min(start + 2, block_count))
        block_all = jnp.concatenate([blocks[b][...] for b in some], axis=0)
        logits = scale[0] * lax.dot_general(
            own_all, block_all, (((1,), (1,)), ((), ())), preferred_element_type=jnp.float32
        ) + bias[0]
        hits = {}
        pieces = []
        for a in range(own_count):
            strip = []
            for n, b in enumerate(some):
                piece = logits[a * rows : (a + 1) * rows, n * rows : (n + 1) * rows]
                if (a, b) in pairs:
                    ids = bases[places[b]] + lax.broadcasted_iota(jnp.int32, (rows, rows), 1)
                    hits[a, b] = columns[a] == ids
                    piece = jnp.where(hits[a, b], -piece, piece)
                strip.append(piece)
            pieces.append(jnp.concatenate(strip, axis=1) if len(strip) > 1 else strip[0])
        logits = jnp.concatenate(pieces, axis=0) if own_count > 1 else pieces[0]
        small = jnp.exp(-jnp.abs(logits))
        inverse = 1.0 / (1.0 + small)
        weight = jnp.where(logits >= 0, inverse, small * inverse)
        if with_loss:
            part = jnp.maximum(logits, 0.0) + jnp.log1p(small)
            lanes = part.shape[1]
            part = jnp.sum(part.reshape(part.shape[0] // 8, 8, lanes), axis=0)
            for lane in range(0, lanes, 128):
                loss = loss + part[:, lane : lane + 128]
        pieces = []
        for a in range(own_count):
            strip = []
            for n, b in enumerate(some):
                piece = weight[a * rows : (a + 1) * rows, n * rows : (n + 1) * rows]
                if (a, b) in pairs:
                    piece = jnp.where(hits[a, b], -piece, piece)
                strip.append(piece)
            pieces.append(jnp.concatenate(strip, axis=1) if len(strip) > 1 else strip[0])
        weight = jnp.concatenate(pieces, axis=0) if own_count > 1 else pieces[0]
        term = jnp.dot(
            weight.astype(jnp.bfloat16), block_all, preferred_element_type=jnp.float32
        )
        totals = term if totals is None else totals + term
    for a in range(own_count):
        sums[a][...] = totals[a * rows : (a + 1) * rows]
    if with_loss:
        losses[...] = loss


def terms(own, blocks, places, targets, pairs, bases, scale, bias, carried, with_loss):
    rows, width = own[0].shape
    first = carried is None
    kernel = functools.partial(
        terms_kernel, len(own), len(blocks), tuple(places), frozenset(pairs), first, with_loss
    )
    shapes = [jax.ShapeDtypeStruct((rows, width), jnp.float32)] * len(own)
    if with_loss:
        shapes = shapes + [jax.ShapeDtypeStruct((8, 128), jnp.float32)]
    operands = [scale, bias, bases, *own, *blocks, *targets]
    base = len(operands)
    aliases = {}
    if not first:
        operands += carried
        aliases = {base + n: n for n in range(len(carried))}
    size = len(own) * len(blocks) * rows * rows
    return pl.pallas_call(
        kernel,
        out_shape=shapes,
        in_specs=[SMEM] * 3 + [VMEM] * (len(operands) - 3),
        out_specs=[VMEM] * len(shapes),
        input_output_aliases=aliases,
        cost_estimate=pl.CostEstimate(
            flops=4 * size * width,
            transcendentals=3 * size,
            bytes_accessed=(2 * len(blocks) + 10 * len(own)) * rows * width,
        ),
        compiler_params=PARAMS,
    )(*operands)


def factor(count):
    best = 1
    while (best + 1) ** 2 <= count:
        best += 1
    while count % best:
        best -= 1
    return count // best, best


def per_device(images, texts, lang_order, position, logit_scale, logit_bias):
    rows, _ = images.shape
    dev_count = lax.axis_size("dev")
    group_count = lax.axis_size("group")
    cores = 2 if group_count % 2 == 0 else 1
    wide = group_count // cores
    slow, fast = factor(dev_count)
    sizes = (wide, cores, slow, fast)

    def shift(array, dim, by):
        pairs = []
        for index in range(group_count * dev_count):
            place, rest = [], index
            for size in reversed(sizes):
                place.insert(0, rest % size)
                rest //= size
            place[dim] = (place[dim] + by) % sizes[dim]
            target = 0
            for size, at in zip(sizes, place):
                target = target * size + at
            pairs.append((index, target))
        return lax.ppermute(array, AXES, pairs)

    dev_index = lax.axis_index("dev")
    slow_index, fast_index = dev_index // fast, dev_index % fast
    offsets = jnp.arange(slow * fast, dtype=jnp.int32)
    bases = rows * (
        (slow_index - offsets // fast) % slow * fast + (fast_index - offsets % fast) % fast
    )
    bases = bases.astype(jnp.int32)

    img_half, txt_half = normalize(images, texts)

    def spread(block, dim):
        blocks = [block]
        for _ in range(sizes[dim] - 1):
            blocks.append(shift(blocks[-1], dim, 1))
        return blocks

    def with_cores(blocks):
        out = []
        for block in blocks:
            out.append([block] + [shift(block, 1, by) for by in range(1, cores)])
        return out

    orders = spread(lang_order.reshape(1, rows), 3)
    img_targets = [position.reshape(1, rows)] * wide
    txt_targets = orders

    txt_line, img_line, txt_sets, img_sets = [txt_half], [img_half], [], []
    for step in range(slow):
        if step:
            txt_line.append(shift(txt_line[-1], 2, 1))
            img_line.append(shift(img_line[-1], 2, 1))
        txt_sets.append(with_cores(spread(txt_line[-1], 3)))
        img_sets.append(with_cores(spread(img_line[-1], 0)))
    img_own = [cores_of[0] for cores_of in img_sets[0]]
    txt_own = [cores_of[0] for cores_of in txt_sets[0]]

    def gradient(own, targets, sets, sums, step, part, with_loss):
        blocks, places, pairs = [], [], []
        for at in range(*part):
            if with_loss:
                pairs.append((0, len(blocks)))
            elif at == 0:
                pairs += [(a, len(blocks)) for a in range(len(own))]
            for block in sets[step][at]:
                blocks.append(block)
                places.append(step * fast + (at if with_loss else 0))
        return terms(
            own, blocks, places, targets, pairs, bases, logit_scale, logit_bias, sums,
            with_loss,
        )

    img_sums = txt_sums = None
    for step in range(slow):
        tail = step == slow - 1
        for part in [(0, 1), (1, fast)] if tail and fast > 1 else [(0, fast)]:
            img_sums = gradient(img_own, img_targets, txt_sets, img_sums, step, part, True)
        for part in [(0, 1), (1, wide)] if tail and wide > 1 else [(0, wide)]:
            txt_sums = gradient(txt_own, txt_targets, img_sets, txt_sums, step, part, False)

    loss = img_sums[wide]
    for dim in (0, 3, 1, 2):
        size = sizes[dim]
        if size & (size - 1) == 0:
            by = 1
            while by < size:
                loss = loss + shift(loss, dim, by)
                by = 2 * by
        else:
            loss = sum((shift(loss, dim, by) for by in range(1, size)), loss)
    total = jnp.float32(rows * dev_count * group_count)
    loss = (jnp.sum(loss) / (total * total)).reshape(1)
    img_parts = [img_sums[0]] + [shift(img_sums[a], 0, -a) for a in range(1, wide)]
    txt_parts = [txt_sums[0]] + [shift(txt_sums[a], 3, -a) for a in range(1, fast)]
    image_grad = project(images, logit_scale, img_parts)
    text_grad = project(texts, logit_scale, txt_parts)
    return (image_grad, text_grad, loss)


def solution(mesh):
    return jax.shard_map(
        per_device,
        mesh=mesh,
        in_specs=(
            P(AXES, None),
            P(AXES, None),
            P(AXES),
            P(AXES),
            P(),
            P(),
        ),
        out_specs=(P(AXES, None), P(AXES, None), P()),
        check_vma=False,
    )
```

profile of v0, /device:TPU:0, one launch (start us, length us, event | category | flops | bytes accessed | tf_op | source)
XLA Modules:
  0.0 119.7 jit_solution(18335292046283697463)
XLA Ops:
  0.6 1.0 copy-done
  1.6 1.0 copy-done.2
  2.8 3.1 %collective-permute-start.14 = (bf16[128,1152]{1,0:T(8,128)(2,1)S(1)}, bf16[128,1152]{1,0:T(8,128)(2,1)S(1)}, u32[]{:S(2)}, u32[]{:S(2)}) collective-permute-start(bf16[128,1152]{1,0:T(8,128)(2,1)S(1)} %get-tuple-element.31.refs_2_.refs_0_), channel_id=1, source_target_pairs={{0,1},{1,0},{2,3},{3,2},{4,5},{5,4},{6,7},{7,6},{8,9},{9,8},{10,11... | collective-permute-start | bytes 884744 | tf_op jit(solution)/shard_map/ppermute | solution.py:188
  5.8 1.5 %collective-permute-start = (bf16[128,1152]{1,0:T(8,128)(2,1)S(1)}, bf16[128,1152]{1,0:T(8,128)(2,1)S(1)}, u32[]{:S(2)}, u32[]{:S(2)}) collective-permute-start(bf16[128,1152]{1,0:T(8,128)(2,1)S(1)} %get-tuple-element.30.refs_0_.refs_2_), channel_id=1, source_target_pairs={{0,16},{1,17},{2,18},{3,19},{4,20},{5,21},{6,22},{7,23},{8,24},{9,... | collective-permute-start | bytes 884744 | tf_op jit(solution)/shard_map/ppermute | solution.py:188
  7.3 1.6 %collective-permute-start.1 = (bf16[128,1152]{1,0:T(8,128)(2,1)S(1)}, bf16[128,1152]{1,0:T(8,128)(2,1)S(1)}, u32[]{:S(2)}, u32[]{:S(2)}) collective-permute-start(bf16[128,1152]{1,0:T(8,128)(2,1)S(1)} %get-tuple-element.31.refs_2_.refs_0_), channel_id=1, source_target_pairs={{0,2},{1,3},{2,4},{3,5},{4,6},{5,7},{6,0},{7,1},{8,10},{9,11},{10,... | collective-permute-start | bytes 884744 | tf_op jit(solution)/shard_map/ppermute | solution.py:188
  8.9 0.5 collective-permute-start.22
  9.4 3.5 %collective-permute-done.22.refs_7_.refs_5_ = s32[1,128]{1,0:T(1,128)S(1)} collective-permute-done((s32[1,128]{1,0:T(1,128)S(1)}, s32[1,128]{1,0:T(1,128)S(1)}, u32[]{:S(2)}, u32[]{:S(2)}) %collective-permute-start.22) | collective-permute-done | bytes 544 | tf_op jit(solution)/shard_map/ppermute | solution.py:188
  12.9 1.8 %collective-permute-start.17 = (bf16[128,1152]{1,0:T(8,128)(2,1)S(1)}, bf16[128,1152]{1,0:T(8,128)(2,1)S(1)}, u32[]{:S(2)}, u32[]{:S(2)}) collective-permute-start(bf16[128,1152]{1,0:T(8,128)(2,1)S(1)} %get-tuple-element.30.refs_0_.refs_2_), channel_id=1, source_target_pairs={{0,2},{1,3},{2,4},{3,5},{4,6},{5,7},{6,0},{7,1},{8,10},{9,11},{10,... | collective-permute-start | bytes 884744 | tf_op jit(solution)/shard_map/ppermute | solution.py:188
  15.0 2.4 %collective-permute-done.1.refs_2_ = bf16[128,1152]{1,0:T(8,128)(2,1)S(1)} collective-permute-done((bf16[128,1152]{1,0:T(8,128)(2,1)S(1)}, bf16[128,1152]{1,0:T(8,128)(2,1)S(1)}, u32[]{:S(2)}, u32[]{:S(2)}) %collective-permute-start.1) | collective-permute-done | bytes 294944 | tf_op jit(solution)/shard_map/ppermute | solution.py:188
  17.4 0.5 collective-permute-start.11
  17.9 0.7 copy-done.34
  18.6 0.7 copy-done.32
  19.5 0.7 copy-done.6
  20.2 4.4 %collective-permute-done.17.refs_2_ = bf16[128,1152]{1,0:T(8,128)(2,1)S(1)} collective-permute-done((bf16[128,1152]{1,0:T(8,128)(2,1)S(1)}, bf16[128,1152]{1,0:T(8,128)(2,1)S(1)}, u32[]{:S(2)}, u32[]{:S(2)}) %collective-permute-start.17) | collective-permute-done | bytes 294944 | tf_op jit(solution)/shard_map/ppermute | solution.py:188
  24.6 0.7 copy-done.36
  25.3 1.7 %collective-permute-start.28 = (bf16[128,1152]{1,0:T(8,128)(2,1)S(1)}, bf16[128,1152]{1,0:T(8,128)(2,1)S(1)}, u32[]{:S(2)}, u32[]{:S(2)}) collective-permute-start(bf16[128,1152]{1,0:T(8,128)(2,1)S(1)} %collective-permute-done.17.refs_2_), channel_id=1, source_target_pairs={{0,16},{1,17},{2,18},{3,19},{4,20},{5,21},{6,22},{7,23},{8,24},{9,... | collective-permute-start | bytes 884744 | tf_op jit(solution)/shard_map/ppermute | solution.py:188
  27.1 0.7 copy-done.12
  28.0 0.7 copy-done.8
  28.7 2.1 %collective-permute-done.2.refs_2_ = bf16[128,1152]{1,0:T(8,128)(2,1)} collective-permute-done((bf16[128,1152]{1,0:T(8,128)(2,1)S(1)}, bf16[128,1152]{1,0:T(8,128)(2,1)}, u32[]{:S(2)}, u32[]{:S(2)}) %collective-permute-start.2) | collective-permute-done | bytes 294944 | tf_op jit(solution)/shard_map/ppermute | solution.py:188
  30.9 0.7 copy-done.10
  31.6 0.7 copy-done.38
  32.3 1.5 %collective-permute-start.8 = (bf16[128,1152]{1,0:T(8,128)(2,1)}, bf16[128,1152]{1,0:T(8,128)(2,1)}, u32[]{:S(2)}, u32[]{:S(2)}) collective-permute-start(bf16[128,1152]{1,0:T(8,128)(2,1)} %collective-permute-done.2.refs_2_), channel_id=1, source_target_pairs={{0,1},{1,0},{2,3},{3,2},{4,5},{5,4},{6,7},{7,6},{8,9},{9,8},{10,11... | collective-permute-start | bytes 884744 | tf_op jit(solution)/shard_map/ppermute | solution.py:188
  33.8 1.0 collective-permute-done.28.refs_4_
  34.8 3.2 %collective-permute-done.18.refs_2_ = bf16[128,1152]{1,0:T(8,128)(2,1)S(1)} collective-permute-done((bf16[128,1152]{1,0:T(8,128)(2,1)S(1)}, bf16[128,1152]{1,0:T(8,128)(2,1)S(1)}, u32[]{:S(2)}, u32[]{:S(2)}) %collective-permute-start.18) | collective-permute-done | bytes 294944 | tf_op jit(solution)/shard_map/ppermute | solution.py:188
  38.0 0.6 collective-permute-start.25
  38.6 0.7 copy-done.20
  39.3 0.7 copy-done.18
  40.0 0.7 copy-done.16
  40.7 1.3 %collective-permute-done.8.refs_4_ = bf16[128,1152]{1,0:T(8,128)(2,1)} collective-permute-done((bf16[128,1152]{1,0:T(8,128)(2,1)}, bf16[128,1152]{1,0:T(8,128)(2,1)}, u32[]{:S(2)}, u32[]{:S(2)}) %collective-permute-start.8) | collective-permute-done | bytes 294944 | tf_op jit(solution)/shard_map/ppermute | solution.py:188
  42.0 0.7 copy-done.14
  42.8 4.0 %collective-permute-done.3.refs_2_ = bf16[128,1152]{1,0:T(8,128)(2,1)} collective-permute-done((bf16[128,1152]{1,0:T(8,128)(2,1)}, bf16[128,1152]{1,0:T(8,128)(2,1)}, u32[]{:S(2)}, u32[]{:S(2)}) %collective-permute-start.3) | collective-permute-done | bytes 294944 | tf_op jit(solution)/shard_map/ppermute | solution.py:188
  46.8 1.6 %collective-permute-start.4 = (bf16[128,1152]{1,0:T(8,128)(2,1)}, bf16[128,1152]{1,0:T(8,128)(2,1)S(1)}, u32[]{:S(2)}, u32[]{:S(2)}) collective-permute-start(bf16[128,1152]{1,0:T(8,128)(2,1)} %collective-permute-done.3.refs_2_), channel_id=1, source_target_pairs={{0,1},{1,0},{2,3},{3,2},{4,5},{5,4},{6,7},{7,6},{8,9},{9,8},{10,11... | collective-permute-start | bytes 884744 | tf_op jit(solution)/shard_map/ppermute | solution.py:188
  48.4 0.7 copy-done.22
  49.1 2.7 %collective-permute-done.19.refs_2_ = bf16[128,1152]{1,0:T(8,128)(2,1)} collective-permute-done((bf16[128,1152]{1,0:T(8,128)(2,1)S(1)}, bf16[128,1152]{1,0:T(8,128)(2,1)}, u32[]{:S(2)}, u32[]{:S(2)}) %collective-permute-start.19) | collective-permute-done | bytes 294944 | tf_op jit(solution)/shard_map/ppermute | solution.py:188
  51.8 1.7 %collective-permute-start.20 = (bf16[128,1152]{1,0:T(8,128)(2,1)}, bf16[128,1152]{1,0:T(8,128)(2,1)}, u32[]{:S(2)}, u32[]{:S(2)}) collective-permute-start(bf16[128,1152]{1,0:T(8,128)(2,1)} %collective-permute-done.19.refs_2_), channel_id=1, source_target_pairs={{0,16},{1,17},{2,18},{3,19},{4,20},{5,21},{6,22},{7,23},{8,24},{9,... | collective-permute-start | bytes 884744 | tf_op jit(solution)/shard_map/ppermute | solution.py:188
  53.5 0.7 copy-done.28
  55.6 0.7 copy-done.24
  56.3 0.5 collective-permute-start.7
  56.9 0.6 copy-done.4
  57.5 1.0 copy-done.35
  58.5 1.0 copy-done.37
  59.4 1.8 %shard_map.85 = (f32[128,1152]{1,0:T(8,128)S(1)}, f32[128,1152]{1,0:T(8,128)S(1)}, f32[8,128]{1,0:T(8,128)S(1)}) custom-call(f32[1]{0:T(128)S(6)} %copy.49.scale, f32[1]{0:T(128)S(6)} %copy.50.bias, s32[8]{0:T(128)S(1)} %fusion.5.bases, bf16[128,1152]{1,0:T(8,128)(2,1)S(1)} %get-tuple-element.30.refs_0_.refs_2_, ...), custom_call_target="tpu_custom_call" | custom-call | flops 603979776 | bytes 4128768 | tf_op jit(solution)/shard_map/pallas_call | solution.py:143
  61.3 0.7 copy-done.26
  62.0 0.5 collective-permute-start.21
  62.6 1.6 %shard_map.91 = (f32[128,1152]{1,0:T(8,128)S(1)}, f32[128,1152]{1,0:T(8,128)S(1)}) custom-call(f32[1]{0:T(128)S(6)} %copy.49.scale, f32[1]{0:T(128)S(6)} %copy.50.bias, s32[8]{0:T(128)S(1)} %fusion.5.bases, bf16[128,1152]{1,0:T(8,128)(2,1)S(1)} %get-tuple-element.31.refs_2_.refs_0_, bf16[128,1152]{1,0:T(8,128)(2,1)S(1)} %collective-permute-done.14.refs_4_.refs_1_, ...), custom_call_target="tpu_custom_call" | custom-call | flops 603979776 | bytes 4128768 | tf_op jit(solution)/shard_map/pallas_call | solution.py:143
  64.4 2.3 %shard_map.92 = (f32[128,1152]{1,0:T(8,128)S(1)}, f32[128,1152]{1,0:T(8,128)S(1)}) custom-call(f32[1]{0:T(128)S(6)} %copy.49.scale, f32[1]{0:T(128)S(6)} %copy.50.bias, s32[8]{0:T(128)S(1)} %fusion.5.bases, bf16[128,1152]{1,0:T(8,128)(2,1)S(1)} %get-tuple-element.31.refs_2_.refs_0_, ...), custom_call_target="tpu_custom_call", output_to_operand_aliasing={{0}: (11, {}), {1}: (12, {})} | custom-call | flops 603979776 | bytes 4128768 | tf_op jit(solution)/shard_map/pallas_call | solution.py:143
  66.7 2.4 %shard_map.86 = (f32[128,1152]{1,0:T(8,128)S(1)}, f32[128,1152]{1,0:T(8,128)S(1)}, f32[8,128]{1,0:T(8,128)S(1)}) custom-call(f32[1]{0:T(128)S(6)} %copy.49.scale, f32[1]{0:T(128)S(6)} %copy.50.bias, s32[8]{0:T(128)S(1)} %fusion.5.bases, ...), custom_call_target="tpu_custom_call", output_to_operand_aliasing={{0}: (11, {}), {1}: (12, {}), {2}: (13, {})} | custom-call | flops 603979776 | bytes 4128768 | tf_op jit(solution)/shard_map/pallas_call | solution.py:143
  69.2 2.3 %shard_map.93 = (f32[128,1152]{1,0:T(8,128)S(1)}, f32[128,1152]{1,0:T(8,128)S(1)}) custom-call(f32[1]{0:T(128)S(6)} %copy.49.scale, f32[1]{0:T(128)S(6)} %copy.50.bias, s32[8]{0:T(128)S(1)} %fusion.5.bases, bf16[128,1152]{1,0:T(8,128)(2,1)S(1)} %get-tuple-element.31.refs_2_.refs_0_, ...), custom_call_target="tpu_custom_call", output_to_operand_aliasing={{0}: (11, {}), {1}: (12, {})} | custom-call | flops 603979776 | bytes 4128768 | tf_op jit(solution)/shard_map/pallas_call | solution.py:143
  71.5 2.0 %shard_map.94 = (f32[128,1152]{1,0:T(8,128)S(1)}, f32[128,1152]{1,0:T(8,128)S(1)}) custom-call(f32[1]{0:T(128)S(6)} %copy.49.scale, f32[1]{0:T(128)S(6)} %copy.50.bias, s32[8]{0:T(128)S(1)} %fusion.5.bases, bf16[128,1152]{1,0:T(8,128)(2,1)S(1)} %get-tuple-element.31.refs_2_.refs_0_, ...), custom_call_target="tpu_custom_call", output_to_operand_aliasing={{0}: (9, {}), {1}: (10, {})} | custom-call | flops 301989888 | bytes 3538944 | tf_op jit(solution)/shard_map/pallas_call | solution.py:143
  73.6 3.0 %shard_map.87 = (f32[128,1152]{1,0:T(8,128)S(1)}, f32[128,1152]{1,0:T(8,128)S(1)}, f32[8,128]{1,0:T(8,128)S(1)}) custom-call(f32[1]{0:T(128)S(6)} %copy.49.scale, f32[1]{0:T(128)S(6)} %copy.50.bias, s32[8]{0:T(128)S(1)} %fusion.5.bases, ...), custom_call_target="tpu_custom_call", output_to_operand_aliasing={{0}: (11, {}), {1}: (12, {}), {2}: (13, {})} | custom-call | flops 603979776 | bytes 4128768 | tf_op jit(solution)/shard_map/pallas_call | solution.py:143
  76.5 2.0 %shard_map.88 = (f32[128,1152]{1,0:T(8,128)S(1)}, f32[128,1152]{1,0:T(8,128)S(1)}, f32[8,128]{1,0:T(8,128)S(1)}) custom-call(f32[1]{0:T(128)S(6)} %copy.49.scale, f32[1]{0:T(128)S(6)} %copy.50.bias, s32[8]{0:T(128)S(1)} %fusion.5.bases, ...), custom_call_target="tpu_custom_call", output_to_operand_aliasing={{0}: (9, {}), {1}: (10, {}), {2}: (11, {})} | custom-call | flops 301989888 | bytes 3538944 | tf_op jit(solution)/shard_map/pallas_call | solution.py:143
  78.6 1.9 %shard_map.95 = (f32[128,1152]{1,0:T(8,128)S(1)}, f32[128,1152]{1,0:T(8,128)S(1)}) custom-call(f32[1]{0:T(128)S(6)} %copy.49.scale, f32[1]{0:T(128)S(6)} %copy.50.bias, s32[8]{0:T(128)S(1)} %fusion.5.bases, bf16[128,1152]{1,0:T(8,128)(2,1)S(1)} %get-tuple-element.31.refs_2_.refs_0_, ...), custom_call_target="tpu_custom_call", output_to_operand_aliasing={{0}: (9, {}), {1}: (10, {})} | custom-call | flops 301989888 | bytes 3538944 | tf_op jit(solution)/shard_map/pallas_call | solution.py:143
  80.5 1.6 %collective-permute-start.32 = (f32[128,1152]{1,0:T(8,128)S(1)}, f32[128,1152]{1,0:T(8,128)}, u32[]{:S(2)}, u32[]{:S(2)}) collective-permute-start(f32[128,1152]{1,0:T(8,128)S(1)} %get-tuple-element.55), channel_id=1, source_target_pairs={{0,1},{1,0},{2,3},{3,2},{4,5},{5,4},{6,7},{7,6},{8,9},{9,8},{10,11... | collective-permute-start | bytes 1769480 | tf_op jit(solution)/shard_map/ppermute | solution.py:188
  82.1 1.6 %shard_map.89 = (f32[128,1152]{1,0:T(8,128)S(1)}, f32[128,1152]{1,0:T(8,128)S(1)}, f32[8,128]{1,0:T(8,128)S(1)}) custom-call(f32[1]{0:T(128)S(6)} %copy.49.scale, f32[1]{0:T(128)S(6)} %copy.50.bias, s32[8]{0:T(128)S(1)} %fusion.5.bases, ...), custom_call_target="tpu_custom_call", output_to_operand_aliasing={{0}: (9, {}), {1}: (10, {}), {2}: (11, {})} | custom-call | flops 301989888 | bytes 3538944 | tf_op jit(solution)/shard_map/pallas_call | solution.py:143
  84.2 1.6 %collective-permute-start.33 = (f32[8,128]{1,0:T(8,128)S(1)}, f32[8,128]{1,0:T(8,128)S(1)}, u32[]{:S(2)}, u32[]{:S(2)}) collective-permute-start(f32[8,128]{1,0:T(8,128)S(1)} %get-tuple-element.56), channel_id=1, source_target_pairs={{0,16},{1,17},{2,18},{3,19},{4,20},{5,21},{6,22},{7,23},{8,24},{9,... | collective-permute-start | bytes 12296 | tf_op jit(solution)/shard_map/ppermute | solution.py:188
  85.8 13.5 %collective-permute-done.33 = f32[8,128]{1,0:T(8,128)S(1)} collective-permute-done((f32[8,128]{1,0:T(8,128)S(1)}, f32[8,128]{1,0:T(8,128)S(1)}, u32[]{:S(2)}, u32[]{:S(2)}) %collective-permute-start.33) | collective-permute-done | bytes 4128 | tf_op jit(solution)/shard_map/ppermute | solution.py:188
  99.3 0.5 collective-permute-start.34
  99.8 3.1 %collective-permute-done.34 = f32[8,128]{1,0:T(8,128)S(1)} collective-permute-done((f32[8,128]{1,0:T(8,128)S(1)}, f32[8,128]{1,0:T(8,128)S(1)}, u32[]{:S(2)}, u32[]{:S(2)}) %collective-permute-start.34) | collective-permute-done | bytes 4128 | tf_op jit(solution)/shard_map/ppermute | solution.py:188
  102.9 1.2 collective-permute-done.35
  104.1 5.4 %collective-permute-done.36 = f32[8,128]{1,0:T(8,128)S(1)} collective-permute-done((f32[8,128]{1,0:T(8,128)S(1)}, f32[8,128]{1,0:T(8,128)S(1)}, u32[]{:S(2)}, u32[]{:S(2)}) %collective-permute-start.36) | collective-permute-done | bytes 4128 | tf_op jit(solution)/shard_map/ppermute | solution.py:188
  109.5 4.5 %collective-permute-done.37 = f32[8,128]{1,0:T(8,128)S(1)} collective-permute-done((f32[8,128]{1,0:T(8,128)S(1)}, f32[8,128]{1,0:T(8,128)S(1)}, u32[]{:S(2)}, u32[]{:S(2)}) %collective-permute-start.37) | collective-permute-done | bytes 4128 | tf_op jit(solution)/shard_map/ppermute | solution.py:188
  114.0 0.6 add_reduce_fusion
  115.3 2.2 %shard_map.96 = f32[128,1152]{1,0:T(8,128)} custom-call(f32[1]{0:T(128)S(6)} %copy.49.scale, bf16[128,1152]{1,0:T(8,128)(2,1)S(1)} %copy-done.1, f32[128,1152]{1,0:T(8,128)S(1)} %get-tuple-element.54.refs_0_, f32[128,1152]{1,0:T(8,128)} %collective-permute-done.32.refs_1_), custom_call_target="tpu_custom_call" | custom-call | tf_op jit(solution)/shard_map/pallas_call | solution.py:51
  117.5 1.1 shard_map.90
  (111 shorter events, 1.7 us)
Async XLA Ops:
  0.6 1.0 copy-start
  1.6 1.0 copy-start.2
  2.8 10.2 %collective-permute-start.14 = (bf16[128,1152]{1,0:T(8,128)(2,1)S(1)}, bf16[128,1152]{1,0:T(8,128)(2,1)S(1)}, u32[]{:S(2)}, u32[]{:S(2)}) collective-permute-start(bf16[128,1152]{1,0:T(8,128)(2,1)S(1)} %get-tuple-element.31.refs_2_.refs_0_), channel_id=1, source_target_pairs={{0,1},{1,0},{2,3},{3,2},{4,5},{5,4},{6,7},{7,6},{8,9},{9,8},{10,11... | collective-permute-start | bytes 884744 | tf_op jit(solution)/shard_map/ppermute | solution.py:188
  5.8 3.1 %copy-start.31 = (s32[128]{0:T(128)S(1)}, s32[128]{0:T(128)}, u32[]{:S(2)}) copy-start(s32[128]{0:T(128)} %param.8) | copy-start | bytes 1540
  5.8 8.9 %collective-permute-start = (bf16[128,1152]{1,0:T(8,128)(2,1)S(1)}, bf16[128,1152]{1,0:T(8,128)(2,1)S(1)}, u32[]{:S(2)}, u32[]{:S(2)}) collective-permute-start(bf16[128,1152]{1,0:T(8,128)(2,1)S(1)} %get-tuple-element.30.refs_0_.refs_2_), channel_id=1, source_target_pairs={{0,16},{1,17},{2,18},{3,19},{4,20},{5,21},{6,22},{7,23},{8,24},{9,... | collective-permute-start | bytes 884744 | tf_op jit(solution)/shard_map/ppermute | solution.py:188
  7.3 10.0 %collective-permute-start.1 = (bf16[128,1152]{1,0:T(8,128)(2,1)S(1)}, bf16[128,1152]{1,0:T(8,128)(2,1)S(1)}, u32[]{:S(2)}, u32[]{:S(2)}) collective-permute-start(bf16[128,1152]{1,0:T(8,128)(2,1)S(1)} %get-tuple-element.31.refs_2_.refs_0_), channel_id=1, source_target_pairs={{0,2},{1,3},{2,4},{3,5},{4,6},{5,7},{6,0},{7,1},{8,10},{9,11},{10,... | collective-permute-start | bytes 884744 | tf_op jit(solution)/shard_map/ppermute | solution.py:188
  8.9 9.0 %collective-permute-start.13 = (bf16[128,1152]{1,0:T(8,128)(2,1)S(1)}, bf16[128,1152]{1,0:T(8,128)(2,1)S(1)}, u32[]{:S(2)}, u32[]{:S(2)}) collective-permute-start(bf16[128,1152]{1,0:T(8,128)(2,1)S(1)} %get-tuple-element.31.refs_2_.refs_0_), channel_id=1, source_target_pairs={{0,8},{1,9},{2,10},{3,11},{4,12},{5,13},{6,14},{7,15},{8,0},{9,1},... | collective-permute-start | bytes 884744 | tf_op jit(solution)/shard_map/ppermute | solution.py:188
  8.9 4.0 %collective-permute-start.22 = (s32[1,128]{1,0:T(1,128)S(1)}, s32[1,128]{1,0:T(1,128)S(1)}, u32[]{:S(2)}, u32[]{:S(2)}) collective-permute-start(s32[1,128]{1,0:T(1,128)S(1)} %bitcast.13), channel_id=1, source_target_pairs={{0,1},{1,0},{2,3},{3,2},{4,5},{5,4},{6,7},{7,6},{8,9},{9,8},{10,11... | collective-permute-start | bytes 1544 | tf_op jit(solution)/shard_map/ppermute | solution.py:188
  12.9 5.7 %collective-permute-start.30 = (bf16[128,1152]{1,0:T(8,128)(2,1)S(1)}, bf16[128,1152]{1,0:T(8,128)(2,1)S(1)}, u32[]{:S(2)}, u32[]{:S(2)}) collective-permute-start(bf16[128,1152]{1,0:T(8,128)(2,1)S(1)} %get-tuple-element.30.refs_0_.refs_2_), channel_id=1, source_target_pairs={{0,8},{1,9},{2,10},{3,11},{4,12},{5,13},{6,14},{7,15},{8,0},{9,1},... | collective-permute-start | bytes 884744 | tf_op jit(solution)/shard_map/ppermute | solution.py:188
  12.9 11.7 %collective-permute-start.17 = (bf16[128,1152]{1,0:T(8,128)(2,1)S(1)}, bf16[128,1152]{1,0:T(8,128)(2,1)S(1)}, u32[]{:S(2)}, u32[]{:S(2)}) collective-permute-start(bf16[128,1152]{1,0:T(8,128)(2,1)S(1)} %get-tuple-element.30.refs_0_.refs_2_), channel_id=1, source_target_pairs={{0,2},{1,3},{2,4},{3,5},{4,6},{5,7},{6,0},{7,1},{8,10},{9,11},{10,... | collective-permute-start | bytes 884744 | tf_op jit(solution)/shard_map/ppermute | solution.py:188
  14.7 9.9 %collective-permute-start.15 = (bf16[128,1152]{1,0:T(8,128)(2,1)S(1)}, bf16[128,1152]{1,0:T(8,128)(2,1)S(1)}, u32[]{:S(2)}, u32[]{:S(2)}) collective-permute-start(bf16[128,1152]{1,0:T(8,128)(2,1)S(1)} %collective-permute-done.14.refs_4_.refs_1_), channel_id=1, source_target_pairs={{0,8},{1,9},{2,10},{3,11},{4,12},{5,13},{6,14},{7,15},{8,0},{9,1},... | collective-permute-start | bytes 884744 | tf_op jit(solution)/shard_map/ppermute | solution.py:188
  17.4 9.7 %collective-permute-start.11 = (bf16[128,1152]{1,0:T(8,128)(2,1)S(1)}, bf16[128,1152]{1,0:T(8,128)(2,1)S(1)}, u32[]{:S(2)}, u32[]{:S(2)}) collective-permute-start(bf16[128,1152]{1,0:T(8,128)(2,1)S(1)} %collective-permute-done.1.refs_2_), channel_id=1, source_target_pairs={{0,1},{1,0},{2,3},{3,2},{4,5},{5,4},{6,7},{7,6},{8,9},{9,8},{10,11... | collective-permute-start | bytes 884744 | tf_op jit(solution)/shard_map/ppermute | solution.py:188
  18.6 8.5 %collective-permute-start.10 = (bf16[128,1152]{1,0:T(8,128)(2,1)S(1)}, bf16[128,1152]{1,0:T(8,128)(2,1)S(1)}, u32[]{:S(2)}, u32[]{:S(2)}) collective-permute-start(bf16[128,1152]{1,0:T(8,128)(2,1)S(1)} %collective-permute-done.1.refs_2_), channel_id=1, source_target_pairs={{0,8},{1,9},{2,10},{3,11},{4,12},{5,13},{6,14},{7,15},{8,0},{9,1},... | collective-permute-start | bytes 884744 | tf_op jit(solution)/shard_map/ppermute | solution.py:188
  19.3 11.6 %collective-permute-start.2 = (bf16[128,1152]{1,0:T(8,128)(2,1)S(1)}, bf16[128,1152]{1,0:T(8,128)(2,1)}, u32[]{:S(2)}, u32[]{:S(2)}) collective-permute-start(bf16[128,1152]{1,0:T(8,128)(2,1)S(1)} %collective-permute-done.1.refs_2_), channel_id=1, source_target_pairs={{0,2},{1,3},{2,4},{3,5},{4,6},{5,7},{6,0},{7,1},{8,10},{9,11},{10,... | collective-permute-start | bytes 884744 | tf_op jit(solution)/shard_map/ppermute | solution.py:188
  24.6 7.0 %collective-permute-start.31 = (bf16[128,1152]{1,0:T(8,128)(2,1)S(1)}, bf16[128,1152]{1,0:T(8,128)(2,1)S(1)}, u32[]{:S(2)}, u32[]{:S(2)}) collective-permute-start(bf16[128,1152]{1,0:T(8,128)(2,1)S(1)} %collective-permute-done.refs_1_.refs_4_), channel_id=1, source_target_pairs={{0,8},{1,9},{2,10},{3,11},{4,12},{5,13},{6,14},{7,15},{8,0},{9,1},... | collective-permute-start | bytes 884744 | tf_op jit(solution)/shard_map/ppermute | solution.py:188
  24.6 0.7 copy-start.36
  25.3 9.4 %collective-permute-start.28 = (bf16[128,1152]{1,0:T(8,128)(2,1)S(1)}, bf16[128,1152]{1,0:T(8,128)(2,1)S(1)}, u32[]{:S(2)}, u32[]{:S(2)}) collective-permute-start(bf16[128,1152]{1,0:T(8,128)(2,1)S(1)} %collective-permute-done.17.refs_2_), channel_id=1, source_target_pairs={{0,16},{1,17},{2,18},{3,19},{4,20},{5,21},{6,22},{7,23},{8,24},{9,... | collective-permute-start | bytes 884744 | tf_op jit(solution)/shard_map/ppermute | solution.py:188
  27.1 10.9 %collective-permute-start.18 = (bf16[128,1152]{1,0:T(8,128)(2,1)S(1)}, bf16[128,1152]{1,0:T(8,128)(2,1)S(1)}, u32[]{:S(2)}, u32[]{:S(2)}) collective-permute-start(bf16[128,1152]{1,0:T(8,128)(2,1)S(1)} %collective-permute-done.17.refs_2_), channel_id=1, source_target_pairs={{0,2},{1,3},{2,4},{3,5},{4,6},{5,7},{6,0},{7,1},{8,10},{9,11},{10,... | collective-permute-start | bytes 884744 | tf_op jit(solution)/shard_map/ppermute | solution.py:188
  27.8 10.8 %collective-permute-start.27 = (bf16[128,1152]{1,0:T(8,128)(2,1)S(1)}, bf16[128,1152]{1,0:T(8,128)(2,1)S(1)}, u32[]{:S(2)}, u32[]{:S(2)}) collective-permute-start(bf16[128,1152]{1,0:T(8,128)(2,1)S(1)} %collective-permute-done.17.refs_2_), channel_id=1, source_target_pairs={{0,8},{1,9},{2,10},{3,11},{4,12},{5,13},{6,14},{7,15},{8,0},{9,1},... | collective-permute-start | bytes 884744 | tf_op jit(solution)/shard_map/ppermute | solution.py:188
  30.9 8.4 %collective-permute-start.12 = (bf16[128,1152]{1,0:T(8,128)(2,1)S(1)}, bf16[128,1152]{1,0:T(8,128)(2,1)S(1)}, u32[]{:S(2)}, u32[]{:S(2)}) collective-permute-start(bf16[128,1152]{1,0:T(8,128)(2,1)S(1)} %collective-permute-done.11.refs_4_), channel_id=1, source_target_pairs={{0,8},{1,9},{2,10},{3,11},{4,12},{5,13},{6,14},{7,15},{8,0},{9,1},... | collective-permute-start | bytes 884744 | tf_op jit(solution)/shard_map/ppermute | solution.py:188
  32.3 9.7 %collective-permute-start.8 = (bf16[128,1152]{1,0:T(8,128)(2,1)}, bf16[128,1152]{1,0:T(8,128)(2,1)}, u32[]{:S(2)}, u32[]{:S(2)}) collective-permute-start(bf16[128,1152]{1,0:T(8,128)(2,1)} %collective-permute-done.2.refs_2_), channel_id=1, source_target_pairs={{0,1},{1,0},{2,3},{3,2},{4,5},{5,4},{6,7},{7,6},{8,9},{9,8},{10,11... | collective-permute-start | bytes 884744 | tf_op jit(solution)/shard_map/ppermute | solution.py:188
  34.8 12.0 %collective-permute-start.3 = (bf16[128,1152]{1,0:T(8,128)(2,1)}, bf16[128,1152]{1,0:T(8,128)(2,1)}, u32[]{:S(2)}, u32[]{:S(2)}) collective-permute-start(bf16[128,1152]{1,0:T(8,128)(2,1)} %collective-permute-done.2.refs_2_), channel_id=1, source_target_pairs={{0,2},{1,3},{2,4},{3,5},{4,6},{5,7},{6,0},{7,1},{8,10},{9,11},{10,... | collective-permute-start | bytes 884744 | tf_op jit(solution)/shard_map/ppermute | solution.py:188
  38.0 10.3 %collective-permute-start.25 = (bf16[128,1152]{1,0:T(8,128)(2,1)S(1)}, bf16[128,1152]{1,0:T(8,128)(2,1)S(1)}, u32[]{:S(2)}, u32[]{:S(2)}) collective-permute-start(bf16[128,1152]{1,0:T(8,128)(2,1)S(1)} %collective-permute-done.18.refs_2_), channel_id=1, source_target_pairs={{0,16},{1,17},{2,18},{3,19},{4,20},{5,21},{6,22},{7,23},{8,24},{9,... | collective-permute-start | bytes 884744 | tf_op jit(solution)/shard_map/ppermute | solution.py:188
  39.3 12.5 %collective-permute-start.19 = (bf16[128,1152]{1,0:T(8,128)(2,1)S(1)}, bf16[128,1152]{1,0:T(8,128)(2,1)}, u32[]{:S(2)}, u32[]{:S(2)}) collective-permute-start(bf16[128,1152]{1,0:T(8,128)(2,1)S(1)} %collective-permute-done.18.refs_2_), channel_id=1, source_target_pairs={{0,2},{1,3},{2,4},{3,5},{4,6},{5,7},{6,0},{7,1},{8,10},{9,11},{10,... | collective-permute-start | bytes 884744 | tf_op jit(solution)/shard_map/ppermute | solution.py:188
  40.0 13.5 %collective-permute-start.29 = (bf16[128,1152]{1,0:T(8,128)(2,1)S(1)}, bf16[128,1152]{1,0:T(8,128)(2,1)S(1)}, u32[]{:S(2)}, u32[]{:S(2)}) collective-permute-start(bf16[128,1152]{1,0:T(8,128)(2,1)S(1)} %collective-permute-done.28.refs_4_), channel_id=1, source_target_pairs={{0,8},{1,9},{2,10},{3,11},{4,12},{5,13},{6,14},{7,15},{8,0},{9,1},... | collective-permute-start | bytes 884744 | tf_op jit(solution)/shard_map/ppermute | solution.py:188
  42.0 13.5 %collective-permute-start.24 = (bf16[128,1152]{1,0:T(8,128)(2,1)S(1)}, bf16[128,1152]{1,0:T(8,128)(2,1)S(1)}, u32[]{:S(2)}, u32[]{:S(2)}) collective-permute-start(bf16[128,1152]{1,0:T(8,128)(2,1)S(1)} %collective-permute-done.18.refs_2_), channel_id=1, source_target_pairs={{0,8},{1,9},{2,10},{3,11},{4,12},{5,13},{6,14},{7,15},{8,0},{9,1},... | collective-permute-start | bytes 884744 | tf_op jit(solution)/shard_map/ppermute | solution.py:188
  46.8 10.0 %collective-permute-start.4 = (bf16[128,1152]{1,0:T(8,128)(2,1)}, bf16[128,1152]{1,0:T(8,128)(2,1)S(1)}, u32[]{:S(2)}, u32[]{:S(2)}) collective-permute-start(bf16[128,1152]{1,0:T(8,128)(2,1)} %collective-permute-done.3.refs_2_), channel_id=1, source_target_pairs={{0,1},{1,0},{2,3},{3,2},{4,5},{5,4},{6,7},{7,6},{8,9},{9,8},{10,11... | collective-permute-start | bytes 884744 | tf_op jit(solution)/shard_map/ppermute | solution.py:188
  48.3 13.0 %collective-permute-start.26 = (bf16[128,1152]{1,0:T(8,128)(2,1)S(1)}, bf16[128,1152]{1,0:T(8,128)(2,1)S(1)}, u32[]{:S(2)}, u32[]{:S(2)}) collective-permute-start(bf16[128,1152]{1,0:T(8,128)(2,1)S(1)} %collective-permute-done.25.refs_4_), channel_id=1, source_target_pairs={{0,8},{1,9},{2,10},{3,11},{4,12},{5,13},{6,14},{7,15},{8,0},{9,1},... | collective-permute-start | bytes 884744 | tf_op jit(solution)/shard_map/ppermute | solution.py:188
  48.3 0.7 copy-start.22
  51.8 10.3 %collective-permute-start.20 = (bf16[128,1152]{1,0:T(8,128)(2,1)}, bf16[128,1152]{1,0:T(8,128)(2,1)}, u32[]{:S(2)}, u32[]{:S(2)}) collective-permute-start(bf16[128,1152]{1,0:T(8,128)(2,1)} %collective-permute-done.19.refs_2_), channel_id=1, source_target_pairs={{0,16},{1,17},{2,18},{3,19},{4,20},{5,21},{6,22},{7,23},{8,24},{9,... | collective-permute-start | bytes 884744 | tf_op jit(solution)/shard_map/ppermute | solution.py:188
  53.5 0.7 copy-start.28
  54.2 10.0 %collective-permute-start.23 = (bf16[128,1152]{1,0:T(8,128)(2,1)}, bf16[128,1152]{1,0:T(8,128)(2,1)}, u32[]{:S(2)}, u32[]{:S(2)}) collective-permute-start(bf16[128,1152]{1,0:T(8,128)(2,1)} %collective-permute-done.19.refs_2_), channel_id=1, source_target_pairs={{0,8},{1,9},{2,10},{3,11},{4,12},{5,13},{6,14},{7,15},{8,0},{9,1},... | collective-permute-start | bytes 884744 | tf_op jit(solution)/shard_map/ppermute | solution.py:188
  55.5 2.0 %copy-start.30 = (s32[128]{0:T(128)S(1)}, s32[128]{0:T(128)}, u32[]{:S(2)}) copy-start(s32[128]{0:T(128)} %param.9) | copy-start | bytes 1540
  56.3 17.3 %collective-permute-start.7 = (bf16[128,1152]{1,0:T(8,128)(2,1)}, bf16[128,1152]{1,0:T(8,128)(2,1)S(1)}, u32[]{:S(2)}, u32[]{:S(2)}) collective-permute-start(bf16[128,1152]{1,0:T(8,128)(2,1)} %collective-permute-done.2.refs_2_), channel_id=1, source_target_pairs={{0,8},{1,9},{2,10},{3,11},{4,12},{5,13},{6,14},{7,15},{8,0},{9,1},... | collective-permute-start | bytes 884744 | tf_op jit(solution)/shard_map/ppermute | solution.py:188
  56.8 16.8 %collective-permute-start.9 = (bf16[128,1152]{1,0:T(8,128)(2,1)}, bf16[128,1152]{1,0:T(8,128)(2,1)S(1)}, u32[]{:S(2)}, u32[]{:S(2)}) collective-permute-start(bf16[128,1152]{1,0:T(8,128)(2,1)} %collective-permute-done.8.refs_4_), channel_id=1, source_target_pairs={{0,8},{1,9},{2,10},{3,11},{4,12},{5,13},{6,14},{7,15},{8,0},{9,1},... | collective-permute-start | bytes 884744 | tf_op jit(solution)/shard_map/ppermute | solution.py:188
  57.5 1.0 copy-start.35
  58.5 1.0 copy-start.37
  59.4 3.1 %copy-start.33 = (bf16[128,1152]{1,0:T(8,128)(2,1)S(1)}, bf16[128,1152]{1,0:T(8,128)(2,1)}, u32[]{:S(2)}) copy-start(bf16[128,1152]{1,0:T(8,128)(2,1)} %copy-done.32) | copy-start | bytes 884740
  59.4 3.1 %copy-start.39 = (bf16[128,1152]{1,0:T(8,128)(2,1)S(1)}, bf16[128,1152]{1,0:T(8,128)(2,1)}, u32[]{:S(2)}) copy-start(bf16[128,1152]{1,0:T(8,128)(2,1)} %copy-done.38) | copy-start | bytes 884740
  61.3 2.9 %copy-start.5 = (bf16[128,1152]{1,0:T(8,128)(2,1)S(1)}, bf16[128,1152]{1,0:T(8,128)(2,1)}, u32[]{:S(2)}) copy-start(bf16[128,1152]{1,0:T(8,128)(2,1)} %copy-done.4) | copy-start | bytes 884740
  61.3 3.0 %copy-start.9 = (bf16[128,1152]{1,0:T(8,128)(2,1)S(1)}, bf16[128,1152]{1,0:T(8,128)(2,1)}, u32[]{:S(2)}) copy-start(bf16[128,1152]{1,0:T(8,128)(2,1)} %copy-done.8) | copy-start | bytes 884740
  61.3 3.0 %copy-start.17 = (bf16[128,1152]{1,0:T(8,128)(2,1)S(1)}, bf16[128,1152]{1,0:T(8,128)(2,1)}, u32[]{:S(2)}) copy-start(bf16[128,1152]{1,0:T(8,128)(2,1)} %copy-done.16) | copy-start | bytes 884740
  61.3 3.0 %copy-start.21 = (bf16[128,1152]{1,0:T(8,128)(2,1)S(1)}, bf16[128,1152]{1,0:T(8,128)(2,1)}, u32[]{:S(2)}) copy-start(bf16[128,1152]{1,0:T(8,128)(2,1)} %copy-done.20) | copy-start | bytes 884740
  61.3 3.0 %copy-start.29 = (bf16[128,1152]{1,0:T(8,128)(2,1)S(1)}, bf16[128,1152]{1,0:T(8,128)(2,1)}, u32[]{:S(2)}) copy-start(bf16[128,1152]{1,0:T(8,128)(2,1)} %copy-done.28) | copy-start | bytes 884740
  62.0 14.5 %collective-permute-start.6 = (bf16[128,1152]{1,0:T(8,128)(2,1)}, bf16[128,1152]{1,0:T(8,128)(2,1)S(1)}, u32[]{:S(2)}, u32[]{:S(2)}) collective-permute-start(bf16[128,1152]{1,0:T(8,128)(2,1)} %collective-permute-done.3.refs_2_), channel_id=1, source_target_pairs={{0,8},{1,9},{2,10},{3,11},{4,12},{5,13},{6,14},{7,15},{8,0},{9,1},... | collective-permute-start | bytes 884744 | tf_op jit(solution)/shard_map/ppermute | solution.py:188
  62.0 16.5 %collective-permute-start.21 = (bf16[128,1152]{1,0:T(8,128)(2,1)}, bf16[128,1152]{1,0:T(8,128)(2,1)S(1)}, u32[]{:S(2)}, u32[]{:S(2)}) collective-permute-start(bf16[128,1152]{1,0:T(8,128)(2,1)} %collective-permute-done.20.refs_2_), channel_id=1, source_target_pairs={{0,8},{1,9},{2,10},{3,11},{4,12},{5,13},{6,14},{7,15},{8,0},{9,1},... | collective-permute-start | bytes 884744 | tf_op jit(solution)/shard_map/ppermute | solution.py:188
  64.2 17.9 %collective-permute-start.5 = (bf16[128,1152]{1,0:T(8,128)(2,1)S(1)}, bf16[128,1152]{1,0:T(8,128)(2,1)S(1)}, u32[]{:S(2)}, u32[]{:S(2)}) collective-permute-start(bf16[128,1152]{1,0:T(8,128)(2,1)S(1)} %copy-done.5), channel_id=1, source_target_pairs={{0,8},{1,9},{2,10},{3,11},{4,12},{5,13},{6,14},{7,15},{8,0},{9,1},... | collective-permute-start | bytes 884744 | tf_op jit(solution)/shard_map/ppermute | solution.py:188
  64.3 2.3 %copy-start.7 = (bf16[128,1152]{1,0:T(8,128)(2,1)S(1)}, bf16[128,1152]{1,0:T(8,128)(2,1)}, u32[]{:S(2)}) copy-start(bf16[128,1152]{1,0:T(8,128)(2,1)} %copy-done.6) | copy-start | bytes 884740
  64.4 2.3 %copy-start.11 = (bf16[128,1152]{1,0:T(8,128)(2,1)S(1)}, bf16[128,1152]{1,0:T(8,128)(2,1)}, u32[]{:S(2)}) copy-start(bf16[128,1152]{1,0:T(8,128)(2,1)} %copy-done.10) | copy-start | bytes 884740
  64.4 2.3 %copy-start.13 = (bf16[128,1152]{1,0:T(8,128)(2,1)S(1)}, bf16[128,1152]{1,0:T(8,128)(2,1)}, u32[]{:S(2)}) copy-start(bf16[128,1152]{1,0:T(8,128)(2,1)} %copy-done.12) | copy-start | bytes 884740
  64.4 2.3 %copy-start.19 = (bf16[128,1152]{1,0:T(8,128)(2,1)S(1)}, bf16[128,1152]{1,0:T(8,128)(2,1)}, u32[]{:S(2)}) copy-start(bf16[128,1152]{1,0:T(8,128)(2,1)} %copy-done.18) | copy-start | bytes 884740
  66.7 2.5 %copy-start.15 = (bf16[128,1152]{1,0:T(8,128)(2,1)S(1)}, bf16[128,1152]{1,0:T(8,128)(2,1)}, u32[]{:S(2)}) copy-start(bf16[128,1152]{1,0:T(8,128)(2,1)} %copy-done.14) | copy-start | bytes 884740
  66.7 2.5 %copy-start.23 = (bf16[128,1152]{1,0:T(8,128)(2,1)S(1)}, bf16[128,1152]{1,0:T(8,128)(2,1)}, u32[]{:S(2)}) copy-start(bf16[128,1152]{1,0:T(8,128)(2,1)} %copy-done.22) | copy-start | bytes 884740
  66.7 2.5 %copy-start.25 = (bf16[128,1152]{1,0:T(8,128)(2,1)S(1)}, bf16[128,1152]{1,0:T(8,128)(2,1)}, u32[]{:S(2)}) copy-start(bf16[128,1152]{1,0:T(8,128)(2,1)} %copy-done.24) | copy-start | bytes 884740
  66.7 2.5 %copy-start.27 = (bf16[128,1152]{1,0:T(8,128)(2,1)S(1)}, bf16[128,1152]{1,0:T(8,128)(2,1)}, u32[]{:S(2)}) copy-start(bf16[128,1152]{1,0:T(8,128)(2,1)} %copy-done.26) | copy-start | bytes 884740
  80.5 34.7 %collective-permute-start.32 = (f32[128,1152]{1,0:T(8,128)S(1)}, f32[128,1152]{1,0:T(8,128)}, u32[]{:S(2)}, u32[]{:S(2)}) collective-permute-start(f32[128,1152]{1,0:T(8,128)S(1)} %get-tuple-element.55), channel_id=1, source_target_pairs={{0,1},{1,0},{2,3},{3,2},{4,5},{5,4},{6,7},{7,6},{8,9},{9,8},{10,11... | collective-permute-start | bytes 1769480 | tf_op jit(solution)/shard_map/ppermute | solution.py:188
  82.1 33.1 %copy-start.1 = (bf16[128,1152]{1,0:T(8,128)(2,1)S(1)}, bf16[128,1152]{1,0:T(8,128)(2,1)}, u32[]{:S(2)}) copy-start(bf16[128,1152]{1,0:T(8,128)(2,1)} %values.3) | copy-start | bytes 884740
  83.7 33.7 %collective-permute-start.16 = (f32[128,1152]{1,0:T(8,128)S(1)}, f32[128,1152]{1,0:T(8,128)S(1)}, u32[]{:S(2)}, u32[]{:S(2)}) collective-permute-start(f32[128,1152]{1,0:T(8,128)S(1)} %get-tuple-element.45), channel_id=1, source_target_pairs={{0,16},{1,17},{2,18},{3,19},{4,20},{5,21},{6,22},{7,23},{8,24},{9,... | collective-permute-start | bytes 1769480 | tf_op jit(solution)/shard_map/ppermute | solution.py:188
  84.2 15.1 %collective-permute-start.33 = (f32[8,128]{1,0:T(8,128)S(1)}, f32[8,128]{1,0:T(8,128)S(1)}, u32[]{:S(2)}, u32[]{:S(2)}) collective-permute-start(f32[8,128]{1,0:T(8,128)S(1)} %get-tuple-element.56), channel_id=1, source_target_pairs={{0,16},{1,17},{2,18},{3,19},{4,20},{5,21},{6,22},{7,23},{8,24},{9,... | collective-permute-start | bytes 12296 | tf_op jit(solution)/shard_map/ppermute | solution.py:188
  99.3 3.6 %collective-permute-start.34 = (f32[8,128]{1,0:T(8,128)S(1)}, f32[8,128]{1,0:T(8,128)S(1)}, u32[]{:S(2)}, u32[]{:S(2)}) collective-permute-start(f32[8,128]{1,0:T(8,128)S(1)} %add.43), channel_id=1, source_target_pairs={{0,1},{1,0},{2,3},{3,2},{4,5},{5,4},{6,7},{7,6},{8,9},{9,8},{10,11... | collective-permute-start | bytes 12296 | tf_op jit(solution)/shard_map/ppermute | solution.py:188
  102.9 1.2 collective-permute-start.35
  104.1 5.4 %collective-permute-start.36 = (f32[8,128]{1,0:T(8,128)S(1)}, f32[8,128]{1,0:T(8,128)S(1)}, u32[]{:S(2)}, u32[]{:S(2)}) collective-permute-start(f32[8,128]{1,0:T(8,128)S(1)} %add.45), channel_id=1, source_target_pairs={{0,2},{1,3},{2,4},{3,5},{4,6},{5,7},{6,0},{7,1},{8,10},{9,11},{10,... | collective-permute-start | bytes 12296 | tf_op jit(solution)/shard_map/ppermute | solution.py:188
  109.5 4.5 %collective-permute-start.37 = (f32[8,128]{1,0:T(8,128)S(1)}, f32[8,128]{1,0:T(8,128)S(1)}, u32[]{:S(2)}, u32[]{:S(2)}) collective-permute-start(f32[8,128]{1,0:T(8,128)S(1)} %add.46), channel_id=1, source_target_pairs={{0,4},{1,5},{2,6},{3,7},{4,0},{5,1},{6,2},{7,3},{8,12},{9,13},{10,... | collective-permute-start | bytes 12296 | tf_op jit(solution)/shard_map/ppermute | solution.py:188
  115.3 2.2 %copy-start.3 = (bf16[128,1152]{1,0:T(8,128)(2,1)S(1)}, bf16[128,1152]{1,0:T(8,128)(2,1)}, u32[]{:S(2)}) copy-start(bf16[128,1152]{1,0:T(8,128)(2,1)} %values.2) | copy-start | bytes 884740
  (14 other events, 10.0 us)
where the time goes:
time: 120 us
  waiting for transfers between devices  52.4 us (44%)
  Pallas kernels  24.5 us (20%)
  starting transfers between devices  22.1 us (18%)
  local copies, waits for them, and re-layouts  16 us (13%)
  between operations  4.2 us (4%)
    ppermute x38, waiting for transfers between devices, shift(): return lax.ppermute(array, AXES, pairs)  52.4 us
    ppermute x38, starting transfers between devices, shift(): return lax.ppermute(array, AXES, pairs)  22.1 us
    pallas_call x10, Pallas kernels, terms(): pl.pallas_call(kernel, out_shape=shapes, in_specs=[SMEM] * 3 + [VMEM] * (...  21 us
    unnamed x80, local copies, waits for them, and re-layouts  16 us
    pallas_call x2, Pallas kernels, project(): pl.pallas_call(functools.partial(project_kernel, len(parts)), out_shape=j...  3.26 us
  transfers between devices with their start and end apart: 38, of which 14 were waited for; matrix products, arithmetic and copies ran while one was open for 1% of the time, Pallas kernels for 19%

commit v1 on v0

v1 whole, which is shorter than its diff:
```python
import functools

import jax
import jax.numpy as jnp
from jax import lax
from jax.experimental import pallas as pl
from jax.experimental.pallas import tpu as pltpu
from jax.sharding import PartitionSpec as P

EPSILON = 1e-06
AXES = ("group", "dev")
VMEM = pl.BlockSpec(memory_space=pltpu.VMEM)
PARAMS = pltpu.CompilerParams(vmem_limit_bytes=16 << 20)


def unit_of(values):
    wide = values.astype(jnp.float32)
    recip = lax.rsqrt(jnp.sum(wide * wide, axis=1, keepdims=True) + EPSILON)
    return wide * recip, recip


def normalize_kernel(values, half):
    half[...] = unit_of(values[...])[0].astype(jnp.bfloat16)


def normalize(values):
    return pl.pallas_call(
        normalize_kernel,
        out_shape=jax.ShapeDtypeStruct(values.shape, jnp.bfloat16),
        in_specs=[VMEM],
        out_specs=VMEM,
        compiler_params=PARAMS,
    )(values)


def project_kernel(count, settings, values, *refs):
    parts, out = refs[:count], refs[count]
    unit, recip = unit_of(values[...])
    total = parts[0][...]
    for part in parts[1:]:
        total = total + part[...]
    grad = settings[0:1, 0:1] * total
    out[...] = recip * (grad - unit * jnp.sum(unit * grad, axis=1, keepdims=True))


def project(values, settings, parts):
    return pl.pallas_call(
        functools.partial(project_kernel, len(parts)),
        out_shape=jax.ShapeDtypeStruct(values.shape, jnp.float32),
        in_specs=[VMEM] * (2 + len(parts)),
        out_specs=VMEM,
        compiler_params=PARAMS,
    )(settings, values, *parts)


def terms_kernel(
    own_count, block_count, places, pairs, first, with_loss, settings, ids, *refs
):
    refs = list(refs)
    own = [refs.pop(0) for _ in range(own_count)]
    blocks = [refs.pop(0) for _ in range(block_count)]
    targets = [refs.pop(0) for _ in range(own_count)]
    carried = [] if first else [refs.pop(0) for _ in range(own_count + with_loss)]
    sums = [refs.pop(0) for _ in range(own_count)]
    losses = refs.pop(0) if with_loss else None
    own_rows, block_rows = own[0].shape[0], blocks[0].shape[0]
    columns = {}
    for a, _ in sorted(pairs):
        if a not in columns:
            spread = jnp.broadcast_to(targets[a][...], (own_rows, own_rows))
            columns[a] = jnp.transpose(spread)[:, :1]
    if with_loss:
        loss = jnp.zeros((8, 128), jnp.float32) if first else carried[own_count][...]

    def weigh(a, b, dot):
        nonlocal loss
        logits = settings[0:1, :block_rows] * dot + settings[4:5, :block_rows]
        hit = None
        if (a, b) in pairs:
            at, offset = places[b]
            hit = columns[a] == ids[at : at + 1, offset : offset + block_rows]
            logits = jnp.where(hit, -logits, logits)
        small = jnp.exp(-jnp.abs(logits))
        inverse = 1.0 / (1.0 + small)
        weight = jnp.where(logits >= 0, inverse, small * inverse)
        if with_loss:
            part = jnp.maximum(logits, 0.0) + jnp.log1p(small)
            part = jnp.sum(part.reshape(own_rows // 8, 8, block_rows), axis=0)
            for lane in range(0, block_rows, 128):
                loss = loss + part[:, lane : lane + 128]
        if hit is not None:
            weight = jnp.where(hit, -weight, weight)
        return weight.astype(jnp.bfloat16)

    own_all = jnp.concatenate([ref[...] for ref in own], axis=0) if own_count > 1 else own[0][...]
    weights = [[] for _ in own]
    chosen = []
    group = max(1, 256 // block_rows)
    for start in range(0, block_count, group):
        some = range(start, min(start + group, block_count))
        block_all = jnp.concatenate([blocks[b][...] for b in some], axis=0)
        chosen.append(block_all)
        dots = lax.dot_general(
            own_all, block_all, (((1,), (1,)), ((), ())), preferred_element_type=jnp.float32
        )
        for a in range(own_count):
            for n, b in enumerate(some):
                dot = dots[
                    a * own_rows : (a + 1) * own_rows, n * block_rows : (n + 1) * block_rows
                ]
                weights[a].append(weigh(a, b, dot))
    weight_all = jnp.concatenate([jnp.concatenate(row, axis=1) for row in weights], axis=0)
    block_all = jnp.concatenate(chosen, axis=0)
    term = jnp.dot(weight_all, block_all, preferred_element_type=jnp.float32)
    for a in range(own_count):
        part = term[a * own_rows : (a + 1) * own_rows]
        sums[a][...] = part if first else carried[a][...] + part
    if with_loss:
        losses[...] = loss


def terms(own, blocks, places, targets, pairs, ids, settings, carried, with_loss):
    rows, width = own[0].shape
    first = carried is None
    kernel = functools.partial(
        terms_kernel, len(own), len(blocks), tuple(places), frozenset(pairs), first, with_loss
    )
    shapes = [jax.ShapeDtypeStruct((rows, width), jnp.float32)] * len(own)
    if with_loss:
        shapes = shapes + [jax.ShapeDtypeStruct((8, 128), jnp.float32)]
    operands = [settings, ids, *own, *blocks, *targets]
    base = len(operands)
    aliases = {}
    if not first:
        operands += carried
        aliases = {base + n: n for n in range(len(carried))}
    size = len(own) * len(blocks) * rows * blocks[0].shape[0]
    return pl.pallas_call(
        kernel,
        out_shape=shapes,
        in_specs=[VMEM] * len(operands),
        out_specs=[VMEM] * len(shapes),
        input_output_aliases=aliases,
        cost_estimate=pl.CostEstimate(
            flops=4 * size * width,
            transcendentals=3 * size,
            bytes_accessed=(2 * len(blocks) + 10 * len(own)) * rows * width,
        ),
        compiler_params=PARAMS,
    )(*operands)


def factor(count):
    best = 1
    while (best + 1) ** 2 <= count:
        best += 1
    while count % best:
        best -= 1
    return count // best, best


def per_device(images, texts, lang_order, position, logit_scale, logit_bias):
    rows, _ = images.shape
    dev_count = lax.axis_size("dev")
    group_count = lax.axis_size("group")
    cores = 2 if group_count % 2 == 0 else 1
    wide = group_count // cores
    slow, fast = factor(dev_count)
    sizes = (wide, cores, slow, fast)

    def permuted(array, dim, move):
        pairs = []
        for index in range(group_count * dev_count):
            place, rest = [], index
            for size in reversed(sizes):
                place.insert(0, rest % size)
                rest //= size
            place[dim] = move(place[dim])
            target = 0
            for size, at in zip(sizes, place):
                target = target * size + at
            pairs.append((index, target))
        return lax.ppermute(array, AXES, pairs)

    def shift(array, dim, by):
        return permuted(array, dim, lambda at: (at + by) % sizes[dim])

    def exchange(array, dim, by):
        return permuted(array, dim, lambda at: at ^ by)

    dev_index = lax.axis_index("dev")
    slow_index, fast_index = dev_index // fast, dev_index % fast
    offsets = jnp.arange(slow * fast, dtype=jnp.int32)
    bases = (slow_index - offsets // fast) % slow * fast + (fast_index - offsets % fast) % fast
    ids = (rows * bases[:, None] + jnp.arange(rows, dtype=jnp.int32)[None, :]).astype(jnp.int32)
    settings = jnp.concatenate(
        [
            jnp.broadcast_to(logit_scale[:, None], (4, rows)),
            jnp.broadcast_to(logit_bias[:, None], (4, rows)),
        ],
        axis=0,
    )

    txt_half = normalize(texts)
    img_half = normalize(images)

    def spread(block, dim):
        blocks = [block]
        for _ in range(sizes[dim] - 1):
            blocks.append(shift(blocks[-1], dim, 1))
        return blocks

    def with_cores(blocks):
        out = []
        for block in blocks:
            out.append([block] + [shift(block, 1, by) for by in range(1, cores)])
        return out

    img_targets = [position.reshape(1, rows)] * wide
    txt_targets = spread(lang_order.reshape(1, rows), 3)

    def txt_blocks(block):
        return with_cores(spread(block, 3))

    def img_blocks(block):
        return with_cores(spread(block, 0))

    end = slow - 1
    middle = rows // 2
    txt_line, img_line, txt_sets, img_sets = [txt_half], [img_half], [], []
    for step in range(slow):
        if step:
            txt_line.append(shift(txt_line[-1], 2, 1))
        txt_sets.append(txt_blocks(txt_line[-1]))
        if step < end:
            if step:
                img_line.append(shift(img_line[-1], 2, 1))
            img_sets.append(img_blocks(img_line[-1]))
    first = shift(img_line[-1][:middle], 2, 1)
    second = shift(img_line[-1][middle:], 2, 1)
    first_set, second_set = img_blocks(first), img_blocks(second)
    img_own = [cores_of[0] for cores_of in img_sets[0]]
    txt_own = [cores_of[0] for cores_of in txt_sets[0]]

    def image_terms(sums, parts):
        blocks, places, pairs = [], [], []
        for step, at in parts:
            pairs.append((0, len(blocks)))
            for block in txt_sets[step][at]:
                blocks.append(block)
                places.append((step * fast + at, 0))
        return terms(img_own, blocks, places, img_targets, pairs, ids, settings, sums, True)

    def text_terms(sums, parts):
        blocks, places, pairs = [], [], []
        for cores_of, step, at, offset in parts:
            if at == 0:
                pairs += [(a, len(blocks)) for a in range(fast)]
            for block in cores_of:
                blocks.append(block)
                places.append((step * fast, offset))
        return terms(txt_own, blocks, places, txt_targets, pairs, ids, settings, sums, False)

    img_sums = txt_sums = None
    for step in range(end):
        parts = [(step, at) for at in range(fast)]
        if step == end - 1:
            parts.append((end, 0))
        img_sums = image_terms(img_sums, parts)
        parts = [(img_sets[step][at], step, at, 0) for at in range(wide)]
        txt_sums = text_terms(txt_sums, parts)
    halves = [(first_set, 0), (second_set, middle)]
    txt_sums = text_terms(txt_sums, [(half[0], end, 0, offset) for half, offset in halves])
    if fast > 1:
        img_sums = image_terms(img_sums, [(end, at) for at in range(1, fast)])
    if wide > 1:
        parts = [(half[at], end, at, offset) for at in range(1, wide) for half, offset in halves]
        txt_sums = text_terms(txt_sums, parts)

    loss = img_sums[wide]
    for dim in (0, 3, 1, 2):
        size = sizes[dim]
        if size & (size - 1) == 0:
            by = 1
            while by < size:
                loss = loss + exchange(loss, dim, by)
                by = 2 * by
        else:
            loss = sum((shift(loss, dim, by) for by in range(1, size)), loss)
    total = jnp.float32(rows * dev_count * group_count)
    loss = (jnp.sum(loss) / (total * total)).reshape(1)
    img_parts = [img_sums[0]] + [shift(img_sums[a], 0, -a) for a in range(1, wide)]
    txt_parts = [txt_sums[0]] + [shift(txt_sums[a], 3, -a) for a in range(1, fast)]
    image_grad = project(images, settings, img_parts)
    text_grad = project(texts, settings, txt_parts)
    return (image_grad, text_grad, loss)


def solution(mesh):
    return jax.shard_map(
        per_device,
        mesh=mesh,
        in_specs=(
            P(AXES, None),
            P(AXES, None),
            P(AXES),
            P(AXES),
            P(),
            P(),
        ),
        out_specs=(P(AXES, None), P(AXES, None), P()),
        check_vma=False,
    )
```

time: 120 us -> 117 us (0.975)
  Pallas kernels: 24.5 us -> 17.1 us
  waiting for transfers between devices: 52.4 us -> 59.6 us
  local copies, waits for them, and re-layouts: 16 us -> 13.7 us
    pallas_call x11, Pallas kernels: 21.2 us -> 13.8 us  [the longest x9 13.5 us: terms(): pl.pallas_call(kernel, out_shape=shapes, in_specs=[VMEM] * len(operands),...]
    ppermute x38 -> x42, waiting for transfers between devices: 52.4 us -> 59.6 us  [permuted(): return lax.ppermute(array, AXES, pairs)]
    unnamed x80, local copies, waits for them, and re-layouts: 16 us -> 13.6 us
    ppermute x38 -> x42, starting transfers between devices: 22.1 us -> 21.4 us  [permuted(): return lax.ppermute(array, AXES, pairs)]
  transfers between devices with their start and end apart: 38 -> 42, of which waited for: 14 -> 17; matrix products, arithmetic and copies ran while one was open for 1% -> 1% of each run, Pallas kernels for 19% -> 14%
where the time goes in v1:
time: 117 us
  waiting for transfers between devices  59.6 us (51%)
  starting transfers between devices  21.4 us (18%)
  Pallas kernels  17.1 us (15%)
  local copies, waits for them, and re-layouts  13.7 us (12%)
  between operations  4.17 us (4%)
    ppermute x42, waiting for transfers between devices, permuted(): return lax.ppermute(array, AXES, pairs)  59.6 us
    ppermute x42, starting transfers between devices, permuted(): return lax.ppermute(array, AXES, pairs)  21.4 us
    unnamed x80, local copies, waits for them, and re-layouts  13.6 us
    pallas_call x9, Pallas kernels, terms(): pl.pallas_call(kernel, out_shape=shapes, in_specs=[VMEM] * len(operands),...  13.5 us
    pallas_call x2, Pallas kernels, project(): pl.pallas_call(functools.partial(project_kernel, len(parts)), out_shape=j...  3.27 us
  transfers between devices with their start and end apart: 42, of which 17 were waited for; matrix products, arithmetic and copies ran while one was open for 1% of the time, Pallas kernels for 14%

profile of v1, /device:TPU:0, one launch (start us, length us, event | category | flops | bytes accessed | tf_op | source)
XLA Modules:
  0.0 116.6 jit_solution(11332306913843716951)
XLA Ops:
  0.6 0.6 copy-done.33
  1.3 3.0 %collective-permute-start.25 = (s32[1,128]{1,0:T(1,128)S(1)}, s32[1,128]{1,0:T(1,128)S(1)}, u32[]{:S(2)}, u32[]{:S(2)}) collective-permute-start(s32[1,128]{1,0:T(1,128)S(1)} %bitcast.15), channel_id=1, source_target_pairs={{0,1},{1,0},{2,3},{3,2},{4,5},{5,4},{6,7},{7,6},{8,9},{9,8},{10,11... | collective-permute-start | bytes 1544 | tf_op jit(solution)/shard_map/ppermute | solution.py:183
  4.3 1.0 copy-done
  5.5 0.7 copy-done.2
  6.4 1.6 %collective-permute-start = (bf16[128,1152]{1,0:T(8,128)(2,1)S(1)}, bf16[128,1152]{1,0:T(8,128)(2,1)S(1)}, u32[]{:S(2)}, u32[]{:S(2)}) collective-permute-start(bf16[128,1152]{1,0:T(8,128)(2,1)S(1)} %shard_map.85.refs_0_.refs_2_), channel_id=1, source_target_pairs={{0,16},{1,17},{2,18},{3,19},{4,20},{5,21},{6,22},{7,23},{8,24},{9,... | collective-permute-start | bytes 884744 | tf_op jit(solution)/shard_map/ppermute | solution.py:183
  7.9 1.6 %collective-permute-start.1 = (bf16[128,1152]{1,0:T(8,128)(2,1)S(1)}, bf16[128,1152]{1,0:T(8,128)(2,1)S(1)}, u32[]{:S(2)}, u32[]{:S(2)}) collective-permute-start(bf16[128,1152]{1,0:T(8,128)(2,1)S(1)} %shard_map.86.refs_2_.refs_0_), channel_id=1, source_target_pairs={{0,2},{1,3},{2,4},{3,5},{4,6},{5,7},{6,0},{7,1},{8,10},{9,11},{10,... | collective-permute-start | bytes 884744 | tf_op jit(solution)/shard_map/ppermute | solution.py:183
  9.5 1.6 %collective-permute-start.17 = (bf16[128,1152]{1,0:T(8,128)(2,1)S(1)}, bf16[128,1152]{1,0:T(8,128)(2,1)S(1)}, u32[]{:S(2)}, u32[]{:S(2)}) collective-permute-start(bf16[128,1152]{1,0:T(8,128)(2,1)S(1)} %shard_map.85.refs_0_.refs_2_), channel_id=1, source_target_pairs={{0,2},{1,3},{2,4},{3,5},{4,6},{5,7},{6,0},{7,1},{8,10},{9,11},{10,... | collective-permute-start | bytes 884744 | tf_op jit(solution)/shard_map/ppermute | solution.py:183
  11.1 2.9 %collective-permute-done.14.refs_4_.refs_1_ = bf16[128,1152]{1,0:T(8,128)(2,1)S(1)} collective-permute-done((bf16[128,1152]{1,0:T(8,128)(2,1)S(1)}, bf16[128,1152]{1,0:T(8,128)(2,1)S(1)}, u32[]{:S(2)}, u32[]{:S(2)}) %collective-permute-start.14) | collective-permute-done | bytes 294944 | tf_op jit(solution)/shard_map/ppermute | solution.py:183
  13.9 1.0 collective-permute-done.refs_1_.refs_4_
  14.9 4.7 %collective-permute-done.1.refs_2_ = bf16[128,1152]{1,0:T(8,128)(2,1)S(1)} collective-permute-done((bf16[128,1152]{1,0:T(8,128)(2,1)S(1)}, bf16[128,1152]{1,0:T(8,128)(2,1)S(1)}, u32[]{:S(2)}, u32[]{:S(2)}) %collective-permute-start.1) | collective-permute-done | bytes 294944 | tf_op jit(solution)/shard_map/ppermute | solution.py:183
  19.6 1.3 %collective-permute-start.11 = (bf16[128,1152]{1,0:T(8,128)(2,1)S(1)}, bf16[128,1152]{1,0:T(8,128)(2,1)S(1)}, u32[]{:S(2)}, u32[]{:S(2)}) collective-permute-start(bf16[128,1152]{1,0:T(8,128)(2,1)S(1)} %collective-permute-done.1.refs_2_), channel_id=1, source_target_pairs={{0,1},{1,0},{2,3},{3,2},{4,5},{5,4},{6,7},{7,6},{8,9},{9,8},{10,11... | collective-permute-start | bytes 884744 | tf_op jit(solution)/shard_map/ppermute | solution.py:183
  20.9 3.4 %collective-permute-done.17.refs_2_ = bf16[128,1152]{1,0:T(8,128)(2,1)S(1)} collective-permute-done((bf16[128,1152]{1,0:T(8,128)(2,1)S(1)}, bf16[128,1152]{1,0:T(8,128)(2,1)S(1)}, u32[]{:S(2)}, u32[]{:S(2)}) %collective-permute-start.17) | collective-permute-done | bytes 294944 | tf_op jit(solution)/shard_map/ppermute | solution.py:183
  24.3 0.7 copy-done.34
  25.0 1.3 %collective-permute-start.2 = (bf16[128,1152]{1,0:T(8,128)(2,1)S(1)}, bf16[128,1152]{1,0:T(8,128)(2,1)}, u32[]{:S(2)}, u32[]{:S(2)}) collective-permute-start(bf16[128,1152]{1,0:T(8,128)(2,1)S(1)} %collective-permute-done.1.refs_2_), channel_id=1, source_target_pairs={{0,2},{1,3},{2,4},{3,5},{4,6},{5,7},{6,0},{7,1},{8,10},{9,11},{10,... | collective-permute-start | bytes 884744 | tf_op jit(solution)/shard_map/ppermute | solution.py:183
  26.3 0.7 copy-done.36
  27.0 0.5 collective-permute-start.32
  27.6 0.7 copy-done.8
  28.3 0.7 copy-done.12
  29.5 6.5 %collective-permute-done.18.refs_2_ = bf16[128,1152]{1,0:T(8,128)(2,1)S(1)} collective-permute-done((bf16[128,1152]{1,0:T(8,128)(2,1)S(1)}, bf16[128,1152]{1,0:T(8,128)(2,1)S(1)}, u32[]{:S(2)}, u32[]{:S(2)}) %collective-permute-start.18) | collective-permute-done | bytes 294944 | tf_op jit(solution)/shard_map/ppermute | solution.py:183
  36.0 0.8 copy-done.10
  36.7 3.1 %collective-permute-done.2.refs_2_ = bf16[128,1152]{1,0:T(8,128)(2,1)} collective-permute-done((bf16[128,1152]{1,0:T(8,128)(2,1)S(1)}, bf16[128,1152]{1,0:T(8,128)(2,1)}, u32[]{:S(2)}, u32[]{:S(2)}) %collective-permute-start.2) | collective-permute-done | bytes 294944 | tf_op jit(solution)/shard_map/ppermute | solution.py:183
  39.9 0.7 copy-done.38
  40.6 1.0 collective-permute-start.3
  41.6 0.7 copy-done.16
  42.3 0.7 collective-permute-start.7
  43.0 5.4 %collective-permute-done.19.refs_2_ = bf16[64,1152]{1,0:T(8,128)(2,1)S(1)} collective-permute-done((bf16[64,1152]{1,0:T(8,128)(2,1)S(1)}, bf16[64,1152]{1,0:T(8,128)(2,1)S(1)}, u32[]{:S(2)}, u32[]{:S(2)}) %collective-permute-start.19) | collective-permute-done | bytes 147488 | tf_op jit(solution)/shard_map/ppermute | solution.py:183
  48.4 0.7 copy-done.14
  49.1 2.3 %collective-permute-done.22.refs_4_ = bf16[64,1152]{1,0:T(8,128)(2,1)S(1)} collective-permute-done((bf16[64,1152]{1,0:T(8,128)(2,1)S(1)}, bf16[64,1152]{1,0:T(8,128)(2,1)S(1)}, u32[]{:S(2)}, u32[]{:S(2)}) %collective-permute-start.22) | collective-permute-done | bytes 147488 | tf_op jit(solution)/shard_map/ppermute | solution.py:183
  51.4 0.5 collective-permute-start.29
  51.9 0.7 copy-done.18
  52.7 2.0 %collective-permute-done.3.refs_6_ = bf16[128,1152]{1,0:T(8,128)(2,1)} collective-permute-done((bf16[128,1152]{1,0:T(8,128)(2,1)}, bf16[128,1152]{1,0:T(8,128)(2,1)}, u32[]{:S(2)}, u32[]{:S(2)}) %collective-permute-start.3) | collective-permute-done | bytes 294944 | tf_op jit(solution)/shard_map/ppermute | solution.py:183
  54.7 0.5 collective-permute-start.20
  55.2 0.7 copy-done.24
  57.2 0.7 copy-done.22
  58.2 1.3 %collective-permute-done.29.refs_4_ = bf16[128,1152]{1,0:T(8,128)(2,1)} collective-permute-done((bf16[128,1152]{1,0:T(8,128)(2,1)S(1)}, bf16[128,1152]{1,0:T(8,128)(2,1)}, u32[]{:S(2)}, u32[]{:S(2)}) %collective-permute-start.29) | collective-permute-done | bytes 294944 | tf_op jit(solution)/shard_map/ppermute | solution.py:183
  60.0 0.7 copy-done.26
  60.7 0.7 copy-done.20
  61.4 0.7 collective-permute-start.4
  62.1 0.7 copy-done.30
  63.2 0.7 copy-done.28
  64.0 0.9 collective-permute-done.23.refs_4_
  65.5 0.7 copy-done.32
  66.1 1.3 %shard_map.87 = (f32[128,1152]{1,0:T(8,128)S(1)}, f32[128,1152]{1,0:T(8,128)S(1)}, f32[8,128]{1,0:T(8,128)S(1)}) custom-call(f32[8,128]{1,0:T(8,128)S(1)} %concatenate.6.settings, s32[8,128]{1,0:T(8,128)S(1)} %iota_add_fusion.ids, bf16[128,1152]{1,0:T(8,128)(2,1)S(1)} %shard_map.85.refs_0_.refs_2_, ...), custom_call_target="tpu_custom_call" | custom-call | flops 603979776 | bytes 4128768 | tf_op jit(solution)/shard_map/pallas_call | solution.py:138
  67.5 1.1 shard_map.92
  68.6 1.5 %collective-permute-done.4.refs_2_ = bf16[128,1152]{1,0:T(8,128)(2,1)S(1)} collective-permute-done((bf16[128,1152]{1,0:T(8,128)(2,1)}, bf16[128,1152]{1,0:T(8,128)(2,1)S(1)}, u32[]{:S(2)}, u32[]{:S(2)}) %collective-permute-start.4) | collective-permute-done | bytes 294944 | tf_op jit(solution)/shard_map/ppermute | solution.py:183
  70.7 1.1 shard_map.93
  71.9 1.3 %shard_map.88 = (f32[128,1152]{1,0:T(8,128)S(1)}, f32[128,1152]{1,0:T(8,128)S(1)}, f32[8,128]{1,0:T(8,128)S(1)}) custom-call(f32[8,128]{1,0:T(8,128)S(1)} %concatenate.6.settings, s32[8,128]{1,0:T(8,128)S(1)} %iota_add_fusion.ids, bf16[128,1152]{1,0:T(8,128)(2,1)S(1)} %shard_map.85.refs_0_.refs_2_, ...), custom_call_target="tpu_custom_call", output_to_operand_aliasing={{0}: (10, {}), {1}: (11, {}), {2}: (12, {})} | custom-call | flops 603979776 | bytes 4128768 | tf_op jit(solution)/shard_map/pallas_call | solution.py:138
  73.3 2.1 %shard_map.94 = (f32[128,1152]{1,0:T(8,128)S(1)}, f32[128,1152]{1,0:T(8,128)S(1)}) custom-call(f32[8,128]{1,0:T(8,128)S(1)} %concatenate.6.settings, s32[8,128]{1,0:T(8,128)S(1)} %iota_add_fusion.ids, bf16[128,1152]{1,0:T(8,128)(2,1)S(1)} %shard_map.86.refs_2_.refs_0_, ...), custom_call_target="tpu_custom_call", output_to_operand_aliasing={{0}: (10, {}), {1}: (11, {})} | custom-call | flops 603979776 | bytes 4128768 | tf_op jit(solution)/shard_map/pallas_call | solution.py:138
  75.5 1.2 %shard_map.95 = (f32[128,1152]{1,0:T(8,128)S(1)}, f32[128,1152]{1,0:T(8,128)S(1)}) custom-call(f32[8,128]{1,0:T(8,128)S(1)} %concatenate.6.settings, s32[8,128]{1,0:T(8,128)S(1)} %iota_add_fusion.ids, bf16[128,1152]{1,0:T(8,128)(2,1)S(1)} %shard_map.86.refs_2_.refs_0_, ...), custom_call_target="tpu_custom_call", output_to_operand_aliasing={{0}: (10, {}), {1}: (11, {})} | custom-call | flops 301989888 | bytes 4128768 | tf_op jit(solution)/shard_map/pallas_call | solution.py:138
  76.7 1.1 shard_map.96
  77.8 0.8 collective-permute-start.36
  78.7 3.1 %shard_map.89 = (f32[128,1152]{1,0:T(8,128)S(1)}, f32[128,1152]{1,0:T(8,128)S(1)}, f32[8,128]{1,0:T(8,128)S(1)}) custom-call(f32[8,128]{1,0:T(8,128)S(1)} %concatenate.6.settings, s32[8,128]{1,0:T(8,128)S(1)} %iota_add_fusion.ids, bf16[128,1152]{1,0:T(8,128)(2,1)S(1)} %shard_map.85.refs_0_.refs_2_, ...), custom_call_target="tpu_custom_call", output_to_operand_aliasing={{0}: (12, {}), {1}: (13, {}), {2}: (14, {})} | custom-call | flops 905969664 | bytes 4718592 | tf_op jit(solution)/shard_map/pallas_call | solution.py:138
  81.9 1.1 shard_map.90
  82.9 0.6 collective-permute-start.16
  83.5 1.5 %collective-permute-start.37 = (f32[8,128]{1,0:T(8,128)S(1)}, f32[8,128]{1,0:T(8,128)S(1)}, u32[]{:S(2)}, u32[]{:S(2)}) collective-permute-start(f32[8,128]{1,0:T(8,128)S(1)} %get-tuple-element.46), channel_id=1, source_target_pairs={{0,16},{1,17},{2,18},{3,19},{4,20},{5,21},{6,22},{7,23},{8,24},{9,... | collective-permute-start | bytes 12296 | tf_op jit(solution)/shard_map/ppermute | solution.py:183
  85.0 13.0 %collective-permute-done.37 = f32[8,128]{1,0:T(8,128)S(1)} collective-permute-done((f32[8,128]{1,0:T(8,128)S(1)}, f32[8,128]{1,0:T(8,128)S(1)}, u32[]{:S(2)}, u32[]{:S(2)}) %collective-permute-start.37) | collective-permute-done | bytes 4128 | tf_op jit(solution)/shard_map/ppermute | solution.py:183
  98.1 1.2 %collective-permute-start.38 = (f32[8,128]{1,0:T(8,128)S(1)}, f32[8,128]{1,0:T(8,128)S(1)}, u32[]{:S(2)}, u32[]{:S(2)}) collective-permute-start(f32[8,128]{1,0:T(8,128)S(1)} %add.81), channel_id=1, source_target_pairs={{0,1},{1,0},{2,3},{3,2},{4,5},{5,4},{6,7},{7,6},{8,9},{9,8},{10,11... | collective-permute-start | bytes 12296 | tf_op jit(solution)/shard_map/ppermute | solution.py:183
  99.3 2.4 %collective-permute-done.38 = f32[8,128]{1,0:T(8,128)S(1)} collective-permute-done((f32[8,128]{1,0:T(8,128)S(1)}, f32[8,128]{1,0:T(8,128)S(1)}, u32[]{:S(2)}, u32[]{:S(2)}) %collective-permute-start.38) | collective-permute-done | bytes 4128 | tf_op jit(solution)/shard_map/ppermute | solution.py:183
  101.7 1.2 collective-permute-done.39
  102.8 3.6 %collective-permute-done.40 = f32[8,128]{1,0:T(8,128)S(1)} collective-permute-done((f32[8,128]{1,0:T(8,128)S(1)}, f32[8,128]{1,0:T(8,128)S(1)}, u32[]{:S(2)}, u32[]{:S(2)}) %collective-permute-start.40) | collective-permute-done | bytes 4128 | tf_op jit(solution)/shard_map/ppermute | solution.py:183
  106.5 4.5 %collective-permute-done.41 = f32[8,128]{1,0:T(8,128)S(1)} collective-permute-done((f32[8,128]{1,0:T(8,128)S(1)}, f32[8,128]{1,0:T(8,128)S(1)}, u32[]{:S(2)}, u32[]{:S(2)}) %collective-permute-start.41) | collective-permute-done | bytes 4128 | tf_op jit(solution)/shard_map/ppermute | solution.py:183
  111.0 0.6 add_reduce_fusion
  112.2 2.2 %shard_map.97 = f32[128,1152]{1,0:T(8,128)} custom-call(f32[8,128]{1,0:T(8,128)S(1)} %concatenate.6.settings, bf16[128,1152]{1,0:T(8,128)(2,1)S(1)} %copy-done.1, f32[128,1152]{1,0:T(8,128)S(1)} %get-tuple-element.44.refs_0_, f32[128,1152]{1,0:T(8,128)} %collective-permute-done.36.refs_1_), custom_call_target="tpu_custom_call" | custom-call | tf_op jit(solution)/shard_map/pallas_call | solution.py:47
  114.4 1.1 shard_map.91
  (124 shorter events, 3.6 us)
Async XLA Ops:
  1.3 8.2 %collective-permute-start.25 = (s32[1,128]{1,0:T(1,128)S(1)}, s32[1,128]{1,0:T(1,128)S(1)}, u32[]{:S(2)}, u32[]{:S(2)}) collective-permute-start(s32[1,128]{1,0:T(1,128)S(1)} %bitcast.15), channel_id=1, source_target_pairs={{0,1},{1,0},{2,3},{3,2},{4,5},{5,4},{6,7},{7,6},{8,9},{9,8},{10,11... | collective-permute-start | bytes 1544 | tf_op jit(solution)/shard_map/ppermute | solution.py:183
  4.3 1.0 copy-start
  5.4 8.5 %collective-permute-start.14 = (bf16[128,1152]{1,0:T(8,128)(2,1)S(1)}, bf16[128,1152]{1,0:T(8,128)(2,1)S(1)}, u32[]{:S(2)}, u32[]{:S(2)}) collective-permute-start(bf16[128,1152]{1,0:T(8,128)(2,1)S(1)} %shard_map.86.refs_2_.refs_0_), channel_id=1, source_target_pairs={{0,1},{1,0},{2,3},{3,2},{4,5},{5,4},{6,7},{7,6},{8,9},{9,8},{10,11... | collective-permute-start | bytes 884744 | tf_op jit(solution)/shard_map/ppermute | solution.py:183
  6.4 8.5 %collective-permute-start = (bf16[128,1152]{1,0:T(8,128)(2,1)S(1)}, bf16[128,1152]{1,0:T(8,128)(2,1)S(1)}, u32[]{:S(2)}, u32[]{:S(2)}) collective-permute-start(bf16[128,1152]{1,0:T(8,128)(2,1)S(1)} %shard_map.85.refs_0_.refs_2_), channel_id=1, source_target_pairs={{0,16},{1,17},{2,18},{3,19},{4,20},{5,21},{6,22},{7,23},{8,24},{9,... | collective-permute-start | bytes 884744 | tf_op jit(solution)/shard_map/ppermute | solution.py:183
  7.9 11.7 %collective-permute-start.1 = (bf16[128,1152]{1,0:T(8,128)(2,1)S(1)}, bf16[128,1152]{1,0:T(8,128)(2,1)S(1)}, u32[]{:S(2)}, u32[]{:S(2)}) collective-permute-start(bf16[128,1152]{1,0:T(8,128)(2,1)S(1)} %shard_map.86.refs_2_.refs_0_), channel_id=1, source_target_pairs={{0,2},{1,3},{2,4},{3,5},{4,6},{5,7},{6,0},{7,1},{8,10},{9,11},{10,... | collective-permute-start | bytes 884744 | tf_op jit(solution)/shard_map/ppermute | solution.py:183
  9.5 11.4 %collective-permute-start.13 = (bf16[128,1152]{1,0:T(8,128)(2,1)S(1)}, bf16[128,1152]{1,0:T(8,128)(2,1)S(1)}, u32[]{:S(2)}, u32[]{:S(2)}) collective-permute-start(bf16[128,1152]{1,0:T(8,128)(2,1)S(1)} %shard_map.86.refs_2_.refs_0_), channel_id=1, source_target_pairs={{0,8},{1,9},{2,10},{3,11},{4,12},{5,13},{6,14},{7,15},{8,0},{9,1},... | collective-permute-start | bytes 884744 | tf_op jit(solution)/shard_map/ppermute | solution.py:183
  9.5 14.8 %collective-permute-start.17 = (bf16[128,1152]{1,0:T(8,128)(2,1)S(1)}, bf16[128,1152]{1,0:T(8,128)(2,1)S(1)}, u32[]{:S(2)}, u32[]{:S(2)}) collective-permute-start(bf16[128,1152]{1,0:T(8,128)(2,1)S(1)} %shard_map.85.refs_0_.refs_2_), channel_id=1, source_target_pairs={{0,2},{1,3},{2,4},{3,5},{4,6},{5,7},{6,0},{7,1},{8,10},{9,11},{10,... | collective-permute-start | bytes 884744 | tf_op jit(solution)/shard_map/ppermute | solution.py:183
  13.9 10.4 %collective-permute-start.34 = (bf16[128,1152]{1,0:T(8,128)(2,1)S(1)}, bf16[128,1152]{1,0:T(8,128)(2,1)S(1)}, u32[]{:S(2)}, u32[]{:S(2)}) collective-permute-start(bf16[128,1152]{1,0:T(8,128)(2,1)S(1)} %shard_map.85.refs_0_.refs_2_), channel_id=1, source_target_pairs={{0,8},{1,9},{2,10},{3,11},{4,12},{5,13},{6,14},{7,15},{8,0},{9,1},... | collective-permute-start | bytes 884744 | tf_op jit(solution)/shard_map/ppermute | solution.py:183
  14.9 11.4 %collective-permute-start.15 = (bf16[128,1152]{1,0:T(8,128)(2,1)S(1)}, bf16[128,1152]{1,0:T(8,128)(2,1)S(1)}, u32[]{:S(2)}, u32[]{:S(2)}) collective-permute-start(bf16[128,1152]{1,0:T(8,128)(2,1)S(1)} %collective-permute-done.14.refs_4_.refs_1_), channel_id=1, source_target_pairs={{0,8},{1,9},{2,10},{3,11},{4,12},{5,13},{6,14},{7,15},{8,0},{9,1},... | collective-permute-start | bytes 884744 | tf_op jit(solution)/shard_map/ppermute | solution.py:183
  19.6 20.3 %copy-start.6 = (bf16[128,1152]{1,0:T(8,128)(2,1)}, bf16[128,1152]{1,0:T(8,128)(2,1)S(1)}, u32[]{:S(2)}) copy-start(bf16[128,1152]{1,0:T(8,128)(2,1)S(1)} %collective-permute-done.1.refs_2_) | copy-start | bytes 884740
  19.6 8.0 %collective-permute-start.11 = (bf16[128,1152]{1,0:T(8,128)(2,1)S(1)}, bf16[128,1152]{1,0:T(8,128)(2,1)S(1)}, u32[]{:S(2)}, u32[]{:S(2)}) collective-permute-start(bf16[128,1152]{1,0:T(8,128)(2,1)S(1)} %collective-permute-done.1.refs_2_), channel_id=1, source_target_pairs={{0,1},{1,0},{2,3},{3,2},{4,5},{5,4},{6,7},{7,6},{8,9},{9,8},{10,11... | collective-permute-start | bytes 884744 | tf_op jit(solution)/shard_map/ppermute | solution.py:183
  20.9 7.4 %collective-permute-start.10 = (bf16[128,1152]{1,0:T(8,128)(2,1)S(1)}, bf16[128,1152]{1,0:T(8,128)(2,1)S(1)}, u32[]{:S(2)}, u32[]{:S(2)}) collective-permute-start(bf16[128,1152]{1,0:T(8,128)(2,1)S(1)} %collective-permute-done.1.refs_2_), channel_id=1, source_target_pairs={{0,8},{1,9},{2,10},{3,11},{4,12},{5,13},{6,14},{7,15},{8,0},{9,1},... | collective-permute-start | bytes 884744 | tf_op jit(solution)/shard_map/ppermute | solution.py:183
  24.3 11.7 %collective-permute-start.18 = (bf16[128,1152]{1,0:T(8,128)(2,1)S(1)}, bf16[128,1152]{1,0:T(8,128)(2,1)S(1)}, u32[]{:S(2)}, u32[]{:S(2)}) collective-permute-start(bf16[128,1152]{1,0:T(8,128)(2,1)S(1)} %collective-permute-done.17.refs_2_), channel_id=1, source_target_pairs={{0,2},{1,3},{2,4},{3,5},{4,6},{5,7},{6,0},{7,1},{8,10},{9,11},{10,... | collective-permute-start | bytes 884744 | tf_op jit(solution)/shard_map/ppermute | solution.py:183
  25.0 14.9 %collective-permute-start.2 = (bf16[128,1152]{1,0:T(8,128)(2,1)S(1)}, bf16[128,1152]{1,0:T(8,128)(2,1)}, u32[]{:S(2)}, u32[]{:S(2)}) collective-permute-start(bf16[128,1152]{1,0:T(8,128)(2,1)S(1)} %collective-permute-done.1.refs_2_), channel_id=1, source_target_pairs={{0,2},{1,3},{2,4},{3,5},{4,6},{5,7},{6,0},{7,1},{8,10},{9,11},{10,... | collective-permute-start | bytes 884744 | tf_op jit(solution)/shard_map/ppermute | solution.py:183
  27.0 13.6 %collective-permute-start.32 = (bf16[128,1152]{1,0:T(8,128)(2,1)S(1)}, bf16[128,1152]{1,0:T(8,128)(2,1)S(1)}, u32[]{:S(2)}, u32[]{:S(2)}) collective-permute-start(bf16[128,1152]{1,0:T(8,128)(2,1)S(1)} %collective-permute-done.17.refs_2_), channel_id=1, source_target_pairs={{0,16},{1,17},{2,18},{3,19},{4,20},{5,21},{6,22},{7,23},{8,24},{9,... | collective-permute-start | bytes 884744 | tf_op jit(solution)/shard_map/ppermute | solution.py:183
  27.6 37.9 %copy-start.37 = (bf16[128,1152]{1,0:T(8,128)(2,1)S(1)}, bf16[128,1152]{1,0:T(8,128)(2,1)}, u32[]{:S(2)}) copy-start(bf16[128,1152]{1,0:T(8,128)(2,1)} %copy-done.36) | copy-start | bytes 884740
  27.6 14.1 %collective-permute-start.31 = (bf16[128,1152]{1,0:T(8,128)(2,1)S(1)}, bf16[128,1152]{1,0:T(8,128)(2,1)S(1)}, u32[]{:S(2)}, u32[]{:S(2)}) collective-permute-start(bf16[128,1152]{1,0:T(8,128)(2,1)S(1)} %collective-permute-done.17.refs_2_), channel_id=1, source_target_pairs={{0,8},{1,9},{2,10},{3,11},{4,12},{5,13},{6,14},{7,15},{8,0},{9,1},... | collective-permute-start | bytes 884744 | tf_op jit(solution)/shard_map/ppermute | solution.py:183
  29.0 10.9 %collective-permute-start.35 = (bf16[128,1152]{1,0:T(8,128)(2,1)S(1)}, bf16[128,1152]{1,0:T(8,128)(2,1)S(1)}, u32[]{:S(2)}, u32[]{:S(2)}) collective-permute-start(bf16[128,1152]{1,0:T(8,128)(2,1)S(1)} %collective-permute-done.refs_1_.refs_4_), channel_id=1, source_target_pairs={{0,8},{1,9},{2,10},{3,11},{4,12},{5,13},{6,14},{7,15},{8,0},{9,1},... | collective-permute-start | bytes 884744 | tf_op jit(solution)/shard_map/ppermute | solution.py:183
  36.0 16.0 %copy-start.4 = (bf16[128,1152]{1,0:T(8,128)(2,1)}, bf16[128,1152]{1,0:T(8,128)(2,1)S(1)}, u32[]{:S(2)}) copy-start(bf16[128,1152]{1,0:T(8,128)(2,1)S(1)} %collective-permute-done.18.refs_2_) | copy-start | bytes 884740
  36.0 16.0 %collective-permute-start.12 = (bf16[128,1152]{1,0:T(8,128)(2,1)S(1)}, bf16[128,1152]{1,0:T(8,128)(2,1)S(1)}, u32[]{:S(2)}, u32[]{:S(2)}) collective-permute-start(bf16[128,1152]{1,0:T(8,128)(2,1)S(1)} %collective-permute-done.11.refs_4_), channel_id=1, source_target_pairs={{0,8},{1,9},{2,10},{3,11},{4,12},{5,13},{6,14},{7,15},{8,0},{9,1},... | collective-permute-start | bytes 884744 | tf_op jit(solution)/shard_map/ppermute | solution.py:183
  39.9 8.5 %collective-permute-start.19 = (bf16[64,1152]{1,0:T(8,128)(2,1)S(1)}, bf16[64,1152]{1,0:T(8,128)(2,1)S(1)}, u32[]{:S(2)}, u32[]{:S(2)}) collective-permute-start(bf16[64,1152]{1,0:T(8,128)(2,1)S(1)} %get-tuple-element.48), channel_id=1, source_target_pairs={{0,2},{1,3},{2,4},{3,5},{4,6},{5,7},{6,0},{7,1},{8,10},{9,11},{10,... | collective-permute-start | bytes 442376 | tf_op jit(solution)/shard_map/ppermute | solution.py:183
  40.6 10.8 %collective-permute-start.22 = (bf16[64,1152]{1,0:T(8,128)(2,1)S(1)}, bf16[64,1152]{1,0:T(8,128)(2,1)S(1)}, u32[]{:S(2)}, u32[]{:S(2)}) collective-permute-start(bf16[64,1152]{1,0:T(8,128)(2,1)S(1)} %get-tuple-element.47), channel_id=1, source_target_pairs={{0,2},{1,3},{2,4},{3,5},{4,6},{5,7},{6,0},{7,1},{8,10},{9,11},{10,... | collective-permute-start | bytes 442376 | tf_op jit(solution)/shard_map/ppermute | solution.py:183
  40.6 14.0 %collective-permute-start.3 = (bf16[128,1152]{1,0:T(8,128)(2,1)}, bf16[128,1152]{1,0:T(8,128)(2,1)}, u32[]{:S(2)}, u32[]{:S(2)}) collective-permute-start(bf16[128,1152]{1,0:T(8,128)(2,1)} %collective-permute-done.2.refs_2_), channel_id=1, source_target_pairs={{0,2},{1,3},{2,4},{3,5},{4,6},{5,7},{6,0},{7,1},{8,10},{9,11},{10,... | collective-permute-start | bytes 884744 | tf_op jit(solution)/shard_map/ppermute | solution.py:183
  42.3 12.3 %collective-permute-start.7 = (bf16[128,1152]{1,0:T(8,128)(2,1)}, bf16[128,1152]{1,0:T(8,128)(2,1)}, u32[]{:S(2)}, u32[]{:S(2)}) collective-permute-start(bf16[128,1152]{1,0:T(8,128)(2,1)} %collective-permute-done.2.refs_2_), channel_id=1, source_target_pairs={{0,1},{1,0},{2,3},{3,2},{4,5},{5,4},{6,7},{7,6},{8,9},{9,8},{10,11... | collective-permute-start | bytes 884744 | tf_op jit(solution)/shard_map/ppermute | solution.py:183
  48.4 8.8 %collective-permute-start.33 = (bf16[128,1152]{1,0:T(8,128)(2,1)S(1)}, bf16[128,1152]{1,0:T(8,128)(2,1)S(1)}, u32[]{:S(2)}, u32[]{:S(2)}) collective-permute-start(bf16[128,1152]{1,0:T(8,128)(2,1)S(1)} %collective-permute-done.32.refs_4_), channel_id=1, source_target_pairs={{0,8},{1,9},{2,10},{3,11},{4,12},{5,13},{6,14},{7,15},{8,0},{9,1},... | collective-permute-start | bytes 884744 | tf_op jit(solution)/shard_map/ppermute | solution.py:183
  51.4 8.1 %collective-permute-start.29 = (bf16[128,1152]{1,0:T(8,128)(2,1)S(1)}, bf16[128,1152]{1,0:T(8,128)(2,1)}, u32[]{:S(2)}, u32[]{:S(2)}) collective-permute-start(bf16[128,1152]{1,0:T(8,128)(2,1)S(1)} %collective-permute-done.18.refs_2_), channel_id=1, source_target_pairs={{0,16},{1,17},{2,18},{3,19},{4,20},{5,21},{6,22},{7,23},{8,24},{9,... | collective-permute-start | bytes 884744 | tf_op jit(solution)/shard_map/ppermute | solution.py:183
  52.7 8.0 %collective-permute-start.28 = (bf16[128,1152]{1,0:T(8,128)(2,1)S(1)}, bf16[128,1152]{1,0:T(8,128)(2,1)S(1)}, u32[]{:S(2)}, u32[]{:S(2)}) collective-permute-start(bf16[128,1152]{1,0:T(8,128)(2,1)S(1)} %collective-permute-done.18.refs_2_), channel_id=1, source_target_pairs={{0,8},{1,9},{2,10},{3,11},{4,12},{5,13},{6,14},{7,15},{8,0},{9,1},... | collective-permute-start | bytes 884744 | tf_op jit(solution)/shard_map/ppermute | solution.py:183
  54.7 7.4 %collective-permute-start.26 = (bf16[64,1152]{1,0:T(8,128)(2,1)S(1)}, bf16[64,1152]{1,0:T(8,128)(2,1)S(1)}, u32[]{:S(2)}, u32[]{:S(2)}) collective-permute-start(bf16[64,1152]{1,0:T(8,128)(2,1)S(1)} %collective-permute-done.19.refs_2_), channel_id=1, source_target_pairs={{0,8},{1,9},{2,10},{3,11},{4,12},{5,13},{6,14},{7,15},{8,0},{9,1},... | collective-permute-start | bytes 442376 | tf_op jit(solution)/shard_map/ppermute | solution.py:183
  54.7 8.1 %collective-permute-start.20 = (bf16[64,1152]{1,0:T(8,128)(2,1)S(1)}, bf16[64,1152]{1,0:T(8,128)(2,1)S(1)}, u32[]{:S(2)}, u32[]{:S(2)}) collective-permute-start(bf16[64,1152]{1,0:T(8,128)(2,1)S(1)} %collective-permute-done.19.refs_2_), channel_id=1, source_target_pairs={{0,16},{1,17},{2,18},{3,19},{4,20},{5,21},{6,22},{7,23},{8,24},{9,... | collective-permute-start | bytes 442376 | tf_op jit(solution)/shard_map/ppermute | solution.py:183
  57.9 6.0 %collective-permute-start.27 = (bf16[64,1152]{1,0:T(8,128)(2,1)S(1)}, bf16[64,1152]{1,0:T(8,128)(2,1)S(1)}, u32[]{:S(2)}, u32[]{:S(2)}) collective-permute-start(bf16[64,1152]{1,0:T(8,128)(2,1)S(1)} %collective-permute-done.22.refs_4_), channel_id=1, source_target_pairs={{0,8},{1,9},{2,10},{3,11},{4,12},{5,13},{6,14},{7,15},{8,0},{9,1},... | collective-permute-start | bytes 442376 | tf_op jit(solution)/shard_map/ppermute | solution.py:183
  59.5 5.4 %collective-permute-start.23 = (bf16[64,1152]{1,0:T(8,128)(2,1)S(1)}, bf16[64,1152]{1,0:T(8,128)(2,1)S(1)}, u32[]{:S(2)}, u32[]{:S(2)}) collective-permute-start(bf16[64,1152]{1,0:T(8,128)(2,1)S(1)} %collective-permute-done.22.refs_4_), channel_id=1, source_target_pairs={{0,16},{1,17},{2,18},{3,19},{4,20},{5,21},{6,22},{7,23},{8,24},{9,... | collective-permute-start | bytes 442376 | tf_op jit(solution)/shard_map/ppermute | solution.py:183
  61.4 8.8 %collective-permute-start.4 = (bf16[128,1152]{1,0:T(8,128)(2,1)}, bf16[128,1152]{1,0:T(8,128)(2,1)S(1)}, u32[]{:S(2)}, u32[]{:S(2)}) collective-permute-start(bf16[128,1152]{1,0:T(8,128)(2,1)} %collective-permute-done.3.refs_6_), channel_id=1, source_target_pairs={{0,1},{1,0},{2,3},{3,2},{4,5},{5,4},{6,7},{7,6},{8,9},{9,8},{10,11... | collective-permute-start | bytes 884744 | tf_op jit(solution)/shard_map/ppermute | solution.py:183
  62.7 7.5 %collective-permute-start.30 = (bf16[128,1152]{1,0:T(8,128)(2,1)}, bf16[128,1152]{1,0:T(8,128)(2,1)S(1)}, u32[]{:S(2)}, u32[]{:S(2)}) collective-permute-start(bf16[128,1152]{1,0:T(8,128)(2,1)} %collective-permute-done.29.refs_4_), channel_id=1, source_target_pairs={{0,8},{1,9},{2,10},{3,11},{4,12},{5,13},{6,14},{7,15},{8,0},{9,1},... | collective-permute-start | bytes 884744 | tf_op jit(solution)/shard_map/ppermute | solution.py:183
  62.7 2.2 %collective-permute-start.21 = (bf16[64,1152]{1,0:T(8,128)(2,1)S(1)}, bf16[64,1152]{1,0:T(8,128)(2,1)S(1)}, u32[]{:S(2)}, u32[]{:S(2)}) collective-permute-start(bf16[64,1152]{1,0:T(8,128)(2,1)S(1)} %collective-permute-done.20.refs_2_), channel_id=1, source_target_pairs={{0,8},{1,9},{2,10},{3,11},{4,12},{5,13},{6,14},{7,15},{8,0},{9,1},... | collective-permute-start | bytes 442376 | tf_op jit(solution)/shard_map/ppermute | solution.py:183
  64.0 14.7 %collective-permute-start.6 = (bf16[128,1152]{1,0:T(8,128)(2,1)}, bf16[128,1152]{1,0:T(8,128)(2,1)S(1)}, u32[]{:S(2)}, u32[]{:S(2)}) collective-permute-start(bf16[128,1152]{1,0:T(8,128)(2,1)} %collective-permute-done.2.refs_2_), channel_id=1, source_target_pairs={{0,8},{1,9},{2,10},{3,11},{4,12},{5,13},{6,14},{7,15},{8,0},{9,1},... | collective-permute-start | bytes 884744 | tf_op jit(solution)/shard_map/ppermute | solution.py:183
  64.9 13.8 %collective-permute-start.9 = (bf16[128,1152]{1,0:T(8,128)(2,1)}, bf16[128,1152]{1,0:T(8,128)(2,1)S(1)}, u32[]{:S(2)}, u32[]{:S(2)}) collective-permute-start(bf16[128,1152]{1,0:T(8,128)(2,1)} %collective-permute-done.3.refs_6_), channel_id=1, source_target_pairs={{0,8},{1,9},{2,10},{3,11},{4,12},{5,13},{6,14},{7,15},{8,0},{9,1},... | collective-permute-start | bytes 884744 | tf_op jit(solution)/shard_map/ppermute | solution.py:183
  64.9 13.8 %collective-permute-start.8 = (bf16[128,1152]{1,0:T(8,128)(2,1)}, bf16[128,1152]{1,0:T(8,128)(2,1)S(1)}, u32[]{:S(2)}, u32[]{:S(2)}) collective-permute-start(bf16[128,1152]{1,0:T(8,128)(2,1)} %collective-permute-done.7.refs_4_), channel_id=1, source_target_pairs={{0,8},{1,9},{2,10},{3,11},{4,12},{5,13},{6,14},{7,15},{8,0},{9,1},... | collective-permute-start | bytes 884744 | tf_op jit(solution)/shard_map/ppermute | solution.py:183
  66.1 1.3 %copy-start.35 = (bf16[128,1152]{1,0:T(8,128)(2,1)S(1)}, bf16[128,1152]{1,0:T(8,128)(2,1)}, u32[]{:S(2)}) copy-start(bf16[128,1152]{1,0:T(8,128)(2,1)} %copy-done.34) | copy-start | bytes 884740
  66.1 1.3 %copy-start.39 = (bf16[128,1152]{1,0:T(8,128)(2,1)S(1)}, bf16[128,1152]{1,0:T(8,128)(2,1)}, u32[]{:S(2)}) copy-start(bf16[128,1152]{1,0:T(8,128)(2,1)} %copy-done.38) | copy-start | bytes 884740
  67.5 3.2 %copy-start.9 = (bf16[128,1152]{1,0:T(8,128)(2,1)S(1)}, bf16[128,1152]{1,0:T(8,128)(2,1)}, u32[]{:S(2)}) copy-start(bf16[128,1152]{1,0:T(8,128)(2,1)} %copy-done.8) | copy-start | bytes 884740
  67.5 3.2 %copy-start.15 = (bf16[128,1152]{1,0:T(8,128)(2,1)S(1)}, bf16[128,1152]{1,0:T(8,128)(2,1)}, u32[]{:S(2)}) copy-start(bf16[128,1152]{1,0:T(8,128)(2,1)} %copy-done.14) | copy-start | bytes 884740
  67.5 3.2 %copy-start.17 = (bf16[128,1152]{1,0:T(8,128)(2,1)S(1)}, bf16[128,1152]{1,0:T(8,128)(2,1)}, u32[]{:S(2)}) copy-start(bf16[128,1152]{1,0:T(8,128)(2,1)} %copy-done.16) | copy-start | bytes 884740
  67.5 3.2 %copy-start.23 = (bf16[128,1152]{1,0:T(8,128)(2,1)S(1)}, bf16[128,1152]{1,0:T(8,128)(2,1)}, u32[]{:S(2)}) copy-start(bf16[128,1152]{1,0:T(8,128)(2,1)} %copy-done.22) | copy-start | bytes 884740
  70.2 6.5 %collective-permute-start.24 = (bf16[64,1152]{1,0:T(8,128)(2,1)S(1)}, bf16[64,1152]{1,0:T(8,128)(2,1)S(1)}, u32[]{:S(2)}, u32[]{:S(2)}) collective-permute-start(bf16[64,1152]{1,0:T(8,128)(2,1)S(1)} %collective-permute-done.23.refs_4_), channel_id=1, source_target_pairs={{0,8},{1,9},{2,10},{3,11},{4,12},{5,13},{6,14},{7,15},{8,0},{9,1},... | collective-permute-start | bytes 442376 | tf_op jit(solution)/shard_map/ppermute | solution.py:183
  70.2 11.7 %collective-permute-start.5 = (bf16[128,1152]{1,0:T(8,128)(2,1)S(1)}, bf16[128,1152]{1,0:T(8,128)(2,1)S(1)}, u32[]{:S(2)}, u32[]{:S(2)}) collective-permute-start(bf16[128,1152]{1,0:T(8,128)(2,1)S(1)} %collective-permute-done.4.refs_2_), channel_id=1, source_target_pairs={{0,8},{1,9},{2,10},{3,11},{4,12},{5,13},{6,14},{7,15},{8,0},{9,1},... | collective-permute-start | bytes 884744 | tf_op jit(solution)/shard_map/ppermute | solution.py:183
  70.7 1.2 %copy-start.7 = (bf16[128,1152]{1,0:T(8,128)(2,1)S(1)}, bf16[128,1152]{1,0:T(8,128)(2,1)}, u32[]{:S(2)}) copy-start(bf16[128,1152]{1,0:T(8,128)(2,1)} %copy-done.6) | copy-start | bytes 884740
  70.7 1.2 %copy-start.11 = (bf16[128,1152]{1,0:T(8,128)(2,1)S(1)}, bf16[128,1152]{1,0:T(8,128)(2,1)}, u32[]{:S(2)}) copy-start(bf16[128,1152]{1,0:T(8,128)(2,1)} %copy-done.10) | copy-start | bytes 884740
  70.7 1.2 %copy-start.13 = (bf16[128,1152]{1,0:T(8,128)(2,1)S(1)}, bf16[128,1152]{1,0:T(8,128)(2,1)}, u32[]{:S(2)}) copy-start(bf16[128,1152]{1,0:T(8,128)(2,1)} %copy-done.12) | copy-start | bytes 884740
  70.7 1.2 %copy-start.19 = (bf16[128,1152]{1,0:T(8,128)(2,1)S(1)}, bf16[128,1152]{1,0:T(8,128)(2,1)}, u32[]{:S(2)}) copy-start(bf16[128,1152]{1,0:T(8,128)(2,1)} %copy-done.18) | copy-start | bytes 884740
  71.9 1.3 %copy-start.5 = (bf16[128,1152]{1,0:T(8,128)(2,1)S(1)}, bf16[128,1152]{1,0:T(8,128)(2,1)}, u32[]{:S(2)}) copy-start(bf16[128,1152]{1,0:T(8,128)(2,1)} %copy-done.4) | copy-start | bytes 884740
  71.9 1.3 %copy-start.21 = (bf16[128,1152]{1,0:T(8,128)(2,1)S(1)}, bf16[128,1152]{1,0:T(8,128)(2,1)}, u32[]{:S(2)}) copy-start(bf16[128,1152]{1,0:T(8,128)(2,1)} %copy-done.20) | copy-start | bytes 884740
  73.3 2.2 %copy-start.25 = (bf16[64,1152]{1,0:T(8,128)(2,1)S(1)}, bf16[64,1152]{1,0:T(8,128)(2,1)}, u32[]{:S(2)}) copy-start(bf16[64,1152]{1,0:T(8,128)(2,1)} %copy-done.24) | copy-start | bytes 442372
  73.3 2.2 %copy-start.27 = (bf16[64,1152]{1,0:T(8,128)(2,1)S(1)}, bf16[64,1152]{1,0:T(8,128)(2,1)}, u32[]{:S(2)}) copy-start(bf16[64,1152]{1,0:T(8,128)(2,1)} %copy-done.26) | copy-start | bytes 442372
  73.3 2.2 %copy-start.31 = (bf16[64,1152]{1,0:T(8,128)(2,1)S(1)}, bf16[64,1152]{1,0:T(8,128)(2,1)}, u32[]{:S(2)}) copy-start(bf16[64,1152]{1,0:T(8,128)(2,1)} %copy-done.30) | copy-start | bytes 442372
  75.5 1.2 %copy-start.29 = (bf16[64,1152]{1,0:T(8,128)(2,1)S(1)}, bf16[64,1152]{1,0:T(8,128)(2,1)}, u32[]{:S(2)}) copy-start(bf16[64,1152]{1,0:T(8,128)(2,1)} %copy-done.28) | copy-start | bytes 442372
  77.8 34.4 %collective-permute-start.36 = (f32[128,1152]{1,0:T(8,128)S(1)}, f32[128,1152]{1,0:T(8,128)}, u32[]{:S(2)}, u32[]{:S(2)}) collective-permute-start(f32[128,1152]{1,0:T(8,128)S(1)} %get-tuple-element.45), channel_id=1, source_target_pairs={{0,1},{1,0},{2,3},{3,2},{4,5},{5,4},{6,7},{7,6},{8,9},{9,8},{10,11... | collective-permute-start | bytes 1769480 | tf_op jit(solution)/shard_map/ppermute | solution.py:183
  81.8 30.4 %copy-start.1 = (bf16[128,1152]{1,0:T(8,128)(2,1)S(1)}, bf16[128,1152]{1,0:T(8,128)(2,1)}, u32[]{:S(2)}) copy-start(bf16[128,1152]{1,0:T(8,128)(2,1)} %values.7) | copy-start | bytes 884740
  82.9 31.5 %collective-permute-start.16 = (f32[128,1152]{1,0:T(8,128)S(1)}, f32[128,1152]{1,0:T(8,128)S(1)}, u32[]{:S(2)}, u32[]{:S(2)}) collective-permute-start(f32[128,1152]{1,0:T(8,128)S(1)} %get-tuple-element.35), channel_id=1, source_target_pairs={{0,16},{1,17},{2,18},{3,19},{4,20},{5,21},{6,22},{7,23},{8,24},{9,... | collective-permute-start | bytes 1769480 | tf_op jit(solution)/shard_map/ppermute | solution.py:183
  83.5 14.5 %collective-permute-start.37 = (f32[8,128]{1,0:T(8,128)S(1)}, f32[8,128]{1,0:T(8,128)S(1)}, u32[]{:S(2)}, u32[]{:S(2)}) collective-permute-start(f32[8,128]{1,0:T(8,128)S(1)} %get-tuple-element.46), channel_id=1, source_target_pairs={{0,16},{1,17},{2,18},{3,19},{4,20},{5,21},{6,22},{7,23},{8,24},{9,... | collective-permute-start | bytes 12296 | tf_op jit(solution)/shard_map/ppermute | solution.py:183
  98.1 3.6 %collective-permute-start.38 = (f32[8,128]{1,0:T(8,128)S(1)}, f32[8,128]{1,0:T(8,128)S(1)}, u32[]{:S(2)}, u32[]{:S(2)}) collective-permute-start(f32[8,128]{1,0:T(8,128)S(1)} %add.81), channel_id=1, source_target_pairs={{0,1},{1,0},{2,3},{3,2},{4,5},{5,4},{6,7},{7,6},{8,9},{9,8},{10,11... | collective-permute-start | bytes 12296 | tf_op jit(solution)/shard_map/ppermute | solution.py:183
  101.7 1.2 %collective-permute-start.39 = (f32[8,128]{1,0:T(8,128)S(1)}, f32[8,128]{1,0:T(8,128)S(1)}, u32[]{:S(2)}, u32[]{:S(2)}) collective-permute-start(f32[8,128]{1,0:T(8,128)S(1)} %add.82), channel_id=1, source_target_pairs={{0,8},{1,9},{2,10},{3,11},{4,12},{5,13},{6,14},{7,15},{8,0},{9,1},... | collective-permute-start | bytes 12296 | tf_op jit(solution)/shard_map/ppermute | solution.py:183
  102.8 3.6 %collective-permute-start.40 = (f32[8,128]{1,0:T(8,128)S(1)}, f32[8,128]{1,0:T(8,128)S(1)}, u32[]{:S(2)}, u32[]{:S(2)}) collective-permute-start(f32[8,128]{1,0:T(8,128)S(1)} %add.83), channel_id=1, source_target_pairs={{0,2},{1,3},{2,0},{3,1},{4,6},{5,7},{6,4},{7,5},{8,10},{9,11},{10,... | collective-permute-start | bytes 12296 | tf_op jit(solution)/shard_map/ppermute | solution.py:183
  106.5 4.5 %collective-permute-start.41 = (f32[8,128]{1,0:T(8,128)S(1)}, f32[8,128]{1,0:T(8,128)S(1)}, u32[]{:S(2)}, u32[]{:S(2)}) collective-permute-start(f32[8,128]{1,0:T(8,128)S(1)} %add.84), channel_id=1, source_target_pairs={{0,4},{1,5},{2,6},{3,7},{4,0},{5,1},{6,2},{7,3},{8,12},{9,13},{10,... | collective-permute-start | bytes 12296 | tf_op jit(solution)/shard_map/ppermute | solution.py:183
  112.2 2.2 %copy-start.3 = (bf16[128,1152]{1,0:T(8,128)(2,1)S(1)}, bf16[128,1152]{1,0:T(8,128)(2,1)}, u32[]{:S(2)}) copy-start(bf16[128,1152]{1,0:T(8,128)(2,1)} %values.6) | copy-start | bytes 884740
  (18 other events, 12.8 us)

commit v2 on v1

--- a/solution.py
+++ b/solution.py
@@ -54,23 +54,25 @@
 
 
 def terms_kernel(
-    own_count, block_count, places, pairs, first, with_loss, settings, ids, *refs
+    own_count, block_count, places, pairs, first, loss_own, loss_first, settings, ids, *refs
 ):
     refs = list(refs)
     own = [refs.pop(0) for _ in range(own_count)]
     blocks = [refs.pop(0) for _ in range(block_count)]
     targets = [refs.pop(0) for _ in range(own_count)]
-    carried = [] if first else [refs.pop(0) for _ in range(own_count + with_loss)]
+    carried = [] if first else [refs.pop(0) for _ in range(own_count)]
+    loss_in = refs.pop(0) if loss_own and not loss_first else None
     sums = [refs.pop(0) for _ in range(own_count)]
-    losses = refs.pop(0) if with_loss else None
+    losses = refs.pop(0) if loss_own else None
     own_rows, block_rows = own[0].shape[0], blocks[0].shape[0]
     columns = {}
     for a, _ in sorted(pairs):
         if a not in columns:
             spread = jnp.broadcast_to(targets[a][...], (own_rows, own_rows))
             columns[a] = jnp.transpose(spread)[:, :1]
-    if with_loss:
-        loss = jnp.zeros((8, 128), jnp.float32) if first else carried[own_count][...]
+    loss = None
+    if loss_own:
+        loss = jnp.zeros((8, 128), jnp.float32) if loss_first else loss_in[...]
 
     def weigh(a, b, dot):
         nonlocal loss
@@ -83,7 +85,7 @@
         small = jnp.exp(-jnp.abs(logits))
         inverse = 1.0 / (1.0 + small)
         weight = jnp.where(logits >= 0, inverse, small * inverse)
-        if with_loss:
+        if a in loss_own:
             part = jnp.maximum(logits, 0.0) + jnp.log1p(small)
             part = jnp.sum(part.reshape(own_rows // 8, 8, block_rows), axis=0)
             for lane in range(0, block_rows, 128):
@@ -115,27 +117,35 @@
     for a in range(own_count):
         part = term[a * own_rows : (a + 1) * own_rows]
         sums[a][...] = part if first else carried[a][...] + part
-    if with_loss:
+    if loss_own:
         losses[...] = loss
 
 
-def terms(own, blocks, places, targets, pairs, ids, settings, carried, with_loss):
+def terms(own, blocks, places, targets, pairs, ids, settings, sums, loss_own, loss):
     rows, width = own[0].shape
-    first = carried is None
     kernel = functools.partial(
-        terms_kernel, len(own), len(blocks), tuple(places), frozenset(pairs), first, with_loss
+        terms_kernel,
+        len(own),
+        len(blocks),
+        tuple(places),
+        frozenset(pairs),
+        sums is None,
+        tuple(loss_own),
+        loss is None,
     )
     shapes = [jax.ShapeDtypeStruct((rows, width), jnp.float32)] * len(own)
-    if with_loss:
+    if loss_own:
         shapes = shapes + [jax.ShapeDtypeStruct((8, 128), jnp.float32)]
     operands = [settings, ids, *own, *blocks, *targets]
-    base = len(operands)
     aliases = {}
-    if not first:
-        operands += carried
-        aliases = {base + n: n for n in range(len(carried))}
+    if sums is not None:
+        aliases = {len(operands) + n: n for n in range(len(own))}
+        operands += sums
+    if loss_own and loss is not None:
+        aliases[len(operands)] = len(own)
+        operands.append(loss)
     size = len(own) * len(blocks) * rows * blocks[0].shape[0]
-    return pl.pallas_call(
+    out = pl.pallas_call(
         kernel,
         out_shape=shapes,
         in_specs=[VMEM] * len(operands),
@@ -148,6 +158,7 @@
         ),
         compiler_params=PARAMS,
     )(*operands)
+    return out[: len(own)], out[len(own)] if loss_own else loss
 
 
 def factor(count):
@@ -242,16 +253,19 @@
     img_own = [cores_of[0] for cores_of in img_sets[0]]
     txt_own = [cores_of[0] for cores_of in txt_sets[0]]
 
-    def image_terms(sums, parts):
+    def image_terms(sums, loss, parts, counted=True):
         blocks, places, pairs = [], [], []
         for step, at in parts:
             pairs.append((0, len(blocks)))
             for block in txt_sets[step][at]:
                 blocks.append(block)
                 places.append((step * fast + at, 0))
-        return terms(img_own, blocks, places, img_targets, pairs, ids, settings, sums, True)
-
-    def text_terms(sums, parts):
+        loss_own = range(wide) if counted else ()
+        return terms(
+            img_own, blocks, places, img_targets, pairs, ids, settings, sums, loss_own, loss,
+        )
+
+    def text_terms(sums, loss, parts, loss_own=()):
         blocks, places, pairs = [], [], []
         for cores_of, step, at, offset in parts:
             if at == 0:
@@ -259,25 +273,31 @@
             for block in cores_of:
                 blocks.append(block)
                 places.append((step * fast, offset))
-        return terms(txt_own, blocks, places, txt_targets, pairs, ids, settings, sums, False)
-
-    img_sums = txt_sums = None
+        return terms(
+            txt_own, blocks, places, txt_targets, pairs, ids, settings, sums, loss_own, loss,
+        )
+
+    img_sums = txt_sums = loss = None
     for step in range(end):
         parts = [(step, at) for at in range(fast)]
         if step == end - 1:
             parts.append((end, 0))
-        img_sums = image_terms(img_sums, parts)
+        img_sums, loss = image_terms(img_sums, loss, parts)
         parts = [(img_sets[step][at], step, at, 0) for at in range(wide)]
-        txt_sums = text_terms(txt_sums, parts)
+        counted = range(1, fast) if step == 1 else ()
+        txt_sums, loss = text_terms(txt_sums, loss, parts, counted)
     halves = [(first_set, 0), (second_set, middle)]
-    txt_sums = text_terms(txt_sums, [(half[0], end, 0, offset) for half, offset in halves])
+    txt_sums, loss = text_terms(
+        txt_sums, loss, [(half[0], end, 0, offset) for half, offset in halves],
+        range(1, fast) if end == 1 else (),
+    )
     if fast > 1:
-        img_sums = image_terms(img_sums, [(end, at) for at in range(1, fast)])
+        parts = [(end, at) for at in range(1, fast)]
+        img_sums, loss = image_terms(img_sums, loss, parts, False)
     if wide > 1:
         parts = [(half[at], end, at, offset) for at in range(1, wide) for half, offset in halves]
-        txt_sums = text_terms(txt_sums, parts)
-
-    loss = img_sums[wide]
+        txt_sums, loss = text_terms(txt_sums, loss, parts, range(1, fast) if end == 1 else ())
+
     for dim in (0, 3, 1, 2):
         size = sizes[dim]
         if size & (size - 1) == 0:

time: 117 us -> 117 us (level)
  waiting for transfers between devices: 59.6 us -> 60.8 us
    ppermute x42, waiting for transfers between devices: 59.6 us -> 60.8 us  [permuted(): return lax.ppermute(array, AXES, pairs)]
where the time goes in v2:
time: 117 us
  waiting for transfers between devices  60.8 us (52%)
  starting transfers between devices  20.6 us (18%)
  Pallas kernels  17.1 us (15%)
  local copies, waits for them, and re-layouts  13.7 us (12%)
  between operations  4.24 us (4%)
    ppermute x42, waiting for transfers between devices, permuted(): return lax.ppermute(array, AXES, pairs)  60.8 us
    ppermute x42, starting transfers between devices, permuted(): return lax.ppermute(array, AXES, pairs)  20.6 us
    unnamed x80, local copies, waits for them, and re-layouts  13.6 us
    pallas_call x9, Pallas kernels, terms(): pl.pallas_call(kernel, out_shape=shapes, in_specs=[VMEM] * len(operands),...  13.5 us
    pallas_call x2, Pallas kernels, project(): pl.pallas_call(functools.partial(project_kernel, len(parts)), out_shape=j...  3.27 us
  transfers between devices with their start and end apart: 42, of which 17 were waited for; matrix products, arithmetic and copies ran while one was open for 1% of the time, Pallas kernels for 14%

profile of v2, /device:TPU:0, one launch (start us, length us, event | category | flops | bytes accessed | tf_op | source)
XLA Modules:
  0.0 117.2 jit_solution(13866183266112936187)
XLA Ops:
  0.6 0.6 copy-done.33
  1.3 3.0 %collective-permute-start.20 = (s32[1,128]{1,0:T(1,128)S(1)}, s32[1,128]{1,0:T(1,128)S(1)}, u32[]{:S(2)}, u32[]{:S(2)}) collective-permute-start(s32[1,128]{1,0:T(1,128)S(1)} %bitcast.15), channel_id=1, source_target_pairs={{0,1},{1,0},{2,3},{3,2},{4,5},{5,4},{6,7},{7,6},{8,9},{9,8},{10,11... | collective-permute-start | bytes 1544 | tf_op jit(solution)/shard_map/ppermute | solution.py:194
  4.3 1.0 copy-done
  5.5 0.7 copy-done.2
  6.4 1.6 %collective-permute-start = (bf16[128,1152]{1,0:T(8,128)(2,1)S(1)}, bf16[128,1152]{1,0:T(8,128)(2,1)S(1)}, u32[]{:S(2)}, u32[]{:S(2)}) collective-permute-start(bf16[128,1152]{1,0:T(8,128)(2,1)S(1)} %shard_map.85.refs_0_.refs_2_), channel_id=1, source_target_pairs={{0,16},{1,17},{2,18},{3,19},{4,20},{5,21},{6,22},{7,23},{8,24},{9,... | collective-permute-start | bytes 884744 | tf_op jit(solution)/shard_map/ppermute | solution.py:194
  7.9 1.6 %collective-permute-start.1 = (bf16[128,1152]{1,0:T(8,128)(2,1)S(1)}, bf16[128,1152]{1,0:T(8,128)(2,1)S(1)}, u32[]{:S(2)}, u32[]{:S(2)}) collective-permute-start(bf16[128,1152]{1,0:T(8,128)(2,1)S(1)} %shard_map.86.refs_2_.refs_0_), channel_id=1, source_target_pairs={{0,2},{1,3},{2,4},{3,5},{4,6},{5,7},{6,0},{7,1},{8,10},{9,11},{10,... | collective-permute-start | bytes 884744 | tf_op jit(solution)/shard_map/ppermute | solution.py:194
  9.5 1.6 %collective-permute-start.16 = (bf16[128,1152]{1,0:T(8,128)(2,1)S(1)}, bf16[128,1152]{1,0:T(8,128)(2,1)S(1)}, u32[]{:S(2)}, u32[]{:S(2)}) collective-permute-start(bf16[128,1152]{1,0:T(8,128)(2,1)S(1)} %shard_map.85.refs_0_.refs_2_), channel_id=1, source_target_pairs={{0,2},{1,3},{2,4},{3,5},{4,6},{5,7},{6,0},{7,1},{8,10},{9,11},{10,... | collective-permute-start | bytes 884744 | tf_op jit(solution)/shard_map/ppermute | solution.py:194
  11.1 2.9 %collective-permute-done.14.refs_4_.refs_1_ = bf16[128,1152]{1,0:T(8,128)(2,1)S(1)} collective-permute-done((bf16[128,1152]{1,0:T(8,128)(2,1)S(1)}, bf16[128,1152]{1,0:T(8,128)(2,1)S(1)}, u32[]{:S(2)}, u32[]{:S(2)}) %collective-permute-start.14) | collective-permute-done | bytes 294944 | tf_op jit(solution)/shard_map/ppermute | solution.py:194
  13.9 1.0 collective-permute-done.refs_1_.refs_4_
  14.9 4.7 %collective-permute-done.1.refs_2_ = bf16[128,1152]{1,0:T(8,128)(2,1)S(1)} collective-permute-done((bf16[128,1152]{1,0:T(8,128)(2,1)S(1)}, bf16[128,1152]{1,0:T(8,128)(2,1)S(1)}, u32[]{:S(2)}, u32[]{:S(2)}) %collective-permute-start.1) | collective-permute-done | bytes 294944 | tf_op jit(solution)/shard_map/ppermute | solution.py:194
  19.6 1.3 %collective-permute-start.11 = (bf16[128,1152]{1,0:T(8,128)(2,1)S(1)}, bf16[128,1152]{1,0:T(8,128)(2,1)S(1)}, u32[]{:S(2)}, u32[]{:S(2)}) collective-permute-start(bf16[128,1152]{1,0:T(8,128)(2,1)S(1)} %collective-permute-done.1.refs_2_), channel_id=1, source_target_pairs={{0,1},{1,0},{2,3},{3,2},{4,5},{5,4},{6,7},{7,6},{8,9},{9,8},{10,11... | collective-permute-start | bytes 884744 | tf_op jit(solution)/shard_map/ppermute | solution.py:194
  20.9 3.4 %collective-permute-done.16.refs_2_ = bf16[128,1152]{1,0:T(8,128)(2,1)S(1)} collective-permute-done((bf16[128,1152]{1,0:T(8,128)(2,1)S(1)}, bf16[128,1152]{1,0:T(8,128)(2,1)S(1)}, u32[]{:S(2)}, u32[]{:S(2)}) %collective-permute-start.16) | collective-permute-done | bytes 294944 | tf_op jit(solution)/shard_map/ppermute | solution.py:194
  24.3 0.7 copy-done.34
  25.0 0.5 collective-permute-start.18
  25.6 0.7 copy-done.36
  26.3 1.3 %collective-permute-start.2 = (bf16[128,1152]{1,0:T(8,128)(2,1)S(1)}, bf16[128,1152]{1,0:T(8,128)(2,1)}, u32[]{:S(2)}, u32[]{:S(2)}) collective-permute-start(bf16[128,1152]{1,0:T(8,128)(2,1)S(1)} %collective-permute-done.1.refs_2_), channel_id=1, source_target_pairs={{0,2},{1,3},{2,4},{3,5},{4,6},{5,7},{6,0},{7,1},{8,10},{9,11},{10,... | collective-permute-start | bytes 884744 | tf_op jit(solution)/shard_map/ppermute | solution.py:194
  27.6 0.7 copy-done.8
  28.3 0.7 copy-done.12
  29.2 6.3 %collective-permute-done.24.refs_2_ = bf16[128,1152]{1,0:T(8,128)(2,1)S(1)} collective-permute-done((bf16[128,1152]{1,0:T(8,128)(2,1)S(1)}, bf16[128,1152]{1,0:T(8,128)(2,1)S(1)}, u32[]{:S(2)}, u32[]{:S(2)}) %collective-permute-start.24) | collective-permute-done | bytes 294944 | tf_op jit(solution)/shard_map/ppermute | solution.py:194
  35.5 0.7 copy-done.10
  36.3 0.7 copy-done.38
  37.1 0.7 copy-done.16
  37.8 0.5 collective-permute-start.19
  38.3 0.7 copy-done.14
  39.0 0.9 collective-permute-done.2.refs_2_
  39.9 5.6 %collective-permute-done.25.refs_2_ = bf16[64,1152]{1,0:T(8,128)(2,1)S(1)} collective-permute-done((bf16[64,1152]{1,0:T(8,128)(2,1)S(1)}, bf16[64,1152]{1,0:T(8,128)(2,1)S(1)}, u32[]{:S(2)}, u32[]{:S(2)}) %collective-permute-start.25) | collective-permute-done | bytes 147488 | tf_op jit(solution)/shard_map/ppermute | solution.py:194
  45.5 0.4 collective-permute-start.7
  46.0 2.7 %collective-permute-done.28.refs_4_ = bf16[64,1152]{1,0:T(8,128)(2,1)S(1)} collective-permute-done((bf16[64,1152]{1,0:T(8,128)(2,1)S(1)}, bf16[64,1152]{1,0:T(8,128)(2,1)S(1)}, u32[]{:S(2)}, u32[]{:S(2)}) %collective-permute-start.28) | collective-permute-done | bytes 147488 | tf_op jit(solution)/shard_map/ppermute | solution.py:194
  48.7 0.7 copy-done.18
  49.4 0.7 copy-done.20
  50.1 2.0 %collective-permute-start.26 = (bf16[64,1152]{1,0:T(8,128)(2,1)S(1)}, bf16[64,1152]{1,0:T(8,128)(2,1)S(1)}, u32[]{:S(2)}, u32[]{:S(2)}) collective-permute-start(bf16[64,1152]{1,0:T(8,128)(2,1)S(1)} %collective-permute-done.25.refs_2_), channel_id=1, source_target_pairs={{0,16},{1,17},{2,18},{3,19},{4,20},{5,21},{6,22},{7,23},{8,24},{9,... | collective-permute-start | bytes 442376 | tf_op jit(solution)/shard_map/ppermute | solution.py:194
  52.2 2.5 %collective-permute-done.3.refs_6_ = bf16[128,1152]{1,0:T(8,128)(2,1)} collective-permute-done((bf16[128,1152]{1,0:T(8,128)(2,1)}, bf16[128,1152]{1,0:T(8,128)(2,1)}, u32[]{:S(2)}, u32[]{:S(2)}) %collective-permute-start.3) | collective-permute-done | bytes 294944 | tf_op jit(solution)/shard_map/ppermute | solution.py:194
  54.6 0.7 copy-done.24
  56.7 0.6 collective-permute-start.32
  57.2 1.2 %collective-permute-done.34.refs_4_ = bf16[128,1152]{1,0:T(8,128)(2,1)} collective-permute-done((bf16[128,1152]{1,0:T(8,128)(2,1)S(1)}, bf16[128,1152]{1,0:T(8,128)(2,1)}, u32[]{:S(2)}, u32[]{:S(2)}) %collective-permute-start.34) | collective-permute-done | bytes 294944 | tf_op jit(solution)/shard_map/ppermute | solution.py:194
  58.7 0.7 copy-done.26
  59.4 0.7 copy-done.22
  60.1 0.5 collective-permute-start.27
  60.6 0.7 copy-done.28
  61.3 0.7 copy-done.30
  62.4 1.2 collective-permute-done.29.refs_4_
  63.6 0.5 collective-permute-start.8
  64.2 0.7 copy-done.32
  64.8 1.3 %shard_map.87 = (f32[128,1152]{1,0:T(8,128)S(1)}, f32[128,1152]{1,0:T(8,128)S(1)}, f32[8,128]{1,0:T(8,128)S(1)}) custom-call(f32[8,128]{1,0:T(8,128)S(1)} %concatenate.6.settings, s32[8,128]{1,0:T(8,128)S(1)} %iota_add_fusion.ids, bf16[128,1152]{1,0:T(8,128)(2,1)S(1)} %shard_map.85.refs_0_.refs_2_, ...), custom_call_target="tpu_custom_call" | custom-call | flops 603979776 | bytes 4128768 | tf_op jit(solution)/shard_map/pallas_call | solution.py:148
  66.2 1.1 shard_map.89
  67.4 3.6 %collective-permute-done.4.refs_2_ = bf16[128,1152]{1,0:T(8,128)(2,1)S(1)} collective-permute-done((bf16[128,1152]{1,0:T(8,128)(2,1)}, bf16[128,1152]{1,0:T(8,128)(2,1)S(1)}, u32[]{:S(2)}, u32[]{:S(2)}) %collective-permute-start.4) | collective-permute-done | bytes 294944 | tf_op jit(solution)/shard_map/ppermute | solution.py:194
  71.1 1.3 %shard_map.88 = (f32[128,1152]{1,0:T(8,128)S(1)}, f32[128,1152]{1,0:T(8,128)S(1)}, f32[8,128]{1,0:T(8,128)S(1)}) custom-call(f32[8,128]{1,0:T(8,128)S(1)} %concatenate.6.settings, s32[8,128]{1,0:T(8,128)S(1)} %iota_add_fusion.ids, bf16[128,1152]{1,0:T(8,128)(2,1)S(1)} %shard_map.85.refs_0_.refs_2_, ...), custom_call_target="tpu_custom_call", output_to_operand_aliasing={{0}: (10, {}), {1}: (11, {}), {2}: (12, {})} | custom-call | flops 603979776 | bytes 4128768 | tf_op jit(solution)/shard_map/pallas_call | solution.py:148
  72.5 1.2 %shard_map.90 = (f32[128,1152]{1,0:T(8,128)S(1)}, f32[128,1152]{1,0:T(8,128)S(1)}, f32[8,128]{1,0:T(8,128)S(1)}) custom-call(f32[8,128]{1,0:T(8,128)S(1)} %concatenate.6.settings, s32[8,128]{1,0:T(8,128)S(1)} %iota_add_fusion.ids, bf16[128,1152]{1,0:T(8,128)(2,1)S(1)} %shard_map.86.refs_2_.refs_0_, ...), custom_call_target="tpu_custom_call", output_to_operand_aliasing={{0}: (10, {}), {1}: (11, {}), {2}: (12, {})} | custom-call | flops 603979776 | bytes 4128768 | tf_op jit(solution)/shard_map/pallas_call | solution.py:148
  73.8 2.1 %shard_map.94 = (f32[128,1152]{1,0:T(8,128)S(1)}, f32[128,1152]{1,0:T(8,128)S(1)}) custom-call(f32[8,128]{1,0:T(8,128)S(1)} %concatenate.6.settings, s32[8,128]{1,0:T(8,128)S(1)} %iota_add_fusion.ids, bf16[128,1152]{1,0:T(8,128)(2,1)S(1)} %shard_map.86.refs_2_.refs_0_, ...), custom_call_target="tpu_custom_call", output_to_operand_aliasing={{0}: (10, {}), {1}: (11, {})} | custom-call | flops 603979776 | bytes 4128768 | tf_op jit(solution)/shard_map/pallas_call | solution.py:148
  76.0 1.2 %shard_map.95 = (f32[128,1152]{1,0:T(8,128)S(1)}, f32[128,1152]{1,0:T(8,128)S(1)}) custom-call(f32[8,128]{1,0:T(8,128)S(1)} %concatenate.6.settings, s32[8,128]{1,0:T(8,128)S(1)} %iota_add_fusion.ids, bf16[128,1152]{1,0:T(8,128)(2,1)S(1)} %shard_map.86.refs_2_.refs_0_, ...), custom_call_target="tpu_custom_call", output_to_operand_aliasing={{0}: (10, {}), {1}: (11, {})} | custom-call | flops 301989888 | bytes 4128768 | tf_op jit(solution)/shard_map/pallas_call | solution.py:148
  77.2 1.1 shard_map.96
  78.3 0.5 collective-permute-start.36
  78.8 3.1 %shard_map.91 = (f32[128,1152]{1,0:T(8,128)S(1)}, f32[128,1152]{1,0:T(8,128)S(1)}, f32[8,128]{1,0:T(8,128)S(1)}) custom-call(f32[8,128]{1,0:T(8,128)S(1)} %concatenate.6.settings, s32[8,128]{1,0:T(8,128)S(1)} %iota_add_fusion.ids, bf16[128,1152]{1,0:T(8,128)(2,1)S(1)} %shard_map.85.refs_0_.refs_2_, ...), custom_call_target="tpu_custom_call", output_to_operand_aliasing={{0}: (12, {}), {1}: (13, {}), {2}: (14, {})} | custom-call | flops 905969664 | bytes 4718592 | tf_op jit(solution)/shard_map/pallas_call | solution.py:148
  82.0 1.0 shard_map.92
  83.0 1.8 %collective-permute-start.23 = (f32[128,1152]{1,0:T(8,128)S(1)}, f32[128,1152]{1,0:T(8,128)S(1)}, u32[]{:S(2)}, u32[]{:S(2)}) collective-permute-start(f32[128,1152]{1,0:T(8,128)S(1)} %get-tuple-element.37), channel_id=1, source_target_pairs={{0,16},{1,17},{2,18},{3,19},{4,20},{5,21},{6,22},{7,23},{8,24},{9,... | collective-permute-start | bytes 1769480 | tf_op jit(solution)/shard_map/ppermute | solution.py:194
  85.1 13.5 %collective-permute-done.37 = f32[8,128]{1,0:T(8,128)S(1)} collective-permute-done((f32[8,128]{1,0:T(8,128)S(1)}, f32[8,128]{1,0:T(8,128)S(1)}, u32[]{:S(2)}, u32[]{:S(2)}) %collective-permute-start.37) | collective-permute-done | bytes 4128 | tf_op jit(solution)/shard_map/ppermute | solution.py:194
  98.6 1.6 %collective-permute-start.38 = (f32[8,128]{1,0:T(8,128)S(1)}, f32[8,128]{1,0:T(8,128)S(1)}, u32[]{:S(2)}, u32[]{:S(2)}) collective-permute-start(f32[8,128]{1,0:T(8,128)S(1)} %add.81), channel_id=1, source_target_pairs={{0,1},{1,0},{2,3},{3,2},{4,5},{5,4},{6,7},{7,6},{8,9},{9,8},{10,11... | collective-permute-start | bytes 12296 | tf_op jit(solution)/shard_map/ppermute | solution.py:194
  100.2 2.0 %collective-permute-done.38 = f32[8,128]{1,0:T(8,128)S(1)} collective-permute-done((f32[8,128]{1,0:T(8,128)S(1)}, f32[8,128]{1,0:T(8,128)S(1)}, u32[]{:S(2)}, u32[]{:S(2)}) %collective-permute-start.38) | collective-permute-done | bytes 4128 | tf_op jit(solution)/shard_map/ppermute | solution.py:194
  102.2 1.2 collective-permute-done.39
  103.4 3.6 %collective-permute-done.40 = f32[8,128]{1,0:T(8,128)S(1)} collective-permute-done((f32[8,128]{1,0:T(8,128)S(1)}, f32[8,128]{1,0:T(8,128)S(1)}, u32[]{:S(2)}, u32[]{:S(2)}) %collective-permute-start.40) | collective-permute-done | bytes 4128 | tf_op jit(solution)/shard_map/ppermute | solution.py:194
  107.0 4.5 %collective-permute-done.41 = f32[8,128]{1,0:T(8,128)S(1)} collective-permute-done((f32[8,128]{1,0:T(8,128)S(1)}, f32[8,128]{1,0:T(8,128)S(1)}, u32[]{:S(2)}, u32[]{:S(2)}) %collective-permute-start.41) | collective-permute-done | bytes 4128 | tf_op jit(solution)/shard_map/ppermute | solution.py:194
  111.5 0.6 add_reduce_fusion
  112.8 2.2 %shard_map.97 = f32[128,1152]{1,0:T(8,128)} custom-call(f32[8,128]{1,0:T(8,128)S(1)} %concatenate.6.settings, bf16[128,1152]{1,0:T(8,128)(2,1)S(1)} %copy-done.1, f32[128,1152]{1,0:T(8,128)S(1)} %get-tuple-element.44.refs_0_, f32[128,1152]{1,0:T(8,128)} %collective-permute-done.36.refs_1_), custom_call_target="tpu_custom_call" | custom-call | tf_op jit(solution)/shard_map/pallas_call | solution.py:47
  115.0 1.1 shard_map.93
  (124 shorter events, 2.1 us)
Async XLA Ops:
  1.3 8.2 %collective-permute-start.20 = (s32[1,128]{1,0:T(1,128)S(1)}, s32[1,128]{1,0:T(1,128)S(1)}, u32[]{:S(2)}, u32[]{:S(2)}) collective-permute-start(s32[1,128]{1,0:T(1,128)S(1)} %bitcast.15), channel_id=1, source_target_pairs={{0,1},{1,0},{2,3},{3,2},{4,5},{5,4},{6,7},{7,6},{8,9},{9,8},{10,11... | collective-permute-start | bytes 1544 | tf_op jit(solution)/shard_map/ppermute | solution.py:194
  4.3 1.0 copy-start
  5.4 8.5 %collective-permute-start.14 = (bf16[128,1152]{1,0:T(8,128)(2,1)S(1)}, bf16[128,1152]{1,0:T(8,128)(2,1)S(1)}, u32[]{:S(2)}, u32[]{:S(2)}) collective-permute-start(bf16[128,1152]{1,0:T(8,128)(2,1)S(1)} %shard_map.86.refs_2_.refs_0_), channel_id=1, source_target_pairs={{0,1},{1,0},{2,3},{3,2},{4,5},{5,4},{6,7},{7,6},{8,9},{9,8},{10,11... | collective-permute-start | bytes 884744 | tf_op jit(solution)/shard_map/ppermute | solution.py:194
  6.4 8.5 %collective-permute-start = (bf16[128,1152]{1,0:T(8,128)(2,1)S(1)}, bf16[128,1152]{1,0:T(8,128)(2,1)S(1)}, u32[]{:S(2)}, u32[]{:S(2)}) collective-permute-start(bf16[128,1152]{1,0:T(8,128)(2,1)S(1)} %shard_map.85.refs_0_.refs_2_), channel_id=1, source_target_pairs={{0,16},{1,17},{2,18},{3,19},{4,20},{5,21},{6,22},{7,23},{8,24},{9,... | collective-permute-start | bytes 884744 | tf_op jit(solution)/shard_map/ppermute | solution.py:194
  7.9 11.7 %collective-permute-start.1 = (bf16[128,1152]{1,0:T(8,128)(2,1)S(1)}, bf16[128,1152]{1,0:T(8,128)(2,1)S(1)}, u32[]{:S(2)}, u32[]{:S(2)}) collective-permute-start(bf16[128,1152]{1,0:T(8,128)(2,1)S(1)} %shard_map.86.refs_2_.refs_0_), channel_id=1, source_target_pairs={{0,2},{1,3},{2,4},{3,5},{4,6},{5,7},{6,0},{7,1},{8,10},{9,11},{10,... | collective-permute-start | bytes 884744 | tf_op jit(solution)/shard_map/ppermute | solution.py:194
  9.5 11.4 %collective-permute-start.13 = (bf16[128,1152]{1,0:T(8,128)(2,1)S(1)}, bf16[128,1152]{1,0:T(8,128)(2,1)S(1)}, u32[]{:S(2)}, u32[]{:S(2)}) collective-permute-start(bf16[128,1152]{1,0:T(8,128)(2,1)S(1)} %shard_map.86.refs_2_.refs_0_), channel_id=1, source_target_pairs={{0,8},{1,9},{2,10},{3,11},{4,12},{5,13},{6,14},{7,15},{8,0},{9,1},... | collective-permute-start | bytes 884744 | tf_op jit(solution)/shard_map/ppermute | solution.py:194
  9.5 14.8 %collective-permute-start.16 = (bf16[128,1152]{1,0:T(8,128)(2,1)S(1)}, bf16[128,1152]{1,0:T(8,128)(2,1)S(1)}, u32[]{:S(2)}, u32[]{:S(2)}) collective-permute-start(bf16[128,1152]{1,0:T(8,128)(2,1)S(1)} %shard_map.85.refs_0_.refs_2_), channel_id=1, source_target_pairs={{0,2},{1,3},{2,4},{3,5},{4,6},{5,7},{6,0},{7,1},{8,10},{9,11},{10,... | collective-permute-start | bytes 884744 | tf_op jit(solution)/shard_map/ppermute | solution.py:194
  13.9 10.4 %collective-permute-start.21 = (bf16[128,1152]{1,0:T(8,128)(2,1)S(1)}, bf16[128,1152]{1,0:T(8,128)(2,1)S(1)}, u32[]{:S(2)}, u32[]{:S(2)}) collective-permute-start(bf16[128,1152]{1,0:T(8,128)(2,1)S(1)} %shard_map.85.refs_0_.refs_2_), channel_id=1, source_target_pairs={{0,8},{1,9},{2,10},{3,11},{4,12},{5,13},{6,14},{7,15},{8,0},{9,1},... | collective-permute-start | bytes 884744 | tf_op jit(solution)/shard_map/ppermute | solution.py:194
  14.9 10.7 %collective-permute-start.15 = (bf16[128,1152]{1,0:T(8,128)(2,1)S(1)}, bf16[128,1152]{1,0:T(8,128)(2,1)S(1)}, u32[]{:S(2)}, u32[]{:S(2)}) collective-permute-start(bf16[128,1152]{1,0:T(8,128)(2,1)S(1)} %collective-permute-done.14.refs_4_.refs_1_), channel_id=1, source_target_pairs={{0,8},{1,9},{2,10},{3,11},{4,12},{5,13},{6,14},{7,15},{8,0},{9,1},... | collective-permute-start | bytes 884744 | tf_op jit(solution)/shard_map/ppermute | solution.py:194
  19.6 6.7 %collective-permute-start.11 = (bf16[128,1152]{1,0:T(8,128)(2,1)S(1)}, bf16[128,1152]{1,0:T(8,128)(2,1)S(1)}, u32[]{:S(2)}, u32[]{:S(2)}) collective-permute-start(bf16[128,1152]{1,0:T(8,128)(2,1)S(1)} %collective-permute-done.1.refs_2_), channel_id=1, source_target_pairs={{0,1},{1,0},{2,3},{3,2},{4,5},{5,4},{6,7},{7,6},{8,9},{9,8},{10,11... | collective-permute-start | bytes 884744 | tf_op jit(solution)/shard_map/ppermute | solution.py:194
  20.9 7.4 %collective-permute-start.10 = (bf16[128,1152]{1,0:T(8,128)(2,1)S(1)}, bf16[128,1152]{1,0:T(8,128)(2,1)S(1)}, u32[]{:S(2)}, u32[]{:S(2)}) collective-permute-start(bf16[128,1152]{1,0:T(8,128)(2,1)S(1)} %collective-permute-done.1.refs_2_), channel_id=1, source_target_pairs={{0,8},{1,9},{2,10},{3,11},{4,12},{5,13},{6,14},{7,15},{8,0},{9,1},... | collective-permute-start | bytes 884744 | tf_op jit(solution)/shard_map/ppermute | solution.py:194
  24.3 12.7 %copy-start.6 = (bf16[128,1152]{1,0:T(8,128)(2,1)}, bf16[128,1152]{1,0:T(8,128)(2,1)S(1)}, u32[]{:S(2)}) copy-start(bf16[128,1152]{1,0:T(8,128)(2,1)S(1)} %collective-permute-done.16.refs_2_) | copy-start | bytes 884740
  24.3 11.2 %collective-permute-start.24 = (bf16[128,1152]{1,0:T(8,128)(2,1)S(1)}, bf16[128,1152]{1,0:T(8,128)(2,1)S(1)}, u32[]{:S(2)}, u32[]{:S(2)}) collective-permute-start(bf16[128,1152]{1,0:T(8,128)(2,1)S(1)} %collective-permute-done.16.refs_2_), channel_id=1, source_target_pairs={{0,2},{1,3},{2,4},{3,5},{4,6},{5,7},{6,0},{7,1},{8,10},{9,11},{10,... | collective-permute-start | bytes 884744 | tf_op jit(solution)/shard_map/ppermute | solution.py:194
  25.0 12.0 %collective-permute-start.18 = (bf16[128,1152]{1,0:T(8,128)(2,1)S(1)}, bf16[128,1152]{1,0:T(8,128)(2,1)S(1)}, u32[]{:S(2)}, u32[]{:S(2)}) collective-permute-start(bf16[128,1152]{1,0:T(8,128)(2,1)S(1)} %collective-permute-done.16.refs_2_), channel_id=1, source_target_pairs={{0,16},{1,17},{2,18},{3,19},{4,20},{5,21},{6,22},{7,23},{8,24},{9,... | collective-permute-start | bytes 884744 | tf_op jit(solution)/shard_map/ppermute | solution.py:194
  26.3 10.8 %collective-permute-start.17 = (bf16[128,1152]{1,0:T(8,128)(2,1)S(1)}, bf16[128,1152]{1,0:T(8,128)(2,1)S(1)}, u32[]{:S(2)}, u32[]{:S(2)}) collective-permute-start(bf16[128,1152]{1,0:T(8,128)(2,1)S(1)} %collective-permute-done.16.refs_2_), channel_id=1, source_target_pairs={{0,8},{1,9},{2,10},{3,11},{4,12},{5,13},{6,14},{7,15},{8,0},{9,1},... | collective-permute-start | bytes 884744 | tf_op jit(solution)/shard_map/ppermute | solution.py:194
  26.3 37.9 %copy-start.37 = (bf16[128,1152]{1,0:T(8,128)(2,1)S(1)}, bf16[128,1152]{1,0:T(8,128)(2,1)}, u32[]{:S(2)}) copy-start(bf16[128,1152]{1,0:T(8,128)(2,1)} %copy-done.36) | copy-start | bytes 884740
  26.3 13.6 %collective-permute-start.2 = (bf16[128,1152]{1,0:T(8,128)(2,1)S(1)}, bf16[128,1152]{1,0:T(8,128)(2,1)}, u32[]{:S(2)}, u32[]{:S(2)}) collective-permute-start(bf16[128,1152]{1,0:T(8,128)(2,1)S(1)} %collective-permute-done.1.refs_2_), channel_id=1, source_target_pairs={{0,2},{1,3},{2,4},{3,5},{4,6},{5,7},{6,0},{7,1},{8,10},{9,11},{10,... | collective-permute-start | bytes 884744 | tf_op jit(solution)/shard_map/ppermute | solution.py:194
  29.0 7.3 %collective-permute-start.22 = (bf16[128,1152]{1,0:T(8,128)(2,1)S(1)}, bf16[128,1152]{1,0:T(8,128)(2,1)S(1)}, u32[]{:S(2)}, u32[]{:S(2)}) collective-permute-start(bf16[128,1152]{1,0:T(8,128)(2,1)S(1)} %collective-permute-done.refs_1_.refs_4_), channel_id=1, source_target_pairs={{0,8},{1,9},{2,10},{3,11},{4,12},{5,13},{6,14},{7,15},{8,0},{9,1},... | collective-permute-start | bytes 884744 | tf_op jit(solution)/shard_map/ppermute | solution.py:194
  35.5 13.2 %copy-start.4 = (bf16[128,1152]{1,0:T(8,128)(2,1)}, bf16[128,1152]{1,0:T(8,128)(2,1)S(1)}, u32[]{:S(2)}) copy-start(bf16[128,1152]{1,0:T(8,128)(2,1)S(1)} %collective-permute-done.24.refs_2_) | copy-start | bytes 884740
  35.5 13.2 %collective-permute-start.12 = (bf16[128,1152]{1,0:T(8,128)(2,1)S(1)}, bf16[128,1152]{1,0:T(8,128)(2,1)S(1)}, u32[]{:S(2)}, u32[]{:S(2)}) collective-permute-start(bf16[128,1152]{1,0:T(8,128)(2,1)S(1)} %collective-permute-done.11.refs_4_), channel_id=1, source_target_pairs={{0,8},{1,9},{2,10},{3,11},{4,12},{5,13},{6,14},{7,15},{8,0},{9,1},... | collective-permute-start | bytes 884744 | tf_op jit(solution)/shard_map/ppermute | solution.py:194
  37.0 8.5 %collective-permute-start.25 = (bf16[64,1152]{1,0:T(8,128)(2,1)S(1)}, bf16[64,1152]{1,0:T(8,128)(2,1)S(1)}, u32[]{:S(2)}, u32[]{:S(2)}) collective-permute-start(bf16[64,1152]{1,0:T(8,128)(2,1)S(1)} %get-tuple-element.48), channel_id=1, source_target_pairs={{0,2},{1,3},{2,4},{3,5},{4,6},{5,7},{6,0},{7,1},{8,10},{9,11},{10,... | collective-permute-start | bytes 442376 | tf_op jit(solution)/shard_map/ppermute | solution.py:194
  37.0 11.7 %collective-permute-start.28 = (bf16[64,1152]{1,0:T(8,128)(2,1)S(1)}, bf16[64,1152]{1,0:T(8,128)(2,1)S(1)}, u32[]{:S(2)}, u32[]{:S(2)}) collective-permute-start(bf16[64,1152]{1,0:T(8,128)(2,1)S(1)} %get-tuple-element.47), channel_id=1, source_target_pairs={{0,2},{1,3},{2,4},{3,5},{4,6},{5,7},{6,0},{7,1},{8,10},{9,11},{10,... | collective-permute-start | bytes 442376 | tf_op jit(solution)/shard_map/ppermute | solution.py:194
  37.8 11.6 %collective-permute-start.19 = (bf16[128,1152]{1,0:T(8,128)(2,1)S(1)}, bf16[128,1152]{1,0:T(8,128)(2,1)S(1)}, u32[]{:S(2)}, u32[]{:S(2)}) collective-permute-start(bf16[128,1152]{1,0:T(8,128)(2,1)S(1)} %collective-permute-done.18.refs_4_), channel_id=1, source_target_pairs={{0,8},{1,9},{2,10},{3,11},{4,12},{5,13},{6,14},{7,15},{8,0},{9,1},... | collective-permute-start | bytes 884744 | tf_op jit(solution)/shard_map/ppermute | solution.py:194
  39.9 14.7 %collective-permute-start.3 = (bf16[128,1152]{1,0:T(8,128)(2,1)}, bf16[128,1152]{1,0:T(8,128)(2,1)}, u32[]{:S(2)}, u32[]{:S(2)}) collective-permute-start(bf16[128,1152]{1,0:T(8,128)(2,1)} %collective-permute-done.2.refs_2_), channel_id=1, source_target_pairs={{0,2},{1,3},{2,4},{3,5},{4,6},{5,7},{6,0},{7,1},{8,10},{9,11},{10,... | collective-permute-start | bytes 884744 | tf_op jit(solution)/shard_map/ppermute | solution.py:194
  45.5 11.1 %collective-permute-start.7 = (bf16[128,1152]{1,0:T(8,128)(2,1)}, bf16[128,1152]{1,0:T(8,128)(2,1)}, u32[]{:S(2)}, u32[]{:S(2)}) collective-permute-start(bf16[128,1152]{1,0:T(8,128)(2,1)} %collective-permute-done.2.refs_2_), channel_id=1, source_target_pairs={{0,1},{1,0},{2,3},{3,2},{4,5},{5,4},{6,7},{7,6},{8,9},{9,8},{10,11... | collective-permute-start | bytes 884744 | tf_op jit(solution)/shard_map/ppermute | solution.py:194
  48.7 9.7 %collective-permute-start.34 = (bf16[128,1152]{1,0:T(8,128)(2,1)S(1)}, bf16[128,1152]{1,0:T(8,128)(2,1)}, u32[]{:S(2)}, u32[]{:S(2)}) collective-permute-start(bf16[128,1152]{1,0:T(8,128)(2,1)S(1)} %collective-permute-done.24.refs_2_), channel_id=1, source_target_pairs={{0,16},{1,17},{2,18},{3,19},{4,20},{5,21},{6,22},{7,23},{8,24},{9,... | collective-permute-start | bytes 884744 | tf_op jit(solution)/shard_map/ppermute | solution.py:194
  49.4 9.9 %collective-permute-start.33 = (bf16[128,1152]{1,0:T(8,128)(2,1)S(1)}, bf16[128,1152]{1,0:T(8,128)(2,1)S(1)}, u32[]{:S(2)}, u32[]{:S(2)}) collective-permute-start(bf16[128,1152]{1,0:T(8,128)(2,1)S(1)} %collective-permute-done.24.refs_2_), channel_id=1, source_target_pairs={{0,8},{1,9},{2,10},{3,11},{4,12},{5,13},{6,14},{7,15},{8,0},{9,1},... | collective-permute-start | bytes 884744 | tf_op jit(solution)/shard_map/ppermute | solution.py:194
  50.1 9.9 %collective-permute-start.26 = (bf16[64,1152]{1,0:T(8,128)(2,1)S(1)}, bf16[64,1152]{1,0:T(8,128)(2,1)S(1)}, u32[]{:S(2)}, u32[]{:S(2)}) collective-permute-start(bf16[64,1152]{1,0:T(8,128)(2,1)S(1)} %collective-permute-done.25.refs_2_), channel_id=1, source_target_pairs={{0,16},{1,17},{2,18},{3,19},{4,20},{5,21},{6,22},{7,23},{8,24},{9,... | collective-permute-start | bytes 442376 | tf_op jit(solution)/shard_map/ppermute | solution.py:194
  54.6 6.6 %collective-permute-start.31 = (bf16[64,1152]{1,0:T(8,128)(2,1)S(1)}, bf16[64,1152]{1,0:T(8,128)(2,1)S(1)}, u32[]{:S(2)}, u32[]{:S(2)}) collective-permute-start(bf16[64,1152]{1,0:T(8,128)(2,1)S(1)} %collective-permute-done.25.refs_2_), channel_id=1, source_target_pairs={{0,8},{1,9},{2,10},{3,11},{4,12},{5,13},{6,14},{7,15},{8,0},{9,1},... | collective-permute-start | bytes 442376 | tf_op jit(solution)/shard_map/ppermute | solution.py:194
  56.7 5.8 %collective-permute-start.32 = (bf16[64,1152]{1,0:T(8,128)(2,1)S(1)}, bf16[64,1152]{1,0:T(8,128)(2,1)S(1)}, u32[]{:S(2)}, u32[]{:S(2)}) collective-permute-start(bf16[64,1152]{1,0:T(8,128)(2,1)S(1)} %collective-permute-done.28.refs_4_), channel_id=1, source_target_pairs={{0,8},{1,9},{2,10},{3,11},{4,12},{5,13},{6,14},{7,15},{8,0},{9,1},... | collective-permute-start | bytes 442376 | tf_op jit(solution)/shard_map/ppermute | solution.py:194
  58.4 5.1 %collective-permute-start.29 = (bf16[64,1152]{1,0:T(8,128)(2,1)S(1)}, bf16[64,1152]{1,0:T(8,128)(2,1)S(1)}, u32[]{:S(2)}, u32[]{:S(2)}) collective-permute-start(bf16[64,1152]{1,0:T(8,128)(2,1)S(1)} %collective-permute-done.28.refs_4_), channel_id=1, source_target_pairs={{0,16},{1,17},{2,18},{3,19},{4,20},{5,21},{6,22},{7,23},{8,24},{9,... | collective-permute-start | bytes 442376 | tf_op jit(solution)/shard_map/ppermute | solution.py:194
  60.1 7.3 %collective-permute-start.35 = (bf16[128,1152]{1,0:T(8,128)(2,1)}, bf16[128,1152]{1,0:T(8,128)(2,1)S(1)}, u32[]{:S(2)}, u32[]{:S(2)}) collective-permute-start(bf16[128,1152]{1,0:T(8,128)(2,1)} %collective-permute-done.34.refs_4_), channel_id=1, source_target_pairs={{0,8},{1,9},{2,10},{3,11},{4,12},{5,13},{6,14},{7,15},{8,0},{9,1},... | collective-permute-start | bytes 884744 | tf_op jit(solution)/shard_map/ppermute | solution.py:194
  60.1 3.5 %collective-permute-start.27 = (bf16[64,1152]{1,0:T(8,128)(2,1)S(1)}, bf16[64,1152]{1,0:T(8,128)(2,1)S(1)}, u32[]{:S(2)}, u32[]{:S(2)}) collective-permute-start(bf16[64,1152]{1,0:T(8,128)(2,1)S(1)} %collective-permute-done.26.refs_2_), channel_id=1, source_target_pairs={{0,8},{1,9},{2,10},{3,11},{4,12},{5,13},{6,14},{7,15},{8,0},{9,1},... | collective-permute-start | bytes 442376 | tf_op jit(solution)/shard_map/ppermute | solution.py:194
  61.9 9.1 %collective-permute-start.4 = (bf16[128,1152]{1,0:T(8,128)(2,1)}, bf16[128,1152]{1,0:T(8,128)(2,1)S(1)}, u32[]{:S(2)}, u32[]{:S(2)}) collective-permute-start(bf16[128,1152]{1,0:T(8,128)(2,1)} %collective-permute-done.3.refs_6_), channel_id=1, source_target_pairs={{0,1},{1,0},{2,3},{3,2},{4,5},{5,4},{6,7},{7,6},{8,9},{9,8},{10,11... | collective-permute-start | bytes 884744 | tf_op jit(solution)/shard_map/ppermute | solution.py:194
  62.4 16.4 %collective-permute-start.6 = (bf16[128,1152]{1,0:T(8,128)(2,1)}, bf16[128,1152]{1,0:T(8,128)(2,1)S(1)}, u32[]{:S(2)}, u32[]{:S(2)}) collective-permute-start(bf16[128,1152]{1,0:T(8,128)(2,1)} %collective-permute-done.2.refs_2_), channel_id=1, source_target_pairs={{0,8},{1,9},{2,10},{3,11},{4,12},{5,13},{6,14},{7,15},{8,0},{9,1},... | collective-permute-start | bytes 884744 | tf_op jit(solution)/shard_map/ppermute | solution.py:194
  63.6 15.2 %collective-permute-start.9 = (bf16[128,1152]{1,0:T(8,128)(2,1)}, bf16[128,1152]{1,0:T(8,128)(2,1)S(1)}, u32[]{:S(2)}, u32[]{:S(2)}) collective-permute-start(bf16[128,1152]{1,0:T(8,128)(2,1)} %collective-permute-done.3.refs_6_), channel_id=1, source_target_pairs={{0,8},{1,9},{2,10},{3,11},{4,12},{5,13},{6,14},{7,15},{8,0},{9,1},... | collective-permute-start | bytes 884744 | tf_op jit(solution)/shard_map/ppermute | solution.py:194
  63.6 15.2 %collective-permute-start.8 = (bf16[128,1152]{1,0:T(8,128)(2,1)}, bf16[128,1152]{1,0:T(8,128)(2,1)S(1)}, u32[]{:S(2)}, u32[]{:S(2)}) collective-permute-start(bf16[128,1152]{1,0:T(8,128)(2,1)} %collective-permute-done.7.refs_4_), channel_id=1, source_target_pairs={{0,8},{1,9},{2,10},{3,11},{4,12},{5,13},{6,14},{7,15},{8,0},{9,1},... | collective-permute-start | bytes 884744 | tf_op jit(solution)/shard_map/ppermute | solution.py:194
  64.8 1.3 %copy-start.35 = (bf16[128,1152]{1,0:T(8,128)(2,1)S(1)}, bf16[128,1152]{1,0:T(8,128)(2,1)}, u32[]{:S(2)}) copy-start(bf16[128,1152]{1,0:T(8,128)(2,1)} %copy-done.34) | copy-start | bytes 884740
  64.8 1.3 %copy-start.39 = (bf16[128,1152]{1,0:T(8,128)(2,1)S(1)}, bf16[128,1152]{1,0:T(8,128)(2,1)}, u32[]{:S(2)}) copy-start(bf16[128,1152]{1,0:T(8,128)(2,1)} %copy-done.38) | copy-start | bytes 884740
  66.1 4.9 %copy-start.9 = (bf16[128,1152]{1,0:T(8,128)(2,1)S(1)}, bf16[128,1152]{1,0:T(8,128)(2,1)}, u32[]{:S(2)}) copy-start(bf16[128,1152]{1,0:T(8,128)(2,1)} %copy-done.8) | copy-start | bytes 884740
  66.2 4.9 %copy-start.11 = (bf16[128,1152]{1,0:T(8,128)(2,1)S(1)}, bf16[128,1152]{1,0:T(8,128)(2,1)}, u32[]{:S(2)}) copy-start(bf16[128,1152]{1,0:T(8,128)(2,1)} %copy-done.10) | copy-start | bytes 884740
  66.2 4.9 %copy-start.13 = (bf16[128,1152]{1,0:T(8,128)(2,1)S(1)}, bf16[128,1152]{1,0:T(8,128)(2,1)}, u32[]{:S(2)}) copy-start(bf16[128,1152]{1,0:T(8,128)(2,1)} %copy-done.12) | copy-start | bytes 884740
  66.2 4.9 %copy-start.19 = (bf16[128,1152]{1,0:T(8,128)(2,1)S(1)}, bf16[128,1152]{1,0:T(8,128)(2,1)}, u32[]{:S(2)}) copy-start(bf16[128,1152]{1,0:T(8,128)(2,1)} %copy-done.18) | copy-start | bytes 884740
  67.3 9.8 %collective-permute-start.30 = (bf16[64,1152]{1,0:T(8,128)(2,1)S(1)}, bf16[64,1152]{1,0:T(8,128)(2,1)S(1)}, u32[]{:S(2)}, u32[]{:S(2)}) collective-permute-start(bf16[64,1152]{1,0:T(8,128)(2,1)S(1)} %collective-permute-done.29.refs_4_), channel_id=1, source_target_pairs={{0,8},{1,9},{2,10},{3,11},{4,12},{5,13},{6,14},{7,15},{8,0},{9,1},... | collective-permute-start | bytes 442376 | tf_op jit(solution)/shard_map/ppermute | solution.py:194
  71.0 10.9 %collective-permute-start.5 = (bf16[128,1152]{1,0:T(8,128)(2,1)S(1)}, bf16[128,1152]{1,0:T(8,128)(2,1)S(1)}, u32[]{:S(2)}, u32[]{:S(2)}) collective-permute-start(bf16[128,1152]{1,0:T(8,128)(2,1)S(1)} %collective-permute-done.4.refs_2_), channel_id=1, source_target_pairs={{0,8},{1,9},{2,10},{3,11},{4,12},{5,13},{6,14},{7,15},{8,0},{9,1},... | collective-permute-start | bytes 884744 | tf_op jit(solution)/shard_map/ppermute | solution.py:194
  71.1 1.4 %copy-start.7 = (bf16[128,1152]{1,0:T(8,128)(2,1)S(1)}, bf16[128,1152]{1,0:T(8,128)(2,1)}, u32[]{:S(2)}) copy-start(bf16[128,1152]{1,0:T(8,128)(2,1)} %copy-done.6) | copy-start | bytes 884740
  71.1 1.4 %copy-start.15 = (bf16[128,1152]{1,0:T(8,128)(2,1)S(1)}, bf16[128,1152]{1,0:T(8,128)(2,1)}, u32[]{:S(2)}) copy-start(bf16[128,1152]{1,0:T(8,128)(2,1)} %copy-done.14) | copy-start | bytes 884740
  71.1 1.4 %copy-start.17 = (bf16[128,1152]{1,0:T(8,128)(2,1)S(1)}, bf16[128,1152]{1,0:T(8,128)(2,1)}, u32[]{:S(2)}) copy-start(bf16[128,1152]{1,0:T(8,128)(2,1)} %copy-done.16) | copy-start | bytes 884740
  71.1 1.4 %copy-start.21 = (bf16[128,1152]{1,0:T(8,128)(2,1)S(1)}, bf16[128,1152]{1,0:T(8,128)(2,1)}, u32[]{:S(2)}) copy-start(bf16[128,1152]{1,0:T(8,128)(2,1)} %copy-done.20) | copy-start | bytes 884740
  72.5 1.3 %copy-start.5 = (bf16[128,1152]{1,0:T(8,128)(2,1)S(1)}, bf16[128,1152]{1,0:T(8,128)(2,1)}, u32[]{:S(2)}) copy-start(bf16[128,1152]{1,0:T(8,128)(2,1)} %copy-done.4) | copy-start | bytes 884740
  72.5 1.3 %copy-start.23 = (bf16[128,1152]{1,0:T(8,128)(2,1)S(1)}, bf16[128,1152]{1,0:T(8,128)(2,1)}, u32[]{:S(2)}) copy-start(bf16[128,1152]{1,0:T(8,128)(2,1)} %copy-done.22) | copy-start | bytes 884740
  73.7 2.2 %copy-start.25 = (bf16[64,1152]{1,0:T(8,128)(2,1)S(1)}, bf16[64,1152]{1,0:T(8,128)(2,1)}, u32[]{:S(2)}) copy-start(bf16[64,1152]{1,0:T(8,128)(2,1)} %copy-done.24) | copy-start | bytes 442372
  73.8 2.2 %copy-start.27 = (bf16[64,1152]{1,0:T(8,128)(2,1)S(1)}, bf16[64,1152]{1,0:T(8,128)(2,1)}, u32[]{:S(2)}) copy-start(bf16[64,1152]{1,0:T(8,128)(2,1)} %copy-done.26) | copy-start | bytes 442372
  73.8 2.2 %copy-start.31 = (bf16[64,1152]{1,0:T(8,128)(2,1)S(1)}, bf16[64,1152]{1,0:T(8,128)(2,1)}, u32[]{:S(2)}) copy-start(bf16[64,1152]{1,0:T(8,128)(2,1)} %copy-done.30) | copy-start | bytes 442372
  76.0 1.2 %copy-start.29 = (bf16[64,1152]{1,0:T(8,128)(2,1)S(1)}, bf16[64,1152]{1,0:T(8,128)(2,1)}, u32[]{:S(2)}) copy-start(bf16[64,1152]{1,0:T(8,128)(2,1)} %copy-done.28) | copy-start | bytes 442372
  78.3 34.4 %collective-permute-start.36 = (f32[128,1152]{1,0:T(8,128)S(1)}, f32[128,1152]{1,0:T(8,128)}, u32[]{:S(2)}, u32[]{:S(2)}) collective-permute-start(f32[128,1152]{1,0:T(8,128)S(1)} %get-tuple-element.45), channel_id=1, source_target_pairs={{0,1},{1,0},{2,3},{3,2},{4,5},{5,4},{6,7},{7,6},{8,9},{9,8},{10,11... | collective-permute-start | bytes 1769480 | tf_op jit(solution)/shard_map/ppermute | solution.py:194
  82.0 30.8 %copy-start.1 = (bf16[128,1152]{1,0:T(8,128)(2,1)S(1)}, bf16[128,1152]{1,0:T(8,128)(2,1)}, u32[]{:S(2)}) copy-start(bf16[128,1152]{1,0:T(8,128)(2,1)} %values.7) | copy-start | bytes 884740
  83.0 32.0 %collective-permute-start.23 = (f32[128,1152]{1,0:T(8,128)S(1)}, f32[128,1152]{1,0:T(8,128)S(1)}, u32[]{:S(2)}, u32[]{:S(2)}) collective-permute-start(f32[128,1152]{1,0:T(8,128)S(1)} %get-tuple-element.37), channel_id=1, source_target_pairs={{0,16},{1,17},{2,18},{3,19},{4,20},{5,21},{6,22},{7,23},{8,24},{9,... | collective-permute-start | bytes 1769480 | tf_op jit(solution)/shard_map/ppermute | solution.py:194
  84.8 13.8 %collective-permute-start.37 = (f32[8,128]{1,0:T(8,128)S(1)}, f32[8,128]{1,0:T(8,128)S(1)}, u32[]{:S(2)}, u32[]{:S(2)}) collective-permute-start(f32[8,128]{1,0:T(8,128)S(1)} %get-tuple-element.46), channel_id=1, source_target_pairs={{0,16},{1,17},{2,18},{3,19},{4,20},{5,21},{6,22},{7,23},{8,24},{9,... | collective-permute-start | bytes 12296 | tf_op jit(solution)/shard_map/ppermute | solution.py:194
  98.6 3.6 %collective-permute-start.38 = (f32[8,128]{1,0:T(8,128)S(1)}, f32[8,128]{1,0:T(8,128)S(1)}, u32[]{:S(2)}, u32[]{:S(2)}) collective-permute-start(f32[8,128]{1,0:T(8,128)S(1)} %add.81), channel_id=1, source_target_pairs={{0,1},{1,0},{2,3},{3,2},{4,5},{5,4},{6,7},{7,6},{8,9},{9,8},{10,11... | collective-permute-start | bytes 12296 | tf_op jit(solution)/shard_map/ppermute | solution.py:194
  102.2 1.2 collective-permute-start.39
  103.4 3.6 %collective-permute-start.40 = (f32[8,128]{1,0:T(8,128)S(1)}, f32[8,128]{1,0:T(8,128)S(1)}, u32[]{:S(2)}, u32[]{:S(2)}) collective-permute-start(f32[8,128]{1,0:T(8,128)S(1)} %add.83), channel_id=1, source_target_pairs={{0,2},{1,3},{2,0},{3,1},{4,6},{5,7},{6,4},{7,5},{8,10},{9,11},{10,... | collective-permute-start | bytes 12296 | tf_op jit(solution)/shard_map/ppermute | solution.py:194
  107.0 4.5 %collective-permute-start.41 = (f32[8,128]{1,0:T(8,128)S(1)}, f32[8,128]{1,0:T(8,128)S(1)}, u32[]{:S(2)}, u32[]{:S(2)}) collective-permute-start(f32[8,128]{1,0:T(8,128)S(1)} %add.84), channel_id=1, source_target_pairs={{0,4},{1,5},{2,6},{3,7},{4,0},{5,1},{6,2},{7,3},{8,12},{9,13},{10,... | collective-permute-start | bytes 12296 | tf_op jit(solution)/shard_map/ppermute | solution.py:194
  112.8 2.2 %copy-start.3 = (bf16[128,1152]{1,0:T(8,128)(2,1)S(1)}, bf16[128,1152]{1,0:T(8,128)(2,1)}, u32[]{:S(2)}) copy-start(bf16[128,1152]{1,0:T(8,128)(2,1)} %values.6) | copy-start | bytes 884740
  (18 other events, 12.8 us)

commit v3 on v2

--- a/solution.py
+++ b/solution.py
@@ -33,24 +33,35 @@
     )(values)
 
 
-def project_kernel(count, settings, values, *refs):
-    parts, out = refs[:count], refs[count]
+def project_kernel(count, loss_count, factor, settings, values, *refs):
+    parts, losses, out = refs[:count], refs[count : count + loss_count], refs[count + loss_count]
     unit, recip = unit_of(values[...])
     total = parts[0][...]
     for part in parts[1:]:
         total = total + part[...]
     grad = settings[0:1, 0:1] * total
     out[...] = recip * (grad - unit * jnp.sum(unit * grad, axis=1, keepdims=True))
-
-
-def project(values, settings, parts):
-    return pl.pallas_call(
-        functools.partial(project_kernel, len(parts)),
-        out_shape=jax.ShapeDtypeStruct(values.shape, jnp.float32),
-        in_specs=[VMEM] * (2 + len(parts)),
-        out_specs=VMEM,
+    if loss_count:
+        loss = losses[0][...]
+        for part in losses[1:]:
+            loss = loss + part[...]
+        refs[-1][0] = factor * jnp.sum(loss)
+
+
+def project(values, settings, parts, losses, factor):
+    shapes = [jax.ShapeDtypeStruct(values.shape, jnp.float32)]
+    specs = [VMEM]
+    if losses:
+        shapes.append(jax.ShapeDtypeStruct((1,), jnp.float32))
+        specs.append(pl.BlockSpec(memory_space=pltpu.SMEM))
+    out = pl.pallas_call(
+        functools.partial(project_kernel, len(parts), len(losses), factor),
+        out_shape=shapes,
+        in_specs=[VMEM] * (2 + len(parts) + len(losses)),
+        out_specs=specs,
         compiler_params=PARAMS,
-    )(settings, values, *parts)
+    )(settings, values, *parts, *losses)
+    return tuple(out) if losses else out[0]
 
 
 def terms_kernel(
@@ -64,7 +75,7 @@
     loss_in = refs.pop(0) if loss_own and not loss_first else None
     sums = [refs.pop(0) for _ in range(own_count)]
     losses = refs.pop(0) if loss_own else None
-    own_rows, block_rows = own[0].shape[0], blocks[0].shape[0]
+    own_rows = own[0].shape[0]
     columns = {}
     for a, _ in sorted(pairs):
         if a not in columns:
@@ -76,6 +87,7 @@
 
     def weigh(a, b, dot):
         nonlocal loss
+        block_rows = dot.shape[1]
         logits = settings[0:1, :block_rows] * dot + settings[4:5, :block_rows]
         hit = None
         if (a, b) in pairs:
@@ -97,20 +109,25 @@
     own_all = jnp.concatenate([ref[...] for ref in own], axis=0) if own_count > 1 else own[0][...]
     weights = [[] for _ in own]
     chosen = []
-    group = max(1, 256 // block_rows)
-    for start in range(0, block_count, group):
-        some = range(start, min(start + group, block_count))
-        block_all = jnp.concatenate([blocks[b][...] for b in some], axis=0)
+    start = 0
+    while start < block_count:
+        stop, count = start, 0
+        while stop < block_count and count < 256:
+            count += blocks[stop].shape[0]
+            stop += 1
+        block_all = jnp.concatenate([blocks[b][...] for b in range(start, stop)], axis=0)
         chosen.append(block_all)
         dots = lax.dot_general(
             own_all, block_all, (((1,), (1,)), ((), ())), preferred_element_type=jnp.float32
         )
         for a in range(own_count):
-            for n, b in enumerate(some):
-                dot = dots[
-                    a * own_rows : (a + 1) * own_rows, n * block_rows : (n + 1) * block_rows
-                ]
+            at = 0
+            for b in range(start, stop):
+                upto = at + blocks[b].shape[0]
+                dot = dots[a * own_rows : (a + 1) * own_rows, at:upto]
                 weights[a].append(weigh(a, b, dot))
+                at = upto
+        start = stop
     weight_all = jnp.concatenate([jnp.concatenate(row, axis=1) for row in weights], axis=0)
     block_all = jnp.concatenate(chosen, axis=0)
     term = jnp.dot(weight_all, block_all, preferred_element_type=jnp.float32)
@@ -144,7 +161,7 @@
     if loss_own and loss is not None:
         aliases[len(operands)] = len(own)
         operands.append(loss)
-    size = len(own) * len(blocks) * rows * blocks[0].shape[0]
+    size = len(own) * rows * sum(block.shape[0] for block in blocks)
     out = pl.pallas_call(
         kernel,
         out_shape=shapes,
@@ -170,6 +187,10 @@
     return count // best, best
 
 
+def ring_order(count):
+    return list(range(0, count, 2)) + list(range(1, count, 2))[::-1]
+
+
 def per_device(images, texts, lang_order, position, logit_scale, logit_bias):
     rows, _ = images.shape
     dev_count = lax.axis_size("dev")
@@ -196,13 +217,21 @@
     def shift(array, dim, by):
         return permuted(array, dim, lambda at: (at + by) % sizes[dim])
 
+    ring = ring_order(slow)
+    place_of = [ring.index(at) for at in range(slow)]
+
+    def ring_shift(array):
+        return permuted(array, 2, lambda at: ring[(place_of[at] + 1) % slow])
+
     def exchange(array, dim, by):
         return permuted(array, dim, lambda at: at ^ by)
 
     dev_index = lax.axis_index("dev")
     slow_index, fast_index = dev_index // fast, dev_index % fast
     offsets = jnp.arange(slow * fast, dtype=jnp.int32)
-    bases = (slow_index - offsets // fast) % slow * fast + (fast_index - offsets % fast) % fast
+    ring_index = jnp.array(place_of, dtype=jnp.int32)[slow_index]
+    sources = jnp.array(ring, dtype=jnp.int32)[(ring_index - offsets // fast) % slow]
+    bases = sources * fast + (fast_index - offsets % fast) % fast
     ids = (rows * bases[:, None] + jnp.arange(rows, dtype=jnp.int32)[None, :]).astype(jnp.int32)
     settings = jnp.concatenate(
         [
@@ -241,14 +270,14 @@
     txt_line, img_line, txt_sets, img_sets = [txt_half], [img_half], [], []
     for step in range(slow):
         if step:
-            txt_line.append(shift(txt_line[-1], 2, 1))
+            txt_line.append(ring_shift(txt_line[-1]))
         txt_sets.append(txt_blocks(txt_line[-1]))
         if step < end:
             if step:
-                img_line.append(shift(img_line[-1], 2, 1))
+                img_line.append(ring_shift(img_line[-1]))
             img_sets.append(img_blocks(img_line[-1]))
-    first = shift(img_line[-1][:middle], 2, 1)
-    second = shift(img_line[-1][middle:], 2, 1)
+    first = ring_shift(img_line[-1][:middle])
+    second = ring_shift(img_line[-1][middle:])
     first_set, second_set = img_blocks(first), img_blocks(second)
     img_own = [cores_of[0] for cores_of in img_sets[0]]
     txt_own = [cores_of[0] for cores_of in txt_sets[0]]
@@ -278,41 +307,36 @@
         )
 
     img_sums = txt_sums = loss = None
+    halves = [(first_set, 0), (second_set, middle)]
     for step in range(end):
         parts = [(step, at) for at in range(fast)]
         if step == end - 1:
             parts.append((end, 0))
         img_sums, loss = image_terms(img_sums, loss, parts)
         parts = [(img_sets[step][at], step, at, 0) for at in range(wide)]
+        if step == end - 1:
+            parts += [(half[0], end, 0, offset) for half, offset in halves]
         counted = range(1, fast) if step == 1 else ()
         txt_sums, loss = text_terms(txt_sums, loss, parts, counted)
-    halves = [(first_set, 0), (second_set, middle)]
-    txt_sums, loss = text_terms(
-        txt_sums, loss, [(half[0], end, 0, offset) for half, offset in halves],
-        range(1, fast) if end == 1 else (),
-    )
     if fast > 1:
         parts = [(end, at) for at in range(1, fast)]
         img_sums, loss = image_terms(img_sums, loss, parts, False)
     if wide > 1:
         parts = [(half[at], end, at, offset) for at in range(1, wide) for half, offset in halves]
-        txt_sums, loss = text_terms(txt_sums, loss, parts, range(1, fast) if end == 1 else ())
-
-    for dim in (0, 3, 1, 2):
-        size = sizes[dim]
-        if size & (size - 1) == 0:
-            by = 1
-            while by < size:
-                loss = loss + exchange(loss, dim, by)
-                by = 2 * by
-        else:
-            loss = sum((shift(loss, dim, by) for by in range(1, size)), loss)
-    total = jnp.float32(rows * dev_count * group_count)
-    loss = (jnp.sum(loss) / (total * total)).reshape(1)
+        txt_sums, loss = text_terms(txt_sums, loss, parts)
+
+    addends = [loss]
+    for dim in (0, 1, 2, 3):
+        by = 1
+        while by < sizes[dim]:
+            loss = sum(addends[1:], addends[0])
+            addends = [loss, exchange(loss, dim, by)]
+            by = 2 * by
+    total = float(rows * dev_count * group_count)
     img_parts = [img_sums[0]] + [shift(img_sums[a], 0, -a) for a in range(1, wide)]
     txt_parts = [txt_sums[0]] + [shift(txt_sums[a], 3, -a) for a in range(1, fast)]
-    image_grad = project(images, settings, img_parts)
-    text_grad = project(texts, settings, txt_parts)
+    image_grad = project(images, settings, img_parts, [], 0.0)
+    text_grad, loss = project(texts, settings, txt_parts, addends, 1 / (total * total))
     return (image_grad, text_grad, loss)
 
 

time: 117 us -> 116 us (level)
  starting transfers between devices: 20.6 us -> 39.1 us
  waiting for transfers between devices: 60.8 us -> 46 us
  local copies, waits for them, and re-layouts: 13.7 us -> 11.1 us
  between operations: 4.24 us -> 2.2 us
    ppermute x42, starting transfers between devices: 20.6 us -> 39.1 us  [permuted(): return lax.ppermute(array, AXES, pairs)]
    ppermute x42, waiting for transfers between devices: 60.8 us -> 46 us  [permuted(): return lax.ppermute(array, AXES, pairs)]
    unnamed x80 -> x40, local copies, waits for them, and re-layouts: 13.6 us -> 8.56 us
    pallas_call x9 -> x8, Pallas kernels: 13.5 us -> 14 us  [terms(): pl.pallas_call(kernel, out_shape=shapes, in_specs=[VMEM] * len(operands),...]
  transfers between devices with their start and end apart: 42 -> 42, of which waited for: 17 -> 14; matrix products, arithmetic and copies ran while one was open for 1% -> 3% of each run, Pallas kernels for 14% -> 13%
where the time goes in v3:
time: 116 us
  waiting for transfers between devices  46 us (40%)
  starting transfers between devices  39.1 us (34%)
  Pallas kernels  16.5 us (14%)
  local copies, waits for them, and re-layouts  11.1 us (10%)
  between operations  2.2 us (2%)
    ppermute x42, waiting for transfers between devices, permuted(): return lax.ppermute(array, AXES, pairs)  46 us
    ppermute x42, starting transfers between devices, permuted(): return lax.ppermute(array, AXES, pairs)  39.1 us
    pallas_call x8, Pallas kernels, terms(): pl.pallas_call(kernel, out_shape=shapes, in_specs=[VMEM] * len(operands),...  14 us
    unnamed x40, local copies, waits for them, and re-layouts  8.56 us
  transfers between devices with their start and end apart: 42, of which 14 were waited for; matrix products, arithmetic and copies ran while one was open for 3% of the time, Pallas kernels for 13%

profile of v3, /device:TPU:0, one launch (start us, length us, event | category | flops | bytes accessed | tf_op | source)
XLA Modules:
  0.0 115.6 jit_solution(9555256443325070101)
XLA Ops:
  0.6 1.0 copy-done
  1.7 3.1 %collective-permute-start.14 = (bf16[128,1152]{1,0:T(8,128)(2,1)S(1)}, bf16[128,1152]{1,0:T(8,128)(2,1)S(1)}, u32[]{:S(2)}, u32[]{:S(2)}) collective-permute-start(bf16[128,1152]{1,0:T(8,128)(2,1)S(1)} %shard_map.104.refs_2_.refs_0_), channel_id=1, source_target_pairs={{0,1},{1,0},{2,3},{3,2},{4,5},{5,4},{6,7},{7,6},{8,9},{9,8},{10,11... | collective-permute-start | bytes 884744 | tf_op jit(solution)/shard_map/ppermute | solution.py:215
  5.0 1.6 %collective-permute-start = (bf16[128,1152]{1,0:T(8,128)(2,1)S(1)}, bf16[128,1152]{1,0:T(8,128)(2,1)S(1)}, u32[]{:S(2)}, u32[]{:S(2)}) collective-permute-start(bf16[128,1152]{1,0:T(8,128)(2,1)S(1)} %shard_map.103.refs_0_.refs_2_), channel_id=1, source_target_pairs={{0,16},{1,17},{2,18},{3,19},{4,20},{5,21},{6,22},{7,23},{8,24},{9,... | collective-permute-start | bytes 884744 | tf_op jit(solution)/shard_map/ppermute | solution.py:215
  6.5 2.6 %collective-permute-start.1 = (bf16[128,1152]{1,0:T(8,128)(2,1)S(1)}, bf16[128,1152]{1,0:T(8,128)(2,1)S(1)}, u32[]{:S(2)}, u32[]{:S(2)}) collective-permute-start(bf16[128,1152]{1,0:T(8,128)(2,1)S(1)} %shard_map.104.refs_2_.refs_0_), channel_id=1, source_target_pairs={{0,4},{1,5},{2,0},{3,1},{4,6},{5,7},{6,2},{7,3},{8,12},{9,13},{10,... | collective-permute-start | bytes 884744 | tf_op jit(solution)/shard_map/ppermute | solution.py:215
  9.1 1.6 %collective-permute-start.16 = (bf16[128,1152]{1,0:T(8,128)(2,1)S(1)}, bf16[128,1152]{1,0:T(8,128)(2,1)S(1)}, u32[]{:S(2)}, u32[]{:S(2)}) collective-permute-start(bf16[128,1152]{1,0:T(8,128)(2,1)S(1)} %shard_map.103.refs_0_.refs_2_), channel_id=1, source_target_pairs={{0,4},{1,5},{2,0},{3,1},{4,6},{5,7},{6,2},{7,3},{8,12},{9,13},{10,... | collective-permute-start | bytes 884744 | tf_op jit(solution)/shard_map/ppermute | solution.py:215
  10.7 0.7 collective-permute-start.20
  11.4 2.8 %collective-permute-done.20.refs_7_.refs_11_ = s32[1,128]{1,0:T(1,128)S(1)} collective-permute-done((s32[1,128]{1,0:T(1,128)S(1)}, s32[1,128]{1,0:T(1,128)S(1)}, u32[]{:S(2)}, u32[]{:S(2)}) %collective-permute-start.20) | collective-permute-done | bytes 544 | tf_op jit(solution)/shard_map/ppermute | solution.py:215
  14.3 0.5 collective-permute-start.21
  14.9 1.7 %collective-permute-done.1.refs_2_ = bf16[128,1152]{1,0:T(8,128)(2,1)S(1)} collective-permute-done((bf16[128,1152]{1,0:T(8,128)(2,1)S(1)}, bf16[128,1152]{1,0:T(8,128)(2,1)S(1)}, u32[]{:S(2)}, u32[]{:S(2)}) %collective-permute-start.1) | collective-permute-done | bytes 294944 | tf_op jit(solution)/shard_map/ppermute | solution.py:215
  16.5 0.7 collective-permute-start.11
  17.3 3.9 %collective-permute-done.16.refs_2_ = bf16[128,1152]{1,0:T(8,128)(2,1)S(1)} collective-permute-done((bf16[128,1152]{1,0:T(8,128)(2,1)S(1)}, bf16[128,1152]{1,0:T(8,128)(2,1)S(1)}, u32[]{:S(2)}, u32[]{:S(2)}) %collective-permute-start.16) | collective-permute-done | bytes 294944 | tf_op jit(solution)/shard_map/ppermute | solution.py:215
  21.1 3.4 %collective-permute-start.24 = (bf16[128,1152]{1,0:T(8,128)(2,1)S(1)}, bf16[128,1152]{1,0:T(8,128)(2,1)S(1)}, u32[]{:S(2)}, u32[]{:S(2)}) collective-permute-start(bf16[128,1152]{1,0:T(8,128)(2,1)S(1)} %collective-permute-done.16.refs_2_), channel_id=1, source_target_pairs={{0,4},{1,5},{2,0},{3,1},{4,6},{5,7},{6,2},{7,3},{8,12},{9,13},{10,... | collective-permute-start | bytes 884744 | tf_op jit(solution)/shard_map/ppermute | solution.py:215
  24.5 0.7 copy-done.9
  25.3 0.7 copy-done.11
  26.0 0.5 collective-permute-start.18
  26.5 0.7 copy-done.13
  27.5 0.7 collective-permute-start.2
  28.2 2.0 %collective-permute-done.24.refs_2_ = bf16[128,1152]{1,0:T(8,128)(2,1)S(1)} collective-permute-done((bf16[128,1152]{1,0:T(8,128)(2,1)S(1)}, bf16[128,1152]{1,0:T(8,128)(2,1)S(1)}, u32[]{:S(2)}, u32[]{:S(2)}) %collective-permute-start.24) | collective-permute-done | bytes 294944 | tf_op jit(solution)/shard_map/ppermute | solution.py:215
  30.2 0.7 fusion.7
  30.9 0.7 copy-done.3
  31.6 3.4 %collective-permute-start.25 = (bf16[64,1152]{1,0:T(8,128)(2,1)S(1)}, bf16[64,1152]{1,0:T(8,128)(2,1)}, u32[]{:S(2)}, u32[]{:S(2)}) collective-permute-start(bf16[64,1152]{1,0:T(8,128)(2,1)S(1)} %get-tuple-element.48), channel_id=1, source_target_pairs={{0,4},{1,5},{2,0},{3,1},{4,6},{5,7},{6,2},{7,3},{8,12},{9,13},{10,... | collective-permute-start | bytes 442376 | tf_op jit(solution)/shard_map/ppermute | solution.py:215
  35.0 0.7 copy-done.15
  36.2 1.1 collective-permute-done.2.refs_2_
  37.4 1.8 %collective-permute-start.3 = (bf16[128,1152]{1,0:T(8,128)(2,1)S(1)}, bf16[128,1152]{1,0:T(8,128)(2,1)S(1)}, u32[]{:S(2)}, u32[]{:S(2)}) collective-permute-start(bf16[128,1152]{1,0:T(8,128)(2,1)S(1)} %collective-permute-done.2.refs_2_), channel_id=1, source_target_pairs={{0,4},{1,5},{2,0},{3,1},{4,6},{5,7},{6,2},{7,3},{8,12},{9,13},{10,... | collective-permute-start | bytes 884744 | tf_op jit(solution)/shard_map/ppermute | solution.py:215
  39.2 0.7 copy-done.5
  39.9 1.2 %collective-permute-start.7 = (bf16[128,1152]{1,0:T(8,128)(2,1)S(1)}, bf16[128,1152]{1,0:T(8,128)(2,1)S(1)}, u32[]{:S(2)}, u32[]{:S(2)}) collective-permute-start(bf16[128,1152]{1,0:T(8,128)(2,1)S(1)} %collective-permute-done.2.refs_2_), channel_id=1, source_target_pairs={{0,1},{1,0},{2,3},{3,2},{4,5},{5,4},{6,7},{7,6},{8,9},{9,8},{10,11... | collective-permute-start | bytes 884744 | tf_op jit(solution)/shard_map/ppermute | solution.py:215
  41.1 1.6 %collective-permute-start.28 = (bf16[64,1152]{1,0:T(8,128)(2,1)}, bf16[64,1152]{1,0:T(8,128)(2,1)}, u32[]{:S(2)}, u32[]{:S(2)}) collective-permute-start(bf16[64,1152]{1,0:T(8,128)(2,1)} %get-tuple-element.47), channel_id=1, source_target_pairs={{0,4},{1,5},{2,0},{3,1},{4,6},{5,7},{6,2},{7,3},{8,12},{9,13},{10,... | collective-permute-start | bytes 442376 | tf_op jit(solution)/shard_map/ppermute | solution.py:215
  42.7 0.7 copy-done.19
  43.4 0.6 dynamic_slice.3
  44.0 0.7 fusion.4
  44.6 4.8 %collective-permute-done.28.refs_8_ = bf16[64,1152]{1,0:T(8,128)(2,1)} collective-permute-done((bf16[64,1152]{1,0:T(8,128)(2,1)}, bf16[64,1152]{1,0:T(8,128)(2,1)}, u32[]{:S(2)}, u32[]{:S(2)}) %collective-permute-start.28) | collective-permute-done | bytes 147488 | tf_op jit(solution)/shard_map/ppermute | solution.py:215
  49.4 1.5 %collective-permute-start.32 = (bf16[128,1152]{1,0:T(8,128)(2,1)S(1)}, bf16[128,1152]{1,0:T(8,128)(2,1)}, u32[]{:S(2)}, u32[]{:S(2)}) collective-permute-start(bf16[128,1152]{1,0:T(8,128)(2,1)S(1)} %collective-permute-done.24.refs_2_), channel_id=1, source_target_pairs={{0,16},{1,17},{2,18},{3,19},{4,20},{5,21},{6,22},{7,23},{8,24},{9,... | collective-permute-start | bytes 884744 | tf_op jit(solution)/shard_map/ppermute | solution.py:215
  50.9 1.2 gather_fusion
  52.1 0.5 collective-permute-start.34
  52.6 0.5 collective-permute-start.26
  54.5 1.6 %collective-permute-start.29 = (bf16[64,1152]{1,0:T(8,128)(2,1)}, bf16[64,1152]{1,0:T(8,128)(2,1)S(1)}, u32[]{:S(2)}, u32[]{:S(2)}) collective-permute-start(bf16[64,1152]{1,0:T(8,128)(2,1)} %collective-permute-done.28.refs_8_), channel_id=1, source_target_pairs={{0,16},{1,17},{2,18},{3,19},{4,20},{5,21},{6,22},{7,23},{8,24},{9,... | collective-permute-start | bytes 442376 | tf_op jit(solution)/shard_map/ppermute | solution.py:215
  56.1 3.3 %collective-permute-done.32.refs_4_ = bf16[128,1152]{1,0:T(8,128)(2,1)} collective-permute-done((bf16[128,1152]{1,0:T(8,128)(2,1)S(1)}, bf16[128,1152]{1,0:T(8,128)(2,1)}, u32[]{:S(2)}, u32[]{:S(2)}) %collective-permute-start.32) | collective-permute-done | bytes 294944 | tf_op jit(solution)/shard_map/ppermute | solution.py:215
  59.3 2.8 %collective-permute-done.26.refs_2_ = bf16[64,1152]{1,0:T(8,128)(2,1)S(1)} collective-permute-done((bf16[64,1152]{1,0:T(8,128)(2,1)}, bf16[64,1152]{1,0:T(8,128)(2,1)S(1)}, u32[]{:S(2)}, u32[]{:S(2)}) %collective-permute-start.26) | collective-permute-done | bytes 147488 | tf_op jit(solution)/shard_map/ppermute | solution.py:215
  62.1 1.3 %collective-permute-start.4 = (bf16[128,1152]{1,0:T(8,128)(2,1)S(1)}, bf16[128,1152]{1,0:T(8,128)(2,1)S(1)}, u32[]{:S(2)}, u32[]{:S(2)}) collective-permute-start(bf16[128,1152]{1,0:T(8,128)(2,1)S(1)} %collective-permute-done.3.refs_6_), channel_id=1, source_target_pairs={{0,1},{1,0},{2,3},{3,2},{4,5},{5,4},{6,7},{7,6},{8,9},{9,8},{10,11... | collective-permute-start | bytes 884744 | tf_op jit(solution)/shard_map/ppermute | solution.py:215
  64.3 0.7 copy-done.7
  65.0 1.0 copy-done.10
  65.9 1.0 copy-done.14
  66.9 1.3 %shard_map.105 = (f32[128,1152]{1,0:T(8,128)S(1)}, f32[128,1152]{1,0:T(8,128)S(1)}, f32[8,128]{1,0:T(8,128)S(1)}) custom-call(f32[8,128]{1,0:T(8,128)S(1)} %concatenate.6.settings, s32[8,128]{1,0:T(8,128)S(1)} %iota_add_fusion.ids, bf16[128,1152]{1,0:T(8,128)(2,1)S(1)} %shard_map.103.refs_0_.refs_2_, ...), custom_call_target="tpu_custom_call" | custom-call | flops 603979776 | bytes 4128768 | tf_op jit(solution)/shard_map/pallas_call | solution.py:165
  68.2 1.1 shard_map.107
  69.7 1.8 %collective-permute-done.4.refs_2_ = bf16[128,1152]{1,0:T(8,128)(2,1)S(1)} collective-permute-done((bf16[128,1152]{1,0:T(8,128)(2,1)S(1)}, bf16[128,1152]{1,0:T(8,128)(2,1)S(1)}, u32[]{:S(2)}, u32[]{:S(2)}) %collective-permute-start.4) | collective-permute-done | bytes 294944 | tf_op jit(solution)/shard_map/ppermute | solution.py:215
  71.5 2.3 %shard_map.106 = (f32[128,1152]{1,0:T(8,128)S(1)}, f32[128,1152]{1,0:T(8,128)S(1)}, f32[8,128]{1,0:T(8,128)S(1)}) custom-call(f32[8,128]{1,0:T(8,128)S(1)} %concatenate.6.settings, s32[8,128]{1,0:T(8,128)S(1)} %iota_add_fusion.ids, bf16[128,1152]{1,0:T(8,128)(2,1)S(1)} %shard_map.103.refs_0_.refs_2_, ...), custom_call_target="tpu_custom_call", output_to_operand_aliasing={{0}: (10, {}), {1}: (11, {}), {2}: (12, {})} | custom-call | flops 603979776 | bytes 4128768 | tf_op jit(solution)/shard_map/pallas_call | solution.py:165
  73.9 2.3 %shard_map.108 = (f32[128,1152]{1,0:T(8,128)S(1)}, f32[128,1152]{1,0:T(8,128)S(1)}, f32[8,128]{1,0:T(8,128)S(1)}) custom-call(f32[8,128]{1,0:T(8,128)S(1)} %concatenate.6.settings, s32[8,128]{1,0:T(8,128)S(1)} %iota_add_fusion.ids, bf16[128,1152]{1,0:T(8,128)(2,1)S(1)} %shard_map.104.refs_2_.refs_0_, ...), custom_call_target="tpu_custom_call", output_to_operand_aliasing={{0}: (10, {}), {1}: (11, {}), {2}: (12, {})} | custom-call | flops 603979776 | bytes 4128768 | tf_op jit(solution)/shard_map/pallas_call | solution.py:165
  76.2 2.9 %shard_map.112 = (f32[128,1152]{1,0:T(8,128)S(1)}, f32[128,1152]{1,0:T(8,128)S(1)}) custom-call(f32[8,128]{1,0:T(8,128)S(1)} %concatenate.6.settings, s32[8,128]{1,0:T(8,128)S(1)} %iota_add_fusion.ids, bf16[128,1152]{1,0:T(8,128)(2,1)S(1)} %shard_map.104.refs_2_.refs_0_, ...), custom_call_target="tpu_custom_call", output_to_operand_aliasing={{0}: (14, {}), {1}: (15, {})} | custom-call | flops 905969664 | bytes 5308416 | tf_op jit(solution)/shard_map/pallas_call | solution.py:165
  79.0 1.1 shard_map.113
  80.2 1.4 %collective-permute-start.36 = (f32[128,1152]{1,0:T(8,128)S(1)}, f32[128,1152]{1,0:T(8,128)S(1)}, u32[]{:S(2)}, u32[]{:S(2)}) collective-permute-start(f32[128,1152]{1,0:T(8,128)S(1)} %get-tuple-element.43), channel_id=1, source_target_pairs={{0,1},{1,0},{2,3},{3,2},{4,5},{5,4},{6,7},{7,6},{8,9},{9,8},{10,11... | collective-permute-start | bytes 1769480 | tf_op jit(solution)/shard_map/ppermute | solution.py:215
  81.6 2.0 %shard_map.109 = (f32[128,1152]{1,0:T(8,128)S(1)}, f32[128,1152]{1,0:T(8,128)S(1)}, f32[8,128]{1,0:T(8,128)S(1)}) custom-call(f32[8,128]{1,0:T(8,128)S(1)} %concatenate.6.settings, s32[8,128]{1,0:T(8,128)S(1)} %iota_add_fusion.ids, bf16[128,1152]{1,0:T(8,128)(2,1)S(1)} %shard_map.103.refs_0_.refs_2_, ...), custom_call_target="tpu_custom_call", output_to_operand_aliasing={{0}: (12, {}), {1}: (13, {}), {2}: (14, {})} | custom-call | flops 905969664 | bytes 4718592 | tf_op jit(solution)/shard_map/pallas_call | solution.py:165
  83.6 1.0 shard_map.110
  84.5 1.3 %collective-permute-start.23 = (f32[128,1152]{1,0:T(8,128)S(1)}, f32[128,1152]{1,0:T(8,128)S(1)}, u32[]{:S(2)}, u32[]{:S(2)}) collective-permute-start(f32[128,1152]{1,0:T(8,128)S(1)} %get-tuple-element.37), channel_id=1, source_target_pairs={{0,16},{1,17},{2,18},{3,19},{4,20},{5,21},{6,22},{7,23},{8,24},{9,... | collective-permute-start | bytes 1769480 | tf_op jit(solution)/shard_map/ppermute | solution.py:215
  85.8 0.8 collective-permute-start.37
  86.6 13.5 %collective-permute-done.37 = f32[8,128]{1,0:T(8,128)S(1)} collective-permute-done((f32[8,128]{1,0:T(8,128)S(1)}, f32[8,128]{1,0:T(8,128)S(1)}, u32[]{:S(2)}, u32[]{:S(2)}) %collective-permute-start.37) | collective-permute-done | bytes 4128 | tf_op jit(solution)/shard_map/ppermute | solution.py:215
  100.2 1.2 %collective-permute-done.38 = f32[8,128]{1,0:T(8,128)S(1)} collective-permute-done((f32[8,128]{1,0:T(8,128)S(1)}, f32[8,128]{1,0:T(8,128)S(1)}, u32[]{:S(2)}, u32[]{:S(2)}) %collective-permute-start.38) | collective-permute-done | bytes 4128 | tf_op jit(solution)/shard_map/ppermute | solution.py:215
  101.3 2.3 %collective-permute-start.39 = (f32[8,128]{1,0:T(8,128)S(1)}, f32[8,128]{1,0:T(8,128)S(1)}, u32[]{:S(2)}, u32[]{:S(2)}) collective-permute-start(f32[8,128]{1,0:T(8,128)S(1)} %add.100), channel_id=1, source_target_pairs={{0,2},{1,3},{2,0},{3,1},{4,6},{5,7},{6,4},{7,5},{8,10},{9,11},{10,... | collective-permute-start | bytes 12296 | tf_op jit(solution)/shard_map/ppermute | solution.py:215
  103.6 1.6 %collective-permute-done.39 = f32[8,128]{1,0:T(8,128)S(1)} collective-permute-done((f32[8,128]{1,0:T(8,128)S(1)}, f32[8,128]{1,0:T(8,128)S(1)}, u32[]{:S(2)}, u32[]{:S(2)}) %collective-permute-start.39) | collective-permute-done | bytes 4128 | tf_op jit(solution)/shard_map/ppermute | solution.py:215
  105.2 2.2 %collective-permute-start.40 = (f32[8,128]{1,0:T(8,128)S(1)}, f32[8,128]{1,0:T(8,128)S(1)}, u32[]{:S(2)}, u32[]{:S(2)}) collective-permute-start(f32[8,128]{1,0:T(8,128)S(1)} %add.101), channel_id=1, source_target_pairs={{0,4},{1,5},{2,6},{3,7},{4,0},{5,1},{6,2},{7,3},{8,12},{9,13},{10,... | collective-permute-start | bytes 12296 | tf_op jit(solution)/shard_map/ppermute | solution.py:215
  107.5 2.3 %collective-permute-done.40 = f32[8,128]{1,0:T(8,128)S(1)} collective-permute-done((f32[8,128]{1,0:T(8,128)S(1)}, f32[8,128]{1,0:T(8,128)S(1)}, u32[]{:S(2)}, u32[]{:S(2)}) %collective-permute-start.40) | collective-permute-done | bytes 4128 | tf_op jit(solution)/shard_map/ppermute | solution.py:215
  109.7 0.4 collective-permute-start.41
  110.2 3.2 %collective-permute-done.41.refs_3_ = f32[8,128]{1,0:T(8,128)S(1)} collective-permute-done((f32[8,128]{1,0:T(8,128)S(1)}, f32[8,128]{1,0:T(8,128)S(1)}, u32[]{:S(2)}, u32[]{:S(2)}) %collective-permute-start.41) | collective-permute-done | bytes 4128 | tf_op jit(solution)/shard_map/ppermute | solution.py:215
  113.4 1.1 shard_map.114
  114.5 1.1 shard_map.111
  (86 shorter events, 2.5 us)
Async XLA Ops:
  0.6 1.0 copy-start
  1.6 3.2 %copy-start.2 = (bf16[128,1152]{1,0:T(8,128)(2,1)S(1)}, bf16[128,1152]{1,0:T(8,128)(2,1)}, u32[]{:S(2)}) copy-start(bf16[128,1152]{1,0:T(8,128)(2,1)} %values.6) | copy-start | bytes 884740
  1.7 12.5 %collective-permute-start.14 = (bf16[128,1152]{1,0:T(8,128)(2,1)S(1)}, bf16[128,1152]{1,0:T(8,128)(2,1)S(1)}, u32[]{:S(2)}, u32[]{:S(2)}) collective-permute-start(bf16[128,1152]{1,0:T(8,128)(2,1)S(1)} %shard_map.104.refs_2_.refs_0_), channel_id=1, source_target_pairs={{0,1},{1,0},{2,3},{3,2},{4,5},{5,4},{6,7},{7,6},{8,9},{9,8},{10,11... | collective-permute-start | bytes 884744 | tf_op jit(solution)/shard_map/ppermute | solution.py:215
  5.0 5.7 %copy-start.8 = (s32[128]{0:T(128)S(1)}, s32[128]{0:T(128)}, u32[]{:S(2)}) copy-start(s32[128]{0:T(128)} %param.10) | copy-start | bytes 1540
  5.0 9.8 %collective-permute-start = (bf16[128,1152]{1,0:T(8,128)(2,1)S(1)}, bf16[128,1152]{1,0:T(8,128)(2,1)S(1)}, u32[]{:S(2)}, u32[]{:S(2)}) collective-permute-start(bf16[128,1152]{1,0:T(8,128)(2,1)S(1)} %shard_map.103.refs_0_.refs_2_), channel_id=1, source_target_pairs={{0,16},{1,17},{2,18},{3,19},{4,20},{5,21},{6,22},{7,23},{8,24},{9,... | collective-permute-start | bytes 884744 | tf_op jit(solution)/shard_map/ppermute | solution.py:215
  6.5 10.0 %collective-permute-start.1 = (bf16[128,1152]{1,0:T(8,128)(2,1)S(1)}, bf16[128,1152]{1,0:T(8,128)(2,1)S(1)}, u32[]{:S(2)}, u32[]{:S(2)}) collective-permute-start(bf16[128,1152]{1,0:T(8,128)(2,1)S(1)} %shard_map.104.refs_2_.refs_0_), channel_id=1, source_target_pairs={{0,4},{1,5},{2,0},{3,1},{4,6},{5,7},{6,2},{7,3},{8,12},{9,13},{10,... | collective-permute-start | bytes 884744 | tf_op jit(solution)/shard_map/ppermute | solution.py:215
  9.1 12.0 %collective-permute-start.16 = (bf16[128,1152]{1,0:T(8,128)(2,1)S(1)}, bf16[128,1152]{1,0:T(8,128)(2,1)S(1)}, u32[]{:S(2)}, u32[]{:S(2)}) collective-permute-start(bf16[128,1152]{1,0:T(8,128)(2,1)S(1)} %shard_map.103.refs_0_.refs_2_), channel_id=1, source_target_pairs={{0,4},{1,5},{2,0},{3,1},{4,6},{5,7},{6,2},{7,3},{8,12},{9,13},{10,... | collective-permute-start | bytes 884744 | tf_op jit(solution)/shard_map/ppermute | solution.py:215
  10.7 3.6 %collective-permute-start.20 = (s32[1,128]{1,0:T(1,128)S(1)}, s32[1,128]{1,0:T(1,128)S(1)}, u32[]{:S(2)}, u32[]{:S(2)}) collective-permute-start(s32[1,128]{1,0:T(1,128)S(1)} %bitcast.17), channel_id=1, source_target_pairs={{0,1},{1,0},{2,3},{3,2},{4,5},{5,4},{6,7},{7,6},{8,9},{9,8},{10,11... | collective-permute-start | bytes 1544 | tf_op jit(solution)/shard_map/ppermute | solution.py:215
  14.3 10.3 %collective-permute-start.13 = (bf16[128,1152]{1,0:T(8,128)(2,1)S(1)}, bf16[128,1152]{1,0:T(8,128)(2,1)S(1)}, u32[]{:S(2)}, u32[]{:S(2)}) collective-permute-start(bf16[128,1152]{1,0:T(8,128)(2,1)S(1)} %shard_map.104.refs_2_.refs_0_), channel_id=1, source_target_pairs={{0,8},{1,9},{2,10},{3,11},{4,12},{5,13},{6,14},{7,15},{8,0},{9,1},... | collective-permute-start | bytes 884744 | tf_op jit(solution)/shard_map/ppermute | solution.py:215
  14.3 11.0 %collective-permute-start.21 = (bf16[128,1152]{1,0:T(8,128)(2,1)S(1)}, bf16[128,1152]{1,0:T(8,128)(2,1)S(1)}, u32[]{:S(2)}, u32[]{:S(2)}) collective-permute-start(bf16[128,1152]{1,0:T(8,128)(2,1)S(1)} %shard_map.103.refs_0_.refs_2_), channel_id=1, source_target_pairs={{0,8},{1,9},{2,10},{3,11},{4,12},{5,13},{6,14},{7,15},{8,0},{9,1},... | collective-permute-start | bytes 884744 | tf_op jit(solution)/shard_map/ppermute | solution.py:215
  14.8 11.7 %collective-permute-start.15 = (bf16[128,1152]{1,0:T(8,128)(2,1)S(1)}, bf16[128,1152]{1,0:T(8,128)(2,1)S(1)}, u32[]{:S(2)}, u32[]{:S(2)}) collective-permute-start(bf16[128,1152]{1,0:T(8,128)(2,1)S(1)} %collective-permute-done.14.refs_4_.refs_1_), channel_id=1, source_target_pairs={{0,8},{1,9},{2,10},{3,11},{4,12},{5,13},{6,14},{7,15},{8,0},{9,1},... | collective-permute-start | bytes 884744 | tf_op jit(solution)/shard_map/ppermute | solution.py:215
  16.5 11.0 %collective-permute-start.11 = (bf16[128,1152]{1,0:T(8,128)(2,1)S(1)}, bf16[128,1152]{1,0:T(8,128)(2,1)S(1)}, u32[]{:S(2)}, u32[]{:S(2)}) collective-permute-start(bf16[128,1152]{1,0:T(8,128)(2,1)S(1)} %collective-permute-done.1.refs_2_), channel_id=1, source_target_pairs={{0,1},{1,0},{2,3},{3,2},{4,5},{5,4},{6,7},{7,6},{8,9},{9,8},{10,11... | collective-permute-start | bytes 884744 | tf_op jit(solution)/shard_map/ppermute | solution.py:215
  21.1 9.0 %collective-permute-start.24 = (bf16[128,1152]{1,0:T(8,128)(2,1)S(1)}, bf16[128,1152]{1,0:T(8,128)(2,1)S(1)}, u32[]{:S(2)}, u32[]{:S(2)}) collective-permute-start(bf16[128,1152]{1,0:T(8,128)(2,1)S(1)} %collective-permute-done.16.refs_2_), channel_id=1, source_target_pairs={{0,4},{1,5},{2,0},{3,1},{4,6},{5,7},{6,2},{7,3},{8,12},{9,13},{10,... | collective-permute-start | bytes 884744 | tf_op jit(solution)/shard_map/ppermute | solution.py:215
  24.5 0.7 copy-start.9
  25.2 5.6 %collective-permute-start.10 = (bf16[128,1152]{1,0:T(8,128)(2,1)S(1)}, bf16[128,1152]{1,0:T(8,128)(2,1)S(1)}, u32[]{:S(2)}, u32[]{:S(2)}) collective-permute-start(bf16[128,1152]{1,0:T(8,128)(2,1)S(1)} %collective-permute-done.1.refs_2_), channel_id=1, source_target_pairs={{0,8},{1,9},{2,10},{3,11},{4,12},{5,13},{6,14},{7,15},{8,0},{9,1},... | collective-permute-start | bytes 884744 | tf_op jit(solution)/shard_map/ppermute | solution.py:215
  25.3 0.7 copy-start.11
  26.0 10.0 %collective-permute-start.18 = (bf16[128,1152]{1,0:T(8,128)(2,1)S(1)}, bf16[128,1152]{1,0:T(8,128)(2,1)}, u32[]{:S(2)}, u32[]{:S(2)}) collective-permute-start(bf16[128,1152]{1,0:T(8,128)(2,1)S(1)} %collective-permute-done.16.refs_2_), channel_id=1, source_target_pairs={{0,16},{1,17},{2,18},{3,19},{4,20},{5,21},{6,22},{7,23},{8,24},{9,... | collective-permute-start | bytes 884744 | tf_op jit(solution)/shard_map/ppermute | solution.py:215
  26.5 0.7 copy-start.13
  27.2 11.9 %collective-permute-start.17 = (bf16[128,1152]{1,0:T(8,128)(2,1)S(1)}, bf16[128,1152]{1,0:T(8,128)(2,1)S(1)}, u32[]{:S(2)}, u32[]{:S(2)}) collective-permute-start(bf16[128,1152]{1,0:T(8,128)(2,1)S(1)} %collective-permute-done.16.refs_2_), channel_id=1, source_target_pairs={{0,8},{1,9},{2,10},{3,11},{4,12},{5,13},{6,14},{7,15},{8,0},{9,1},... | collective-permute-start | bytes 884744 | tf_op jit(solution)/shard_map/ppermute | solution.py:215
  27.5 9.9 %collective-permute-start.2 = (bf16[128,1152]{1,0:T(8,128)(2,1)S(1)}, bf16[128,1152]{1,0:T(8,128)(2,1)S(1)}, u32[]{:S(2)}, u32[]{:S(2)}) collective-permute-start(bf16[128,1152]{1,0:T(8,128)(2,1)S(1)} %collective-permute-done.1.refs_2_), channel_id=1, source_target_pairs={{0,4},{1,5},{2,0},{3,1},{4,6},{5,7},{6,2},{7,3},{8,12},{9,13},{10,... | collective-permute-start | bytes 884744 | tf_op jit(solution)/shard_map/ppermute | solution.py:215
  30.2 4.8 %collective-permute-start.22 = (bf16[128,1152]{1,0:T(8,128)(2,1)S(1)}, bf16[128,1152]{1,0:T(8,128)(2,1)S(1)}, u32[]{:S(2)}, u32[]{:S(2)}) collective-permute-start(bf16[128,1152]{1,0:T(8,128)(2,1)S(1)} %collective-permute-done.refs_1_.refs_4_), channel_id=1, source_target_pairs={{0,8},{1,9},{2,10},{3,11},{4,12},{5,13},{6,14},{7,15},{8,0},{9,1},... | collective-permute-start | bytes 884744 | tf_op jit(solution)/shard_map/ppermute | solution.py:215
  30.9 0.7 copy-start.3
  31.6 9.5 %collective-permute-start.25 = (bf16[64,1152]{1,0:T(8,128)(2,1)S(1)}, bf16[64,1152]{1,0:T(8,128)(2,1)}, u32[]{:S(2)}, u32[]{:S(2)}) collective-permute-start(bf16[64,1152]{1,0:T(8,128)(2,1)S(1)} %get-tuple-element.48), channel_id=1, source_target_pairs={{0,4},{1,5},{2,0},{3,1},{4,6},{5,7},{6,2},{7,3},{8,12},{9,13},{10,... | collective-permute-start | bytes 442376 | tf_op jit(solution)/shard_map/ppermute | solution.py:215
  35.0 0.7 copy-start.15
  35.7 16.4 %collective-permute-start.12 = (bf16[128,1152]{1,0:T(8,128)(2,1)S(1)}, bf16[128,1152]{1,0:T(8,128)(2,1)}, u32[]{:S(2)}, u32[]{:S(2)}) collective-permute-start(bf16[128,1152]{1,0:T(8,128)(2,1)S(1)} %collective-permute-done.11.refs_4_), channel_id=1, source_target_pairs={{0,8},{1,9},{2,10},{3,11},{4,12},{5,13},{6,14},{7,15},{8,0},{9,1},... | collective-permute-start | bytes 884744 | tf_op jit(solution)/shard_map/ppermute | solution.py:215
  35.9 16.2 %collective-permute-start.19 = (bf16[128,1152]{1,0:T(8,128)(2,1)}, bf16[128,1152]{1,0:T(8,128)(2,1)}, u32[]{:S(2)}, u32[]{:S(2)}) collective-permute-start(bf16[128,1152]{1,0:T(8,128)(2,1)} %collective-permute-done.18.refs_4_), channel_id=1, source_target_pairs={{0,8},{1,9},{2,10},{3,11},{4,12},{5,13},{6,14},{7,15},{8,0},{9,1},... | collective-permute-start | bytes 884744 | tf_op jit(solution)/shard_map/ppermute | solution.py:215
  37.4 15.2 %collective-permute-start.3 = (bf16[128,1152]{1,0:T(8,128)(2,1)S(1)}, bf16[128,1152]{1,0:T(8,128)(2,1)S(1)}, u32[]{:S(2)}, u32[]{:S(2)}) collective-permute-start(bf16[128,1152]{1,0:T(8,128)(2,1)S(1)} %collective-permute-done.2.refs_2_), channel_id=1, source_target_pairs={{0,4},{1,5},{2,0},{3,1},{4,6},{5,7},{6,2},{7,3},{8,12},{9,13},{10,... | collective-permute-start | bytes 884744 | tf_op jit(solution)/shard_map/ppermute | solution.py:215
  39.2 0.7 copy-start.5
  39.9 13.2 %collective-permute-start.7 = (bf16[128,1152]{1,0:T(8,128)(2,1)S(1)}, bf16[128,1152]{1,0:T(8,128)(2,1)S(1)}, u32[]{:S(2)}, u32[]{:S(2)}) collective-permute-start(bf16[128,1152]{1,0:T(8,128)(2,1)S(1)} %collective-permute-done.2.refs_2_), channel_id=1, source_target_pairs={{0,1},{1,0},{2,3},{3,2},{4,5},{5,4},{6,7},{7,6},{8,9},{9,8},{10,11... | collective-permute-start | bytes 884744 | tf_op jit(solution)/shard_map/ppermute | solution.py:215
  41.1 8.3 %collective-permute-start.28 = (bf16[64,1152]{1,0:T(8,128)(2,1)}, bf16[64,1152]{1,0:T(8,128)(2,1)}, u32[]{:S(2)}, u32[]{:S(2)}) collective-permute-start(bf16[64,1152]{1,0:T(8,128)(2,1)} %get-tuple-element.47), channel_id=1, source_target_pairs={{0,4},{1,5},{2,0},{3,1},{4,6},{5,7},{6,2},{7,3},{8,12},{9,13},{10,... | collective-permute-start | bytes 442376 | tf_op jit(solution)/shard_map/ppermute | solution.py:215
  42.7 8.2 %copy-start.17 = (s32[4]{0:T(128)S(1)}, s32[4]{0:T(128)}, u32[]{:S(2)}) copy-start(s32[4]{0:T(128)} %constant.75.clone) | copy-start | bytes 52
  42.7 0.7 copy-start.19
  49.4 9.9 %collective-permute-start.32 = (bf16[128,1152]{1,0:T(8,128)(2,1)S(1)}, bf16[128,1152]{1,0:T(8,128)(2,1)}, u32[]{:S(2)}, u32[]{:S(2)}) collective-permute-start(bf16[128,1152]{1,0:T(8,128)(2,1)S(1)} %collective-permute-done.24.refs_2_), channel_id=1, source_target_pairs={{0,16},{1,17},{2,18},{3,19},{4,20},{5,21},{6,22},{7,23},{8,24},{9,... | collective-permute-start | bytes 884744 | tf_op jit(solution)/shard_map/ppermute | solution.py:215
  52.1 1.1 copy-start.18
  52.1 11.4 %collective-permute-start.31 = (bf16[128,1152]{1,0:T(8,128)(2,1)S(1)}, bf16[128,1152]{1,0:T(8,128)(2,1)S(1)}, u32[]{:S(2)}, u32[]{:S(2)}) collective-permute-start(bf16[128,1152]{1,0:T(8,128)(2,1)S(1)} %collective-permute-done.24.refs_2_), channel_id=1, source_target_pairs={{0,8},{1,9},{2,10},{3,11},{4,12},{5,13},{6,14},{7,15},{8,0},{9,1},... | collective-permute-start | bytes 884744 | tf_op jit(solution)/shard_map/ppermute | solution.py:215
  52.1 2.4 %collective-permute-start.34 = (bf16[64,1152]{1,0:T(8,128)(2,1)}, bf16[64,1152]{1,0:T(8,128)(2,1)S(1)}, u32[]{:S(2)}, u32[]{:S(2)}) collective-permute-start(bf16[64,1152]{1,0:T(8,128)(2,1)} %collective-permute-done.25.refs_6_), channel_id=1, source_target_pairs={{0,8},{1,9},{2,10},{3,11},{4,12},{5,13},{6,14},{7,15},{8,0},{9,1},... | collective-permute-start | bytes 442376 | tf_op jit(solution)/shard_map/ppermute | solution.py:215
  52.6 9.5 %collective-permute-start.26 = (bf16[64,1152]{1,0:T(8,128)(2,1)}, bf16[64,1152]{1,0:T(8,128)(2,1)S(1)}, u32[]{:S(2)}, u32[]{:S(2)}) collective-permute-start(bf16[64,1152]{1,0:T(8,128)(2,1)} %collective-permute-done.25.refs_6_), channel_id=1, source_target_pairs={{0,16},{1,17},{2,18},{3,19},{4,20},{5,21},{6,22},{7,23},{8,24},{9,... | collective-permute-start | bytes 442376 | tf_op jit(solution)/shard_map/ppermute | solution.py:215
  53.1 9.0 %collective-permute-start.35 = (bf16[64,1152]{1,0:T(8,128)(2,1)}, bf16[64,1152]{1,0:T(8,128)(2,1)S(1)}, u32[]{:S(2)}, u32[]{:S(2)}) collective-permute-start(bf16[64,1152]{1,0:T(8,128)(2,1)} %collective-permute-done.28.refs_8_), channel_id=1, source_target_pairs={{0,8},{1,9},{2,10},{3,11},{4,12},{5,13},{6,14},{7,15},{8,0},{9,1},... | collective-permute-start | bytes 442376 | tf_op jit(solution)/shard_map/ppermute | solution.py:215
  54.5 9.2 %collective-permute-start.29 = (bf16[64,1152]{1,0:T(8,128)(2,1)}, bf16[64,1152]{1,0:T(8,128)(2,1)S(1)}, u32[]{:S(2)}, u32[]{:S(2)}) collective-permute-start(bf16[64,1152]{1,0:T(8,128)(2,1)} %collective-permute-done.28.refs_8_), channel_id=1, source_target_pairs={{0,16},{1,17},{2,18},{3,19},{4,20},{5,21},{6,22},{7,23},{8,24},{9,... | collective-permute-start | bytes 442376 | tf_op jit(solution)/shard_map/ppermute | solution.py:215
  59.3 10.0 %collective-permute-start.33 = (bf16[128,1152]{1,0:T(8,128)(2,1)}, bf16[128,1152]{1,0:T(8,128)(2,1)S(1)}, u32[]{:S(2)}, u32[]{:S(2)}) collective-permute-start(bf16[128,1152]{1,0:T(8,128)(2,1)} %collective-permute-done.32.refs_4_), channel_id=1, source_target_pairs={{0,8},{1,9},{2,10},{3,11},{4,12},{5,13},{6,14},{7,15},{8,0},{9,1},... | collective-permute-start | bytes 884744 | tf_op jit(solution)/shard_map/ppermute | solution.py:215
  62.1 1.9 %collective-permute-start.27 = (bf16[64,1152]{1,0:T(8,128)(2,1)S(1)}, bf16[64,1152]{1,0:T(8,128)(2,1)S(1)}, u32[]{:S(2)}, u32[]{:S(2)}) collective-permute-start(bf16[64,1152]{1,0:T(8,128)(2,1)S(1)} %collective-permute-done.26.refs_2_), channel_id=1, source_target_pairs={{0,8},{1,9},{2,10},{3,11},{4,12},{5,13},{6,14},{7,15},{8,0},{9,1},... | collective-permute-start | bytes 442376 | tf_op jit(solution)/shard_map/ppermute | solution.py:215
  62.1 9.4 %collective-permute-start.4 = (bf16[128,1152]{1,0:T(8,128)(2,1)S(1)}, bf16[128,1152]{1,0:T(8,128)(2,1)S(1)}, u32[]{:S(2)}, u32[]{:S(2)}) collective-permute-start(bf16[128,1152]{1,0:T(8,128)(2,1)S(1)} %collective-permute-done.3.refs_6_), channel_id=1, source_target_pairs={{0,1},{1,0},{2,3},{3,2},{4,5},{5,4},{6,7},{7,6},{8,9},{9,8},{10,11... | collective-permute-start | bytes 884744 | tf_op jit(solution)/shard_map/ppermute | solution.py:215
  63.5 18.1 %collective-permute-start.6 = (bf16[128,1152]{1,0:T(8,128)(2,1)S(1)}, bf16[128,1152]{1,0:T(8,128)(2,1)S(1)}, u32[]{:S(2)}, u32[]{:S(2)}) collective-permute-start(bf16[128,1152]{1,0:T(8,128)(2,1)S(1)} %collective-permute-done.2.refs_2_), channel_id=1, source_target_pairs={{0,8},{1,9},{2,10},{3,11},{4,12},{5,13},{6,14},{7,15},{8,0},{9,1},... | collective-permute-start | bytes 884744 | tf_op jit(solution)/shard_map/ppermute | solution.py:215
  63.7 17.8 %collective-permute-start.9 = (bf16[128,1152]{1,0:T(8,128)(2,1)S(1)}, bf16[128,1152]{1,0:T(8,128)(2,1)S(1)}, u32[]{:S(2)}, u32[]{:S(2)}) collective-permute-start(bf16[128,1152]{1,0:T(8,128)(2,1)S(1)} %collective-permute-done.3.refs_6_), channel_id=1, source_target_pairs={{0,8},{1,9},{2,10},{3,11},{4,12},{5,13},{6,14},{7,15},{8,0},{9,1},... | collective-permute-start | bytes 884744 | tf_op jit(solution)/shard_map/ppermute | solution.py:215
  64.0 17.5 %collective-permute-start.8 = (bf16[128,1152]{1,0:T(8,128)(2,1)S(1)}, bf16[128,1152]{1,0:T(8,128)(2,1)S(1)}, u32[]{:S(2)}, u32[]{:S(2)}) collective-permute-start(bf16[128,1152]{1,0:T(8,128)(2,1)S(1)} %collective-permute-done.7.refs_4_), channel_id=1, source_target_pairs={{0,8},{1,9},{2,10},{3,11},{4,12},{5,13},{6,14},{7,15},{8,0},{9,1},... | collective-permute-start | bytes 884744 | tf_op jit(solution)/shard_map/ppermute | solution.py:215
  64.3 0.7 copy-start.7
  65.0 1.0 copy-start.10
  65.9 1.0 copy-start.14
  66.9 1.3 %copy-start.12 = (bf16[128,1152]{1,0:T(8,128)(2,1)S(1)}, bf16[128,1152]{1,0:T(8,128)(2,1)}, u32[]{:S(2)}) copy-start(bf16[128,1152]{1,0:T(8,128)(2,1)} %copy-done.11) | copy-start | bytes 884740
  66.9 1.3 %copy-start.16 = (bf16[128,1152]{1,0:T(8,128)(2,1)S(1)}, bf16[128,1152]{1,0:T(8,128)(2,1)}, u32[]{:S(2)}) copy-start(bf16[128,1152]{1,0:T(8,128)(2,1)} %copy-done.15) | copy-start | bytes 884740
  68.2 3.3 %copy-start.4 = (bf16[128,1152]{1,0:T(8,128)(2,1)S(1)}, bf16[128,1152]{1,0:T(8,128)(2,1)}, u32[]{:S(2)}) copy-start(bf16[128,1152]{1,0:T(8,128)(2,1)} %copy-done.3) | copy-start | bytes 884740
  69.4 9.7 %collective-permute-start.30 = (bf16[64,1152]{1,0:T(8,128)(2,1)S(1)}, bf16[64,1152]{1,0:T(8,128)(2,1)S(1)}, u32[]{:S(2)}, u32[]{:S(2)}) collective-permute-start(bf16[64,1152]{1,0:T(8,128)(2,1)S(1)} %collective-permute-done.29.refs_4_), channel_id=1, source_target_pairs={{0,8},{1,9},{2,10},{3,11},{4,12},{5,13},{6,14},{7,15},{8,0},{9,1},... | collective-permute-start | bytes 442376 | tf_op jit(solution)/shard_map/ppermute | solution.py:215
  71.5 12.0 %collective-permute-start.5 = (bf16[128,1152]{1,0:T(8,128)(2,1)S(1)}, bf16[128,1152]{1,0:T(8,128)(2,1)S(1)}, u32[]{:S(2)}, u32[]{:S(2)}) collective-permute-start(bf16[128,1152]{1,0:T(8,128)(2,1)S(1)} %collective-permute-done.4.refs_2_), channel_id=1, source_target_pairs={{0,8},{1,9},{2,10},{3,11},{4,12},{5,13},{6,14},{7,15},{8,0},{9,1},... | collective-permute-start | bytes 884744 | tf_op jit(solution)/shard_map/ppermute | solution.py:215
  71.5 2.4 %copy-start.6 = (bf16[128,1152]{1,0:T(8,128)(2,1)S(1)}, bf16[128,1152]{1,0:T(8,128)(2,1)}, u32[]{:S(2)}) copy-start(bf16[128,1152]{1,0:T(8,128)(2,1)} %copy-done.5) | copy-start | bytes 884740
  80.2 33.2 %collective-permute-start.36 = (f32[128,1152]{1,0:T(8,128)S(1)}, f32[128,1152]{1,0:T(8,128)S(1)}, u32[]{:S(2)}, u32[]{:S(2)}) collective-permute-start(f32[128,1152]{1,0:T(8,128)S(1)} %get-tuple-element.43), channel_id=1, source_target_pairs={{0,1},{1,0},{2,3},{3,2},{4,5},{5,4},{6,7},{7,6},{8,9},{9,8},{10,11... | collective-permute-start | bytes 1769480 | tf_op jit(solution)/shard_map/ppermute | solution.py:215
  83.5 29.8 %copy-start.1 = (bf16[128,1152]{1,0:T(8,128)(2,1)S(1)}, bf16[128,1152]{1,0:T(8,128)(2,1)}, u32[]{:S(2)}) copy-start(bf16[128,1152]{1,0:T(8,128)(2,1)} %values.7) | copy-start | bytes 884740
  84.5 29.9 %collective-permute-start.23 = (f32[128,1152]{1,0:T(8,128)S(1)}, f32[128,1152]{1,0:T(8,128)S(1)}, u32[]{:S(2)}, u32[]{:S(2)}) collective-permute-start(f32[128,1152]{1,0:T(8,128)S(1)} %get-tuple-element.37), channel_id=1, source_target_pairs={{0,16},{1,17},{2,18},{3,19},{4,20},{5,21},{6,22},{7,23},{8,24},{9,... | collective-permute-start | bytes 1769480 | tf_op jit(solution)/shard_map/ppermute | solution.py:215
  85.8 14.4 %collective-permute-start.37 = (f32[8,128]{1,0:T(8,128)S(1)}, f32[8,128]{1,0:T(8,128)S(1)}, u32[]{:S(2)}, u32[]{:S(2)}) collective-permute-start(f32[8,128]{1,0:T(8,128)S(1)} %get-tuple-element.44), channel_id=1, source_target_pairs={{0,16},{1,17},{2,18},{3,19},{4,20},{5,21},{6,22},{7,23},{8,24},{9,... | collective-permute-start | bytes 12296 | tf_op jit(solution)/shard_map/ppermute | solution.py:215
  100.2 1.2 %collective-permute-start.38 = (f32[8,128]{1,0:T(8,128)S(1)}, f32[8,128]{1,0:T(8,128)S(1)}, u32[]{:S(2)}, u32[]{:S(2)}) collective-permute-start(f32[8,128]{1,0:T(8,128)S(1)} %add.99), channel_id=1, source_target_pairs={{0,8},{1,9},{2,10},{3,11},{4,12},{5,13},{6,14},{7,15},{8,0},{9,1},... | collective-permute-start | bytes 12296 | tf_op jit(solution)/shard_map/ppermute | solution.py:215
  101.3 3.9 %collective-permute-start.39 = (f32[8,128]{1,0:T(8,128)S(1)}, f32[8,128]{1,0:T(8,128)S(1)}, u32[]{:S(2)}, u32[]{:S(2)}) collective-permute-start(f32[8,128]{1,0:T(8,128)S(1)} %add.100), channel_id=1, source_target_pairs={{0,2},{1,3},{2,0},{3,1},{4,6},{5,7},{6,4},{7,5},{8,10},{9,11},{10,... | collective-permute-start | bytes 12296 | tf_op jit(solution)/shard_map/ppermute | solution.py:215
  105.2 4.5 %collective-permute-start.40 = (f32[8,128]{1,0:T(8,128)S(1)}, f32[8,128]{1,0:T(8,128)S(1)}, u32[]{:S(2)}, u32[]{:S(2)}) collective-permute-start(f32[8,128]{1,0:T(8,128)S(1)} %add.101), channel_id=1, source_target_pairs={{0,4},{1,5},{2,6},{3,7},{4,0},{5,1},{6,2},{7,3},{8,12},{9,13},{10,... | collective-permute-start | bytes 12296 | tf_op jit(solution)/shard_map/ppermute | solution.py:215
  109.7 3.6 %collective-permute-start.41 = (f32[8,128]{1,0:T(8,128)S(1)}, f32[8,128]{1,0:T(8,128)S(1)}, u32[]{:S(2)}, u32[]{:S(2)}) collective-permute-start(f32[8,128]{1,0:T(8,128)S(1)} %add.102.refs_2_), channel_id=1, source_target_pairs={{0,1},{1,0},{2,3},{3,2},{4,5},{5,4},{6,7},{7,6},{8,9},{9,8},{10,11... | collective-permute-start | bytes 12296 | tf_op jit(solution)/shard_map/ppermute | solution.py:215

commit v4 on v3

--- a/solution.py
+++ b/solution.py
@@ -229,8 +229,11 @@
     dev_index = lax.axis_index("dev")
     slow_index, fast_index = dev_index // fast, dev_index % fast
     offsets = jnp.arange(slow * fast, dtype=jnp.int32)
-    ring_index = jnp.array(place_of, dtype=jnp.int32)[slow_index]
-    sources = jnp.array(ring, dtype=jnp.int32)[(ring_index - offsets // fast) % slow]
+    odd = slow_index % 2 == 1
+    ring_index = jnp.where(odd, slow - 1 - slow_index // 2, slow_index // 2)
+    source_index = (ring_index - offsets // fast) % slow
+    rising = source_index < (slow + 1) // 2
+    sources = jnp.where(rising, 2 * source_index, 2 * (slow - 1 - source_index) + 1)
     bases = sources * fast + (fast_index - offsets % fast) % fast
     ids = (rows * bases[:, None] + jnp.arange(rows, dtype=jnp.int32)[None, :]).astype(jnp.int32)
     settings = jnp.concatenate(
@@ -269,11 +272,17 @@
     middle = rows // 2
     txt_line, img_line, txt_sets, img_sets = [txt_half], [img_half], [], []
     for step in range(slow):
-        if step:
+        if step == 1:
+            block = ring_shift(texts)
+            txt_line.append(normalize(block))
+        elif step:
             txt_line.append(ring_shift(txt_line[-1]))
         txt_sets.append(txt_blocks(txt_line[-1]))
         if step < end:
-            if step:
+            if step == 1:
+                block = ring_shift(images)
+                img_line.append(normalize(block))
+            elif step:
                 img_line.append(ring_shift(img_line[-1]))
             img_sets.append(img_blocks(img_line[-1]))
     first = ring_shift(img_line[-1][:middle])
@@ -282,48 +291,46 @@
     img_own = [cores_of[0] for cores_of in img_sets[0]]
     txt_own = [cores_of[0] for cores_of in txt_sets[0]]
 
-    def image_terms(sums, loss, parts, counted=True):
+    def image_terms(sums, loss, parts, members, counted):
         blocks, places, pairs = [], [], []
         for step, at in parts:
-            pairs.append((0, len(blocks)))
+            if members[0] == 0:
+                pairs.append((0, len(blocks)))
             for block in txt_sets[step][at]:
                 blocks.append(block)
                 places.append((step * fast + at, 0))
-        loss_own = range(wide) if counted else ()
-        return terms(
-            img_own, blocks, places, img_targets, pairs, ids, settings, sums, loss_own, loss,
-        )
-
-    def text_terms(sums, loss, parts, loss_own=()):
+        loss_own = range(len(members)) if counted else ()
+        own, targets = [img_own[a] for a in members], [img_targets[a] for a in members]
+        return terms(own, blocks, places, targets, pairs, ids, settings, sums, loss_own, loss)
+
+    def text_terms(sums, loss, parts, members, counted):
         blocks, places, pairs = [], [], []
         for cores_of, step, at, offset in parts:
             if at == 0:
-                pairs += [(a, len(blocks)) for a in range(fast)]
+                pairs += [(a, len(blocks)) for a in range(len(members))]
             for block in cores_of:
                 blocks.append(block)
                 places.append((step * fast, offset))
-        return terms(
-            txt_own, blocks, places, txt_targets, pairs, ids, settings, sums, loss_own, loss,
-        )
+        loss_own = range(len(members)) if counted else ()
+        own, targets = [txt_own[a] for a in members], [txt_targets[a] for a in members]
+        return terms(own, blocks, places, targets, pairs, ids, settings, sums, loss_own, loss)
 
     img_sums = txt_sums = loss = None
     halves = [(first_set, 0), (second_set, middle)]
     for step in range(end):
         parts = [(step, at) for at in range(fast)]
-        if step == end - 1:
-            parts.append((end, 0))
-        img_sums, loss = image_terms(img_sums, loss, parts)
+        img_sums, loss = image_terms(img_sums, loss, parts, range(wide), True)
         parts = [(img_sets[step][at], step, at, 0) for at in range(wide)]
         if step == end - 1:
             parts += [(half[0], end, 0, offset) for half, offset in halves]
-        counted = range(1, fast) if step == 1 else ()
-        txt_sums, loss = text_terms(txt_sums, loss, parts, counted)
-    if fast > 1:
-        parts = [(end, at) for at in range(1, fast)]
-        img_sums, loss = image_terms(img_sums, loss, parts, False)
-    if wide > 1:
-        parts = [(half[at], end, at, offset) for at in range(1, wide) for half, offset in halves]
-        txt_sums, loss = text_terms(txt_sums, loss, parts)
+        txt_sums, loss = text_terms(txt_sums, loss, parts, range(fast), step == 1)
+    parts = [(end, at) for at in range(fast)]
+    img_far, _ = image_terms(img_sums[1:], None, parts, range(1, wide), False)
+    img_near, _ = image_terms(img_sums[:1], None, parts, range(1), False)
+    parts = [(half[at], end, at, offset) for at in range(1, wide) for half, offset in halves]
+    txt_far, _ = text_terms(txt_sums[1:], None, parts, range(1, fast), False)
+    txt_near, _ = text_terms(txt_sums[:1], None, parts, range(1), False)
+    img_sums, txt_sums = [*img_near, *img_far], [*txt_near, *txt_far]
 
     addends = [loss]
     for dim in (0, 1, 2, 3):

time: 116 us -> 105 us (0.905)
  waiting for transfers between devices: 46 us -> 32.8 us
  starting transfers between devices: 39.1 us -> 43.7 us
    ppermute x42, waiting for transfers between devices: 46 us -> 32.8 us  [permuted(): return lax.ppermute(array, AXES, pairs)]
    ppermute x42, starting transfers between devices: 39.1 us -> 43.7 us  [permuted(): return lax.ppermute(array, AXES, pairs)]
    unnamed x40 -> x50, local copies, waits for them, and re-layouts: 8.56 us -> 10.1 us
    pallas_call x8 -> x10, Pallas kernels: 14 us -> 12.8 us  [terms(): pl.pallas_call(kernel, out_shape=shapes, in_specs=[VMEM] * len(operands),...]
  transfers between devices with their start and end apart: 42 -> 42, of which waited for: 14 -> 15; matrix products, arithmetic and copies ran while one was open for 3% -> 0% of each run, Pallas kernels for 13% -> 14%
where the time goes in v4:
time: 105 us
  starting transfers between devices  43.7 us (42%)
  waiting for transfers between devices  32.8 us (31%)
  Pallas kernels  15.6 us (15%)
  local copies, waits for them, and re-layouts  10.2 us (10%)
  between operations  2.26 us (2%)
    ppermute x42, starting transfers between devices, permuted(): return lax.ppermute(array, AXES, pairs)  43.7 us
    ppermute x42, waiting for transfers between devices, permuted(): return lax.ppermute(array, AXES, pairs)  32.8 us
    pallas_call x10, Pallas kernels, terms(): pl.pallas_call(kernel, out_shape=shapes, in_specs=[VMEM] * len(operands),...  12.8 us
    unnamed x50, local copies, waits for them, and re-layouts  10.1 us
    pallas_call x2, Pallas kernels, project(): pl.pallas_call(functools.partial(project_kernel, len(parts), len(losses),...  2.21 us
  transfers between devices with their start and end apart: 42, of which 15 were waited for; matrix products, arithmetic and copies ran while one was open for 0% of the time, Pallas kernels for 14%

profile of v4, /device:TPU:0, one launch (start us, length us, event | category | flops | bytes accessed | tf_op | source)
XLA Modules:
  0.0 104.6 jit_solution(8111972529093038808)
XLA Ops:
  0.6 4.1 %collective-permute-start = (bf16[128,1152]{1,0:T(8,128)(2,1)}, bf16[128,1152]{1,0:T(8,128)(2,1)S(1)}, u32[]{:S(2)}, u32[]{:S(2)}) collective-permute-start(bf16[128,1152]{1,0:T(8,128)(2,1)} %values.7), channel_id=1, source_target_pairs={{0,4},{1,5},{2,0},{3,1},{4,6},{5,7},{6,2},{7,3},{8,12},{9,13},{10,... | collective-permute-start | bytes 884744 | tf_op jit(solution)/shard_map/ppermute | solution.py:215
  4.7 1.0 copy-done
  5.9 1.6 %collective-permute-start.14 = (bf16[128,1152]{1,0:T(8,128)(2,1)S(1)}, bf16[128,1152]{1,0:T(8,128)(2,1)S(1)}, u32[]{:S(2)}, u32[]{:S(2)}) collective-permute-start(bf16[128,1152]{1,0:T(8,128)(2,1)S(1)} %shard_map.87.refs_2_.refs_0_), channel_id=1, source_target_pairs={{0,1},{1,0},{2,3},{3,2},{4,5},{5,4},{6,7},{7,6},{8,9},{9,8},{10,11... | collective-permute-start | bytes 884744 | tf_op jit(solution)/shard_map/ppermute | solution.py:215
  7.5 1.6 %collective-permute-start.16 = (bf16[128,1152]{1,0:T(8,128)(2,1)S(1)}, bf16[128,1152]{1,0:T(8,128)(2,1)S(1)}, u32[]{:S(2)}, u32[]{:S(2)}) collective-permute-start(bf16[128,1152]{1,0:T(8,128)(2,1)S(1)} %copy-done.2), channel_id=1, source_target_pairs={{0,4},{1,5},{2,0},{3,1},{4,6},{5,7},{6,2},{7,3},{8,12},{9,13},{10,... | collective-permute-start | bytes 884744 | tf_op jit(solution)/shard_map/ppermute | solution.py:215
  9.2 1.6 %collective-permute-start.6 = (bf16[128,1152]{1,0:T(8,128)(2,1)S(1)}, bf16[128,1152]{1,0:T(8,128)(2,1)S(1)}, u32[]{:S(2)}, u32[]{:S(2)}) collective-permute-start(bf16[128,1152]{1,0:T(8,128)(2,1)S(1)} %shard_map.85.refs_0_.refs_2_), channel_id=1, source_target_pairs={{0,16},{1,17},{2,18},{3,19},{4,20},{5,21},{6,22},{7,23},{8,24},{9,... | collective-permute-start | bytes 884744 | tf_op jit(solution)/shard_map/ppermute | solution.py:215
  10.8 0.7 collective-permute-start.20
  11.5 0.9 collective-permute-done.values
  12.6 1.8 %collective-permute-done.14.refs_4_.refs_1_.refs_0_ = bf16[128,1152]{1,0:T(8,128)(2,1)S(1)} collective-permute-done((bf16[128,1152]{1,0:T(8,128)(2,1)S(1)}, bf16[128,1152]{1,0:T(8,128)(2,1)S(1)}, u32[]{:S(2)}, u32[]{:S(2)}) %collective-permute-start.14) | collective-permute-done | bytes 294944 | tf_op jit(solution)/shard_map/ppermute | solution.py:215
  14.4 3.1 %collective-permute-done.16.values = bf16[128,1152]{1,0:T(8,128)(2,1)S(1)} collective-permute-done((bf16[128,1152]{1,0:T(8,128)(2,1)S(1)}, bf16[128,1152]{1,0:T(8,128)(2,1)S(1)}, u32[]{:S(2)}, u32[]{:S(2)}) %collective-permute-start.16) | collective-permute-done | bytes 294944 | tf_op jit(solution)/shard_map/ppermute | solution.py:215
  17.7 1.6 %collective-permute-start.11 = (bf16[128,1152]{1,0:T(8,128)(2,1)S(1)}, bf16[128,1152]{1,0:T(8,128)(2,1)S(1)}, u32[]{:S(2)}, u32[]{:S(2)}) collective-permute-start(bf16[128,1152]{1,0:T(8,128)(2,1)S(1)} %shard_map.86.refs_2_), channel_id=1, source_target_pairs={{0,1},{1,0},{2,3},{3,2},{4,5},{5,4},{6,7},{7,6},{8,9},{9,8},{10,11... | collective-permute-start | bytes 884744 | tf_op jit(solution)/shard_map/ppermute | solution.py:215
  19.3 3.4 %collective-permute-start.24 = (bf16[128,1152]{1,0:T(8,128)(2,1)S(1)}, bf16[128,1152]{1,0:T(8,128)(2,1)S(1)}, u32[]{:S(2)}, u32[]{:S(2)}) collective-permute-start(bf16[128,1152]{1,0:T(8,128)(2,1)S(1)} %shard_map.90.refs_2_), channel_id=1, source_target_pairs={{0,4},{1,5},{2,0},{3,1},{4,6},{5,7},{6,2},{7,3},{8,12},{9,13},{10,... | collective-permute-start | bytes 884744 | tf_op jit(solution)/shard_map/ppermute | solution.py:215
  22.7 0.7 copy-done.19
  23.4 0.7 copy-done.17
  24.1 1.5 %collective-permute-start.18 = (bf16[128,1152]{1,0:T(8,128)(2,1)S(1)}, bf16[128,1152]{1,0:T(8,128)(2,1)S(1)}, u32[]{:S(2)}, u32[]{:S(2)}) collective-permute-start(bf16[128,1152]{1,0:T(8,128)(2,1)S(1)} %shard_map.90.refs_2_), channel_id=1, source_target_pairs={{0,16},{1,17},{2,18},{3,19},{4,20},{5,21},{6,22},{7,23},{8,24},{9,... | collective-permute-start | bytes 884744 | tf_op jit(solution)/shard_map/ppermute | solution.py:215
  25.9 1.3 %collective-permute-done.11.refs_4_ = bf16[128,1152]{1,0:T(8,128)(2,1)S(1)} collective-permute-done((bf16[128,1152]{1,0:T(8,128)(2,1)S(1)}, bf16[128,1152]{1,0:T(8,128)(2,1)S(1)}, u32[]{:S(2)}, u32[]{:S(2)}) %collective-permute-start.11) | collective-permute-done | bytes 294944 | tf_op jit(solution)/shard_map/ppermute | solution.py:215
  27.2 3.4 %collective-permute-start.1 = (bf16[128,1152]{1,0:T(8,128)(2,1)S(1)}, bf16[128,1152]{1,0:T(8,128)(2,1)S(1)}, u32[]{:S(2)}, u32[]{:S(2)}) collective-permute-start(bf16[128,1152]{1,0:T(8,128)(2,1)S(1)} %shard_map.86.refs_2_), channel_id=1, source_target_pairs={{0,4},{1,5},{2,0},{3,1},{4,6},{5,7},{6,2},{7,3},{8,12},{9,13},{10,... | collective-permute-start | bytes 884744 | tf_op jit(solution)/shard_map/ppermute | solution.py:215
  30.6 0.7 copy-done.5
  31.3 0.5 collective-permute-start.12
  32.2 0.7 copy-done.23
  32.9 2.1 %collective-permute-start.25 = (bf16[64,1152]{1,0:T(8,128)(2,1)S(1)}, bf16[64,1152]{1,0:T(8,128)(2,1)S(1)}, u32[]{:S(2)}, u32[]{:S(2)}) collective-permute-start(bf16[64,1152]{1,0:T(8,128)(2,1)S(1)} %get-tuple-element.40), channel_id=1, source_target_pairs={{0,4},{1,5},{2,0},{3,1},{4,6},{5,7},{6,2},{7,3},{8,12},{9,13},{10,... | collective-permute-start | bytes 442376 | tf_op jit(solution)/shard_map/ppermute | solution.py:215
  35.0 0.7 copy-done.3
  35.7 0.7 copy-done.7
  36.7 1.3 %collective-permute-done.1.refs_2_ = bf16[128,1152]{1,0:T(8,128)(2,1)S(1)} collective-permute-done((bf16[128,1152]{1,0:T(8,128)(2,1)S(1)}, bf16[128,1152]{1,0:T(8,128)(2,1)S(1)}, u32[]{:S(2)}, u32[]{:S(2)}) %collective-permute-start.1) | collective-permute-done | bytes 294944 | tf_op jit(solution)/shard_map/ppermute | solution.py:215
  38.0 1.5 %collective-permute-start.8 = (bf16[128,1152]{1,0:T(8,128)(2,1)S(1)}, bf16[128,1152]{1,0:T(8,128)(2,1)S(1)}, u32[]{:S(2)}, u32[]{:S(2)}) collective-permute-start(bf16[128,1152]{1,0:T(8,128)(2,1)S(1)} %collective-permute-done.1.refs_2_), channel_id=1, source_target_pairs={{0,1},{1,0},{2,3},{3,2},{4,5},{5,4},{6,7},{7,6},{8,9},{9,8},{10,11... | collective-permute-start | bytes 884744 | tf_op jit(solution)/shard_map/ppermute | solution.py:215
  39.5 1.6 %collective-permute-done.25.refs_6_ = bf16[64,1152]{1,0:T(8,128)(2,1)S(1)} collective-permute-done((bf16[64,1152]{1,0:T(8,128)(2,1)S(1)}, bf16[64,1152]{1,0:T(8,128)(2,1)S(1)}, u32[]{:S(2)}, u32[]{:S(2)}) %collective-permute-start.25) | collective-permute-done | bytes 147488 | tf_op jit(solution)/shard_map/ppermute | solution.py:215
  41.1 3.4 %collective-permute-start.2 = (bf16[128,1152]{1,0:T(8,128)(2,1)S(1)}, bf16[128,1152]{1,0:T(8,128)(2,1)S(1)}, u32[]{:S(2)}, u32[]{:S(2)}) collective-permute-start(bf16[128,1152]{1,0:T(8,128)(2,1)S(1)} %collective-permute-done.1.refs_2_), channel_id=1, source_target_pairs={{0,4},{1,5},{2,0},{3,1},{4,6},{5,7},{6,2},{7,3},{8,12},{9,13},{10,... | collective-permute-start | bytes 884744 | tf_op jit(solution)/shard_map/ppermute | solution.py:215
  44.5 1.5 %collective-permute-start.32 = (bf16[128,1152]{1,0:T(8,128)(2,1)S(1)}, bf16[128,1152]{1,0:T(8,128)(2,1)}, u32[]{:S(2)}, u32[]{:S(2)}) collective-permute-start(bf16[128,1152]{1,0:T(8,128)(2,1)S(1)} %collective-permute-done.24.refs_2_), channel_id=1, source_target_pairs={{0,16},{1,17},{2,18},{3,19},{4,20},{5,21},{6,22},{7,23},{8,24},{9,... | collective-permute-start | bytes 884744 | tf_op jit(solution)/shard_map/ppermute | solution.py:215
  46.0 0.7 copy-done.11
  46.7 0.7 copy-done.13
  47.5 0.5 collective-permute-start.35
  48.0 0.7 copy-done.9
  48.7 0.5 collective-permute-start.26
  49.3 1.5 %collective-permute-start.4 = (bf16[128,1152]{1,0:T(8,128)(2,1)S(1)}, bf16[128,1152]{1,0:T(8,128)(2,1)S(1)}, u32[]{:S(2)}, u32[]{:S(2)}) collective-permute-start(bf16[128,1152]{1,0:T(8,128)(2,1)S(1)} %collective-permute-done.2.refs_1_), channel_id=1, source_target_pairs={{0,1},{1,0},{2,3},{3,2},{4,5},{5,4},{6,7},{7,6},{8,9},{9,8},{10,11... | collective-permute-start | bytes 884744 | tf_op jit(solution)/shard_map/ppermute | solution.py:215
  50.8 1.6 %collective-permute-start.29 = (bf16[64,1152]{1,0:T(8,128)(2,1)}, bf16[64,1152]{1,0:T(8,128)(2,1)S(1)}, u32[]{:S(2)}, u32[]{:S(2)}) collective-permute-start(bf16[64,1152]{1,0:T(8,128)(2,1)} %collective-permute-done.28.refs_8_), channel_id=1, source_target_pairs={{0,16},{1,17},{2,18},{3,19},{4,20},{5,21},{6,22},{7,23},{8,24},{9,... | collective-permute-start | bytes 442376 | tf_op jit(solution)/shard_map/ppermute | solution.py:215
  52.4 2.8 %collective-permute-done.26.refs_1_ = bf16[64,1152]{1,0:T(8,128)(2,1)S(1)} collective-permute-done((bf16[64,1152]{1,0:T(8,128)(2,1)S(1)}, bf16[64,1152]{1,0:T(8,128)(2,1)S(1)}, u32[]{:S(2)}, u32[]{:S(2)}) %collective-permute-start.26) | collective-permute-done | bytes 147488 | tf_op jit(solution)/shard_map/ppermute | solution.py:215
  56.6 0.6 collective-permute-start.7
  57.2 0.5 collective-permute-done.29.refs_3_
  57.8 0.7 copy-done.15
  58.4 1.0 copy-done.20
  59.4 1.0 copy-done.22
  60.4 1.3 %shard_map.88 = (f32[128,1152]{1,0:T(8,128)S(1)}, f32[128,1152]{1,0:T(8,128)S(1)}, f32[8,128]{1,0:T(8,128)S(1)}) custom-call(f32[8,128]{1,0:T(8,128)S(1)} %concatenate.6.settings, s32[8,128]{1,0:T(8,128)S(1)} %iota_add_fusion.ids, bf16[128,1152]{1,0:T(8,128)(2,1)S(1)} %shard_map.85.refs_0_.refs_2_, ...), custom_call_target="tpu_custom_call" | custom-call | flops 603979776 | bytes 4128768 | tf_op jit(solution)/shard_map/pallas_call | solution.py:165
  61.7 0.6 collective-permute-start.3
  62.4 1.1 %shard_map.91 = (f32[128,1152]{1,0:T(8,128)S(1)}, f32[128,1152]{1,0:T(8,128)S(1)}) custom-call(f32[8,128]{1,0:T(8,128)S(1)} %concatenate.6.settings, s32[8,128]{1,0:T(8,128)S(1)} %iota_add_fusion.ids, bf16[128,1152]{1,0:T(8,128)(2,1)S(1)} %shard_map.87.refs_2_.refs_0_, bf16[128,1152]{1,0:T(8,128)(2,1)S(1)} %collective-permute-done.14.refs_4_.refs_1_.refs_0_, ...), custom_call_target="tpu_custom_call" | custom-call | flops 603979776 | bytes 4128768 | tf_op jit(solution)/shard_map/pallas_call | solution.py:165
  64.0 1.3 %shard_map.89 = (f32[128,1152]{1,0:T(8,128)S(1)}, f32[128,1152]{1,0:T(8,128)S(1)}, f32[8,128]{1,0:T(8,128)S(1)}) custom-call(f32[8,128]{1,0:T(8,128)S(1)} %concatenate.6.settings, s32[8,128]{1,0:T(8,128)S(1)} %iota_add_fusion.ids, bf16[128,1152]{1,0:T(8,128)(2,1)S(1)} %shard_map.85.refs_0_.refs_2_, ...), custom_call_target="tpu_custom_call", output_to_operand_aliasing={{0}: (10, {}), {1}: (11, {}), {2}: (12, {})} | custom-call | flops 603979776 | bytes 4128768 | tf_op jit(solution)/shard_map/pallas_call | solution.py:165
  65.4 1.3 %shard_map.92 = (f32[128,1152]{1,0:T(8,128)S(1)}, f32[128,1152]{1,0:T(8,128)S(1)}, f32[8,128]{1,0:T(8,128)S(1)}) custom-call(f32[8,128]{1,0:T(8,128)S(1)} %concatenate.6.settings, s32[8,128]{1,0:T(8,128)S(1)} %iota_add_fusion.ids, bf16[128,1152]{1,0:T(8,128)(2,1)S(1)} %shard_map.87.refs_2_.refs_0_, ...), custom_call_target="tpu_custom_call", output_to_operand_aliasing={{0}: (10, {}), {1}: (11, {}), {2}: (12, {})} | custom-call | flops 603979776 | bytes 4128768 | tf_op jit(solution)/shard_map/pallas_call | solution.py:165
  66.7 2.9 %shard_map.97 = (f32[128,1152]{1,0:T(8,128)S(1)}, f32[128,1152]{1,0:T(8,128)S(1)}) custom-call(f32[8,128]{1,0:T(8,128)S(1)} %concatenate.6.settings, s32[8,128]{1,0:T(8,128)S(1)} %iota_add_fusion.ids, bf16[128,1152]{1,0:T(8,128)(2,1)S(1)} %shard_map.87.refs_2_.refs_0_, ...), custom_call_target="tpu_custom_call", output_to_operand_aliasing={{0}: (14, {}), {1}: (15, {})} | custom-call | flops 905969664 | bytes 5308416 | tf_op jit(solution)/shard_map/pallas_call | solution.py:165
  69.7 0.8 shard_map.99
  70.5 1.5 %collective-permute-start.36 = (f32[128,1152]{1,0:T(8,128)S(1)}, f32[128,1152]{1,0:T(8,128)S(1)}, u32[]{:S(2)}, u32[]{:S(2)}) collective-permute-start(f32[128,1152]{1,0:T(8,128)S(1)} %shard_map.99), channel_id=1, source_target_pairs={{0,1},{1,0},{2,3},{3,2},{4,5},{5,4},{6,7},{7,6},{8,9},{9,8},{10,11... | collective-permute-start | bytes 1769480 | tf_op jit(solution)/shard_map/ppermute | solution.py:215
  72.0 1.3 %shard_map.93 = (f32[128,1152]{1,0:T(8,128)S(1)}, f32[128,1152]{1,0:T(8,128)S(1)}, f32[8,128]{1,0:T(8,128)S(1)}) custom-call(f32[8,128]{1,0:T(8,128)S(1)} %concatenate.6.settings, s32[8,128]{1,0:T(8,128)S(1)} %iota_add_fusion.ids, bf16[128,1152]{1,0:T(8,128)(2,1)S(1)} %shard_map.85.refs_0_.refs_2_, ...), custom_call_target="tpu_custom_call", output_to_operand_aliasing={{0}: (10, {}), {1}: (11, {}), {2}: (12, {})} | custom-call | flops 603979776 | bytes 4128768 | tf_op jit(solution)/shard_map/pallas_call | solution.py:165
  73.4 0.9 shard_map.95
  74.3 1.5 %collective-permute-start.23 = (f32[128,1152]{1,0:T(8,128)S(1)}, f32[128,1152]{1,0:T(8,128)S(1)}, u32[]{:S(2)}, u32[]{:S(2)}) collective-permute-start(f32[128,1152]{1,0:T(8,128)S(1)} %shard_map.95), channel_id=1, source_target_pairs={{0,16},{1,17},{2,18},{3,19},{4,20},{5,21},{6,22},{7,23},{8,24},{9,... | collective-permute-start | bytes 1769480 | tf_op jit(solution)/shard_map/ppermute | solution.py:215
  75.8 0.6 collective-permute-start.37
  76.3 13.1 %collective-permute-done.37 = f32[8,128]{1,0:T(8,128)S(1)} collective-permute-done((f32[8,128]{1,0:T(8,128)S(1)}, f32[8,128]{1,0:T(8,128)S(1)}, u32[]{:S(2)}, u32[]{:S(2)}) %collective-permute-start.37) | collective-permute-done | bytes 4128 | tf_op jit(solution)/shard_map/ppermute | solution.py:215
  89.5 1.2 %collective-permute-done.38 = f32[8,128]{1,0:T(8,128)S(1)} collective-permute-done((f32[8,128]{1,0:T(8,128)S(1)}, f32[8,128]{1,0:T(8,128)S(1)}, u32[]{:S(2)}, u32[]{:S(2)}) %collective-permute-start.38) | collective-permute-done | bytes 4128 | tf_op jit(solution)/shard_map/ppermute | solution.py:215
  90.6 1.9 %collective-permute-start.39 = (f32[8,128]{1,0:T(8,128)S(1)}, f32[8,128]{1,0:T(8,128)S(1)}, u32[]{:S(2)}, u32[]{:S(2)}) collective-permute-start(f32[8,128]{1,0:T(8,128)S(1)} %add.92), channel_id=1, source_target_pairs={{0,2},{1,3},{2,0},{3,1},{4,6},{5,7},{6,4},{7,5},{8,10},{9,11},{10,... | collective-permute-start | bytes 12296 | tf_op jit(solution)/shard_map/ppermute | solution.py:215
  92.5 1.7 %collective-permute-done.39 = f32[8,128]{1,0:T(8,128)S(1)} collective-permute-done((f32[8,128]{1,0:T(8,128)S(1)}, f32[8,128]{1,0:T(8,128)S(1)}, u32[]{:S(2)}, u32[]{:S(2)}) %collective-permute-start.39) | collective-permute-done | bytes 4128 | tf_op jit(solution)/shard_map/ppermute | solution.py:215
  94.2 2.9 %collective-permute-start.40 = (f32[8,128]{1,0:T(8,128)S(1)}, f32[8,128]{1,0:T(8,128)S(1)}, u32[]{:S(2)}, u32[]{:S(2)}) collective-permute-start(f32[8,128]{1,0:T(8,128)S(1)} %add.93), channel_id=1, source_target_pairs={{0,4},{1,5},{2,6},{3,7},{4,0},{5,1},{6,2},{7,3},{8,12},{9,13},{10,... | collective-permute-start | bytes 12296 | tf_op jit(solution)/shard_map/ppermute | solution.py:215
  97.1 0.8 shard_map.98.refs_0_
  98.0 0.8 collective-permute-done.40
  98.8 0.6 collective-permute-start.41
  99.4 0.9 shard_map.94.refs_0_
  100.3 2.1 %collective-permute-done.41.refs_3_ = f32[8,128]{1,0:T(8,128)S(1)} collective-permute-done((f32[8,128]{1,0:T(8,128)S(1)}, f32[8,128]{1,0:T(8,128)S(1)}, u32[]{:S(2)}, u32[]{:S(2)}) %collective-permute-start.41) | collective-permute-done | bytes 4128 | tf_op jit(solution)/shard_map/ppermute | solution.py:215
  102.4 1.1 %shard_map.100 = (f32[128,1152]{1,0:T(8,128)}, f32[1]{0:T(128)}) custom-call(f32[8,128]{1,0:T(8,128)S(1)} %concatenate.6.settings, bf16[128,1152]{1,0:T(8,128)(2,1)S(1)} %copy-done.1, f32[128,1152]{1,0:T(8,128)S(1)} %shard_map.98.refs_0_, f32[128,1152]{1,0:T(8,128)S(1)} %collective-permute-done.36.refs_1_, f32[8,128]{1,0:T(8,128)S(1)} %add.94.refs_2_, ...), custom_call_target="tpu_custom_call" | custom-call | tf_op jit(solution)/shard_map/pallas_call | solution.py:57
  103.5 1.1 %shard_map.96 = f32[128,1152]{1,0:T(8,128)} custom-call(f32[8,128]{1,0:T(8,128)S(1)} %concatenate.6.settings, bf16[128,1152]{1,0:T(8,128)(2,1)S(1)} %copy-done.2, f32[128,1152]{1,0:T(8,128)S(1)} %shard_map.94.refs_0_, f32[128,1152]{1,0:T(8,128)S(1)} %collective-permute-done.23.refs_1_), custom_call_target="tpu_custom_call" | custom-call | tf_op jit(solution)/shard_map/pallas_call | solution.py:57
  (96 shorter events, 2.4 us)
Async XLA Ops:
  0.6 11.8 %collective-permute-start = (bf16[128,1152]{1,0:T(8,128)(2,1)}, bf16[128,1152]{1,0:T(8,128)(2,1)S(1)}, u32[]{:S(2)}, u32[]{:S(2)}) collective-permute-start(bf16[128,1152]{1,0:T(8,128)(2,1)} %values.7), channel_id=1, source_target_pairs={{0,4},{1,5},{2,0},{3,1},{4,6},{5,7},{6,2},{7,3},{8,12},{9,13},{10,... | collective-permute-start | bytes 884744 | tf_op jit(solution)/shard_map/ppermute | solution.py:215
  4.7 1.0 copy-start
  5.7 1.7 %copy-start.2 = (bf16[128,1152]{1,0:T(8,128)(2,1)S(1)}, bf16[128,1152]{1,0:T(8,128)(2,1)}, u32[]{:S(2)}) copy-start(bf16[128,1152]{1,0:T(8,128)(2,1)} %values.6) | copy-start | bytes 884740
  5.9 8.5 %collective-permute-start.14 = (bf16[128,1152]{1,0:T(8,128)(2,1)S(1)}, bf16[128,1152]{1,0:T(8,128)(2,1)S(1)}, u32[]{:S(2)}, u32[]{:S(2)}) collective-permute-start(bf16[128,1152]{1,0:T(8,128)(2,1)S(1)} %shard_map.87.refs_2_.refs_0_), channel_id=1, source_target_pairs={{0,1},{1,0},{2,3},{3,2},{4,5},{5,4},{6,7},{7,6},{8,9},{9,8},{10,11... | collective-permute-start | bytes 884744 | tf_op jit(solution)/shard_map/ppermute | solution.py:215
  7.5 10.1 %collective-permute-start.16 = (bf16[128,1152]{1,0:T(8,128)(2,1)S(1)}, bf16[128,1152]{1,0:T(8,128)(2,1)S(1)}, u32[]{:S(2)}, u32[]{:S(2)}) collective-permute-start(bf16[128,1152]{1,0:T(8,128)(2,1)S(1)} %copy-done.2), channel_id=1, source_target_pairs={{0,4},{1,5},{2,0},{3,1},{4,6},{5,7},{6,2},{7,3},{8,12},{9,13},{10,... | collective-permute-start | bytes 884744 | tf_op jit(solution)/shard_map/ppermute | solution.py:215
  9.2 1.6 %copy-start.16 = (s32[128]{0:T(128)S(1)}, s32[128]{0:T(128)}, u32[]{:S(2)}) copy-start(s32[128]{0:T(128)} %param.8) | copy-start | bytes 1540
  9.2 10.1 %collective-permute-start.6 = (bf16[128,1152]{1,0:T(8,128)(2,1)S(1)}, bf16[128,1152]{1,0:T(8,128)(2,1)S(1)}, u32[]{:S(2)}, u32[]{:S(2)}) collective-permute-start(bf16[128,1152]{1,0:T(8,128)(2,1)S(1)} %shard_map.85.refs_0_.refs_2_), channel_id=1, source_target_pairs={{0,16},{1,17},{2,18},{3,19},{4,20},{5,21},{6,22},{7,23},{8,24},{9,... | collective-permute-start | bytes 884744 | tf_op jit(solution)/shard_map/ppermute | solution.py:215
  10.8 6.9 %collective-permute-start.20 = (s32[1,128]{1,0:T(1,128)S(1)}, s32[1,128]{1,0:T(1,128)S(1)}, u32[]{:S(2)}, u32[]{:S(2)}) collective-permute-start(s32[1,128]{1,0:T(1,128)S(1)} %bitcast.14), channel_id=1, source_target_pairs={{0,1},{1,0},{2,3},{3,2},{4,5},{5,4},{6,7},{7,6},{8,9},{9,8},{10,11... | collective-permute-start | bytes 1544 | tf_op jit(solution)/shard_map/ppermute | solution.py:215
  12.5 10.2 %collective-permute-start.13 = (bf16[128,1152]{1,0:T(8,128)(2,1)S(1)}, bf16[128,1152]{1,0:T(8,128)(2,1)S(1)}, u32[]{:S(2)}, u32[]{:S(2)}) collective-permute-start(bf16[128,1152]{1,0:T(8,128)(2,1)S(1)} %shard_map.87.refs_2_.refs_0_), channel_id=1, source_target_pairs={{0,8},{1,9},{2,10},{3,11},{4,12},{5,13},{6,14},{7,15},{8,0},{9,1},... | collective-permute-start | bytes 884744 | tf_op jit(solution)/shard_map/ppermute | solution.py:215
  14.4 9.0 %collective-permute-start.21 = (bf16[128,1152]{1,0:T(8,128)(2,1)S(1)}, bf16[128,1152]{1,0:T(8,128)(2,1)S(1)}, u32[]{:S(2)}, u32[]{:S(2)}) collective-permute-start(bf16[128,1152]{1,0:T(8,128)(2,1)S(1)} %shard_map.85.refs_0_.refs_2_), channel_id=1, source_target_pairs={{0,8},{1,9},{2,10},{3,11},{4,12},{5,13},{6,14},{7,15},{8,0},{9,1},... | collective-permute-start | bytes 884744 | tf_op jit(solution)/shard_map/ppermute | solution.py:215
  17.5 8.1 %collective-permute-start.15 = (bf16[128,1152]{1,0:T(8,128)(2,1)S(1)}, bf16[128,1152]{1,0:T(8,128)(2,1)S(1)}, u32[]{:S(2)}, u32[]{:S(2)}) collective-permute-start(bf16[128,1152]{1,0:T(8,128)(2,1)S(1)} %collective-permute-done.14.refs_4_.refs_1_.refs_0_), channel_id=1, source_target_pairs={{0,8},{1,9},{2,10},{3,11},{4,12},{5,13},{6,14},{7,15},{8,0},{9,1},... | collective-permute-start | bytes 884744 | tf_op jit(solution)/shard_map/ppermute | solution.py:215
  17.7 9.5 %collective-permute-start.11 = (bf16[128,1152]{1,0:T(8,128)(2,1)S(1)}, bf16[128,1152]{1,0:T(8,128)(2,1)S(1)}, u32[]{:S(2)}, u32[]{:S(2)}) collective-permute-start(bf16[128,1152]{1,0:T(8,128)(2,1)S(1)} %shard_map.86.refs_2_), channel_id=1, source_target_pairs={{0,1},{1,0},{2,3},{3,2},{4,5},{5,4},{6,7},{7,6},{8,9},{9,8},{10,11... | collective-permute-start | bytes 884744 | tf_op jit(solution)/shard_map/ppermute | solution.py:215
  19.3 11.3 %collective-permute-start.24 = (bf16[128,1152]{1,0:T(8,128)(2,1)S(1)}, bf16[128,1152]{1,0:T(8,128)(2,1)S(1)}, u32[]{:S(2)}, u32[]{:S(2)}) collective-permute-start(bf16[128,1152]{1,0:T(8,128)(2,1)S(1)} %shard_map.90.refs_2_), channel_id=1, source_target_pairs={{0,4},{1,5},{2,0},{3,1},{4,6},{5,7},{6,2},{7,3},{8,12},{9,13},{10,... | collective-permute-start | bytes 884744 | tf_op jit(solution)/shard_map/ppermute | solution.py:215
  23.4 7.2 %collective-permute-start.10 = (bf16[128,1152]{1,0:T(8,128)(2,1)S(1)}, bf16[128,1152]{1,0:T(8,128)(2,1)S(1)}, u32[]{:S(2)}, u32[]{:S(2)}) collective-permute-start(bf16[128,1152]{1,0:T(8,128)(2,1)S(1)} %shard_map.86.refs_2_), channel_id=1, source_target_pairs={{0,8},{1,9},{2,10},{3,11},{4,12},{5,13},{6,14},{7,15},{8,0},{9,1},... | collective-permute-start | bytes 884744 | tf_op jit(solution)/shard_map/ppermute | solution.py:215
  23.4 0.7 copy-start.17
  24.1 10.9 %collective-permute-start.18 = (bf16[128,1152]{1,0:T(8,128)(2,1)S(1)}, bf16[128,1152]{1,0:T(8,128)(2,1)S(1)}, u32[]{:S(2)}, u32[]{:S(2)}) collective-permute-start(bf16[128,1152]{1,0:T(8,128)(2,1)S(1)} %shard_map.90.refs_2_), channel_id=1, source_target_pairs={{0,16},{1,17},{2,18},{3,19},{4,20},{5,21},{6,22},{7,23},{8,24},{9,... | collective-permute-start | bytes 884744 | tf_op jit(solution)/shard_map/ppermute | solution.py:215
  25.6 7.2 %copy-start.21 = (bf16[128,1152]{1,0:T(8,128)(2,1)}, bf16[128,1152]{1,0:T(8,128)(2,1)S(1)}, u32[]{:S(2)}) copy-start(bf16[128,1152]{1,0:T(8,128)(2,1)S(1)} %collective-permute-done.15.refs_5_) | copy-start | bytes 884740
  25.6 10.1 %collective-permute-start.17 = (bf16[128,1152]{1,0:T(8,128)(2,1)S(1)}, bf16[128,1152]{1,0:T(8,128)(2,1)S(1)}, u32[]{:S(2)}, u32[]{:S(2)}) collective-permute-start(bf16[128,1152]{1,0:T(8,128)(2,1)S(1)} %shard_map.90.refs_2_), channel_id=1, source_target_pairs={{0,8},{1,9},{2,10},{3,11},{4,12},{5,13},{6,14},{7,15},{8,0},{9,1},... | collective-permute-start | bytes 884744 | tf_op jit(solution)/shard_map/ppermute | solution.py:215
  27.2 10.8 %collective-permute-start.1 = (bf16[128,1152]{1,0:T(8,128)(2,1)S(1)}, bf16[128,1152]{1,0:T(8,128)(2,1)S(1)}, u32[]{:S(2)}, u32[]{:S(2)}) collective-permute-start(bf16[128,1152]{1,0:T(8,128)(2,1)S(1)} %shard_map.86.refs_2_), channel_id=1, source_target_pairs={{0,4},{1,5},{2,0},{3,1},{4,6},{5,7},{6,2},{7,3},{8,12},{9,13},{10,... | collective-permute-start | bytes 884744 | tf_op jit(solution)/shard_map/ppermute | solution.py:215
  30.6 1.6 %collective-permute-start.22 = (bf16[128,1152]{1,0:T(8,128)(2,1)S(1)}, bf16[128,1152]{1,0:T(8,128)(2,1)S(1)}, u32[]{:S(2)}, u32[]{:S(2)}) collective-permute-start(bf16[128,1152]{1,0:T(8,128)(2,1)S(1)} %collective-permute-done.6.refs_1_.refs_4_.refs_0_), channel_id=1, source_target_pairs={{0,8},{1,9},{2,10},{3,11},{4,12},{5,13},{6,14},{7,15},{8,0},{9,1},... | collective-permute-start | bytes 884744 | tf_op jit(solution)/shard_map/ppermute | solution.py:215
  30.6 0.7 copy-start.5
  31.3 14.7 %collective-permute-start.12 = (bf16[128,1152]{1,0:T(8,128)(2,1)S(1)}, bf16[128,1152]{1,0:T(8,128)(2,1)S(1)}, u32[]{:S(2)}, u32[]{:S(2)}) collective-permute-start(bf16[128,1152]{1,0:T(8,128)(2,1)S(1)} %collective-permute-done.11.refs_4_), channel_id=1, source_target_pairs={{0,8},{1,9},{2,10},{3,11},{4,12},{5,13},{6,14},{7,15},{8,0},{9,1},... | collective-permute-start | bytes 884744 | tf_op jit(solution)/shard_map/ppermute | solution.py:215
  32.2 0.7 copy-start.23
  32.9 8.3 %collective-permute-start.25 = (bf16[64,1152]{1,0:T(8,128)(2,1)S(1)}, bf16[64,1152]{1,0:T(8,128)(2,1)S(1)}, u32[]{:S(2)}, u32[]{:S(2)}) collective-permute-start(bf16[64,1152]{1,0:T(8,128)(2,1)S(1)} %get-tuple-element.40), channel_id=1, source_target_pairs={{0,4},{1,5},{2,0},{3,1},{4,6},{5,7},{6,2},{7,3},{8,12},{9,13},{10,... | collective-permute-start | bytes 442376 | tf_op jit(solution)/shard_map/ppermute | solution.py:215
  35.0 11.7 %collective-permute-start.19 = (bf16[128,1152]{1,0:T(8,128)(2,1)S(1)}, bf16[128,1152]{1,0:T(8,128)(2,1)S(1)}, u32[]{:S(2)}, u32[]{:S(2)}) collective-permute-start(bf16[128,1152]{1,0:T(8,128)(2,1)S(1)} %collective-permute-done.18.refs_4_), channel_id=1, source_target_pairs={{0,8},{1,9},{2,10},{3,11},{4,12},{5,13},{6,14},{7,15},{8,0},{9,1},... | collective-permute-start | bytes 884744 | tf_op jit(solution)/shard_map/ppermute | solution.py:215
  35.0 0.7 copy-start.3
  35.7 0.7 copy-start.7
  36.5 8.1 %collective-permute-start.28 = (bf16[64,1152]{1,0:T(8,128)(2,1)S(1)}, bf16[64,1152]{1,0:T(8,128)(2,1)}, u32[]{:S(2)}, u32[]{:S(2)}) collective-permute-start(bf16[64,1152]{1,0:T(8,128)(2,1)S(1)} %get-tuple-element.39), channel_id=1, source_target_pairs={{0,4},{1,5},{2,0},{3,1},{4,6},{5,7},{6,2},{7,3},{8,12},{9,13},{10,... | collective-permute-start | bytes 442376 | tf_op jit(solution)/shard_map/ppermute | solution.py:215
  38.0 10.0 %collective-permute-start.8 = (bf16[128,1152]{1,0:T(8,128)(2,1)S(1)}, bf16[128,1152]{1,0:T(8,128)(2,1)S(1)}, u32[]{:S(2)}, u32[]{:S(2)}) collective-permute-start(bf16[128,1152]{1,0:T(8,128)(2,1)S(1)} %collective-permute-done.1.refs_2_), channel_id=1, source_target_pairs={{0,1},{1,0},{2,3},{3,2},{4,5},{5,4},{6,7},{7,6},{8,9},{9,8},{10,11... | collective-permute-start | bytes 884744 | tf_op jit(solution)/shard_map/ppermute | solution.py:215
  41.1 8.2 %collective-permute-start.2 = (bf16[128,1152]{1,0:T(8,128)(2,1)S(1)}, bf16[128,1152]{1,0:T(8,128)(2,1)S(1)}, u32[]{:S(2)}, u32[]{:S(2)}) collective-permute-start(bf16[128,1152]{1,0:T(8,128)(2,1)S(1)} %collective-permute-done.1.refs_2_), channel_id=1, source_target_pairs={{0,4},{1,5},{2,0},{3,1},{4,6},{5,7},{6,2},{7,3},{8,12},{9,13},{10,... | collective-permute-start | bytes 884744 | tf_op jit(solution)/shard_map/ppermute | solution.py:215
  44.5 7.9 %collective-permute-start.32 = (bf16[128,1152]{1,0:T(8,128)(2,1)S(1)}, bf16[128,1152]{1,0:T(8,128)(2,1)}, u32[]{:S(2)}, u32[]{:S(2)}) collective-permute-start(bf16[128,1152]{1,0:T(8,128)(2,1)S(1)} %collective-permute-done.24.refs_2_), channel_id=1, source_target_pairs={{0,16},{1,17},{2,18},{3,19},{4,20},{5,21},{6,22},{7,23},{8,24},{9,... | collective-permute-start | bytes 884744 | tf_op jit(solution)/shard_map/ppermute | solution.py:215
  46.0 0.7 copy-start.11
  46.7 2.5 %collective-permute-start.34 = (bf16[64,1152]{1,0:T(8,128)(2,1)S(1)}, bf16[64,1152]{1,0:T(8,128)(2,1)}, u32[]{:S(2)}, u32[]{:S(2)}) collective-permute-start(bf16[64,1152]{1,0:T(8,128)(2,1)S(1)} %collective-permute-done.25.refs_6_), channel_id=1, source_target_pairs={{0,8},{1,9},{2,10},{3,11},{4,12},{5,13},{6,14},{7,15},{8,0},{9,1},... | collective-permute-start | bytes 442376 | tf_op jit(solution)/shard_map/ppermute | solution.py:215
  47.5 3.4 %collective-permute-start.35 = (bf16[64,1152]{1,0:T(8,128)(2,1)}, bf16[64,1152]{1,0:T(8,128)(2,1)}, u32[]{:S(2)}, u32[]{:S(2)}) collective-permute-start(bf16[64,1152]{1,0:T(8,128)(2,1)} %collective-permute-done.28.refs_8_), channel_id=1, source_target_pairs={{0,8},{1,9},{2,10},{3,11},{4,12},{5,13},{6,14},{7,15},{8,0},{9,1},... | collective-permute-start | bytes 442376 | tf_op jit(solution)/shard_map/ppermute | solution.py:215
  48.0 0.7 copy-start.9
  48.7 6.6 %collective-permute-start.26 = (bf16[64,1152]{1,0:T(8,128)(2,1)S(1)}, bf16[64,1152]{1,0:T(8,128)(2,1)S(1)}, u32[]{:S(2)}, u32[]{:S(2)}) collective-permute-start(bf16[64,1152]{1,0:T(8,128)(2,1)S(1)} %collective-permute-done.25.refs_6_), channel_id=1, source_target_pairs={{0,16},{1,17},{2,18},{3,19},{4,20},{5,21},{6,22},{7,23},{8,24},{9,... | collective-permute-start | bytes 442376 | tf_op jit(solution)/shard_map/ppermute | solution.py:215
  49.2 7.4 %collective-permute-start.31 = (bf16[128,1152]{1,0:T(8,128)(2,1)S(1)}, bf16[128,1152]{1,0:T(8,128)(2,1)S(1)}, u32[]{:S(2)}, u32[]{:S(2)}) collective-permute-start(bf16[128,1152]{1,0:T(8,128)(2,1)S(1)} %collective-permute-done.24.refs_2_), channel_id=1, source_target_pairs={{0,8},{1,9},{2,10},{3,11},{4,12},{5,13},{6,14},{7,15},{8,0},{9,1},... | collective-permute-start | bytes 884744 | tf_op jit(solution)/shard_map/ppermute | solution.py:215
  49.3 13.0 %collective-permute-start.4 = (bf16[128,1152]{1,0:T(8,128)(2,1)S(1)}, bf16[128,1152]{1,0:T(8,128)(2,1)S(1)}, u32[]{:S(2)}, u32[]{:S(2)}) collective-permute-start(bf16[128,1152]{1,0:T(8,128)(2,1)S(1)} %collective-permute-done.2.refs_1_), channel_id=1, source_target_pairs={{0,1},{1,0},{2,3},{3,2},{4,5},{5,4},{6,7},{7,6},{8,9},{9,8},{10,11... | collective-permute-start | bytes 884744 | tf_op jit(solution)/shard_map/ppermute | solution.py:215
  50.8 6.9 %collective-permute-start.29 = (bf16[64,1152]{1,0:T(8,128)(2,1)}, bf16[64,1152]{1,0:T(8,128)(2,1)S(1)}, u32[]{:S(2)}, u32[]{:S(2)}) collective-permute-start(bf16[64,1152]{1,0:T(8,128)(2,1)} %collective-permute-done.28.refs_8_), channel_id=1, source_target_pairs={{0,16},{1,17},{2,18},{3,19},{4,20},{5,21},{6,22},{7,23},{8,24},{9,... | collective-permute-start | bytes 442376 | tf_op jit(solution)/shard_map/ppermute | solution.py:215
  52.4 11.1 %collective-permute-start.33 = (bf16[128,1152]{1,0:T(8,128)(2,1)}, bf16[128,1152]{1,0:T(8,128)(2,1)S(1)}, u32[]{:S(2)}, u32[]{:S(2)}) collective-permute-start(bf16[128,1152]{1,0:T(8,128)(2,1)} %collective-permute-done.32.refs_4_), channel_id=1, source_target_pairs={{0,8},{1,9},{2,10},{3,11},{4,12},{5,13},{6,14},{7,15},{8,0},{9,1},... | collective-permute-start | bytes 884744 | tf_op jit(solution)/shard_map/ppermute | solution.py:215
  55.2 6.5 %collective-permute-start.27 = (bf16[64,1152]{1,0:T(8,128)(2,1)S(1)}, bf16[64,1152]{1,0:T(8,128)(2,1)S(1)}, u32[]{:S(2)}, u32[]{:S(2)}) collective-permute-start(bf16[64,1152]{1,0:T(8,128)(2,1)S(1)} %collective-permute-done.26.refs_1_), channel_id=1, source_target_pairs={{0,8},{1,9},{2,10},{3,11},{4,12},{5,13},{6,14},{7,15},{8,0},{9,1},... | collective-permute-start | bytes 442376 | tf_op jit(solution)/shard_map/ppermute | solution.py:215
  56.6 15.4 %collective-permute-start.7 = (bf16[128,1152]{1,0:T(8,128)(2,1)S(1)}, bf16[128,1152]{1,0:T(8,128)(2,1)S(1)}, u32[]{:S(2)}, u32[]{:S(2)}) collective-permute-start(bf16[128,1152]{1,0:T(8,128)(2,1)S(1)} %collective-permute-done.1.refs_2_), channel_id=1, source_target_pairs={{0,8},{1,9},{2,10},{3,11},{4,12},{5,13},{6,14},{7,15},{8,0},{9,1},... | collective-permute-start | bytes 884744 | tf_op jit(solution)/shard_map/ppermute | solution.py:215
  57.7 14.3 %collective-permute-start.9 = (bf16[128,1152]{1,0:T(8,128)(2,1)}, bf16[128,1152]{1,0:T(8,128)(2,1)S(1)}, u32[]{:S(2)}, u32[]{:S(2)}) collective-permute-start(bf16[128,1152]{1,0:T(8,128)(2,1)} %copy-done.9), channel_id=1, source_target_pairs={{0,8},{1,9},{2,10},{3,11},{4,12},{5,13},{6,14},{7,15},{8,0},{9,1},... | collective-permute-start | bytes 884744 | tf_op jit(solution)/shard_map/ppermute | solution.py:215
  58.4 1.0 copy-start.20
  59.4 1.0 copy-start.22
  60.4 2.0 %copy-start.18 = (bf16[128,1152]{1,0:T(8,128)(2,1)S(1)}, bf16[128,1152]{1,0:T(8,128)(2,1)}, u32[]{:S(2)}) copy-start(bf16[128,1152]{1,0:T(8,128)(2,1)} %copy-done.17) | copy-start | bytes 884740
  60.4 2.0 %copy-start.24 = (bf16[128,1152]{1,0:T(8,128)(2,1)S(1)}, bf16[128,1152]{1,0:T(8,128)(2,1)}, u32[]{:S(2)}) copy-start(bf16[128,1152]{1,0:T(8,128)(2,1)} %copy-done.23) | copy-start | bytes 884740
  61.7 2.3 %copy-start.6 = (bf16[128,1152]{1,0:T(8,128)(2,1)S(1)}, bf16[128,1152]{1,0:T(8,128)(2,1)}, u32[]{:S(2)}) copy-start(bf16[128,1152]{1,0:T(8,128)(2,1)} %copy-done.5) | copy-start | bytes 884740
  61.7 2.3 %copy-start.12 = (bf16[128,1152]{1,0:T(8,128)(2,1)S(1)}, bf16[128,1152]{1,0:T(8,128)(2,1)}, u32[]{:S(2)}) copy-start(bf16[128,1152]{1,0:T(8,128)(2,1)} %copy-done.11) | copy-start | bytes 884740
  61.7 11.6 %collective-permute-start.3 = (bf16[128,1152]{1,0:T(8,128)(2,1)S(1)}, bf16[128,1152]{1,0:T(8,128)(2,1)S(1)}, u32[]{:S(2)}, u32[]{:S(2)}) collective-permute-start(bf16[128,1152]{1,0:T(8,128)(2,1)S(1)} %collective-permute-done.2.refs_1_), channel_id=1, source_target_pairs={{0,8},{1,9},{2,10},{3,11},{4,12},{5,13},{6,14},{7,15},{8,0},{9,1},... | collective-permute-start | bytes 884744 | tf_op jit(solution)/shard_map/ppermute | solution.py:215
  62.3 11.1 %collective-permute-start.5 = (bf16[128,1152]{1,0:T(8,128)(2,1)S(1)}, bf16[128,1152]{1,0:T(8,128)(2,1)S(1)}, u32[]{:S(2)}, u32[]{:S(2)}) collective-permute-start(bf16[128,1152]{1,0:T(8,128)(2,1)S(1)} %collective-permute-done.4.refs_3_), channel_id=1, source_target_pairs={{0,8},{1,9},{2,10},{3,11},{4,12},{5,13},{6,14},{7,15},{8,0},{9,1},... | collective-permute-start | bytes 884744 | tf_op jit(solution)/shard_map/ppermute | solution.py:215
  63.5 6.1 %collective-permute-start.30 = (bf16[64,1152]{1,0:T(8,128)(2,1)S(1)}, bf16[64,1152]{1,0:T(8,128)(2,1)S(1)}, u32[]{:S(2)}, u32[]{:S(2)}) collective-permute-start(bf16[64,1152]{1,0:T(8,128)(2,1)S(1)} %collective-permute-done.29.refs_3_), channel_id=1, source_target_pairs={{0,8},{1,9},{2,10},{3,11},{4,12},{5,13},{6,14},{7,15},{8,0},{9,1},... | collective-permute-start | bytes 442376 | tf_op jit(solution)/shard_map/ppermute | solution.py:215
  64.0 1.3 %copy-start.4 = (bf16[128,1152]{1,0:T(8,128)(2,1)S(1)}, bf16[128,1152]{1,0:T(8,128)(2,1)}, u32[]{:S(2)}) copy-start(bf16[128,1152]{1,0:T(8,128)(2,1)} %copy-done.3) | copy-start | bytes 884740
  64.0 1.4 %copy-start.8 = (bf16[128,1152]{1,0:T(8,128)(2,1)S(1)}, bf16[128,1152]{1,0:T(8,128)(2,1)}, u32[]{:S(2)}) copy-start(bf16[128,1152]{1,0:T(8,128)(2,1)} %copy-done.7) | copy-start | bytes 884740
  64.0 1.4 %copy-start.14 = (bf16[128,1152]{1,0:T(8,128)(2,1)S(1)}, bf16[128,1152]{1,0:T(8,128)(2,1)}, u32[]{:S(2)}) copy-start(bf16[128,1152]{1,0:T(8,128)(2,1)} %copy-done.13) | copy-start | bytes 884740
  69.7 2.4 %copy-start.10 = (bf16[128,1152]{1,0:T(8,128)(2,1)S(1)}, bf16[128,1152]{1,0:T(8,128)(2,1)}, u32[]{:S(2)}) copy-start(bf16[128,1152]{1,0:T(8,128)(2,1)} %copy-done.9) | copy-start | bytes 884740
  70.5 31.8 %collective-permute-start.36 = (f32[128,1152]{1,0:T(8,128)S(1)}, f32[128,1152]{1,0:T(8,128)S(1)}, u32[]{:S(2)}, u32[]{:S(2)}) collective-permute-start(f32[128,1152]{1,0:T(8,128)S(1)} %shard_map.99), channel_id=1, source_target_pairs={{0,1},{1,0},{2,3},{3,2},{4,5},{5,4},{6,7},{7,6},{8,9},{9,8},{10,11... | collective-permute-start | bytes 1769480 | tf_op jit(solution)/shard_map/ppermute | solution.py:215
  74.3 29.2 %collective-permute-start.23 = (f32[128,1152]{1,0:T(8,128)S(1)}, f32[128,1152]{1,0:T(8,128)S(1)}, u32[]{:S(2)}, u32[]{:S(2)}) collective-permute-start(f32[128,1152]{1,0:T(8,128)S(1)} %shard_map.95), channel_id=1, source_target_pairs={{0,16},{1,17},{2,18},{3,19},{4,20},{5,21},{6,22},{7,23},{8,24},{9,... | collective-permute-start | bytes 1769480 | tf_op jit(solution)/shard_map/ppermute | solution.py:215
  75.8 13.7 %collective-permute-start.37 = (f32[8,128]{1,0:T(8,128)S(1)}, f32[8,128]{1,0:T(8,128)S(1)}, u32[]{:S(2)}, u32[]{:S(2)}) collective-permute-start(f32[8,128]{1,0:T(8,128)S(1)} %get-tuple-element.36), channel_id=1, source_target_pairs={{0,16},{1,17},{2,18},{3,19},{4,20},{5,21},{6,22},{7,23},{8,24},{9,... | collective-permute-start | bytes 12296 | tf_op jit(solution)/shard_map/ppermute | solution.py:215
  89.5 1.2 %collective-permute-start.38 = (f32[8,128]{1,0:T(8,128)S(1)}, f32[8,128]{1,0:T(8,128)S(1)}, u32[]{:S(2)}, u32[]{:S(2)}) collective-permute-start(f32[8,128]{1,0:T(8,128)S(1)} %add.91), channel_id=1, source_target_pairs={{0,8},{1,9},{2,10},{3,11},{4,12},{5,13},{6,14},{7,15},{8,0},{9,1},... | collective-permute-start | bytes 12296 | tf_op jit(solution)/shard_map/ppermute | solution.py:215
  90.6 3.6 %collective-permute-start.39 = (f32[8,128]{1,0:T(8,128)S(1)}, f32[8,128]{1,0:T(8,128)S(1)}, u32[]{:S(2)}, u32[]{:S(2)}) collective-permute-start(f32[8,128]{1,0:T(8,128)S(1)} %add.92), channel_id=1, source_target_pairs={{0,2},{1,3},{2,0},{3,1},{4,6},{5,7},{6,4},{7,5},{8,10},{9,11},{10,... | collective-permute-start | bytes 12296 | tf_op jit(solution)/shard_map/ppermute | solution.py:215
  94.2 4.5 %collective-permute-start.40 = (f32[8,128]{1,0:T(8,128)S(1)}, f32[8,128]{1,0:T(8,128)S(1)}, u32[]{:S(2)}, u32[]{:S(2)}) collective-permute-start(f32[8,128]{1,0:T(8,128)S(1)} %add.93), channel_id=1, source_target_pairs={{0,4},{1,5},{2,6},{3,7},{4,0},{5,1},{6,2},{7,3},{8,12},{9,13},{10,... | collective-permute-start | bytes 12296 | tf_op jit(solution)/shard_map/ppermute | solution.py:215
  98.8 3.6 %collective-permute-start.41 = (f32[8,128]{1,0:T(8,128)S(1)}, f32[8,128]{1,0:T(8,128)S(1)}, u32[]{:S(2)}, u32[]{:S(2)}) collective-permute-start(f32[8,128]{1,0:T(8,128)S(1)} %add.94.refs_2_), channel_id=1, source_target_pairs={{0,1},{1,0},{2,3},{3,2},{4,5},{5,4},{6,7},{7,6},{8,9},{9,8},{10,11... | collective-permute-start | bytes 12296 | tf_op jit(solution)/shard_map/ppermute | solution.py:215
  99.4 3.0 %copy-start.1 = (bf16[128,1152]{1,0:T(8,128)(2,1)S(1)}, bf16[128,1152]{1,0:T(8,128)(2,1)}, u32[]{:S(2)}) copy-start(bf16[128,1152]{1,0:T(8,128)(2,1)} %values.7) | copy-start | bytes 884740
  (3 other events, 2.1 us)

commit v5 on v4

--- a/solution.py
+++ b/solution.py
@@ -34,23 +34,35 @@
 
 
 def project_kernel(count, loss_count, factor, settings, values, *refs):
-    parts, losses, out = refs[:count], refs[count : count + loss_count], refs[count + loss_count]
-    unit, recip = unit_of(values[...])
-    total = parts[0][...]
-    for part in parts[1:]:
-        total = total + part[...]
-    grad = settings[0:1, 0:1] * total
-    out[...] = recip * (grad - unit * jnp.sum(unit * grad, axis=1, keepdims=True))
+    parts, losses = refs[:count], refs[count : count + loss_count]
+    outs, (held, sems) = refs[count + loss_count : -2], refs[-2:]
+    rows = values.shape[0]
+    pieces = sems.shape[0]
+    copies = []
+    for piece in range(pieces):
+        some = pl.ds(piece * (rows // pieces), rows // pieces)
+        unit, recip = unit_of(values[some, :])
+        total = parts[0][some, :]
+        for part in parts[1:]:
+            total = total + part[some, :]
+        grad = settings[0:1, 0:1] * total
+        held[some, :] = recip * (grad - unit * jnp.sum(unit * grad, axis=1, keepdims=True))
+        copies.append(pltpu.make_async_copy(held.at[some], outs[0].at[some], sems.at[piece]))
+        copies[-1].start()
     if loss_count:
         loss = losses[0][...]
         for part in losses[1:]:
             loss = loss + part[...]
-        refs[-1][0] = factor * jnp.sum(loss)
+        outs[1][0] = factor * jnp.sum(loss)
+    for copy in copies:
+        copy.wait()
 
 
 def project(values, settings, parts, losses, factor):
+    rows = values.shape[0]
+    pieces = 4 if rows % 64 == 0 else 1
     shapes = [jax.ShapeDtypeStruct(values.shape, jnp.float32)]
-    specs = [VMEM]
+    specs = [pl.BlockSpec(memory_space=pl.ANY)]
     if losses:
         shapes.append(jax.ShapeDtypeStruct((1,), jnp.float32))
         specs.append(pl.BlockSpec(memory_space=pltpu.SMEM))
@@ -59,6 +71,10 @@
         out_shape=shapes,
         in_specs=[VMEM] * (2 + len(parts) + len(losses)),
         out_specs=specs,
+        scratch_shapes=[
+            pltpu.VMEM(values.shape, jnp.float32),
+            pltpu.SemaphoreType.DMA((pieces,)),
+        ],
         compiler_params=PARAMS,
     )(settings, values, *parts, *losses)
     return tuple(out) if losses else out[0]
@@ -322,12 +338,13 @@
         img_sums, loss = image_terms(img_sums, loss, parts, range(wide), True)
         parts = [(img_sets[step][at], step, at, 0) for at in range(wide)]
         if step == end - 1:
-            parts += [(half[0], end, 0, offset) for half, offset in halves]
+            parts.append((first_set[0], end, 0, 0))
         txt_sums, loss = text_terms(txt_sums, loss, parts, range(fast), step == 1)
     parts = [(end, at) for at in range(fast)]
     img_far, _ = image_terms(img_sums[1:], None, parts, range(1, wide), False)
     img_near, _ = image_terms(img_sums[:1], None, parts, range(1), False)
-    parts = [(half[at], end, at, offset) for at in range(1, wide) for half, offset in halves]
+    parts = [(second_set[0], end, 0, middle)]
+    parts += [(half[at], end, at, offset) for at in range(1, wide) for half, offset in halves]
     txt_far, _ = text_terms(txt_sums[1:], None, parts, range(1, fast), False)
     txt_near, _ = text_terms(txt_sums[:1], None, parts, range(1), False)
     img_sums, txt_sums = [*img_near, *img_far], [*txt_near, *txt_far]

time: 105 us -> 107 us (1.019)
  Pallas kernels: 15.6 us -> 17.1 us
    pallas_call x10, Pallas kernels: 12.8 us -> 13.9 us  [terms(): pl.pallas_call(kernel, out_shape=shapes, in_specs=[VMEM] * len(operands),...]
  transfers between devices with their start and end apart: 42 -> 42, of which waited for: 15 -> 15; matrix products, arithmetic and copies ran while one was open for 0% -> 0% of each run, Pallas kernels for 14% -> 15%
where the time goes in v5:
time: 107 us
  starting transfers between devices  44.1 us (41%)
  waiting for transfers between devices  33.4 us (31%)
  Pallas kernels  17.1 us (16%)
  local copies, waits for them, and re-layouts  9.5 us (9%)
  between operations  2.42 us (2%)
    ppermute x42, starting transfers between devices, permuted(): return lax.ppermute(array, AXES, pairs)  44.1 us
    ppermute x42, waiting for transfers between devices, permuted(): return lax.ppermute(array, AXES, pairs)  33.4 us
    pallas_call x10, Pallas kernels, terms(): pl.pallas_call(kernel, out_shape=shapes, in_specs=[VMEM] * len(operands),...  13.9 us
    unnamed x50, local copies, waits for them, and re-layouts  9.4 us
    pallas_call x2, Pallas kernels, project(): pl.pallas_call(functools.partial(project_kernel, len(parts), len(losses),...  2.62 us
  transfers between devices with their start and end apart: 42, of which 15 were waited for; matrix products, arithmetic and copies ran while one was open for 0% of the time, Pallas kernels for 15%

profile of v5, /device:TPU:0, one launch (start us, length us, event | category | flops | bytes accessed | tf_op | source)
XLA Modules:
  0.0 106.6 jit_solution(3039902767221473374)
XLA Ops:
  0.6 4.1 %collective-permute-start = (bf16[128,1152]{1,0:T(8,128)(2,1)}, bf16[128,1152]{1,0:T(8,128)(2,1)S(1)}, u32[]{:S(2)}, u32[]{:S(2)}) collective-permute-start(bf16[128,1152]{1,0:T(8,128)(2,1)} %values.7), channel_id=1, source_target_pairs={{0,4},{1,5},{2,0},{3,1},{4,6},{5,7},{6,2},{7,3},{8,12},{9,13},{10,... | collective-permute-start | bytes 884744 | tf_op jit(solution)/shard_map/ppermute | solution.py:231
  4.7 1.0 copy-done
  5.9 1.6 %collective-permute-start.14 = (bf16[128,1152]{1,0:T(8,128)(2,1)S(1)}, bf16[128,1152]{1,0:T(8,128)(2,1)S(1)}, u32[]{:S(2)}, u32[]{:S(2)}) collective-permute-start(bf16[128,1152]{1,0:T(8,128)(2,1)S(1)} %shard_map.87.refs_2_.refs_0_), channel_id=1, source_target_pairs={{0,1},{1,0},{2,3},{3,2},{4,5},{5,4},{6,7},{7,6},{8,9},{9,8},{10,11... | collective-permute-start | bytes 884744 | tf_op jit(solution)/shard_map/ppermute | solution.py:231
  7.5 1.6 %collective-permute-start.16 = (bf16[128,1152]{1,0:T(8,128)(2,1)S(1)}, bf16[128,1152]{1,0:T(8,128)(2,1)S(1)}, u32[]{:S(2)}, u32[]{:S(2)}) collective-permute-start(bf16[128,1152]{1,0:T(8,128)(2,1)S(1)} %copy-done.2), channel_id=1, source_target_pairs={{0,4},{1,5},{2,0},{3,1},{4,6},{5,7},{6,2},{7,3},{8,12},{9,13},{10,... | collective-permute-start | bytes 884744 | tf_op jit(solution)/shard_map/ppermute | solution.py:231
  9.2 1.6 %collective-permute-start.6 = (bf16[128,1152]{1,0:T(8,128)(2,1)S(1)}, bf16[128,1152]{1,0:T(8,128)(2,1)S(1)}, u32[]{:S(2)}, u32[]{:S(2)}) collective-permute-start(bf16[128,1152]{1,0:T(8,128)(2,1)S(1)} %shard_map.85.refs_0_.refs_2_), channel_id=1, source_target_pairs={{0,16},{1,17},{2,18},{3,19},{4,20},{5,21},{6,22},{7,23},{8,24},{9,... | collective-permute-start | bytes 884744 | tf_op jit(solution)/shard_map/ppermute | solution.py:231
  10.8 1.7 %collective-permute-done.values = bf16[128,1152]{1,0:T(8,128)(2,1)S(1)} collective-permute-done((bf16[128,1152]{1,0:T(8,128)(2,1)}, bf16[128,1152]{1,0:T(8,128)(2,1)S(1)}, u32[]{:S(2)}, u32[]{:S(2)}) %collective-permute-start) | collective-permute-done | bytes 294944 | tf_op jit(solution)/shard_map/ppermute | solution.py:231
  12.5 1.5 %collective-permute-start.20 = (s32[1,128]{1,0:T(1,128)S(1)}, s32[1,128]{1,0:T(1,128)S(1)}, u32[]{:S(2)}, u32[]{:S(2)}) collective-permute-start(s32[1,128]{1,0:T(1,128)S(1)} %bitcast.14), channel_id=1, source_target_pairs={{0,1},{1,0},{2,3},{3,2},{4,5},{5,4},{6,7},{7,6},{8,9},{9,8},{10,11... | collective-permute-start | bytes 1544 | tf_op jit(solution)/shard_map/ppermute | solution.py:231
  14.4 3.1 %collective-permute-done.16.values = bf16[128,1152]{1,0:T(8,128)(2,1)S(1)} collective-permute-done((bf16[128,1152]{1,0:T(8,128)(2,1)S(1)}, bf16[128,1152]{1,0:T(8,128)(2,1)S(1)}, u32[]{:S(2)}, u32[]{:S(2)}) %collective-permute-start.16) | collective-permute-done | bytes 294944 | tf_op jit(solution)/shard_map/ppermute | solution.py:231
  17.7 1.6 %collective-permute-start.11 = (bf16[128,1152]{1,0:T(8,128)(2,1)S(1)}, bf16[128,1152]{1,0:T(8,128)(2,1)S(1)}, u32[]{:S(2)}, u32[]{:S(2)}) collective-permute-start(bf16[128,1152]{1,0:T(8,128)(2,1)S(1)} %shard_map.86.refs_2_), channel_id=1, source_target_pairs={{0,1},{1,0},{2,3},{3,2},{4,5},{5,4},{6,7},{7,6},{8,9},{9,8},{10,11... | collective-permute-start | bytes 884744 | tf_op jit(solution)/shard_map/ppermute | solution.py:231
  19.5 0.7 copy-done.19
  20.3 3.4 %collective-permute-start.24 = (bf16[128,1152]{1,0:T(8,128)(2,1)S(1)}, bf16[128,1152]{1,0:T(8,128)(2,1)S(1)}, u32[]{:S(2)}, u32[]{:S(2)}) collective-permute-start(bf16[128,1152]{1,0:T(8,128)(2,1)S(1)} %shard_map.90.refs_2_), channel_id=1, source_target_pairs={{0,4},{1,5},{2,0},{3,1},{4,6},{5,7},{6,2},{7,3},{8,12},{9,13},{10,... | collective-permute-start | bytes 884744 | tf_op jit(solution)/shard_map/ppermute | solution.py:231
  23.7 0.7 copy-done.17
  24.4 1.5 %collective-permute-start.18 = (bf16[128,1152]{1,0:T(8,128)(2,1)S(1)}, bf16[128,1152]{1,0:T(8,128)(2,1)S(1)}, u32[]{:S(2)}, u32[]{:S(2)}) collective-permute-start(bf16[128,1152]{1,0:T(8,128)(2,1)S(1)} %shard_map.90.refs_2_), channel_id=1, source_target_pairs={{0,16},{1,17},{2,18},{3,19},{4,20},{5,21},{6,22},{7,23},{8,24},{9,... | collective-permute-start | bytes 884744 | tf_op jit(solution)/shard_map/ppermute | solution.py:231
  25.9 0.7 copy-done.21
  26.6 0.6 collective-permute-done.11.refs_4_
  27.2 3.4 %collective-permute-start.1 = (bf16[128,1152]{1,0:T(8,128)(2,1)S(1)}, bf16[128,1152]{1,0:T(8,128)(2,1)}, u32[]{:S(2)}, u32[]{:S(2)}) collective-permute-start(bf16[128,1152]{1,0:T(8,128)(2,1)S(1)} %shard_map.86.refs_2_), channel_id=1, source_target_pairs={{0,4},{1,5},{2,0},{3,1},{4,6},{5,7},{6,2},{7,3},{8,12},{9,13},{10,... | collective-permute-start | bytes 884744 | tf_op jit(solution)/shard_map/ppermute | solution.py:231
  30.6 0.5 collective-permute-start.12
  31.1 1.0 collective-permute-done.22.refs_5_
  32.2 0.7 copy-done.23
  32.9 1.6 %collective-permute-start.27 = (bf16[64,1152]{1,0:T(8,128)(2,1)S(1)}, bf16[64,1152]{1,0:T(8,128)(2,1)}, u32[]{:S(2)}, u32[]{:S(2)}) collective-permute-start(bf16[64,1152]{1,0:T(8,128)(2,1)S(1)} %get-tuple-element.39), channel_id=1, source_target_pairs={{0,4},{1,5},{2,0},{3,1},{4,6},{5,7},{6,2},{7,3},{8,12},{9,13},{10,... | collective-permute-start | bytes 442376 | tf_op jit(solution)/shard_map/ppermute | solution.py:231
  34.8 0.7 copy-done.7
  35.5 0.7 copy-done.9
  36.6 1.4 %collective-permute-done.1.refs_2_ = bf16[128,1152]{1,0:T(8,128)(2,1)} collective-permute-done((bf16[128,1152]{1,0:T(8,128)(2,1)S(1)}, bf16[128,1152]{1,0:T(8,128)(2,1)}, u32[]{:S(2)}, u32[]{:S(2)}) %collective-permute-start.1) | collective-permute-done | bytes 294944 | tf_op jit(solution)/shard_map/ppermute | solution.py:231
  38.0 1.5 %collective-permute-start.8 = (bf16[128,1152]{1,0:T(8,128)(2,1)}, bf16[128,1152]{1,0:T(8,128)(2,1)}, u32[]{:S(2)}, u32[]{:S(2)}) collective-permute-start(bf16[128,1152]{1,0:T(8,128)(2,1)} %collective-permute-done.1.refs_2_), channel_id=1, source_target_pairs={{0,1},{1,0},{2,3},{3,2},{4,5},{5,4},{6,7},{7,6},{8,9},{9,8},{10,11... | collective-permute-start | bytes 884744 | tf_op jit(solution)/shard_map/ppermute | solution.py:231
  39.5 1.6 %collective-permute-done.27.refs_6_ = bf16[64,1152]{1,0:T(8,128)(2,1)} collective-permute-done((bf16[64,1152]{1,0:T(8,128)(2,1)S(1)}, bf16[64,1152]{1,0:T(8,128)(2,1)}, u32[]{:S(2)}, u32[]{:S(2)}) %collective-permute-start.27) | collective-permute-done | bytes 147488 | tf_op jit(solution)/shard_map/ppermute | solution.py:231
  41.1 3.5 %collective-permute-start.2 = (bf16[128,1152]{1,0:T(8,128)(2,1)}, bf16[128,1152]{1,0:T(8,128)(2,1)S(1)}, u32[]{:S(2)}, u32[]{:S(2)}) collective-permute-start(bf16[128,1152]{1,0:T(8,128)(2,1)} %collective-permute-done.1.refs_2_), channel_id=1, source_target_pairs={{0,4},{1,5},{2,0},{3,1},{4,6},{5,7},{6,2},{7,3},{8,12},{9,13},{10,... | collective-permute-start | bytes 884744 | tf_op jit(solution)/shard_map/ppermute | solution.py:231
  44.6 1.5 %collective-permute-start.33 = (bf16[128,1152]{1,0:T(8,128)(2,1)S(1)}, bf16[128,1152]{1,0:T(8,128)(2,1)S(1)}, u32[]{:S(2)}, u32[]{:S(2)}) collective-permute-start(bf16[128,1152]{1,0:T(8,128)(2,1)S(1)} %collective-permute-done.24.refs_2_), channel_id=1, source_target_pairs={{0,16},{1,17},{2,18},{3,19},{4,20},{5,21},{6,22},{7,23},{8,24},{9,... | collective-permute-start | bytes 884744 | tf_op jit(solution)/shard_map/ppermute | solution.py:231
  46.1 0.7 copy-done.11
  46.9 0.7 copy-done.13
  47.6 0.5 collective-permute-start.35
  48.1 0.5 collective-permute-start.30
  48.6 0.8 collective-permute-done.2.refs_1_
  49.4 1.5 %collective-permute-start.4 = (bf16[128,1152]{1,0:T(8,128)(2,1)S(1)}, bf16[128,1152]{1,0:T(8,128)(2,1)S(1)}, u32[]{:S(2)}, u32[]{:S(2)}) collective-permute-start(bf16[128,1152]{1,0:T(8,128)(2,1)S(1)} %collective-permute-done.2.refs_1_), channel_id=1, source_target_pairs={{0,1},{1,0},{2,3},{3,2},{4,5},{5,4},{6,7},{7,6},{8,9},{9,8},{10,11... | collective-permute-start | bytes 884744 | tf_op jit(solution)/shard_map/ppermute | solution.py:231
  50.9 1.6 %collective-permute-start.28 = (bf16[64,1152]{1,0:T(8,128)(2,1)}, bf16[64,1152]{1,0:T(8,128)(2,1)S(1)}, u32[]{:S(2)}, u32[]{:S(2)}) collective-permute-start(bf16[64,1152]{1,0:T(8,128)(2,1)} %collective-permute-done.27.refs_6_), channel_id=1, source_target_pairs={{0,16},{1,17},{2,18},{3,19},{4,20},{5,21},{6,22},{7,23},{8,24},{9,... | collective-permute-start | bytes 442376 | tf_op jit(solution)/shard_map/ppermute | solution.py:231
  52.5 0.5 collective-permute-start.34
  53.0 2.2 %collective-permute-done.30.refs_5_ = bf16[64,1152]{1,0:T(8,128)(2,1)S(1)} collective-permute-done((bf16[64,1152]{1,0:T(8,128)(2,1)S(1)}, bf16[64,1152]{1,0:T(8,128)(2,1)S(1)}, u32[]{:S(2)}, u32[]{:S(2)}) %collective-permute-start.30) | collective-permute-done | bytes 147488 | tf_op jit(solution)/shard_map/ppermute | solution.py:231
  56.6 1.1 %collective-permute-done.28.refs_3_ = bf16[64,1152]{1,0:T(8,128)(2,1)S(1)} collective-permute-done((bf16[64,1152]{1,0:T(8,128)(2,1)}, bf16[64,1152]{1,0:T(8,128)(2,1)S(1)}, u32[]{:S(2)}, u32[]{:S(2)}) %collective-permute-start.28) | collective-permute-done | bytes 147488 | tf_op jit(solution)/shard_map/ppermute | solution.py:231
  57.7 0.5 collective-permute-start.9
  58.3 0.7 copy-done.15
  58.9 1.0 copy-done.20
  59.9 1.0 copy-done.22
  60.9 1.3 %shard_map.88 = (f32[128,1152]{1,0:T(8,128)S(1)}, f32[128,1152]{1,0:T(8,128)S(1)}, f32[8,128]{1,0:T(8,128)S(1)}) custom-call(f32[8,128]{1,0:T(8,128)S(1)} %concatenate.6.settings, s32[8,128]{1,0:T(8,128)S(1)} %iota_add_fusion.ids, bf16[128,1152]{1,0:T(8,128)(2,1)S(1)} %shard_map.85.refs_0_.refs_2_, ...), custom_call_target="tpu_custom_call" | custom-call | flops 603979776 | bytes 4128768 | tf_op jit(solution)/shard_map/pallas_call | solution.py:181
  62.3 0.5 collective-permute-start.5
  62.8 1.1 %shard_map.91 = (f32[128,1152]{1,0:T(8,128)S(1)}, f32[128,1152]{1,0:T(8,128)S(1)}) custom-call(f32[8,128]{1,0:T(8,128)S(1)} %concatenate.6.settings, s32[8,128]{1,0:T(8,128)S(1)} %iota_add_fusion.ids, bf16[128,1152]{1,0:T(8,128)(2,1)S(1)} %shard_map.87.refs_2_.refs_0_, bf16[128,1152]{1,0:T(8,128)(2,1)S(1)} %collective-permute-done.14.refs_4_.refs_1_.refs_0_, ...), custom_call_target="tpu_custom_call" | custom-call | flops 603979776 | bytes 4128768 | tf_op jit(solution)/shard_map/pallas_call | solution.py:181
  64.1 1.3 %shard_map.89 = (f32[128,1152]{1,0:T(8,128)S(1)}, f32[128,1152]{1,0:T(8,128)S(1)}, f32[8,128]{1,0:T(8,128)S(1)}) custom-call(f32[8,128]{1,0:T(8,128)S(1)} %concatenate.6.settings, s32[8,128]{1,0:T(8,128)S(1)} %iota_add_fusion.ids, bf16[128,1152]{1,0:T(8,128)(2,1)S(1)} %shard_map.85.refs_0_.refs_2_, ...), custom_call_target="tpu_custom_call", output_to_operand_aliasing={{0}: (10, {}), {1}: (11, {}), {2}: (12, {})} | custom-call | flops 603979776 | bytes 4128768 | tf_op jit(solution)/shard_map/pallas_call | solution.py:181
  65.5 1.3 %shard_map.92 = (f32[128,1152]{1,0:T(8,128)S(1)}, f32[128,1152]{1,0:T(8,128)S(1)}, f32[8,128]{1,0:T(8,128)S(1)}) custom-call(f32[8,128]{1,0:T(8,128)S(1)} %concatenate.6.settings, s32[8,128]{1,0:T(8,128)S(1)} %iota_add_fusion.ids, bf16[128,1152]{1,0:T(8,128)(2,1)S(1)} %shard_map.87.refs_2_.refs_0_, ...), custom_call_target="tpu_custom_call", output_to_operand_aliasing={{0}: (10, {}), {1}: (11, {}), {2}: (12, {})} | custom-call | flops 603979776 | bytes 4128768 | tf_op jit(solution)/shard_map/pallas_call | solution.py:181
  66.8 2.7 %shard_map.97 = (f32[128,1152]{1,0:T(8,128)S(1)}, f32[128,1152]{1,0:T(8,128)S(1)}) custom-call(f32[8,128]{1,0:T(8,128)S(1)} %concatenate.6.settings, s32[8,128]{1,0:T(8,128)S(1)} %iota_add_fusion.ids, bf16[128,1152]{1,0:T(8,128)(2,1)S(1)} %shard_map.87.refs_2_.refs_0_, ...), custom_call_target="tpu_custom_call", output_to_operand_aliasing={{0}: (12, {}), {1}: (13, {})} | custom-call | flops 754974720 | bytes 4718592 | tf_op jit(solution)/shard_map/pallas_call | solution.py:181
  69.5 1.0 shard_map.99
  70.5 1.6 %collective-permute-start.36 = (f32[128,1152]{1,0:T(8,128)S(1)}, f32[128,1152]{1,0:T(8,128)S(1)}, u32[]{:S(2)}, u32[]{:S(2)}) collective-permute-start(f32[128,1152]{1,0:T(8,128)S(1)} %shard_map.99), channel_id=1, source_target_pairs={{0,1},{1,0},{2,3},{3,2},{4,5},{5,4},{6,7},{7,6},{8,9},{9,8},{10,11... | collective-permute-start | bytes 1769480 | tf_op jit(solution)/shard_map/ppermute | solution.py:231
  72.1 2.4 %shard_map.93 = (f32[128,1152]{1,0:T(8,128)S(1)}, f32[128,1152]{1,0:T(8,128)S(1)}, f32[8,128]{1,0:T(8,128)S(1)}) custom-call(f32[8,128]{1,0:T(8,128)S(1)} %concatenate.6.settings, s32[8,128]{1,0:T(8,128)S(1)} %iota_add_fusion.ids, bf16[128,1152]{1,0:T(8,128)(2,1)S(1)} %shard_map.85.refs_0_.refs_2_, ...), custom_call_target="tpu_custom_call", output_to_operand_aliasing={{0}: (10, {}), {1}: (11, {}), {2}: (12, {})} | custom-call | flops 603979776 | bytes 4128768 | tf_op jit(solution)/shard_map/pallas_call | solution.py:181
  74.5 0.9 shard_map.95
  75.3 1.9 %collective-permute-start.23 = (f32[128,1152]{1,0:T(8,128)S(1)}, f32[128,1152]{1,0:T(8,128)S(1)}, u32[]{:S(2)}, u32[]{:S(2)}) collective-permute-start(f32[128,1152]{1,0:T(8,128)S(1)} %shard_map.95), channel_id=1, source_target_pairs={{0,16},{1,17},{2,18},{3,19},{4,20},{5,21},{6,22},{7,23},{8,24},{9,... | collective-permute-start | bytes 1769480 | tf_op jit(solution)/shard_map/ppermute | solution.py:231
  77.4 13.5 %collective-permute-done.37 = f32[8,128]{1,0:T(8,128)S(1)} collective-permute-done((f32[8,128]{1,0:T(8,128)S(1)}, f32[8,128]{1,0:T(8,128)S(1)}, u32[]{:S(2)}, u32[]{:S(2)}) %collective-permute-start.37) | collective-permute-done | bytes 4128 | tf_op jit(solution)/shard_map/ppermute | solution.py:231
  90.9 1.2 %collective-permute-done.38 = f32[8,128]{1,0:T(8,128)S(1)} collective-permute-done((f32[8,128]{1,0:T(8,128)S(1)}, f32[8,128]{1,0:T(8,128)S(1)}, u32[]{:S(2)}, u32[]{:S(2)}) %collective-permute-start.38) | collective-permute-done | bytes 4128 | tf_op jit(solution)/shard_map/ppermute | solution.py:231
  92.1 1.7 %collective-permute-start.39 = (f32[8,128]{1,0:T(8,128)S(1)}, f32[8,128]{1,0:T(8,128)S(1)}, u32[]{:S(2)}, u32[]{:S(2)}) collective-permute-start(f32[8,128]{1,0:T(8,128)S(1)} %add.92), channel_id=1, source_target_pairs={{0,2},{1,3},{2,0},{3,1},{4,6},{5,7},{6,4},{7,5},{8,10},{9,11},{10,... | collective-permute-start | bytes 12296 | tf_op jit(solution)/shard_map/ppermute | solution.py:231
  93.8 1.9 %collective-permute-done.39 = f32[8,128]{1,0:T(8,128)S(1)} collective-permute-done((f32[8,128]{1,0:T(8,128)S(1)}, f32[8,128]{1,0:T(8,128)S(1)}, u32[]{:S(2)}, u32[]{:S(2)}) %collective-permute-start.39) | collective-permute-done | bytes 4128 | tf_op jit(solution)/shard_map/ppermute | solution.py:231
  95.7 2.7 %collective-permute-start.40 = (f32[8,128]{1,0:T(8,128)S(1)}, f32[8,128]{1,0:T(8,128)S(1)}, u32[]{:S(2)}, u32[]{:S(2)}) collective-permute-start(f32[8,128]{1,0:T(8,128)S(1)} %add.93), channel_id=1, source_target_pairs={{0,4},{1,5},{2,6},{3,7},{4,0},{5,1},{6,2},{7,3},{8,12},{9,13},{10,... | collective-permute-start | bytes 12296 | tf_op jit(solution)/shard_map/ppermute | solution.py:231
  98.4 1.0 shard_map.98.refs_0_
  99.4 0.8 collective-permute-done.40
  100.2 0.5 collective-permute-start.41
  100.7 0.9 shard_map.94.refs_0_
  101.6 2.2 %collective-permute-done.41.refs_3_ = f32[8,128]{1,0:T(8,128)S(1)} collective-permute-done((f32[8,128]{1,0:T(8,128)S(1)}, f32[8,128]{1,0:T(8,128)S(1)}, u32[]{:S(2)}, u32[]{:S(2)}) %collective-permute-start.41) | collective-permute-done | bytes 4128 | tf_op jit(solution)/shard_map/ppermute | solution.py:231
  103.8 1.6 %shard_map.100 = (f32[128,1152]{1,0:T(8,128)}, f32[1]{0:T(128)}) custom-call(f32[8,128]{1,0:T(8,128)S(1)} %concatenate.6.settings, bf16[128,1152]{1,0:T(8,128)(2,1)S(1)} %copy-done.1, f32[128,1152]{1,0:T(8,128)S(1)} %shard_map.98.refs_0_, f32[128,1152]{1,0:T(8,128)S(1)} %collective-permute-done.36.refs_1_, f32[8,128]{1,0:T(8,128)S(1)} %add.94.refs_2_, ...), custom_call_target="tpu_custom_call" | custom-call | tf_op jit(solution)/shard_map/pallas_call | solution.py:69
  105.4 1.1 shard_map.96
  (96 shorter events, 2.5 us)
Async XLA Ops:
  0.6 11.8 %collective-permute-start = (bf16[128,1152]{1,0:T(8,128)(2,1)}, bf16[128,1152]{1,0:T(8,128)(2,1)S(1)}, u32[]{:S(2)}, u32[]{:S(2)}) collective-permute-start(bf16[128,1152]{1,0:T(8,128)(2,1)} %values.7), channel_id=1, source_target_pairs={{0,4},{1,5},{2,0},{3,1},{4,6},{5,7},{6,2},{7,3},{8,12},{9,13},{10,... | collective-permute-start | bytes 884744 | tf_op jit(solution)/shard_map/ppermute | solution.py:231
  4.7 1.0 copy-start
  5.7 1.7 %copy-start.2 = (bf16[128,1152]{1,0:T(8,128)(2,1)S(1)}, bf16[128,1152]{1,0:T(8,128)(2,1)}, u32[]{:S(2)}) copy-start(bf16[128,1152]{1,0:T(8,128)(2,1)} %values.6) | copy-start | bytes 884740
  5.9 8.5 %collective-permute-start.14 = (bf16[128,1152]{1,0:T(8,128)(2,1)S(1)}, bf16[128,1152]{1,0:T(8,128)(2,1)S(1)}, u32[]{:S(2)}, u32[]{:S(2)}) collective-permute-start(bf16[128,1152]{1,0:T(8,128)(2,1)S(1)} %shard_map.87.refs_2_.refs_0_), channel_id=1, source_target_pairs={{0,1},{1,0},{2,3},{3,2},{4,5},{5,4},{6,7},{7,6},{8,9},{9,8},{10,11... | collective-permute-start | bytes 884744 | tf_op jit(solution)/shard_map/ppermute | solution.py:231
  7.5 10.1 %collective-permute-start.16 = (bf16[128,1152]{1,0:T(8,128)(2,1)S(1)}, bf16[128,1152]{1,0:T(8,128)(2,1)S(1)}, u32[]{:S(2)}, u32[]{:S(2)}) collective-permute-start(bf16[128,1152]{1,0:T(8,128)(2,1)S(1)} %copy-done.2), channel_id=1, source_target_pairs={{0,4},{1,5},{2,0},{3,1},{4,6},{5,7},{6,2},{7,3},{8,12},{9,13},{10,... | collective-permute-start | bytes 884744 | tf_op jit(solution)/shard_map/ppermute | solution.py:231
  9.2 3.3 %copy-start.16 = (s32[128]{0:T(128)S(1)}, s32[128]{0:T(128)}, u32[]{:S(2)}) copy-start(s32[128]{0:T(128)} %param.8) | copy-start | bytes 1540
  9.2 10.1 %collective-permute-start.6 = (bf16[128,1152]{1,0:T(8,128)(2,1)S(1)}, bf16[128,1152]{1,0:T(8,128)(2,1)S(1)}, u32[]{:S(2)}, u32[]{:S(2)}) collective-permute-start(bf16[128,1152]{1,0:T(8,128)(2,1)S(1)} %shard_map.85.refs_0_.refs_2_), channel_id=1, source_target_pairs={{0,16},{1,17},{2,18},{3,19},{4,20},{5,21},{6,22},{7,23},{8,24},{9,... | collective-permute-start | bytes 884744 | tf_op jit(solution)/shard_map/ppermute | solution.py:231
  10.8 8.7 %collective-permute-start.13 = (bf16[128,1152]{1,0:T(8,128)(2,1)S(1)}, bf16[128,1152]{1,0:T(8,128)(2,1)S(1)}, u32[]{:S(2)}, u32[]{:S(2)}) collective-permute-start(bf16[128,1152]{1,0:T(8,128)(2,1)S(1)} %shard_map.87.refs_2_.refs_0_), channel_id=1, source_target_pairs={{0,8},{1,9},{2,10},{3,11},{4,12},{5,13},{6,14},{7,15},{8,0},{9,1},... | collective-permute-start | bytes 884744 | tf_op jit(solution)/shard_map/ppermute | solution.py:231
  12.5 5.2 %collective-permute-start.20 = (s32[1,128]{1,0:T(1,128)S(1)}, s32[1,128]{1,0:T(1,128)S(1)}, u32[]{:S(2)}, u32[]{:S(2)}) collective-permute-start(s32[1,128]{1,0:T(1,128)S(1)} %bitcast.14), channel_id=1, source_target_pairs={{0,1},{1,0},{2,3},{3,2},{4,5},{5,4},{6,7},{7,6},{8,9},{9,8},{10,11... | collective-permute-start | bytes 1544 | tf_op jit(solution)/shard_map/ppermute | solution.py:231
  14.4 9.2 %collective-permute-start.21 = (bf16[128,1152]{1,0:T(8,128)(2,1)S(1)}, bf16[128,1152]{1,0:T(8,128)(2,1)S(1)}, u32[]{:S(2)}, u32[]{:S(2)}) collective-permute-start(bf16[128,1152]{1,0:T(8,128)(2,1)S(1)} %shard_map.85.refs_0_.refs_2_), channel_id=1, source_target_pairs={{0,8},{1,9},{2,10},{3,11},{4,12},{5,13},{6,14},{7,15},{8,0},{9,1},... | collective-permute-start | bytes 884744 | tf_op jit(solution)/shard_map/ppermute | solution.py:231
  17.5 8.3 %collective-permute-start.15 = (bf16[128,1152]{1,0:T(8,128)(2,1)S(1)}, bf16[128,1152]{1,0:T(8,128)(2,1)S(1)}, u32[]{:S(2)}, u32[]{:S(2)}) collective-permute-start(bf16[128,1152]{1,0:T(8,128)(2,1)S(1)} %collective-permute-done.14.refs_4_.refs_1_.refs_0_), channel_id=1, source_target_pairs={{0,8},{1,9},{2,10},{3,11},{4,12},{5,13},{6,14},{7,15},{8,0},{9,1},... | collective-permute-start | bytes 884744 | tf_op jit(solution)/shard_map/ppermute | solution.py:231
  17.7 9.5 %collective-permute-start.11 = (bf16[128,1152]{1,0:T(8,128)(2,1)S(1)}, bf16[128,1152]{1,0:T(8,128)(2,1)S(1)}, u32[]{:S(2)}, u32[]{:S(2)}) collective-permute-start(bf16[128,1152]{1,0:T(8,128)(2,1)S(1)} %shard_map.86.refs_2_), channel_id=1, source_target_pairs={{0,1},{1,0},{2,3},{3,2},{4,5},{5,4},{6,7},{7,6},{8,9},{9,8},{10,11... | collective-permute-start | bytes 884744 | tf_op jit(solution)/shard_map/ppermute | solution.py:231
  19.3 11.3 %collective-permute-start.10 = (bf16[128,1152]{1,0:T(8,128)(2,1)S(1)}, bf16[128,1152]{1,0:T(8,128)(2,1)S(1)}, u32[]{:S(2)}, u32[]{:S(2)}) collective-permute-start(bf16[128,1152]{1,0:T(8,128)(2,1)S(1)} %shard_map.86.refs_2_), channel_id=1, source_target_pairs={{0,8},{1,9},{2,10},{3,11},{4,12},{5,13},{6,14},{7,15},{8,0},{9,1},... | collective-permute-start | bytes 884744 | tf_op jit(solution)/shard_map/ppermute | solution.py:231
  19.5 0.7 copy-start.19
  20.3 10.3 %collective-permute-start.24 = (bf16[128,1152]{1,0:T(8,128)(2,1)S(1)}, bf16[128,1152]{1,0:T(8,128)(2,1)S(1)}, u32[]{:S(2)}, u32[]{:S(2)}) collective-permute-start(bf16[128,1152]{1,0:T(8,128)(2,1)S(1)} %shard_map.90.refs_2_), channel_id=1, source_target_pairs={{0,4},{1,5},{2,0},{3,1},{4,6},{5,7},{6,2},{7,3},{8,12},{9,13},{10,... | collective-permute-start | bytes 884744 | tf_op jit(solution)/shard_map/ppermute | solution.py:231
  23.7 0.7 copy-start.17
  24.4 10.2 %collective-permute-start.18 = (bf16[128,1152]{1,0:T(8,128)(2,1)S(1)}, bf16[128,1152]{1,0:T(8,128)(2,1)S(1)}, u32[]{:S(2)}, u32[]{:S(2)}) collective-permute-start(bf16[128,1152]{1,0:T(8,128)(2,1)S(1)} %shard_map.90.refs_2_), channel_id=1, source_target_pairs={{0,16},{1,17},{2,18},{3,19},{4,20},{5,21},{6,22},{7,23},{8,24},{9,... | collective-permute-start | bytes 884744 | tf_op jit(solution)/shard_map/ppermute | solution.py:231
  26.6 8.9 %collective-permute-start.17 = (bf16[128,1152]{1,0:T(8,128)(2,1)S(1)}, bf16[128,1152]{1,0:T(8,128)(2,1)S(1)}, u32[]{:S(2)}, u32[]{:S(2)}) collective-permute-start(bf16[128,1152]{1,0:T(8,128)(2,1)S(1)} %shard_map.90.refs_2_), channel_id=1, source_target_pairs={{0,8},{1,9},{2,10},{3,11},{4,12},{5,13},{6,14},{7,15},{8,0},{9,1},... | collective-permute-start | bytes 884744 | tf_op jit(solution)/shard_map/ppermute | solution.py:231
  27.2 5.7 %copy-start.3 = (bf16[128,1152]{1,0:T(8,128)(2,1)}, bf16[128,1152]{1,0:T(8,128)(2,1)S(1)}, u32[]{:S(2)}) copy-start(bf16[128,1152]{1,0:T(8,128)(2,1)S(1)} %collective-permute-done.11.refs_4_) | copy-start | bytes 884740
  27.2 10.8 %collective-permute-start.1 = (bf16[128,1152]{1,0:T(8,128)(2,1)S(1)}, bf16[128,1152]{1,0:T(8,128)(2,1)}, u32[]{:S(2)}, u32[]{:S(2)}) collective-permute-start(bf16[128,1152]{1,0:T(8,128)(2,1)S(1)} %shard_map.86.refs_2_), channel_id=1, source_target_pairs={{0,4},{1,5},{2,0},{3,1},{4,6},{5,7},{6,2},{7,3},{8,12},{9,13},{10,... | collective-permute-start | bytes 884744 | tf_op jit(solution)/shard_map/ppermute | solution.py:231
  30.6 2.3 %copy-start.5 = (bf16[128,1152]{1,0:T(8,128)(2,1)}, bf16[128,1152]{1,0:T(8,128)(2,1)S(1)}, u32[]{:S(2)}) copy-start(bf16[128,1152]{1,0:T(8,128)(2,1)S(1)} %collective-permute-done.10.refs_3_) | copy-start | bytes 884740
  30.6 1.6 %collective-permute-start.22 = (bf16[128,1152]{1,0:T(8,128)(2,1)S(1)}, bf16[128,1152]{1,0:T(8,128)(2,1)S(1)}, u32[]{:S(2)}, u32[]{:S(2)}) collective-permute-start(bf16[128,1152]{1,0:T(8,128)(2,1)S(1)} %collective-permute-done.6.refs_1_.refs_4_.refs_0_), channel_id=1, source_target_pairs={{0,8},{1,9},{2,10},{3,11},{4,12},{5,13},{6,14},{7,15},{8,0},{9,1},... | collective-permute-start | bytes 884744 | tf_op jit(solution)/shard_map/ppermute | solution.py:231
  30.6 15.5 %collective-permute-start.12 = (bf16[128,1152]{1,0:T(8,128)(2,1)S(1)}, bf16[128,1152]{1,0:T(8,128)(2,1)S(1)}, u32[]{:S(2)}, u32[]{:S(2)}) collective-permute-start(bf16[128,1152]{1,0:T(8,128)(2,1)S(1)} %collective-permute-done.11.refs_4_), channel_id=1, source_target_pairs={{0,8},{1,9},{2,10},{3,11},{4,12},{5,13},{6,14},{7,15},{8,0},{9,1},... | collective-permute-start | bytes 884744 | tf_op jit(solution)/shard_map/ppermute | solution.py:231
  32.9 8.3 %collective-permute-start.27 = (bf16[64,1152]{1,0:T(8,128)(2,1)S(1)}, bf16[64,1152]{1,0:T(8,128)(2,1)}, u32[]{:S(2)}, u32[]{:S(2)}) collective-permute-start(bf16[64,1152]{1,0:T(8,128)(2,1)S(1)} %get-tuple-element.39), channel_id=1, source_target_pairs={{0,4},{1,5},{2,0},{3,1},{4,6},{5,7},{6,2},{7,3},{8,12},{9,13},{10,... | collective-permute-start | bytes 442376 | tf_op jit(solution)/shard_map/ppermute | solution.py:231
  34.5 12.3 %collective-permute-start.19 = (bf16[128,1152]{1,0:T(8,128)(2,1)S(1)}, bf16[128,1152]{1,0:T(8,128)(2,1)S(1)}, u32[]{:S(2)}, u32[]{:S(2)}) collective-permute-start(bf16[128,1152]{1,0:T(8,128)(2,1)S(1)} %collective-permute-done.18.refs_4_), channel_id=1, source_target_pairs={{0,8},{1,9},{2,10},{3,11},{4,12},{5,13},{6,14},{7,15},{8,0},{9,1},... | collective-permute-start | bytes 884744 | tf_op jit(solution)/shard_map/ppermute | solution.py:231
  34.8 0.7 copy-start.7
  35.5 0.7 copy-start.9
  36.2 8.4 %collective-permute-start.25 = (bf16[64,1152]{1,0:T(8,128)(2,1)S(1)}, bf16[64,1152]{1,0:T(8,128)(2,1)S(1)}, u32[]{:S(2)}, u32[]{:S(2)}) collective-permute-start(bf16[64,1152]{1,0:T(8,128)(2,1)S(1)} %get-tuple-element.40), channel_id=1, source_target_pairs={{0,4},{1,5},{2,0},{3,1},{4,6},{5,7},{6,2},{7,3},{8,12},{9,13},{10,... | collective-permute-start | bytes 442376 | tf_op jit(solution)/shard_map/ppermute | solution.py:231
  38.0 10.1 %collective-permute-start.8 = (bf16[128,1152]{1,0:T(8,128)(2,1)}, bf16[128,1152]{1,0:T(8,128)(2,1)}, u32[]{:S(2)}, u32[]{:S(2)}) collective-permute-start(bf16[128,1152]{1,0:T(8,128)(2,1)} %collective-permute-done.1.refs_2_), channel_id=1, source_target_pairs={{0,1},{1,0},{2,3},{3,2},{4,5},{5,4},{6,7},{7,6},{8,9},{9,8},{10,11... | collective-permute-start | bytes 884744 | tf_op jit(solution)/shard_map/ppermute | solution.py:231
  41.1 8.3 %collective-permute-start.2 = (bf16[128,1152]{1,0:T(8,128)(2,1)}, bf16[128,1152]{1,0:T(8,128)(2,1)S(1)}, u32[]{:S(2)}, u32[]{:S(2)}) collective-permute-start(bf16[128,1152]{1,0:T(8,128)(2,1)} %collective-permute-done.1.refs_2_), channel_id=1, source_target_pairs={{0,4},{1,5},{2,0},{3,1},{4,6},{5,7},{6,2},{7,3},{8,12},{9,13},{10,... | collective-permute-start | bytes 884744 | tf_op jit(solution)/shard_map/ppermute | solution.py:231
  44.6 7.9 %collective-permute-start.33 = (bf16[128,1152]{1,0:T(8,128)(2,1)S(1)}, bf16[128,1152]{1,0:T(8,128)(2,1)S(1)}, u32[]{:S(2)}, u32[]{:S(2)}) collective-permute-start(bf16[128,1152]{1,0:T(8,128)(2,1)S(1)} %collective-permute-done.24.refs_2_), channel_id=1, source_target_pairs={{0,16},{1,17},{2,18},{3,19},{4,20},{5,21},{6,22},{7,23},{8,24},{9,... | collective-permute-start | bytes 884744 | tf_op jit(solution)/shard_map/ppermute | solution.py:231
  46.1 0.7 copy-start.11
  46.9 5.7 %collective-permute-start.32 = (bf16[128,1152]{1,0:T(8,128)(2,1)S(1)}, bf16[128,1152]{1,0:T(8,128)(2,1)S(1)}, u32[]{:S(2)}, u32[]{:S(2)}) collective-permute-start(bf16[128,1152]{1,0:T(8,128)(2,1)S(1)} %collective-permute-done.24.refs_2_), channel_id=1, source_target_pairs={{0,8},{1,9},{2,10},{3,11},{4,12},{5,13},{6,14},{7,15},{8,0},{9,1},... | collective-permute-start | bytes 884744 | tf_op jit(solution)/shard_map/ppermute | solution.py:231
  46.9 0.7 copy-start.13
  47.6 3.4 %collective-permute-start.35 = (bf16[64,1152]{1,0:T(8,128)(2,1)}, bf16[64,1152]{1,0:T(8,128)(2,1)}, u32[]{:S(2)}, u32[]{:S(2)}) collective-permute-start(bf16[64,1152]{1,0:T(8,128)(2,1)} %collective-permute-done.27.refs_6_), channel_id=1, source_target_pairs={{0,8},{1,9},{2,10},{3,11},{4,12},{5,13},{6,14},{7,15},{8,0},{9,1},... | collective-permute-start | bytes 442376 | tf_op jit(solution)/shard_map/ppermute | solution.py:231
  48.1 7.1 %collective-permute-start.30 = (bf16[64,1152]{1,0:T(8,128)(2,1)S(1)}, bf16[64,1152]{1,0:T(8,128)(2,1)S(1)}, u32[]{:S(2)}, u32[]{:S(2)}) collective-permute-start(bf16[64,1152]{1,0:T(8,128)(2,1)S(1)} %collective-permute-done.25.refs_1_), channel_id=1, source_target_pairs={{0,16},{1,17},{2,18},{3,19},{4,20},{5,21},{6,22},{7,23},{8,24},{9,... | collective-permute-start | bytes 442376 | tf_op jit(solution)/shard_map/ppermute | solution.py:231
  49.4 12.9 %collective-permute-start.4 = (bf16[128,1152]{1,0:T(8,128)(2,1)S(1)}, bf16[128,1152]{1,0:T(8,128)(2,1)S(1)}, u32[]{:S(2)}, u32[]{:S(2)}) collective-permute-start(bf16[128,1152]{1,0:T(8,128)(2,1)S(1)} %collective-permute-done.2.refs_1_), channel_id=1, source_target_pairs={{0,1},{1,0},{2,3},{3,2},{4,5},{5,4},{6,7},{7,6},{8,9},{9,8},{10,11... | collective-permute-start | bytes 884744 | tf_op jit(solution)/shard_map/ppermute | solution.py:231
  50.9 6.7 %collective-permute-start.28 = (bf16[64,1152]{1,0:T(8,128)(2,1)}, bf16[64,1152]{1,0:T(8,128)(2,1)S(1)}, u32[]{:S(2)}, u32[]{:S(2)}) collective-permute-start(bf16[64,1152]{1,0:T(8,128)(2,1)} %collective-permute-done.27.refs_6_), channel_id=1, source_target_pairs={{0,16},{1,17},{2,18},{3,19},{4,20},{5,21},{6,22},{7,23},{8,24},{9,... | collective-permute-start | bytes 442376 | tf_op jit(solution)/shard_map/ppermute | solution.py:231
  52.5 5.2 %collective-permute-start.26 = (bf16[64,1152]{1,0:T(8,128)(2,1)S(1)}, bf16[64,1152]{1,0:T(8,128)(2,1)S(1)}, u32[]{:S(2)}, u32[]{:S(2)}) collective-permute-start(bf16[64,1152]{1,0:T(8,128)(2,1)S(1)} %collective-permute-done.25.refs_1_), channel_id=1, source_target_pairs={{0,8},{1,9},{2,10},{3,11},{4,12},{5,13},{6,14},{7,15},{8,0},{9,1},... | collective-permute-start | bytes 442376 | tf_op jit(solution)/shard_map/ppermute | solution.py:231
  52.5 11.4 %collective-permute-start.34 = (bf16[128,1152]{1,0:T(8,128)(2,1)S(1)}, bf16[128,1152]{1,0:T(8,128)(2,1)S(1)}, u32[]{:S(2)}, u32[]{:S(2)}) collective-permute-start(bf16[128,1152]{1,0:T(8,128)(2,1)S(1)} %collective-permute-done.33.refs_4_), channel_id=1, source_target_pairs={{0,8},{1,9},{2,10},{3,11},{4,12},{5,13},{6,14},{7,15},{8,0},{9,1},... | collective-permute-start | bytes 884744 | tf_op jit(solution)/shard_map/ppermute | solution.py:231
  55.2 7.0 %collective-permute-start.31 = (bf16[64,1152]{1,0:T(8,128)(2,1)S(1)}, bf16[64,1152]{1,0:T(8,128)(2,1)S(1)}, u32[]{:S(2)}, u32[]{:S(2)}) collective-permute-start(bf16[64,1152]{1,0:T(8,128)(2,1)S(1)} %collective-permute-done.30.refs_5_), channel_id=1, source_target_pairs={{0,8},{1,9},{2,10},{3,11},{4,12},{5,13},{6,14},{7,15},{8,0},{9,1},... | collective-permute-start | bytes 442376 | tf_op jit(solution)/shard_map/ppermute | solution.py:231
  57.7 14.4 %collective-permute-start.7 = (bf16[128,1152]{1,0:T(8,128)(2,1)}, bf16[128,1152]{1,0:T(8,128)(2,1)S(1)}, u32[]{:S(2)}, u32[]{:S(2)}) collective-permute-start(bf16[128,1152]{1,0:T(8,128)(2,1)} %collective-permute-done.1.refs_2_), channel_id=1, source_target_pairs={{0,8},{1,9},{2,10},{3,11},{4,12},{5,13},{6,14},{7,15},{8,0},{9,1},... | collective-permute-start | bytes 884744 | tf_op jit(solution)/shard_map/ppermute | solution.py:231
  57.7 14.4 %collective-permute-start.9 = (bf16[128,1152]{1,0:T(8,128)(2,1)}, bf16[128,1152]{1,0:T(8,128)(2,1)S(1)}, u32[]{:S(2)}, u32[]{:S(2)}) collective-permute-start(bf16[128,1152]{1,0:T(8,128)(2,1)} %collective-permute-done.8.refs_4_), channel_id=1, source_target_pairs={{0,8},{1,9},{2,10},{3,11},{4,12},{5,13},{6,14},{7,15},{8,0},{9,1},... | collective-permute-start | bytes 884744 | tf_op jit(solution)/shard_map/ppermute | solution.py:231
  58.9 1.0 copy-start.20
  59.9 1.0 copy-start.22
  60.9 1.9 %copy-start.18 = (bf16[128,1152]{1,0:T(8,128)(2,1)S(1)}, bf16[128,1152]{1,0:T(8,128)(2,1)}, u32[]{:S(2)}) copy-start(bf16[128,1152]{1,0:T(8,128)(2,1)} %copy-done.17) | copy-start | bytes 884740
  60.9 1.9 %copy-start.24 = (bf16[128,1152]{1,0:T(8,128)(2,1)S(1)}, bf16[128,1152]{1,0:T(8,128)(2,1)}, u32[]{:S(2)}) copy-start(bf16[128,1152]{1,0:T(8,128)(2,1)} %copy-done.23) | copy-start | bytes 884740
  62.2 1.9 %copy-start.4 = (bf16[128,1152]{1,0:T(8,128)(2,1)S(1)}, bf16[128,1152]{1,0:T(8,128)(2,1)}, u32[]{:S(2)}) copy-start(bf16[128,1152]{1,0:T(8,128)(2,1)} %copy-done.3) | copy-start | bytes 884740
  62.2 1.9 %copy-start.6 = (bf16[128,1152]{1,0:T(8,128)(2,1)S(1)}, bf16[128,1152]{1,0:T(8,128)(2,1)}, u32[]{:S(2)}) copy-start(bf16[128,1152]{1,0:T(8,128)(2,1)} %copy-done.5) | copy-start | bytes 884740
  62.2 1.9 %copy-start.12 = (bf16[128,1152]{1,0:T(8,128)(2,1)S(1)}, bf16[128,1152]{1,0:T(8,128)(2,1)}, u32[]{:S(2)}) copy-start(bf16[128,1152]{1,0:T(8,128)(2,1)} %copy-done.11) | copy-start | bytes 884740
  62.2 12.2 %collective-permute-start.3 = (bf16[128,1152]{1,0:T(8,128)(2,1)S(1)}, bf16[128,1152]{1,0:T(8,128)(2,1)S(1)}, u32[]{:S(2)}, u32[]{:S(2)}) collective-permute-start(bf16[128,1152]{1,0:T(8,128)(2,1)S(1)} %collective-permute-done.2.refs_1_), channel_id=1, source_target_pairs={{0,8},{1,9},{2,10},{3,11},{4,12},{5,13},{6,14},{7,15},{8,0},{9,1},... | collective-permute-start | bytes 884744 | tf_op jit(solution)/shard_map/ppermute | solution.py:231
  62.3 12.2 %collective-permute-start.5 = (bf16[128,1152]{1,0:T(8,128)(2,1)S(1)}, bf16[128,1152]{1,0:T(8,128)(2,1)S(1)}, u32[]{:S(2)}, u32[]{:S(2)}) collective-permute-start(bf16[128,1152]{1,0:T(8,128)(2,1)S(1)} %collective-permute-done.4.refs_3_), channel_id=1, source_target_pairs={{0,8},{1,9},{2,10},{3,11},{4,12},{5,13},{6,14},{7,15},{8,0},{9,1},... | collective-permute-start | bytes 884744 | tf_op jit(solution)/shard_map/ppermute | solution.py:231
  63.9 5.5 %collective-permute-start.29 = (bf16[64,1152]{1,0:T(8,128)(2,1)S(1)}, bf16[64,1152]{1,0:T(8,128)(2,1)S(1)}, u32[]{:S(2)}, u32[]{:S(2)}) collective-permute-start(bf16[64,1152]{1,0:T(8,128)(2,1)S(1)} %collective-permute-done.28.refs_3_), channel_id=1, source_target_pairs={{0,8},{1,9},{2,10},{3,11},{4,12},{5,13},{6,14},{7,15},{8,0},{9,1},... | collective-permute-start | bytes 442376 | tf_op jit(solution)/shard_map/ppermute | solution.py:231
  64.1 1.3 %copy-start.8 = (bf16[128,1152]{1,0:T(8,128)(2,1)S(1)}, bf16[128,1152]{1,0:T(8,128)(2,1)}, u32[]{:S(2)}) copy-start(bf16[128,1152]{1,0:T(8,128)(2,1)} %copy-done.7) | copy-start | bytes 884740
  64.1 1.4 %copy-start.10 = (bf16[128,1152]{1,0:T(8,128)(2,1)S(1)}, bf16[128,1152]{1,0:T(8,128)(2,1)}, u32[]{:S(2)}) copy-start(bf16[128,1152]{1,0:T(8,128)(2,1)} %copy-done.9) | copy-start | bytes 884740
  64.1 1.4 %copy-start.14 = (bf16[128,1152]{1,0:T(8,128)(2,1)S(1)}, bf16[128,1152]{1,0:T(8,128)(2,1)}, u32[]{:S(2)}) copy-start(bf16[128,1152]{1,0:T(8,128)(2,1)} %copy-done.13) | copy-start | bytes 884740
  70.5 33.3 %collective-permute-start.36 = (f32[128,1152]{1,0:T(8,128)S(1)}, f32[128,1152]{1,0:T(8,128)S(1)}, u32[]{:S(2)}, u32[]{:S(2)}) collective-permute-start(f32[128,1152]{1,0:T(8,128)S(1)} %shard_map.99), channel_id=1, source_target_pairs={{0,1},{1,0},{2,3},{3,2},{4,5},{5,4},{6,7},{7,6},{8,9},{9,8},{10,11... | collective-permute-start | bytes 1769480 | tf_op jit(solution)/shard_map/ppermute | solution.py:231
  75.3 30.0 %collective-permute-start.23 = (f32[128,1152]{1,0:T(8,128)S(1)}, f32[128,1152]{1,0:T(8,128)S(1)}, u32[]{:S(2)}, u32[]{:S(2)}) collective-permute-start(f32[128,1152]{1,0:T(8,128)S(1)} %shard_map.95), channel_id=1, source_target_pairs={{0,16},{1,17},{2,18},{3,19},{4,20},{5,21},{6,22},{7,23},{8,24},{9,... | collective-permute-start | bytes 1769480 | tf_op jit(solution)/shard_map/ppermute | solution.py:231
  77.2 13.7 %collective-permute-start.37 = (f32[8,128]{1,0:T(8,128)S(1)}, f32[8,128]{1,0:T(8,128)S(1)}, u32[]{:S(2)}, u32[]{:S(2)}) collective-permute-start(f32[8,128]{1,0:T(8,128)S(1)} %get-tuple-element.36), channel_id=1, source_target_pairs={{0,16},{1,17},{2,18},{3,19},{4,20},{5,21},{6,22},{7,23},{8,24},{9,... | collective-permute-start | bytes 12296 | tf_op jit(solution)/shard_map/ppermute | solution.py:231
  90.9 1.2 %collective-permute-start.38 = (f32[8,128]{1,0:T(8,128)S(1)}, f32[8,128]{1,0:T(8,128)S(1)}, u32[]{:S(2)}, u32[]{:S(2)}) collective-permute-start(f32[8,128]{1,0:T(8,128)S(1)} %add.91), channel_id=1, source_target_pairs={{0,8},{1,9},{2,10},{3,11},{4,12},{5,13},{6,14},{7,15},{8,0},{9,1},... | collective-permute-start | bytes 12296 | tf_op jit(solution)/shard_map/ppermute | solution.py:231
  92.1 3.6 %collective-permute-start.39 = (f32[8,128]{1,0:T(8,128)S(1)}, f32[8,128]{1,0:T(8,128)S(1)}, u32[]{:S(2)}, u32[]{:S(2)}) collective-permute-start(f32[8,128]{1,0:T(8,128)S(1)} %add.92), channel_id=1, source_target_pairs={{0,2},{1,3},{2,0},{3,1},{4,6},{5,7},{6,4},{7,5},{8,10},{9,11},{10,... | collective-permute-start | bytes 12296 | tf_op jit(solution)/shard_map/ppermute | solution.py:231
  95.7 4.5 %collective-permute-start.40 = (f32[8,128]{1,0:T(8,128)S(1)}, f32[8,128]{1,0:T(8,128)S(1)}, u32[]{:S(2)}, u32[]{:S(2)}) collective-permute-start(f32[8,128]{1,0:T(8,128)S(1)} %add.93), channel_id=1, source_target_pairs={{0,4},{1,5},{2,6},{3,7},{4,0},{5,1},{6,2},{7,3},{8,12},{9,13},{10,... | collective-permute-start | bytes 12296 | tf_op jit(solution)/shard_map/ppermute | solution.py:231
  100.2 3.6 %collective-permute-start.41 = (f32[8,128]{1,0:T(8,128)S(1)}, f32[8,128]{1,0:T(8,128)S(1)}, u32[]{:S(2)}, u32[]{:S(2)}) collective-permute-start(f32[8,128]{1,0:T(8,128)S(1)} %add.94.refs_2_), channel_id=1, source_target_pairs={{0,1},{1,0},{2,3},{3,2},{4,5},{5,4},{6,7},{7,6},{8,9},{9,8},{10,11... | collective-permute-start | bytes 12296 | tf_op jit(solution)/shard_map/ppermute | solution.py:231
  100.7 3.1 %copy-start.1 = (bf16[128,1152]{1,0:T(8,128)(2,1)S(1)}, bf16[128,1152]{1,0:T(8,128)(2,1)}, u32[]{:S(2)}) copy-start(bf16[128,1152]{1,0:T(8,128)(2,1)} %values.7) | copy-start | bytes 884740
  (3 other events, 2.1 us)

commit v6 on v4

--- a/solution.py
+++ b/solution.py
@@ -322,12 +322,13 @@
         img_sums, loss = image_terms(img_sums, loss, parts, range(wide), True)
         parts = [(img_sets[step][at], step, at, 0) for at in range(wide)]
         if step == end - 1:
-            parts += [(half[0], end, 0, offset) for half, offset in halves]
+            parts.append((first_set[0], end, 0, 0))
         txt_sums, loss = text_terms(txt_sums, loss, parts, range(fast), step == 1)
     parts = [(end, at) for at in range(fast)]
     img_far, _ = image_terms(img_sums[1:], None, parts, range(1, wide), False)
     img_near, _ = image_terms(img_sums[:1], None, parts, range(1), False)
-    parts = [(half[at], end, at, offset) for at in range(1, wide) for half, offset in halves]
+    parts = [(second_set[0], end, 0, middle)]
+    parts += [(half[at], end, at, offset) for at in range(1, wide) for half, offset in halves]
     txt_far, _ = text_terms(txt_sums[1:], None, parts, range(1, fast), False)
     txt_near, _ = text_terms(txt_sums[:1], None, parts, range(1), False)
     img_sums, txt_sums = [*img_near, *img_far], [*txt_near, *txt_far]

time: 105 us -> 106 us (level)
  Pallas kernels: 15.6 us -> 16.7 us
    pallas_call x10, Pallas kernels: 12.8 us -> 13.9 us  [terms(): pl.pallas_call(kernel, out_shape=shapes, in_specs=[VMEM] * len(operands),...]
  transfers between devices with their start and end apart: 42 -> 42, of which waited for: 15 -> 15; matrix products, arithmetic and copies ran while one was open for 0% -> 0% of each run, Pallas kernels for 14% -> 15%
where the time goes in v6:
time: 106 us
  starting transfers between devices  44.1 us (42%)
  waiting for transfers between devices  33.4 us (32%)
  Pallas kernels  16.7 us (16%)
  local copies, waits for them, and re-layouts  9.5 us (9%)
  between operations  2.26 us (2%)
    ppermute x42, starting transfers between devices, permuted(): return lax.ppermute(array, AXES, pairs)  44.1 us
    ppermute x42, waiting for transfers between devices, permuted(): return lax.ppermute(array, AXES, pairs)  33.4 us
    pallas_call x10, Pallas kernels, terms(): pl.pallas_call(kernel, out_shape=shapes, in_specs=[VMEM] * len(operands),...  13.9 us
    unnamed x50, local copies, waits for them, and re-layouts  9.4 us
    pallas_call x2, Pallas kernels, project(): pl.pallas_call(functools.partial(project_kernel, len(parts), len(losses),...  2.18 us
  transfers between devices with their start and end apart: 42, of which 15 were waited for; matrix products, arithmetic and copies ran while one was open for 0% of the time, Pallas kernels for 15%

profile of v6, /device:TPU:0, one launch (start us, length us, event | category | flops | bytes accessed | tf_op | source)
XLA Modules:
  0.0 106.0 jit_solution(2046027016879177842)
XLA Ops:
  0.6 4.1 %collective-permute-start = (bf16[128,1152]{1,0:T(8,128)(2,1)}, bf16[128,1152]{1,0:T(8,128)(2,1)S(1)}, u32[]{:S(2)}, u32[]{:S(2)}) collective-permute-start(bf16[128,1152]{1,0:T(8,128)(2,1)} %values.7), channel_id=1, source_target_pairs={{0,4},{1,5},{2,0},{3,1},{4,6},{5,7},{6,2},{7,3},{8,12},{9,13},{10,... | collective-permute-start | bytes 884744 | tf_op jit(solution)/shard_map/ppermute | solution.py:215
  4.7 1.0 copy-done
  5.9 1.6 %collective-permute-start.14 = (bf16[128,1152]{1,0:T(8,128)(2,1)S(1)}, bf16[128,1152]{1,0:T(8,128)(2,1)S(1)}, u32[]{:S(2)}, u32[]{:S(2)}) collective-permute-start(bf16[128,1152]{1,0:T(8,128)(2,1)S(1)} %shard_map.87.refs_2_.refs_0_), channel_id=1, source_target_pairs={{0,1},{1,0},{2,3},{3,2},{4,5},{5,4},{6,7},{7,6},{8,9},{9,8},{10,11... | collective-permute-start | bytes 884744 | tf_op jit(solution)/shard_map/ppermute | solution.py:215
  7.5 1.6 %collective-permute-start.16 = (bf16[128,1152]{1,0:T(8,128)(2,1)S(1)}, bf16[128,1152]{1,0:T(8,128)(2,1)S(1)}, u32[]{:S(2)}, u32[]{:S(2)}) collective-permute-start(bf16[128,1152]{1,0:T(8,128)(2,1)S(1)} %copy-done.2), channel_id=1, source_target_pairs={{0,4},{1,5},{2,0},{3,1},{4,6},{5,7},{6,2},{7,3},{8,12},{9,13},{10,... | collective-permute-start | bytes 884744 | tf_op jit(solution)/shard_map/ppermute | solution.py:215
  9.2 1.6 %collective-permute-start.6 = (bf16[128,1152]{1,0:T(8,128)(2,1)S(1)}, bf16[128,1152]{1,0:T(8,128)(2,1)S(1)}, u32[]{:S(2)}, u32[]{:S(2)}) collective-permute-start(bf16[128,1152]{1,0:T(8,128)(2,1)S(1)} %shard_map.85.refs_0_.refs_2_), channel_id=1, source_target_pairs={{0,16},{1,17},{2,18},{3,19},{4,20},{5,21},{6,22},{7,23},{8,24},{9,... | collective-permute-start | bytes 884744 | tf_op jit(solution)/shard_map/ppermute | solution.py:215
  10.8 1.7 %collective-permute-done.values = bf16[128,1152]{1,0:T(8,128)(2,1)S(1)} collective-permute-done((bf16[128,1152]{1,0:T(8,128)(2,1)}, bf16[128,1152]{1,0:T(8,128)(2,1)S(1)}, u32[]{:S(2)}, u32[]{:S(2)}) %collective-permute-start) | collective-permute-done | bytes 294944 | tf_op jit(solution)/shard_map/ppermute | solution.py:215
  12.5 1.5 %collective-permute-start.20 = (s32[1,128]{1,0:T(1,128)S(1)}, s32[1,128]{1,0:T(1,128)S(1)}, u32[]{:S(2)}, u32[]{:S(2)}) collective-permute-start(s32[1,128]{1,0:T(1,128)S(1)} %bitcast.14), channel_id=1, source_target_pairs={{0,1},{1,0},{2,3},{3,2},{4,5},{5,4},{6,7},{7,6},{8,9},{9,8},{10,11... | collective-permute-start | bytes 1544 | tf_op jit(solution)/shard_map/ppermute | solution.py:215
  14.4 3.1 %collective-permute-done.16.values = bf16[128,1152]{1,0:T(8,128)(2,1)S(1)} collective-permute-done((bf16[128,1152]{1,0:T(8,128)(2,1)S(1)}, bf16[128,1152]{1,0:T(8,128)(2,1)S(1)}, u32[]{:S(2)}, u32[]{:S(2)}) %collective-permute-start.16) | collective-permute-done | bytes 294944 | tf_op jit(solution)/shard_map/ppermute | solution.py:215
  17.7 1.6 %collective-permute-start.11 = (bf16[128,1152]{1,0:T(8,128)(2,1)S(1)}, bf16[128,1152]{1,0:T(8,128)(2,1)S(1)}, u32[]{:S(2)}, u32[]{:S(2)}) collective-permute-start(bf16[128,1152]{1,0:T(8,128)(2,1)S(1)} %shard_map.86.refs_2_), channel_id=1, source_target_pairs={{0,1},{1,0},{2,3},{3,2},{4,5},{5,4},{6,7},{7,6},{8,9},{9,8},{10,11... | collective-permute-start | bytes 884744 | tf_op jit(solution)/shard_map/ppermute | solution.py:215
  19.5 0.7 copy-done.19
  20.3 3.4 %collective-permute-start.24 = (bf16[128,1152]{1,0:T(8,128)(2,1)S(1)}, bf16[128,1152]{1,0:T(8,128)(2,1)S(1)}, u32[]{:S(2)}, u32[]{:S(2)}) collective-permute-start(bf16[128,1152]{1,0:T(8,128)(2,1)S(1)} %shard_map.90.refs_2_), channel_id=1, source_target_pairs={{0,4},{1,5},{2,0},{3,1},{4,6},{5,7},{6,2},{7,3},{8,12},{9,13},{10,... | collective-permute-start | bytes 884744 | tf_op jit(solution)/shard_map/ppermute | solution.py:215
  23.7 0.7 copy-done.17
  24.4 1.5 %collective-permute-start.18 = (bf16[128,1152]{1,0:T(8,128)(2,1)S(1)}, bf16[128,1152]{1,0:T(8,128)(2,1)S(1)}, u32[]{:S(2)}, u32[]{:S(2)}) collective-permute-start(bf16[128,1152]{1,0:T(8,128)(2,1)S(1)} %shard_map.90.refs_2_), channel_id=1, source_target_pairs={{0,16},{1,17},{2,18},{3,19},{4,20},{5,21},{6,22},{7,23},{8,24},{9,... | collective-permute-start | bytes 884744 | tf_op jit(solution)/shard_map/ppermute | solution.py:215
  25.9 0.7 copy-done.21
  26.6 0.6 collective-permute-done.11.refs_4_
  27.2 3.4 %collective-permute-start.1 = (bf16[128,1152]{1,0:T(8,128)(2,1)S(1)}, bf16[128,1152]{1,0:T(8,128)(2,1)}, u32[]{:S(2)}, u32[]{:S(2)}) collective-permute-start(bf16[128,1152]{1,0:T(8,128)(2,1)S(1)} %shard_map.86.refs_2_), channel_id=1, source_target_pairs={{0,4},{1,5},{2,0},{3,1},{4,6},{5,7},{6,2},{7,3},{8,12},{9,13},{10,... | collective-permute-start | bytes 884744 | tf_op jit(solution)/shard_map/ppermute | solution.py:215
  30.6 0.5 collective-permute-start.12
  31.1 1.0 collective-permute-done.22.refs_5_
  32.2 0.7 copy-done.23
  32.9 1.6 %collective-permute-start.27 = (bf16[64,1152]{1,0:T(8,128)(2,1)S(1)}, bf16[64,1152]{1,0:T(8,128)(2,1)}, u32[]{:S(2)}, u32[]{:S(2)}) collective-permute-start(bf16[64,1152]{1,0:T(8,128)(2,1)S(1)} %get-tuple-element.39), channel_id=1, source_target_pairs={{0,4},{1,5},{2,0},{3,1},{4,6},{5,7},{6,2},{7,3},{8,12},{9,13},{10,... | collective-permute-start | bytes 442376 | tf_op jit(solution)/shard_map/ppermute | solution.py:215
  34.8 0.7 copy-done.7
  35.5 0.7 copy-done.9
  36.6 1.4 %collective-permute-done.1.refs_2_ = bf16[128,1152]{1,0:T(8,128)(2,1)} collective-permute-done((bf16[128,1152]{1,0:T(8,128)(2,1)S(1)}, bf16[128,1152]{1,0:T(8,128)(2,1)}, u32[]{:S(2)}, u32[]{:S(2)}) %collective-permute-start.1) | collective-permute-done | bytes 294944 | tf_op jit(solution)/shard_map/ppermute | solution.py:215
  38.0 1.5 %collective-permute-start.8 = (bf16[128,1152]{1,0:T(8,128)(2,1)}, bf16[128,1152]{1,0:T(8,128)(2,1)}, u32[]{:S(2)}, u32[]{:S(2)}) collective-permute-start(bf16[128,1152]{1,0:T(8,128)(2,1)} %collective-permute-done.1.refs_2_), channel_id=1, source_target_pairs={{0,1},{1,0},{2,3},{3,2},{4,5},{5,4},{6,7},{7,6},{8,9},{9,8},{10,11... | collective-permute-start | bytes 884744 | tf_op jit(solution)/shard_map/ppermute | solution.py:215
  39.5 1.6 %collective-permute-done.27.refs_6_ = bf16[64,1152]{1,0:T(8,128)(2,1)} collective-permute-done((bf16[64,1152]{1,0:T(8,128)(2,1)S(1)}, bf16[64,1152]{1,0:T(8,128)(2,1)}, u32[]{:S(2)}, u32[]{:S(2)}) %collective-permute-start.27) | collective-permute-done | bytes 147488 | tf_op jit(solution)/shard_map/ppermute | solution.py:215
  41.1 3.5 %collective-permute-start.2 = (bf16[128,1152]{1,0:T(8,128)(2,1)}, bf16[128,1152]{1,0:T(8,128)(2,1)S(1)}, u32[]{:S(2)}, u32[]{:S(2)}) collective-permute-start(bf16[128,1152]{1,0:T(8,128)(2,1)} %collective-permute-done.1.refs_2_), channel_id=1, source_target_pairs={{0,4},{1,5},{2,0},{3,1},{4,6},{5,7},{6,2},{7,3},{8,12},{9,13},{10,... | collective-permute-start | bytes 884744 | tf_op jit(solution)/shard_map/ppermute | solution.py:215
  44.6 1.5 %collective-permute-start.33 = (bf16[128,1152]{1,0:T(8,128)(2,1)S(1)}, bf16[128,1152]{1,0:T(8,128)(2,1)S(1)}, u32[]{:S(2)}, u32[]{:S(2)}) collective-permute-start(bf16[128,1152]{1,0:T(8,128)(2,1)S(1)} %collective-permute-done.24.refs_2_), channel_id=1, source_target_pairs={{0,16},{1,17},{2,18},{3,19},{4,20},{5,21},{6,22},{7,23},{8,24},{9,... | collective-permute-start | bytes 884744 | tf_op jit(solution)/shard_map/ppermute | solution.py:215
  46.1 0.7 copy-done.11
  46.9 0.7 copy-done.13
  47.6 0.5 collective-permute-start.35
  48.1 0.5 collective-permute-start.30
  48.6 0.8 collective-permute-done.2.refs_1_
  49.4 1.5 %collective-permute-start.4 = (bf16[128,1152]{1,0:T(8,128)(2,1)S(1)}, bf16[128,1152]{1,0:T(8,128)(2,1)S(1)}, u32[]{:S(2)}, u32[]{:S(2)}) collective-permute-start(bf16[128,1152]{1,0:T(8,128)(2,1)S(1)} %collective-permute-done.2.refs_1_), channel_id=1, source_target_pairs={{0,1},{1,0},{2,3},{3,2},{4,5},{5,4},{6,7},{7,6},{8,9},{9,8},{10,11... | collective-permute-start | bytes 884744 | tf_op jit(solution)/shard_map/ppermute | solution.py:215
  50.9 1.6 %collective-permute-start.28 = (bf16[64,1152]{1,0:T(8,128)(2,1)}, bf16[64,1152]{1,0:T(8,128)(2,1)S(1)}, u32[]{:S(2)}, u32[]{:S(2)}) collective-permute-start(bf16[64,1152]{1,0:T(8,128)(2,1)} %collective-permute-done.27.refs_6_), channel_id=1, source_target_pairs={{0,16},{1,17},{2,18},{3,19},{4,20},{5,21},{6,22},{7,23},{8,24},{9,... | collective-permute-start | bytes 442376 | tf_op jit(solution)/shard_map/ppermute | solution.py:215
  52.5 0.5 collective-permute-start.34
  53.0 2.2 %collective-permute-done.30.refs_5_ = bf16[64,1152]{1,0:T(8,128)(2,1)S(1)} collective-permute-done((bf16[64,1152]{1,0:T(8,128)(2,1)S(1)}, bf16[64,1152]{1,0:T(8,128)(2,1)S(1)}, u32[]{:S(2)}, u32[]{:S(2)}) %collective-permute-start.30) | collective-permute-done | bytes 147488 | tf_op jit(solution)/shard_map/ppermute | solution.py:215
  56.6 1.1 %collective-permute-done.28.refs_3_ = bf16[64,1152]{1,0:T(8,128)(2,1)S(1)} collective-permute-done((bf16[64,1152]{1,0:T(8,128)(2,1)}, bf16[64,1152]{1,0:T(8,128)(2,1)S(1)}, u32[]{:S(2)}, u32[]{:S(2)}) %collective-permute-start.28) | collective-permute-done | bytes 147488 | tf_op jit(solution)/shard_map/ppermute | solution.py:215
  57.7 0.5 collective-permute-start.9
  58.3 0.7 copy-done.15
  58.9 1.0 copy-done.20
  59.9 1.0 copy-done.22
  60.9 1.3 %shard_map.88 = (f32[128,1152]{1,0:T(8,128)S(1)}, f32[128,1152]{1,0:T(8,128)S(1)}, f32[8,128]{1,0:T(8,128)S(1)}) custom-call(f32[8,128]{1,0:T(8,128)S(1)} %concatenate.6.settings, s32[8,128]{1,0:T(8,128)S(1)} %iota_add_fusion.ids, bf16[128,1152]{1,0:T(8,128)(2,1)S(1)} %shard_map.85.refs_0_.refs_2_, ...), custom_call_target="tpu_custom_call" | custom-call | flops 603979776 | bytes 4128768 | tf_op jit(solution)/shard_map/pallas_call | solution.py:165
  62.3 0.5 collective-permute-start.5
  62.8 1.1 %shard_map.91 = (f32[128,1152]{1,0:T(8,128)S(1)}, f32[128,1152]{1,0:T(8,128)S(1)}) custom-call(f32[8,128]{1,0:T(8,128)S(1)} %concatenate.6.settings, s32[8,128]{1,0:T(8,128)S(1)} %iota_add_fusion.ids, bf16[128,1152]{1,0:T(8,128)(2,1)S(1)} %shard_map.87.refs_2_.refs_0_, bf16[128,1152]{1,0:T(8,128)(2,1)S(1)} %collective-permute-done.14.refs_4_.refs_1_.refs_0_, ...), custom_call_target="tpu_custom_call" | custom-call | flops 603979776 | bytes 4128768 | tf_op jit(solution)/shard_map/pallas_call | solution.py:165
  64.1 1.3 %shard_map.89 = (f32[128,1152]{1,0:T(8,128)S(1)}, f32[128,1152]{1,0:T(8,128)S(1)}, f32[8,128]{1,0:T(8,128)S(1)}) custom-call(f32[8,128]{1,0:T(8,128)S(1)} %concatenate.6.settings, s32[8,128]{1,0:T(8,128)S(1)} %iota_add_fusion.ids, bf16[128,1152]{1,0:T(8,128)(2,1)S(1)} %shard_map.85.refs_0_.refs_2_, ...), custom_call_target="tpu_custom_call", output_to_operand_aliasing={{0}: (10, {}), {1}: (11, {}), {2}: (12, {})} | custom-call | flops 603979776 | bytes 4128768 | tf_op jit(solution)/shard_map/pallas_call | solution.py:165
  65.5 1.3 %shard_map.92 = (f32[128,1152]{1,0:T(8,128)S(1)}, f32[128,1152]{1,0:T(8,128)S(1)}, f32[8,128]{1,0:T(8,128)S(1)}) custom-call(f32[8,128]{1,0:T(8,128)S(1)} %concatenate.6.settings, s32[8,128]{1,0:T(8,128)S(1)} %iota_add_fusion.ids, bf16[128,1152]{1,0:T(8,128)(2,1)S(1)} %shard_map.87.refs_2_.refs_0_, ...), custom_call_target="tpu_custom_call", output_to_operand_aliasing={{0}: (10, {}), {1}: (11, {}), {2}: (12, {})} | custom-call | flops 603979776 | bytes 4128768 | tf_op jit(solution)/shard_map/pallas_call | solution.py:165
  66.8 2.7 %shard_map.97 = (f32[128,1152]{1,0:T(8,128)S(1)}, f32[128,1152]{1,0:T(8,128)S(1)}) custom-call(f32[8,128]{1,0:T(8,128)S(1)} %concatenate.6.settings, s32[8,128]{1,0:T(8,128)S(1)} %iota_add_fusion.ids, bf16[128,1152]{1,0:T(8,128)(2,1)S(1)} %shard_map.87.refs_2_.refs_0_, ...), custom_call_target="tpu_custom_call", output_to_operand_aliasing={{0}: (12, {}), {1}: (13, {})} | custom-call | flops 754974720 | bytes 4718592 | tf_op jit(solution)/shard_map/pallas_call | solution.py:165
  69.5 1.0 shard_map.99
  70.5 1.6 %collective-permute-start.36 = (f32[128,1152]{1,0:T(8,128)S(1)}, f32[128,1152]{1,0:T(8,128)S(1)}, u32[]{:S(2)}, u32[]{:S(2)}) collective-permute-start(f32[128,1152]{1,0:T(8,128)S(1)} %shard_map.99), channel_id=1, source_target_pairs={{0,1},{1,0},{2,3},{3,2},{4,5},{5,4},{6,7},{7,6},{8,9},{9,8},{10,11... | collective-permute-start | bytes 1769480 | tf_op jit(solution)/shard_map/ppermute | solution.py:215
  72.1 2.4 %shard_map.93 = (f32[128,1152]{1,0:T(8,128)S(1)}, f32[128,1152]{1,0:T(8,128)S(1)}, f32[8,128]{1,0:T(8,128)S(1)}) custom-call(f32[8,128]{1,0:T(8,128)S(1)} %concatenate.6.settings, s32[8,128]{1,0:T(8,128)S(1)} %iota_add_fusion.ids, bf16[128,1152]{1,0:T(8,128)(2,1)S(1)} %shard_map.85.refs_0_.refs_2_, ...), custom_call_target="tpu_custom_call", output_to_operand_aliasing={{0}: (10, {}), {1}: (11, {}), {2}: (12, {})} | custom-call | flops 603979776 | bytes 4128768 | tf_op jit(solution)/shard_map/pallas_call | solution.py:165
  74.5 0.9 shard_map.95
  75.3 1.9 %collective-permute-start.23 = (f32[128,1152]{1,0:T(8,128)S(1)}, f32[128,1152]{1,0:T(8,128)S(1)}, u32[]{:S(2)}, u32[]{:S(2)}) collective-permute-start(f32[128,1152]{1,0:T(8,128)S(1)} %shard_map.95), channel_id=1, source_target_pairs={{0,16},{1,17},{2,18},{3,19},{4,20},{5,21},{6,22},{7,23},{8,24},{9,... | collective-permute-start | bytes 1769480 | tf_op jit(solution)/shard_map/ppermute | solution.py:215
  77.4 13.5 %collective-permute-done.37 = f32[8,128]{1,0:T(8,128)S(1)} collective-permute-done((f32[8,128]{1,0:T(8,128)S(1)}, f32[8,128]{1,0:T(8,128)S(1)}, u32[]{:S(2)}, u32[]{:S(2)}) %collective-permute-start.37) | collective-permute-done | bytes 4128 | tf_op jit(solution)/shard_map/ppermute | solution.py:215
  90.9 1.2 %collective-permute-done.38 = f32[8,128]{1,0:T(8,128)S(1)} collective-permute-done((f32[8,128]{1,0:T(8,128)S(1)}, f32[8,128]{1,0:T(8,128)S(1)}, u32[]{:S(2)}, u32[]{:S(2)}) %collective-permute-start.38) | collective-permute-done | bytes 4128 | tf_op jit(solution)/shard_map/ppermute | solution.py:215
  92.1 1.7 %collective-permute-start.39 = (f32[8,128]{1,0:T(8,128)S(1)}, f32[8,128]{1,0:T(8,128)S(1)}, u32[]{:S(2)}, u32[]{:S(2)}) collective-permute-start(f32[8,128]{1,0:T(8,128)S(1)} %add.92), channel_id=1, source_target_pairs={{0,2},{1,3},{2,0},{3,1},{4,6},{5,7},{6,4},{7,5},{8,10},{9,11},{10,... | collective-permute-start | bytes 12296 | tf_op jit(solution)/shard_map/ppermute | solution.py:215
  93.8 1.9 %collective-permute-done.39 = f32[8,128]{1,0:T(8,128)S(1)} collective-permute-done((f32[8,128]{1,0:T(8,128)S(1)}, f32[8,128]{1,0:T(8,128)S(1)}, u32[]{:S(2)}, u32[]{:S(2)}) %collective-permute-start.39) | collective-permute-done | bytes 4128 | tf_op jit(solution)/shard_map/ppermute | solution.py:215
  95.7 2.7 %collective-permute-start.40 = (f32[8,128]{1,0:T(8,128)S(1)}, f32[8,128]{1,0:T(8,128)S(1)}, u32[]{:S(2)}, u32[]{:S(2)}) collective-permute-start(f32[8,128]{1,0:T(8,128)S(1)} %add.93), channel_id=1, source_target_pairs={{0,4},{1,5},{2,6},{3,7},{4,0},{5,1},{6,2},{7,3},{8,12},{9,13},{10,... | collective-permute-start | bytes 12296 | tf_op jit(solution)/shard_map/ppermute | solution.py:215
  98.4 1.0 shard_map.98.refs_0_
  99.4 0.8 collective-permute-done.40
  100.2 0.5 collective-permute-start.41
  100.7 0.9 shard_map.94.refs_0_
  101.6 2.2 %collective-permute-done.41.refs_3_ = f32[8,128]{1,0:T(8,128)S(1)} collective-permute-done((f32[8,128]{1,0:T(8,128)S(1)}, f32[8,128]{1,0:T(8,128)S(1)}, u32[]{:S(2)}, u32[]{:S(2)}) %collective-permute-start.41) | collective-permute-done | bytes 4128 | tf_op jit(solution)/shard_map/ppermute | solution.py:215
  103.8 1.1 %shard_map.100 = (f32[128,1152]{1,0:T(8,128)}, f32[1]{0:T(128)}) custom-call(f32[8,128]{1,0:T(8,128)S(1)} %concatenate.6.settings, bf16[128,1152]{1,0:T(8,128)(2,1)S(1)} %copy-done.1, f32[128,1152]{1,0:T(8,128)S(1)} %shard_map.98.refs_0_, f32[128,1152]{1,0:T(8,128)S(1)} %collective-permute-done.36.refs_1_, f32[8,128]{1,0:T(8,128)S(1)} %add.94.refs_2_, ...), custom_call_target="tpu_custom_call" | custom-call | tf_op jit(solution)/shard_map/pallas_call | solution.py:57
  104.9 1.1 %shard_map.96 = f32[128,1152]{1,0:T(8,128)} custom-call(f32[8,128]{1,0:T(8,128)S(1)} %concatenate.6.settings, bf16[128,1152]{1,0:T(8,128)(2,1)S(1)} %copy-done.2, f32[128,1152]{1,0:T(8,128)S(1)} %shard_map.94.refs_0_, f32[128,1152]{1,0:T(8,128)S(1)} %collective-permute-done.23.refs_1_), custom_call_target="tpu_custom_call" | custom-call | tf_op jit(solution)/shard_map/pallas_call | solution.py:57
  (96 shorter events, 2.5 us)
Async XLA Ops:
  0.6 11.8 %collective-permute-start = (bf16[128,1152]{1,0:T(8,128)(2,1)}, bf16[128,1152]{1,0:T(8,128)(2,1)S(1)}, u32[]{:S(2)}, u32[]{:S(2)}) collective-permute-start(bf16[128,1152]{1,0:T(8,128)(2,1)} %values.7), channel_id=1, source_target_pairs={{0,4},{1,5},{2,0},{3,1},{4,6},{5,7},{6,2},{7,3},{8,12},{9,13},{10,... | collective-permute-start | bytes 884744 | tf_op jit(solution)/shard_map/ppermute | solution.py:215
  4.7 1.0 copy-start
  5.7 1.7 %copy-start.2 = (bf16[128,1152]{1,0:T(8,128)(2,1)S(1)}, bf16[128,1152]{1,0:T(8,128)(2,1)}, u32[]{:S(2)}) copy-start(bf16[128,1152]{1,0:T(8,128)(2,1)} %values.6) | copy-start | bytes 884740
  5.9 8.5 %collective-permute-start.14 = (bf16[128,1152]{1,0:T(8,128)(2,1)S(1)}, bf16[128,1152]{1,0:T(8,128)(2,1)S(1)}, u32[]{:S(2)}, u32[]{:S(2)}) collective-permute-start(bf16[128,1152]{1,0:T(8,128)(2,1)S(1)} %shard_map.87.refs_2_.refs_0_), channel_id=1, source_target_pairs={{0,1},{1,0},{2,3},{3,2},{4,5},{5,4},{6,7},{7,6},{8,9},{9,8},{10,11... | collective-permute-start | bytes 884744 | tf_op jit(solution)/shard_map/ppermute | solution.py:215
  7.5 10.1 %collective-permute-start.16 = (bf16[128,1152]{1,0:T(8,128)(2,1)S(1)}, bf16[128,1152]{1,0:T(8,128)(2,1)S(1)}, u32[]{:S(2)}, u32[]{:S(2)}) collective-permute-start(bf16[128,1152]{1,0:T(8,128)(2,1)S(1)} %copy-done.2), channel_id=1, source_target_pairs={{0,4},{1,5},{2,0},{3,1},{4,6},{5,7},{6,2},{7,3},{8,12},{9,13},{10,... | collective-permute-start | bytes 884744 | tf_op jit(solution)/shard_map/ppermute | solution.py:215
  9.2 3.3 %copy-start.16 = (s32[128]{0:T(128)S(1)}, s32[128]{0:T(128)}, u32[]{:S(2)}) copy-start(s32[128]{0:T(128)} %param.8) | copy-start | bytes 1540
  9.2 10.1 %collective-permute-start.6 = (bf16[128,1152]{1,0:T(8,128)(2,1)S(1)}, bf16[128,1152]{1,0:T(8,128)(2,1)S(1)}, u32[]{:S(2)}, u32[]{:S(2)}) collective-permute-start(bf16[128,1152]{1,0:T(8,128)(2,1)S(1)} %shard_map.85.refs_0_.refs_2_), channel_id=1, source_target_pairs={{0,16},{1,17},{2,18},{3,19},{4,20},{5,21},{6,22},{7,23},{8,24},{9,... | collective-permute-start | bytes 884744 | tf_op jit(solution)/shard_map/ppermute | solution.py:215
  10.8 8.7 %collective-permute-start.13 = (bf16[128,1152]{1,0:T(8,128)(2,1)S(1)}, bf16[128,1152]{1,0:T(8,128)(2,1)S(1)}, u32[]{:S(2)}, u32[]{:S(2)}) collective-permute-start(bf16[128,1152]{1,0:T(8,128)(2,1)S(1)} %shard_map.87.refs_2_.refs_0_), channel_id=1, source_target_pairs={{0,8},{1,9},{2,10},{3,11},{4,12},{5,13},{6,14},{7,15},{8,0},{9,1},... | collective-permute-start | bytes 884744 | tf_op jit(solution)/shard_map/ppermute | solution.py:215
  12.5 5.2 %collective-permute-start.20 = (s32[1,128]{1,0:T(1,128)S(1)}, s32[1,128]{1,0:T(1,128)S(1)}, u32[]{:S(2)}, u32[]{:S(2)}) collective-permute-start(s32[1,128]{1,0:T(1,128)S(1)} %bitcast.14), channel_id=1, source_target_pairs={{0,1},{1,0},{2,3},{3,2},{4,5},{5,4},{6,7},{7,6},{8,9},{9,8},{10,11... | collective-permute-start | bytes 1544 | tf_op jit(solution)/shard_map/ppermute | solution.py:215
  14.4 9.2 %collective-permute-start.21 = (bf16[128,1152]{1,0:T(8,128)(2,1)S(1)}, bf16[128,1152]{1,0:T(8,128)(2,1)S(1)}, u32[]{:S(2)}, u32[]{:S(2)}) collective-permute-start(bf16[128,1152]{1,0:T(8,128)(2,1)S(1)} %shard_map.85.refs_0_.refs_2_), channel_id=1, source_target_pairs={{0,8},{1,9},{2,10},{3,11},{4,12},{5,13},{6,14},{7,15},{8,0},{9,1},... | collective-permute-start | bytes 884744 | tf_op jit(solution)/shard_map/ppermute | solution.py:215
  17.5 8.3 %collective-permute-start.15 = (bf16[128,1152]{1,0:T(8,128)(2,1)S(1)}, bf16[128,1152]{1,0:T(8,128)(2,1)S(1)}, u32[]{:S(2)}, u32[]{:S(2)}) collective-permute-start(bf16[128,1152]{1,0:T(8,128)(2,1)S(1)} %collective-permute-done.14.refs_4_.refs_1_.refs_0_), channel_id=1, source_target_pairs={{0,8},{1,9},{2,10},{3,11},{4,12},{5,13},{6,14},{7,15},{8,0},{9,1},... | collective-permute-start | bytes 884744 | tf_op jit(solution)/shard_map/ppermute | solution.py:215
  17.7 9.5 %collective-permute-start.11 = (bf16[128,1152]{1,0:T(8,128)(2,1)S(1)}, bf16[128,1152]{1,0:T(8,128)(2,1)S(1)}, u32[]{:S(2)}, u32[]{:S(2)}) collective-permute-start(bf16[128,1152]{1,0:T(8,128)(2,1)S(1)} %shard_map.86.refs_2_), channel_id=1, source_target_pairs={{0,1},{1,0},{2,3},{3,2},{4,5},{5,4},{6,7},{7,6},{8,9},{9,8},{10,11... | collective-permute-start | bytes 884744 | tf_op jit(solution)/shard_map/ppermute | solution.py:215
  19.3 11.3 %collective-permute-start.10 = (bf16[128,1152]{1,0:T(8,128)(2,1)S(1)}, bf16[128,1152]{1,0:T(8,128)(2,1)S(1)}, u32[]{:S(2)}, u32[]{:S(2)}) collective-permute-start(bf16[128,1152]{1,0:T(8,128)(2,1)S(1)} %shard_map.86.refs_2_), channel_id=1, source_target_pairs={{0,8},{1,9},{2,10},{3,11},{4,12},{5,13},{6,14},{7,15},{8,0},{9,1},... | collective-permute-start | bytes 884744 | tf_op jit(solution)/shard_map/ppermute | solution.py:215
  19.5 0.7 copy-start.19
  20.3 10.3 %collective-permute-start.24 = (bf16[128,1152]{1,0:T(8,128)(2,1)S(1)}, bf16[128,1152]{1,0:T(8,128)(2,1)S(1)}, u32[]{:S(2)}, u32[]{:S(2)}) collective-permute-start(bf16[128,1152]{1,0:T(8,128)(2,1)S(1)} %shard_map.90.refs_2_), channel_id=1, source_target_pairs={{0,4},{1,5},{2,0},{3,1},{4,6},{5,7},{6,2},{7,3},{8,12},{9,13},{10,... | collective-permute-start | bytes 884744 | tf_op jit(solution)/shard_map/ppermute | solution.py:215
  23.7 0.7 copy-start.17
  24.4 10.2 %collective-permute-start.18 = (bf16[128,1152]{1,0:T(8,128)(2,1)S(1)}, bf16[128,1152]{1,0:T(8,128)(2,1)S(1)}, u32[]{:S(2)}, u32[]{:S(2)}) collective-permute-start(bf16[128,1152]{1,0:T(8,128)(2,1)S(1)} %shard_map.90.refs_2_), channel_id=1, source_target_pairs={{0,16},{1,17},{2,18},{3,19},{4,20},{5,21},{6,22},{7,23},{8,24},{9,... | collective-permute-start | bytes 884744 | tf_op jit(solution)/shard_map/ppermute | solution.py:215
  26.6 8.9 %collective-permute-start.17 = (bf16[128,1152]{1,0:T(8,128)(2,1)S(1)}, bf16[128,1152]{1,0:T(8,128)(2,1)S(1)}, u32[]{:S(2)}, u32[]{:S(2)}) collective-permute-start(bf16[128,1152]{1,0:T(8,128)(2,1)S(1)} %shard_map.90.refs_2_), channel_id=1, source_target_pairs={{0,8},{1,9},{2,10},{3,11},{4,12},{5,13},{6,14},{7,15},{8,0},{9,1},... | collective-permute-start | bytes 884744 | tf_op jit(solution)/shard_map/ppermute | solution.py:215
  27.2 5.7 %copy-start.3 = (bf16[128,1152]{1,0:T(8,128)(2,1)}, bf16[128,1152]{1,0:T(8,128)(2,1)S(1)}, u32[]{:S(2)}) copy-start(bf16[128,1152]{1,0:T(8,128)(2,1)S(1)} %collective-permute-done.11.refs_4_) | copy-start | bytes 884740
  27.2 10.8 %collective-permute-start.1 = (bf16[128,1152]{1,0:T(8,128)(2,1)S(1)}, bf16[128,1152]{1,0:T(8,128)(2,1)}, u32[]{:S(2)}, u32[]{:S(2)}) collective-permute-start(bf16[128,1152]{1,0:T(8,128)(2,1)S(1)} %shard_map.86.refs_2_), channel_id=1, source_target_pairs={{0,4},{1,5},{2,0},{3,1},{4,6},{5,7},{6,2},{7,3},{8,12},{9,13},{10,... | collective-permute-start | bytes 884744 | tf_op jit(solution)/shard_map/ppermute | solution.py:215
  30.6 2.3 %copy-start.5 = (bf16[128,1152]{1,0:T(8,128)(2,1)}, bf16[128,1152]{1,0:T(8,128)(2,1)S(1)}, u32[]{:S(2)}) copy-start(bf16[128,1152]{1,0:T(8,128)(2,1)S(1)} %collective-permute-done.10.refs_3_) | copy-start | bytes 884740
  30.6 1.6 %collective-permute-start.22 = (bf16[128,1152]{1,0:T(8,128)(2,1)S(1)}, bf16[128,1152]{1,0:T(8,128)(2,1)S(1)}, u32[]{:S(2)}, u32[]{:S(2)}) collective-permute-start(bf16[128,1152]{1,0:T(8,128)(2,1)S(1)} %collective-permute-done.6.refs_1_.refs_4_.refs_0_), channel_id=1, source_target_pairs={{0,8},{1,9},{2,10},{3,11},{4,12},{5,13},{6,14},{7,15},{8,0},{9,1},... | collective-permute-start | bytes 884744 | tf_op jit(solution)/shard_map/ppermute | solution.py:215
  30.6 15.5 %collective-permute-start.12 = (bf16[128,1152]{1,0:T(8,128)(2,1)S(1)}, bf16[128,1152]{1,0:T(8,128)(2,1)S(1)}, u32[]{:S(2)}, u32[]{:S(2)}) collective-permute-start(bf16[128,1152]{1,0:T(8,128)(2,1)S(1)} %collective-permute-done.11.refs_4_), channel_id=1, source_target_pairs={{0,8},{1,9},{2,10},{3,11},{4,12},{5,13},{6,14},{7,15},{8,0},{9,1},... | collective-permute-start | bytes 884744 | tf_op jit(solution)/shard_map/ppermute | solution.py:215
  32.9 8.3 %collective-permute-start.27 = (bf16[64,1152]{1,0:T(8,128)(2,1)S(1)}, bf16[64,1152]{1,0:T(8,128)(2,1)}, u32[]{:S(2)}, u32[]{:S(2)}) collective-permute-start(bf16[64,1152]{1,0:T(8,128)(2,1)S(1)} %get-tuple-element.39), channel_id=1, source_target_pairs={{0,4},{1,5},{2,0},{3,1},{4,6},{5,7},{6,2},{7,3},{8,12},{9,13},{10,... | collective-permute-start | bytes 442376 | tf_op jit(solution)/shard_map/ppermute | solution.py:215
  34.5 12.3 %collective-permute-start.19 = (bf16[128,1152]{1,0:T(8,128)(2,1)S(1)}, bf16[128,1152]{1,0:T(8,128)(2,1)S(1)}, u32[]{:S(2)}, u32[]{:S(2)}) collective-permute-start(bf16[128,1152]{1,0:T(8,128)(2,1)S(1)} %collective-permute-done.18.refs_4_), channel_id=1, source_target_pairs={{0,8},{1,9},{2,10},{3,11},{4,12},{5,13},{6,14},{7,15},{8,0},{9,1},... | collective-permute-start | bytes 884744 | tf_op jit(solution)/shard_map/ppermute | solution.py:215
  34.8 0.7 copy-start.7
  35.5 0.7 copy-start.9
  36.2 8.4 %collective-permute-start.25 = (bf16[64,1152]{1,0:T(8,128)(2,1)S(1)}, bf16[64,1152]{1,0:T(8,128)(2,1)S(1)}, u32[]{:S(2)}, u32[]{:S(2)}) collective-permute-start(bf16[64,1152]{1,0:T(8,128)(2,1)S(1)} %get-tuple-element.40), channel_id=1, source_target_pairs={{0,4},{1,5},{2,0},{3,1},{4,6},{5,7},{6,2},{7,3},{8,12},{9,13},{10,... | collective-permute-start | bytes 442376 | tf_op jit(solution)/shard_map/ppermute | solution.py:215
  38.0 10.1 %collective-permute-start.8 = (bf16[128,1152]{1,0:T(8,128)(2,1)}, bf16[128,1152]{1,0:T(8,128)(2,1)}, u32[]{:S(2)}, u32[]{:S(2)}) collective-permute-start(bf16[128,1152]{1,0:T(8,128)(2,1)} %collective-permute-done.1.refs_2_), channel_id=1, source_target_pairs={{0,1},{1,0},{2,3},{3,2},{4,5},{5,4},{6,7},{7,6},{8,9},{9,8},{10,11... | collective-permute-start | bytes 884744 | tf_op jit(solution)/shard_map/ppermute | solution.py:215
  41.1 8.3 %collective-permute-start.2 = (bf16[128,1152]{1,0:T(8,128)(2,1)}, bf16[128,1152]{1,0:T(8,128)(2,1)S(1)}, u32[]{:S(2)}, u32[]{:S(2)}) collective-permute-start(bf16[128,1152]{1,0:T(8,128)(2,1)} %collective-permute-done.1.refs_2_), channel_id=1, source_target_pairs={{0,4},{1,5},{2,0},{3,1},{4,6},{5,7},{6,2},{7,3},{8,12},{9,13},{10,... | collective-permute-start | bytes 884744 | tf_op jit(solution)/shard_map/ppermute | solution.py:215
  44.6 7.9 %collective-permute-start.33 = (bf16[128,1152]{1,0:T(8,128)(2,1)S(1)}, bf16[128,1152]{1,0:T(8,128)(2,1)S(1)}, u32[]{:S(2)}, u32[]{:S(2)}) collective-permute-start(bf16[128,1152]{1,0:T(8,128)(2,1)S(1)} %collective-permute-done.24.refs_2_), channel_id=1, source_target_pairs={{0,16},{1,17},{2,18},{3,19},{4,20},{5,21},{6,22},{7,23},{8,24},{9,... | collective-permute-start | bytes 884744 | tf_op jit(solution)/shard_map/ppermute | solution.py:215
  46.1 0.7 copy-start.11
  46.9 5.7 %collective-permute-start.32 = (bf16[128,1152]{1,0:T(8,128)(2,1)S(1)}, bf16[128,1152]{1,0:T(8,128)(2,1)S(1)}, u32[]{:S(2)}, u32[]{:S(2)}) collective-permute-start(bf16[128,1152]{1,0:T(8,128)(2,1)S(1)} %collective-permute-done.24.refs_2_), channel_id=1, source_target_pairs={{0,8},{1,9},{2,10},{3,11},{4,12},{5,13},{6,14},{7,15},{8,0},{9,1},... | collective-permute-start | bytes 884744 | tf_op jit(solution)/shard_map/ppermute | solution.py:215
  46.9 0.7 copy-start.13
  47.6 3.4 %collective-permute-start.35 = (bf16[64,1152]{1,0:T(8,128)(2,1)}, bf16[64,1152]{1,0:T(8,128)(2,1)}, u32[]{:S(2)}, u32[]{:S(2)}) collective-permute-start(bf16[64,1152]{1,0:T(8,128)(2,1)} %collective-permute-done.27.refs_6_), channel_id=1, source_target_pairs={{0,8},{1,9},{2,10},{3,11},{4,12},{5,13},{6,14},{7,15},{8,0},{9,1},... | collective-permute-start | bytes 442376 | tf_op jit(solution)/shard_map/ppermute | solution.py:215
  48.1 7.1 %collective-permute-start.30 = (bf16[64,1152]{1,0:T(8,128)(2,1)S(1)}, bf16[64,1152]{1,0:T(8,128)(2,1)S(1)}, u32[]{:S(2)}, u32[]{:S(2)}) collective-permute-start(bf16[64,1152]{1,0:T(8,128)(2,1)S(1)} %collective-permute-done.25.refs_1_), channel_id=1, source_target_pairs={{0,16},{1,17},{2,18},{3,19},{4,20},{5,21},{6,22},{7,23},{8,24},{9,... | collective-permute-start | bytes 442376 | tf_op jit(solution)/shard_map/ppermute | solution.py:215
  49.4 12.9 %collective-permute-start.4 = (bf16[128,1152]{1,0:T(8,128)(2,1)S(1)}, bf16[128,1152]{1,0:T(8,128)(2,1)S(1)}, u32[]{:S(2)}, u32[]{:S(2)}) collective-permute-start(bf16[128,1152]{1,0:T(8,128)(2,1)S(1)} %collective-permute-done.2.refs_1_), channel_id=1, source_target_pairs={{0,1},{1,0},{2,3},{3,2},{4,5},{5,4},{6,7},{7,6},{8,9},{9,8},{10,11... | collective-permute-start | bytes 884744 | tf_op jit(solution)/shard_map/ppermute | solution.py:215
  50.9 6.7 %collective-permute-start.28 = (bf16[64,1152]{1,0:T(8,128)(2,1)}, bf16[64,1152]{1,0:T(8,128)(2,1)S(1)}, u32[]{:S(2)}, u32[]{:S(2)}) collective-permute-start(bf16[64,1152]{1,0:T(8,128)(2,1)} %collective-permute-done.27.refs_6_), channel_id=1, source_target_pairs={{0,16},{1,17},{2,18},{3,19},{4,20},{5,21},{6,22},{7,23},{8,24},{9,... | collective-permute-start | bytes 442376 | tf_op jit(solution)/shard_map/ppermute | solution.py:215
  52.5 5.2 %collective-permute-start.26 = (bf16[64,1152]{1,0:T(8,128)(2,1)S(1)}, bf16[64,1152]{1,0:T(8,128)(2,1)S(1)}, u32[]{:S(2)}, u32[]{:S(2)}) collective-permute-start(bf16[64,1152]{1,0:T(8,128)(2,1)S(1)} %collective-permute-done.25.refs_1_), channel_id=1, source_target_pairs={{0,8},{1,9},{2,10},{3,11},{4,12},{5,13},{6,14},{7,15},{8,0},{9,1},... | collective-permute-start | bytes 442376 | tf_op jit(solution)/shard_map/ppermute | solution.py:215
  52.5 11.4 %collective-permute-start.34 = (bf16[128,1152]{1,0:T(8,128)(2,1)S(1)}, bf16[128,1152]{1,0:T(8,128)(2,1)S(1)}, u32[]{:S(2)}, u32[]{:S(2)}) collective-permute-start(bf16[128,1152]{1,0:T(8,128)(2,1)S(1)} %collective-permute-done.33.refs_4_), channel_id=1, source_target_pairs={{0,8},{1,9},{2,10},{3,11},{4,12},{5,13},{6,14},{7,15},{8,0},{9,1},... | collective-permute-start | bytes 884744 | tf_op jit(solution)/shard_map/ppermute | solution.py:215
  55.2 7.0 %collective-permute-start.31 = (bf16[64,1152]{1,0:T(8,128)(2,1)S(1)}, bf16[64,1152]{1,0:T(8,128)(2,1)S(1)}, u32[]{:S(2)}, u32[]{:S(2)}) collective-permute-start(bf16[64,1152]{1,0:T(8,128)(2,1)S(1)} %collective-permute-done.30.refs_5_), channel_id=1, source_target_pairs={{0,8},{1,9},{2,10},{3,11},{4,12},{5,13},{6,14},{7,15},{8,0},{9,1},... | collective-permute-start | bytes 442376 | tf_op jit(solution)/shard_map/ppermute | solution.py:215
  57.7 14.4 %collective-permute-start.7 = (bf16[128,1152]{1,0:T(8,128)(2,1)}, bf16[128,1152]{1,0:T(8,128)(2,1)S(1)}, u32[]{:S(2)}, u32[]{:S(2)}) collective-permute-start(bf16[128,1152]{1,0:T(8,128)(2,1)} %collective-permute-done.1.refs_2_), channel_id=1, source_target_pairs={{0,8},{1,9},{2,10},{3,11},{4,12},{5,13},{6,14},{7,15},{8,0},{9,1},... | collective-permute-start | bytes 884744 | tf_op jit(solution)/shard_map/ppermute | solution.py:215
  57.7 14.4 %collective-permute-start.9 = (bf16[128,1152]{1,0:T(8,128)(2,1)}, bf16[128,1152]{1,0:T(8,128)(2,1)S(1)}, u32[]{:S(2)}, u32[]{:S(2)}) collective-permute-start(bf16[128,1152]{1,0:T(8,128)(2,1)} %collective-permute-done.8.refs_4_), channel_id=1, source_target_pairs={{0,8},{1,9},{2,10},{3,11},{4,12},{5,13},{6,14},{7,15},{8,0},{9,1},... | collective-permute-start | bytes 884744 | tf_op jit(solution)/shard_map/ppermute | solution.py:215
  58.9 1.0 copy-start.20
  59.9 1.0 copy-start.22
  60.9 1.9 %copy-start.18 = (bf16[128,1152]{1,0:T(8,128)(2,1)S(1)}, bf16[128,1152]{1,0:T(8,128)(2,1)}, u32[]{:S(2)}) copy-start(bf16[128,1152]{1,0:T(8,128)(2,1)} %copy-done.17) | copy-start | bytes 884740
  60.9 1.9 %copy-start.24 = (bf16[128,1152]{1,0:T(8,128)(2,1)S(1)}, bf16[128,1152]{1,0:T(8,128)(2,1)}, u32[]{:S(2)}) copy-start(bf16[128,1152]{1,0:T(8,128)(2,1)} %copy-done.23) | copy-start | bytes 884740
  62.2 1.9 %copy-start.4 = (bf16[128,1152]{1,0:T(8,128)(2,1)S(1)}, bf16[128,1152]{1,0:T(8,128)(2,1)}, u32[]{:S(2)}) copy-start(bf16[128,1152]{1,0:T(8,128)(2,1)} %copy-done.3) | copy-start | bytes 884740
  62.2 1.9 %copy-start.6 = (bf16[128,1152]{1,0:T(8,128)(2,1)S(1)}, bf16[128,1152]{1,0:T(8,128)(2,1)}, u32[]{:S(2)}) copy-start(bf16[128,1152]{1,0:T(8,128)(2,1)} %copy-done.5) | copy-start | bytes 884740
  62.2 1.9 %copy-start.12 = (bf16[128,1152]{1,0:T(8,128)(2,1)S(1)}, bf16[128,1152]{1,0:T(8,128)(2,1)}, u32[]{:S(2)}) copy-start(bf16[128,1152]{1,0:T(8,128)(2,1)} %copy-done.11) | copy-start | bytes 884740
  62.2 12.2 %collective-permute-start.3 = (bf16[128,1152]{1,0:T(8,128)(2,1)S(1)}, bf16[128,1152]{1,0:T(8,128)(2,1)S(1)}, u32[]{:S(2)}, u32[]{:S(2)}) collective-permute-start(bf16[128,1152]{1,0:T(8,128)(2,1)S(1)} %collective-permute-done.2.refs_1_), channel_id=1, source_target_pairs={{0,8},{1,9},{2,10},{3,11},{4,12},{5,13},{6,14},{7,15},{8,0},{9,1},... | collective-permute-start | bytes 884744 | tf_op jit(solution)/shard_map/ppermute | solution.py:215
  62.3 12.2 %collective-permute-start.5 = (bf16[128,1152]{1,0:T(8,128)(2,1)S(1)}, bf16[128,1152]{1,0:T(8,128)(2,1)S(1)}, u32[]{:S(2)}, u32[]{:S(2)}) collective-permute-start(bf16[128,1152]{1,0:T(8,128)(2,1)S(1)} %collective-permute-done.4.refs_3_), channel_id=1, source_target_pairs={{0,8},{1,9},{2,10},{3,11},{4,12},{5,13},{6,14},{7,15},{8,0},{9,1},... | collective-permute-start | bytes 884744 | tf_op jit(solution)/shard_map/ppermute | solution.py:215
  63.9 5.5 %collective-permute-start.29 = (bf16[64,1152]{1,0:T(8,128)(2,1)S(1)}, bf16[64,1152]{1,0:T(8,128)(2,1)S(1)}, u32[]{:S(2)}, u32[]{:S(2)}) collective-permute-start(bf16[64,1152]{1,0:T(8,128)(2,1)S(1)} %collective-permute-done.28.refs_3_), channel_id=1, source_target_pairs={{0,8},{1,9},{2,10},{3,11},{4,12},{5,13},{6,14},{7,15},{8,0},{9,1},... | collective-permute-start | bytes 442376 | tf_op jit(solution)/shard_map/ppermute | solution.py:215
  64.1 1.3 %copy-start.8 = (bf16[128,1152]{1,0:T(8,128)(2,1)S(1)}, bf16[128,1152]{1,0:T(8,128)(2,1)}, u32[]{:S(2)}) copy-start(bf16[128,1152]{1,0:T(8,128)(2,1)} %copy-done.7) | copy-start | bytes 884740
  64.1 1.4 %copy-start.10 = (bf16[128,1152]{1,0:T(8,128)(2,1)S(1)}, bf16[128,1152]{1,0:T(8,128)(2,1)}, u32[]{:S(2)}) copy-start(bf16[128,1152]{1,0:T(8,128)(2,1)} %copy-done.9) | copy-start | bytes 884740
  64.1 1.4 %copy-start.14 = (bf16[128,1152]{1,0:T(8,128)(2,1)S(1)}, bf16[128,1152]{1,0:T(8,128)(2,1)}, u32[]{:S(2)}) copy-start(bf16[128,1152]{1,0:T(8,128)(2,1)} %copy-done.13) | copy-start | bytes 884740
  70.5 33.3 %collective-permute-start.36 = (f32[128,1152]{1,0:T(8,128)S(1)}, f32[128,1152]{1,0:T(8,128)S(1)}, u32[]{:S(2)}, u32[]{:S(2)}) collective-permute-start(f32[128,1152]{1,0:T(8,128)S(1)} %shard_map.99), channel_id=1, source_target_pairs={{0,1},{1,0},{2,3},{3,2},{4,5},{5,4},{6,7},{7,6},{8,9},{9,8},{10,11... | collective-permute-start | bytes 1769480 | tf_op jit(solution)/shard_map/ppermute | solution.py:215
  75.3 29.6 %collective-permute-start.23 = (f32[128,1152]{1,0:T(8,128)S(1)}, f32[128,1152]{1,0:T(8,128)S(1)}, u32[]{:S(2)}, u32[]{:S(2)}) collective-permute-start(f32[128,1152]{1,0:T(8,128)S(1)} %shard_map.95), channel_id=1, source_target_pairs={{0,16},{1,17},{2,18},{3,19},{4,20},{5,21},{6,22},{7,23},{8,24},{9,... | collective-permute-start | bytes 1769480 | tf_op jit(solution)/shard_map/ppermute | solution.py:215
  77.2 13.7 %collective-permute-start.37 = (f32[8,128]{1,0:T(8,128)S(1)}, f32[8,128]{1,0:T(8,128)S(1)}, u32[]{:S(2)}, u32[]{:S(2)}) collective-permute-start(f32[8,128]{1,0:T(8,128)S(1)} %get-tuple-element.36), channel_id=1, source_target_pairs={{0,16},{1,17},{2,18},{3,19},{4,20},{5,21},{6,22},{7,23},{8,24},{9,... | collective-permute-start | bytes 12296 | tf_op jit(solution)/shard_map/ppermute | solution.py:215
  90.9 1.2 %collective-permute-start.38 = (f32[8,128]{1,0:T(8,128)S(1)}, f32[8,128]{1,0:T(8,128)S(1)}, u32[]{:S(2)}, u32[]{:S(2)}) collective-permute-start(f32[8,128]{1,0:T(8,128)S(1)} %add.91), channel_id=1, source_target_pairs={{0,8},{1,9},{2,10},{3,11},{4,12},{5,13},{6,14},{7,15},{8,0},{9,1},... | collective-permute-start | bytes 12296 | tf_op jit(solution)/shard_map/ppermute | solution.py:215
  92.1 3.6 %collective-permute-start.39 = (f32[8,128]{1,0:T(8,128)S(1)}, f32[8,128]{1,0:T(8,128)S(1)}, u32[]{:S(2)}, u32[]{:S(2)}) collective-permute-start(f32[8,128]{1,0:T(8,128)S(1)} %add.92), channel_id=1, source_target_pairs={{0,2},{1,3},{2,0},{3,1},{4,6},{5,7},{6,4},{7,5},{8,10},{9,11},{10,... | collective-permute-start | bytes 12296 | tf_op jit(solution)/shard_map/ppermute | solution.py:215
  95.7 4.5 %collective-permute-start.40 = (f32[8,128]{1,0:T(8,128)S(1)}, f32[8,128]{1,0:T(8,128)S(1)}, u32[]{:S(2)}, u32[]{:S(2)}) collective-permute-start(f32[8,128]{1,0:T(8,128)S(1)} %add.93), channel_id=1, source_target_pairs={{0,4},{1,5},{2,6},{3,7},{4,0},{5,1},{6,2},{7,3},{8,12},{9,13},{10,... | collective-permute-start | bytes 12296 | tf_op jit(solution)/shard_map/ppermute | solution.py:215
  100.2 3.6 %collective-permute-start.41 = (f32[8,128]{1,0:T(8,128)S(1)}, f32[8,128]{1,0:T(8,128)S(1)}, u32[]{:S(2)}, u32[]{:S(2)}) collective-permute-start(f32[8,128]{1,0:T(8,128)S(1)} %add.94.refs_2_), channel_id=1, source_target_pairs={{0,1},{1,0},{2,3},{3,2},{4,5},{5,4},{6,7},{7,6},{8,9},{9,8},{10,11... | collective-permute-start | bytes 12296 | tf_op jit(solution)/shard_map/ppermute | solution.py:215
  100.7 3.1 %copy-start.1 = (bf16[128,1152]{1,0:T(8,128)(2,1)S(1)}, bf16[128,1152]{1,0:T(8,128)(2,1)}, u32[]{:S(2)}) copy-start(bf16[128,1152]{1,0:T(8,128)(2,1)} %values.7) | copy-start | bytes 884740
  (3 other events, 2.1 us)

commit v7 on v4

--- a/solution.py
+++ b/solution.py
@@ -322,14 +322,16 @@
         img_sums, loss = image_terms(img_sums, loss, parts, range(wide), True)
         parts = [(img_sets[step][at], step, at, 0) for at in range(wide)]
         if step == end - 1:
-            parts += [(half[0], end, 0, offset) for half, offset in halves]
+            parts.append((first_set[0], end, 0, 0))
         txt_sums, loss = text_terms(txt_sums, loss, parts, range(fast), step == 1)
     parts = [(end, at) for at in range(fast)]
     img_far, _ = image_terms(img_sums[1:], None, parts, range(1, wide), False)
     img_near, _ = image_terms(img_sums[:1], None, parts, range(1), False)
+    early = [(second_set[0], end, 0, middle)]
     parts = [(half[at], end, at, offset) for at in range(1, wide) for half, offset in halves]
-    txt_far, _ = text_terms(txt_sums[1:], None, parts, range(1, fast), False)
-    txt_near, _ = text_terms(txt_sums[:1], None, parts, range(1), False)
+    txt_far, _ = text_terms(txt_sums[1:], None, early, range(1, fast), False)
+    txt_far, _ = text_terms(txt_far, None, parts, range(1, fast), False)
+    txt_near, _ = text_terms(txt_sums[:1], None, early + parts, range(1), False)
     img_sums, txt_sums = [*img_near, *img_far], [*txt_near, *txt_far]
 
     addends = [loss]

time: 105 us -> 107 us (1.019)
  Pallas kernels: 15.6 us -> 17.2 us
  starting transfers between devices: 43.7 us -> 45.1 us
    pallas_call x10 -> x11, Pallas kernels: 12.8 us -> 14.4 us  [terms(): pl.pallas_call(kernel, out_shape=shapes, in_specs=[VMEM] * len(operands),...]
    ppermute x42, starting transfers between devices: 43.7 us -> 45.1 us  [permuted(): return lax.ppermute(array, AXES, pairs)]
  transfers between devices with their start and end apart: 42 -> 42, of which waited for: 15 -> 16; matrix products, arithmetic and copies ran while one was open for 0% -> 0% of each run, Pallas kernels for 14% -> 15%
where the time goes in v7:
time: 107 us; the launch traced here: 106 us
  starting transfers between devices  45.1 us (42%)
  waiting for transfers between devices  32.3 us (30%)
  Pallas kernels  17.2 us (16%)
  local copies, waits for them, and re-layouts  9.5 us (9%)
  between operations  2.27 us (2%)
    ppermute x42, starting transfers between devices, permuted(): return lax.ppermute(array, AXES, pairs)  45.1 us
    ppermute x42, waiting for transfers between devices, permuted(): return lax.ppermute(array, AXES, pairs)  32.3 us
    pallas_call x11, Pallas kernels, terms(): pl.pallas_call(kernel, out_shape=shapes, in_specs=[VMEM] * len(operands),...  14.4 us
    unnamed x50, local copies, waits for them, and re-layouts  9.4 us
    pallas_call x2, Pallas kernels, project(): pl.pallas_call(functools.partial(project_kernel, len(parts), len(losses),...  2.19 us
  transfers between devices with their start and end apart: 42, of which 16 were waited for; matrix products, arithmetic and copies ran while one was open for 0% of the time, Pallas kernels for 15%

profile of v7, /device:TPU:0, one launch (start us, length us, event | category | flops | bytes accessed | tf_op | source)
XLA Modules:
  0.0 106.5 jit_solution(8211061393826539375)
XLA Ops:
  0.6 4.1 %collective-permute-start = (bf16[128,1152]{1,0:T(8,128)(2,1)}, bf16[128,1152]{1,0:T(8,128)(2,1)S(1)}, u32[]{:S(2)}, u32[]{:S(2)}) collective-permute-start(bf16[128,1152]{1,0:T(8,128)(2,1)} %values.7), channel_id=1, source_target_pairs={{0,4},{1,5},{2,0},{3,1},{4,6},{5,7},{6,2},{7,3},{8,12},{9,13},{10,... | collective-permute-start | bytes 884744 | tf_op jit(solution)/shard_map/ppermute | solution.py:215
  4.7 1.0 copy-done
  5.9 1.6 %collective-permute-start.14 = (bf16[128,1152]{1,0:T(8,128)(2,1)S(1)}, bf16[128,1152]{1,0:T(8,128)(2,1)S(1)}, u32[]{:S(2)}, u32[]{:S(2)}) collective-permute-start(bf16[128,1152]{1,0:T(8,128)(2,1)S(1)} %shard_map.87.refs_2_.refs_0_), channel_id=1, source_target_pairs={{0,1},{1,0},{2,3},{3,2},{4,5},{5,4},{6,7},{7,6},{8,9},{9,8},{10,11... | collective-permute-start | bytes 884744 | tf_op jit(solution)/shard_map/ppermute | solution.py:215
  7.5 1.6 %collective-permute-start.16 = (bf16[128,1152]{1,0:T(8,128)(2,1)S(1)}, bf16[128,1152]{1,0:T(8,128)(2,1)S(1)}, u32[]{:S(2)}, u32[]{:S(2)}) collective-permute-start(bf16[128,1152]{1,0:T(8,128)(2,1)S(1)} %copy-done.2), channel_id=1, source_target_pairs={{0,4},{1,5},{2,0},{3,1},{4,6},{5,7},{6,2},{7,3},{8,12},{9,13},{10,... | collective-permute-start | bytes 884744 | tf_op jit(solution)/shard_map/ppermute | solution.py:215
  9.2 1.6 %collective-permute-start.6 = (bf16[128,1152]{1,0:T(8,128)(2,1)S(1)}, bf16[128,1152]{1,0:T(8,128)(2,1)S(1)}, u32[]{:S(2)}, u32[]{:S(2)}) collective-permute-start(bf16[128,1152]{1,0:T(8,128)(2,1)S(1)} %shard_map.85.refs_0_.refs_2_), channel_id=1, source_target_pairs={{0,16},{1,17},{2,18},{3,19},{4,20},{5,21},{6,22},{7,23},{8,24},{9,... | collective-permute-start | bytes 884744 | tf_op jit(solution)/shard_map/ppermute | solution.py:215
  10.8 1.7 %collective-permute-done.values = bf16[128,1152]{1,0:T(8,128)(2,1)S(1)} collective-permute-done((bf16[128,1152]{1,0:T(8,128)(2,1)}, bf16[128,1152]{1,0:T(8,128)(2,1)S(1)}, u32[]{:S(2)}, u32[]{:S(2)}) %collective-permute-start) | collective-permute-done | bytes 294944 | tf_op jit(solution)/shard_map/ppermute | solution.py:215
  12.5 1.5 %collective-permute-start.20 = (s32[1,128]{1,0:T(1,128)S(1)}, s32[1,128]{1,0:T(1,128)S(1)}, u32[]{:S(2)}, u32[]{:S(2)}) collective-permute-start(s32[1,128]{1,0:T(1,128)S(1)} %bitcast.14), channel_id=1, source_target_pairs={{0,1},{1,0},{2,3},{3,2},{4,5},{5,4},{6,7},{7,6},{8,9},{9,8},{10,11... | collective-permute-start | bytes 1544 | tf_op jit(solution)/shard_map/ppermute | solution.py:215
  14.4 3.1 %collective-permute-done.16.values = bf16[128,1152]{1,0:T(8,128)(2,1)S(1)} collective-permute-done((bf16[128,1152]{1,0:T(8,128)(2,1)S(1)}, bf16[128,1152]{1,0:T(8,128)(2,1)S(1)}, u32[]{:S(2)}, u32[]{:S(2)}) %collective-permute-start.16) | collective-permute-done | bytes 294944 | tf_op jit(solution)/shard_map/ppermute | solution.py:215
  17.7 1.6 %collective-permute-start.11 = (bf16[128,1152]{1,0:T(8,128)(2,1)S(1)}, bf16[128,1152]{1,0:T(8,128)(2,1)S(1)}, u32[]{:S(2)}, u32[]{:S(2)}) collective-permute-start(bf16[128,1152]{1,0:T(8,128)(2,1)S(1)} %shard_map.86.refs_2_), channel_id=1, source_target_pairs={{0,1},{1,0},{2,3},{3,2},{4,5},{5,4},{6,7},{7,6},{8,9},{9,8},{10,11... | collective-permute-start | bytes 884744 | tf_op jit(solution)/shard_map/ppermute | solution.py:215
  19.5 0.7 copy-done.19
  20.3 3.4 %collective-permute-start.24 = (bf16[128,1152]{1,0:T(8,128)(2,1)S(1)}, bf16[128,1152]{1,0:T(8,128)(2,1)S(1)}, u32[]{:S(2)}, u32[]{:S(2)}) collective-permute-start(bf16[128,1152]{1,0:T(8,128)(2,1)S(1)} %shard_map.90.refs_2_), channel_id=1, source_target_pairs={{0,4},{1,5},{2,0},{3,1},{4,6},{5,7},{6,2},{7,3},{8,12},{9,13},{10,... | collective-permute-start | bytes 884744 | tf_op jit(solution)/shard_map/ppermute | solution.py:215
  23.7 0.7 copy-done.17
  24.4 1.5 %collective-permute-start.18 = (bf16[128,1152]{1,0:T(8,128)(2,1)S(1)}, bf16[128,1152]{1,0:T(8,128)(2,1)S(1)}, u32[]{:S(2)}, u32[]{:S(2)}) collective-permute-start(bf16[128,1152]{1,0:T(8,128)(2,1)S(1)} %shard_map.90.refs_2_), channel_id=1, source_target_pairs={{0,16},{1,17},{2,18},{3,19},{4,20},{5,21},{6,22},{7,23},{8,24},{9,... | collective-permute-start | bytes 884744 | tf_op jit(solution)/shard_map/ppermute | solution.py:215
  25.9 0.7 copy-done.21
  26.6 0.6 collective-permute-done.11.refs_4_
  27.2 3.4 %collective-permute-start.1 = (bf16[128,1152]{1,0:T(8,128)(2,1)S(1)}, bf16[128,1152]{1,0:T(8,128)(2,1)}, u32[]{:S(2)}, u32[]{:S(2)}) collective-permute-start(bf16[128,1152]{1,0:T(8,128)(2,1)S(1)} %shard_map.86.refs_2_), channel_id=1, source_target_pairs={{0,4},{1,5},{2,0},{3,1},{4,6},{5,7},{6,2},{7,3},{8,12},{9,13},{10,... | collective-permute-start | bytes 884744 | tf_op jit(solution)/shard_map/ppermute | solution.py:215
  30.6 0.5 collective-permute-start.12
  31.1 1.0 collective-permute-done.22.refs_5_
  32.2 0.7 copy-done.23
  32.9 1.6 %collective-permute-start.27 = (bf16[64,1152]{1,0:T(8,128)(2,1)S(1)}, bf16[64,1152]{1,0:T(8,128)(2,1)}, u32[]{:S(2)}, u32[]{:S(2)}) collective-permute-start(bf16[64,1152]{1,0:T(8,128)(2,1)S(1)} %get-tuple-element.39), channel_id=1, source_target_pairs={{0,4},{1,5},{2,0},{3,1},{4,6},{5,7},{6,2},{7,3},{8,12},{9,13},{10,... | collective-permute-start | bytes 442376 | tf_op jit(solution)/shard_map/ppermute | solution.py:215
  34.8 0.7 copy-done.7
  35.5 0.7 copy-done.9
  36.6 1.4 %collective-permute-done.1.refs_2_ = bf16[128,1152]{1,0:T(8,128)(2,1)} collective-permute-done((bf16[128,1152]{1,0:T(8,128)(2,1)S(1)}, bf16[128,1152]{1,0:T(8,128)(2,1)}, u32[]{:S(2)}, u32[]{:S(2)}) %collective-permute-start.1) | collective-permute-done | bytes 294944 | tf_op jit(solution)/shard_map/ppermute | solution.py:215
  38.0 1.5 %collective-permute-start.8 = (bf16[128,1152]{1,0:T(8,128)(2,1)}, bf16[128,1152]{1,0:T(8,128)(2,1)}, u32[]{:S(2)}, u32[]{:S(2)}) collective-permute-start(bf16[128,1152]{1,0:T(8,128)(2,1)} %collective-permute-done.1.refs_2_), channel_id=1, source_target_pairs={{0,1},{1,0},{2,3},{3,2},{4,5},{5,4},{6,7},{7,6},{8,9},{9,8},{10,11... | collective-permute-start | bytes 884744 | tf_op jit(solution)/shard_map/ppermute | solution.py:215
  39.5 1.6 %collective-permute-done.27.refs_6_ = bf16[64,1152]{1,0:T(8,128)(2,1)} collective-permute-done((bf16[64,1152]{1,0:T(8,128)(2,1)S(1)}, bf16[64,1152]{1,0:T(8,128)(2,1)}, u32[]{:S(2)}, u32[]{:S(2)}) %collective-permute-start.27) | collective-permute-done | bytes 147488 | tf_op jit(solution)/shard_map/ppermute | solution.py:215
  41.1 3.5 %collective-permute-start.2 = (bf16[128,1152]{1,0:T(8,128)(2,1)}, bf16[128,1152]{1,0:T(8,128)(2,1)S(1)}, u32[]{:S(2)}, u32[]{:S(2)}) collective-permute-start(bf16[128,1152]{1,0:T(8,128)(2,1)} %collective-permute-done.1.refs_2_), channel_id=1, source_target_pairs={{0,4},{1,5},{2,0},{3,1},{4,6},{5,7},{6,2},{7,3},{8,12},{9,13},{10,... | collective-permute-start | bytes 884744 | tf_op jit(solution)/shard_map/ppermute | solution.py:215
  44.6 1.5 %collective-permute-start.33 = (bf16[128,1152]{1,0:T(8,128)(2,1)S(1)}, bf16[128,1152]{1,0:T(8,128)(2,1)S(1)}, u32[]{:S(2)}, u32[]{:S(2)}) collective-permute-start(bf16[128,1152]{1,0:T(8,128)(2,1)S(1)} %collective-permute-done.24.refs_2_), channel_id=1, source_target_pairs={{0,16},{1,17},{2,18},{3,19},{4,20},{5,21},{6,22},{7,23},{8,24},{9,... | collective-permute-start | bytes 884744 | tf_op jit(solution)/shard_map/ppermute | solution.py:215
  46.1 0.7 copy-done.11
  46.9 0.7 copy-done.13
  47.6 0.5 collective-permute-start.35
  48.1 0.5 collective-permute-start.30
  48.6 0.8 collective-permute-done.2.refs_1_
  49.4 1.5 %collective-permute-start.4 = (bf16[128,1152]{1,0:T(8,128)(2,1)S(1)}, bf16[128,1152]{1,0:T(8,128)(2,1)S(1)}, u32[]{:S(2)}, u32[]{:S(2)}) collective-permute-start(bf16[128,1152]{1,0:T(8,128)(2,1)S(1)} %collective-permute-done.2.refs_1_), channel_id=1, source_target_pairs={{0,1},{1,0},{2,3},{3,2},{4,5},{5,4},{6,7},{7,6},{8,9},{9,8},{10,11... | collective-permute-start | bytes 884744 | tf_op jit(solution)/shard_map/ppermute | solution.py:215
  51.0 1.0 collective-permute-done.33.refs_4_
  52.0 2.4 %collective-permute-start.28 = (bf16[64,1152]{1,0:T(8,128)(2,1)}, bf16[64,1152]{1,0:T(8,128)(2,1)S(1)}, u32[]{:S(2)}, u32[]{:S(2)}) collective-permute-start(bf16[64,1152]{1,0:T(8,128)(2,1)} %collective-permute-done.27.refs_6_), channel_id=1, source_target_pairs={{0,16},{1,17},{2,18},{3,19},{4,20},{5,21},{6,22},{7,23},{8,24},{9,... | collective-permute-start | bytes 442376 | tf_op jit(solution)/shard_map/ppermute | solution.py:215
  56.7 1.1 %collective-permute-done.28.refs_3_.refs_1_ = bf16[64,1152]{1,0:T(8,128)(2,1)S(1)} collective-permute-done((bf16[64,1152]{1,0:T(8,128)(2,1)}, bf16[64,1152]{1,0:T(8,128)(2,1)S(1)}, u32[]{:S(2)}, u32[]{:S(2)}) %collective-permute-start.28) | collective-permute-done | bytes 147488 | tf_op jit(solution)/shard_map/ppermute | solution.py:215
  57.8 0.7 copy-done.15
  58.5 1.0 copy-done.20
  59.5 1.0 copy-done.22
  60.4 1.3 %shard_map.88 = (f32[128,1152]{1,0:T(8,128)S(1)}, f32[128,1152]{1,0:T(8,128)S(1)}, f32[8,128]{1,0:T(8,128)S(1)}) custom-call(f32[8,128]{1,0:T(8,128)S(1)} %concatenate.6.settings, s32[8,128]{1,0:T(8,128)S(1)} %iota_add_fusion.ids, bf16[128,1152]{1,0:T(8,128)(2,1)S(1)} %shard_map.85.refs_0_.refs_2_, ...), custom_call_target="tpu_custom_call" | custom-call | flops 603979776 | bytes 4128768 | tf_op jit(solution)/shard_map/pallas_call | solution.py:165
  61.8 0.6 collective-permute-start.3
  62.4 1.1 %shard_map.91 = (f32[128,1152]{1,0:T(8,128)S(1)}, f32[128,1152]{1,0:T(8,128)S(1)}) custom-call(f32[8,128]{1,0:T(8,128)S(1)} %concatenate.6.settings, s32[8,128]{1,0:T(8,128)S(1)} %iota_add_fusion.ids, bf16[128,1152]{1,0:T(8,128)(2,1)S(1)} %shard_map.87.refs_2_.refs_0_, bf16[128,1152]{1,0:T(8,128)(2,1)S(1)} %collective-permute-done.14.refs_4_.refs_1_.refs_0_, ...), custom_call_target="tpu_custom_call" | custom-call | flops 603979776 | bytes 4128768 | tf_op jit(solution)/shard_map/pallas_call | solution.py:165
  63.6 0.5 collective-permute-start.29
  64.1 1.3 %shard_map.89 = (f32[128,1152]{1,0:T(8,128)S(1)}, f32[128,1152]{1,0:T(8,128)S(1)}, f32[8,128]{1,0:T(8,128)S(1)}) custom-call(f32[8,128]{1,0:T(8,128)S(1)} %concatenate.6.settings, s32[8,128]{1,0:T(8,128)S(1)} %iota_add_fusion.ids, bf16[128,1152]{1,0:T(8,128)(2,1)S(1)} %shard_map.85.refs_0_.refs_2_, ...), custom_call_target="tpu_custom_call", output_to_operand_aliasing={{0}: (10, {}), {1}: (11, {}), {2}: (12, {})} | custom-call | flops 603979776 | bytes 4128768 | tf_op jit(solution)/shard_map/pallas_call | solution.py:165
  65.5 1.3 %shard_map.92 = (f32[128,1152]{1,0:T(8,128)S(1)}, f32[128,1152]{1,0:T(8,128)S(1)}, f32[8,128]{1,0:T(8,128)S(1)}) custom-call(f32[8,128]{1,0:T(8,128)S(1)} %concatenate.6.settings, s32[8,128]{1,0:T(8,128)S(1)} %iota_add_fusion.ids, bf16[128,1152]{1,0:T(8,128)(2,1)S(1)} %shard_map.87.refs_2_.refs_0_, ...), custom_call_target="tpu_custom_call", output_to_operand_aliasing={{0}: (10, {}), {1}: (11, {}), {2}: (12, {})} | custom-call | flops 603979776 | bytes 4128768 | tf_op jit(solution)/shard_map/pallas_call | solution.py:165
  66.8 2.6 %shard_map.97 = (f32[128,1152]{1,0:T(8,128)S(1)}, f32[128,1152]{1,0:T(8,128)S(1)}) custom-call(f32[8,128]{1,0:T(8,128)S(1)} %concatenate.6.settings, s32[8,128]{1,0:T(8,128)S(1)} %iota_add_fusion.ids, bf16[128,1152]{1,0:T(8,128)(2,1)S(1)} %shard_map.87.refs_2_.refs_0_, ...), custom_call_target="tpu_custom_call", output_to_operand_aliasing={{0}: (12, {}), {1}: (13, {})} | custom-call | flops 754974720 | bytes 4718592 | tf_op jit(solution)/shard_map/pallas_call | solution.py:165
  69.4 0.7 shard_map.99.refs_6_
  70.2 0.8 shard_map.100
  71.0 1.6 %collective-permute-start.36 = (f32[128,1152]{1,0:T(8,128)S(1)}, f32[128,1152]{1,0:T(8,128)S(1)}, u32[]{:S(2)}, u32[]{:S(2)}) collective-permute-start(f32[128,1152]{1,0:T(8,128)S(1)} %shard_map.100), channel_id=1, source_target_pairs={{0,1},{1,0},{2,3},{3,2},{4,5},{5,4},{6,7},{7,6},{8,9},{9,8},{10,11... | collective-permute-start | bytes 1769480 | tf_op jit(solution)/shard_map/ppermute | solution.py:215
  72.6 2.4 %shard_map.93 = (f32[128,1152]{1,0:T(8,128)S(1)}, f32[128,1152]{1,0:T(8,128)S(1)}, f32[8,128]{1,0:T(8,128)S(1)}) custom-call(f32[8,128]{1,0:T(8,128)S(1)} %concatenate.6.settings, s32[8,128]{1,0:T(8,128)S(1)} %iota_add_fusion.ids, bf16[128,1152]{1,0:T(8,128)(2,1)S(1)} %shard_map.85.refs_0_.refs_2_, ...), custom_call_target="tpu_custom_call", output_to_operand_aliasing={{0}: (10, {}), {1}: (11, {}), {2}: (12, {})} | custom-call | flops 603979776 | bytes 4128768 | tf_op jit(solution)/shard_map/pallas_call | solution.py:165
  75.0 0.9 shard_map.95
  75.9 2.1 %collective-permute-start.23 = (f32[128,1152]{1,0:T(8,128)S(1)}, f32[128,1152]{1,0:T(8,128)S(1)}, u32[]{:S(2)}, u32[]{:S(2)}) collective-permute-start(f32[128,1152]{1,0:T(8,128)S(1)} %shard_map.95), channel_id=1, source_target_pairs={{0,16},{1,17},{2,18},{3,19},{4,20},{5,21},{6,22},{7,23},{8,24},{9,... | collective-permute-start | bytes 1769480 | tf_op jit(solution)/shard_map/ppermute | solution.py:215
  78.1 13.3 %collective-permute-done.37 = f32[8,128]{1,0:T(8,128)S(1)} collective-permute-done((f32[8,128]{1,0:T(8,128)S(1)}, f32[8,128]{1,0:T(8,128)S(1)}, u32[]{:S(2)}, u32[]{:S(2)}) %collective-permute-start.37) | collective-permute-done | bytes 4128 | tf_op jit(solution)/shard_map/ppermute | solution.py:215
  91.4 1.2 %collective-permute-done.38 = f32[8,128]{1,0:T(8,128)S(1)} collective-permute-done((f32[8,128]{1,0:T(8,128)S(1)}, f32[8,128]{1,0:T(8,128)S(1)}, u32[]{:S(2)}, u32[]{:S(2)}) %collective-permute-start.38) | collective-permute-done | bytes 4128 | tf_op jit(solution)/shard_map/ppermute | solution.py:215
  92.5 1.7 %collective-permute-start.39 = (f32[8,128]{1,0:T(8,128)S(1)}, f32[8,128]{1,0:T(8,128)S(1)}, u32[]{:S(2)}, u32[]{:S(2)}) collective-permute-start(f32[8,128]{1,0:T(8,128)S(1)} %add.92), channel_id=1, source_target_pairs={{0,2},{1,3},{2,0},{3,1},{4,6},{5,7},{6,4},{7,5},{8,10},{9,11},{10,... | collective-permute-start | bytes 12296 | tf_op jit(solution)/shard_map/ppermute | solution.py:215
  94.3 1.9 %collective-permute-done.39 = f32[8,128]{1,0:T(8,128)S(1)} collective-permute-done((f32[8,128]{1,0:T(8,128)S(1)}, f32[8,128]{1,0:T(8,128)S(1)}, u32[]{:S(2)}, u32[]{:S(2)}) %collective-permute-start.39) | collective-permute-done | bytes 4128 | tf_op jit(solution)/shard_map/ppermute | solution.py:215
  96.2 2.7 %collective-permute-start.40 = (f32[8,128]{1,0:T(8,128)S(1)}, f32[8,128]{1,0:T(8,128)S(1)}, u32[]{:S(2)}, u32[]{:S(2)}) collective-permute-start(f32[8,128]{1,0:T(8,128)S(1)} %add.93), channel_id=1, source_target_pairs={{0,4},{1,5},{2,6},{3,7},{4,0},{5,1},{6,2},{7,3},{8,12},{9,13},{10,... | collective-permute-start | bytes 12296 | tf_op jit(solution)/shard_map/ppermute | solution.py:215
  98.9 1.0 shard_map.98.refs_0_
  99.9 0.8 collective-permute-done.40
  100.7 0.5 collective-permute-start.41
  101.2 0.9 shard_map.94.refs_0_
  102.1 2.2 %collective-permute-done.41.refs_3_ = f32[8,128]{1,0:T(8,128)S(1)} collective-permute-done((f32[8,128]{1,0:T(8,128)S(1)}, f32[8,128]{1,0:T(8,128)S(1)}, u32[]{:S(2)}, u32[]{:S(2)}) %collective-permute-start.41) | collective-permute-done | bytes 4128 | tf_op jit(solution)/shard_map/ppermute | solution.py:215
  104.3 1.1 %shard_map.101 = (f32[128,1152]{1,0:T(8,128)}, f32[1]{0:T(128)}) custom-call(f32[8,128]{1,0:T(8,128)S(1)} %concatenate.6.settings, bf16[128,1152]{1,0:T(8,128)(2,1)S(1)} %copy-done.1, f32[128,1152]{1,0:T(8,128)S(1)} %shard_map.98.refs_0_, f32[128,1152]{1,0:T(8,128)S(1)} %collective-permute-done.36.refs_1_, f32[8,128]{1,0:T(8,128)S(1)} %add.94.refs_2_, ...), custom_call_target="tpu_custom_call" | custom-call | tf_op jit(solution)/shard_map/pallas_call | solution.py:57
  105.4 1.1 %shard_map.96 = f32[128,1152]{1,0:T(8,128)} custom-call(f32[8,128]{1,0:T(8,128)S(1)} %concatenate.6.settings, bf16[128,1152]{1,0:T(8,128)(2,1)S(1)} %copy-done.2, f32[128,1152]{1,0:T(8,128)S(1)} %shard_map.94.refs_0_, f32[128,1152]{1,0:T(8,128)S(1)} %collective-permute-done.23.refs_1_), custom_call_target="tpu_custom_call" | custom-call | tf_op jit(solution)/shard_map/pallas_call | solution.py:57
  (97 shorter events, 3.2 us)
Async XLA Ops:
  0.6 11.8 %collective-permute-start = (bf16[128,1152]{1,0:T(8,128)(2,1)}, bf16[128,1152]{1,0:T(8,128)(2,1)S(1)}, u32[]{:S(2)}, u32[]{:S(2)}) collective-permute-start(bf16[128,1152]{1,0:T(8,128)(2,1)} %values.7), channel_id=1, source_target_pairs={{0,4},{1,5},{2,0},{3,1},{4,6},{5,7},{6,2},{7,3},{8,12},{9,13},{10,... | collective-permute-start | bytes 884744 | tf_op jit(solution)/shard_map/ppermute | solution.py:215
  4.7 1.0 copy-start
  5.7 1.7 %copy-start.2 = (bf16[128,1152]{1,0:T(8,128)(2,1)S(1)}, bf16[128,1152]{1,0:T(8,128)(2,1)}, u32[]{:S(2)}) copy-start(bf16[128,1152]{1,0:T(8,128)(2,1)} %values.6) | copy-start | bytes 884740
  5.9 8.5 %collective-permute-start.14 = (bf16[128,1152]{1,0:T(8,128)(2,1)S(1)}, bf16[128,1152]{1,0:T(8,128)(2,1)S(1)}, u32[]{:S(2)}, u32[]{:S(2)}) collective-permute-start(bf16[128,1152]{1,0:T(8,128)(2,1)S(1)} %shard_map.87.refs_2_.refs_0_), channel_id=1, source_target_pairs={{0,1},{1,0},{2,3},{3,2},{4,5},{5,4},{6,7},{7,6},{8,9},{9,8},{10,11... | collective-permute-start | bytes 884744 | tf_op jit(solution)/shard_map/ppermute | solution.py:215
  7.5 10.1 %collective-permute-start.16 = (bf16[128,1152]{1,0:T(8,128)(2,1)S(1)}, bf16[128,1152]{1,0:T(8,128)(2,1)S(1)}, u32[]{:S(2)}, u32[]{:S(2)}) collective-permute-start(bf16[128,1152]{1,0:T(8,128)(2,1)S(1)} %copy-done.2), channel_id=1, source_target_pairs={{0,4},{1,5},{2,0},{3,1},{4,6},{5,7},{6,2},{7,3},{8,12},{9,13},{10,... | collective-permute-start | bytes 884744 | tf_op jit(solution)/shard_map/ppermute | solution.py:215
  9.2 3.3 %copy-start.16 = (s32[128]{0:T(128)S(1)}, s32[128]{0:T(128)}, u32[]{:S(2)}) copy-start(s32[128]{0:T(128)} %param.8) | copy-start | bytes 1540
  9.2 10.1 %collective-permute-start.6 = (bf16[128,1152]{1,0:T(8,128)(2,1)S(1)}, bf16[128,1152]{1,0:T(8,128)(2,1)S(1)}, u32[]{:S(2)}, u32[]{:S(2)}) collective-permute-start(bf16[128,1152]{1,0:T(8,128)(2,1)S(1)} %shard_map.85.refs_0_.refs_2_), channel_id=1, source_target_pairs={{0,16},{1,17},{2,18},{3,19},{4,20},{5,21},{6,22},{7,23},{8,24},{9,... | collective-permute-start | bytes 884744 | tf_op jit(solution)/shard_map/ppermute | solution.py:215
  10.8 8.7 %collective-permute-start.13 = (bf16[128,1152]{1,0:T(8,128)(2,1)S(1)}, bf16[128,1152]{1,0:T(8,128)(2,1)S(1)}, u32[]{:S(2)}, u32[]{:S(2)}) collective-permute-start(bf16[128,1152]{1,0:T(8,128)(2,1)S(1)} %shard_map.87.refs_2_.refs_0_), channel_id=1, source_target_pairs={{0,8},{1,9},{2,10},{3,11},{4,12},{5,13},{6,14},{7,15},{8,0},{9,1},... | collective-permute-start | bytes 884744 | tf_op jit(solution)/shard_map/ppermute | solution.py:215
  12.5 5.2 %collective-permute-start.20 = (s32[1,128]{1,0:T(1,128)S(1)}, s32[1,128]{1,0:T(1,128)S(1)}, u32[]{:S(2)}, u32[]{:S(2)}) collective-permute-start(s32[1,128]{1,0:T(1,128)S(1)} %bitcast.14), channel_id=1, source_target_pairs={{0,1},{1,0},{2,3},{3,2},{4,5},{5,4},{6,7},{7,6},{8,9},{9,8},{10,11... | collective-permute-start | bytes 1544 | tf_op jit(solution)/shard_map/ppermute | solution.py:215
  14.4 9.2 %collective-permute-start.21 = (bf16[128,1152]{1,0:T(8,128)(2,1)S(1)}, bf16[128,1152]{1,0:T(8,128)(2,1)S(1)}, u32[]{:S(2)}, u32[]{:S(2)}) collective-permute-start(bf16[128,1152]{1,0:T(8,128)(2,1)S(1)} %shard_map.85.refs_0_.refs_2_), channel_id=1, source_target_pairs={{0,8},{1,9},{2,10},{3,11},{4,12},{5,13},{6,14},{7,15},{8,0},{9,1},... | collective-permute-start | bytes 884744 | tf_op jit(solution)/shard_map/ppermute | solution.py:215
  17.5 8.3 %collective-permute-start.15 = (bf16[128,1152]{1,0:T(8,128)(2,1)S(1)}, bf16[128,1152]{1,0:T(8,128)(2,1)S(1)}, u32[]{:S(2)}, u32[]{:S(2)}) collective-permute-start(bf16[128,1152]{1,0:T(8,128)(2,1)S(1)} %collective-permute-done.14.refs_4_.refs_1_.refs_0_), channel_id=1, source_target_pairs={{0,8},{1,9},{2,10},{3,11},{4,12},{5,13},{6,14},{7,15},{8,0},{9,1},... | collective-permute-start | bytes 884744 | tf_op jit(solution)/shard_map/ppermute | solution.py:215
  17.7 9.5 %collective-permute-start.11 = (bf16[128,1152]{1,0:T(8,128)(2,1)S(1)}, bf16[128,1152]{1,0:T(8,128)(2,1)S(1)}, u32[]{:S(2)}, u32[]{:S(2)}) collective-permute-start(bf16[128,1152]{1,0:T(8,128)(2,1)S(1)} %shard_map.86.refs_2_), channel_id=1, source_target_pairs={{0,1},{1,0},{2,3},{3,2},{4,5},{5,4},{6,7},{7,6},{8,9},{9,8},{10,11... | collective-permute-start | bytes 884744 | tf_op jit(solution)/shard_map/ppermute | solution.py:215
  19.3 11.3 %collective-permute-start.10 = (bf16[128,1152]{1,0:T(8,128)(2,1)S(1)}, bf16[128,1152]{1,0:T(8,128)(2,1)S(1)}, u32[]{:S(2)}, u32[]{:S(2)}) collective-permute-start(bf16[128,1152]{1,0:T(8,128)(2,1)S(1)} %shard_map.86.refs_2_), channel_id=1, source_target_pairs={{0,8},{1,9},{2,10},{3,11},{4,12},{5,13},{6,14},{7,15},{8,0},{9,1},... | collective-permute-start | bytes 884744 | tf_op jit(solution)/shard_map/ppermute | solution.py:215
  19.5 0.7 copy-start.19
  20.3 10.3 %collective-permute-start.24 = (bf16[128,1152]{1,0:T(8,128)(2,1)S(1)}, bf16[128,1152]{1,0:T(8,128)(2,1)S(1)}, u32[]{:S(2)}, u32[]{:S(2)}) collective-permute-start(bf16[128,1152]{1,0:T(8,128)(2,1)S(1)} %shard_map.90.refs_2_), channel_id=1, source_target_pairs={{0,4},{1,5},{2,0},{3,1},{4,6},{5,7},{6,2},{7,3},{8,12},{9,13},{10,... | collective-permute-start | bytes 884744 | tf_op jit(solution)/shard_map/ppermute | solution.py:215
  23.7 0.7 copy-start.17
  24.4 10.2 %collective-permute-start.18 = (bf16[128,1152]{1,0:T(8,128)(2,1)S(1)}, bf16[128,1152]{1,0:T(8,128)(2,1)S(1)}, u32[]{:S(2)}, u32[]{:S(2)}) collective-permute-start(bf16[128,1152]{1,0:T(8,128)(2,1)S(1)} %shard_map.90.refs_2_), channel_id=1, source_target_pairs={{0,16},{1,17},{2,18},{3,19},{4,20},{5,21},{6,22},{7,23},{8,24},{9,... | collective-permute-start | bytes 884744 | tf_op jit(solution)/shard_map/ppermute | solution.py:215
  26.6 8.9 %collective-permute-start.17 = (bf16[128,1152]{1,0:T(8,128)(2,1)S(1)}, bf16[128,1152]{1,0:T(8,128)(2,1)S(1)}, u32[]{:S(2)}, u32[]{:S(2)}) collective-permute-start(bf16[128,1152]{1,0:T(8,128)(2,1)S(1)} %shard_map.90.refs_2_), channel_id=1, source_target_pairs={{0,8},{1,9},{2,10},{3,11},{4,12},{5,13},{6,14},{7,15},{8,0},{9,1},... | collective-permute-start | bytes 884744 | tf_op jit(solution)/shard_map/ppermute | solution.py:215
  27.2 5.7 %copy-start.3 = (bf16[128,1152]{1,0:T(8,128)(2,1)}, bf16[128,1152]{1,0:T(8,128)(2,1)S(1)}, u32[]{:S(2)}) copy-start(bf16[128,1152]{1,0:T(8,128)(2,1)S(1)} %collective-permute-done.11.refs_4_) | copy-start | bytes 884740
  27.2 10.8 %collective-permute-start.1 = (bf16[128,1152]{1,0:T(8,128)(2,1)S(1)}, bf16[128,1152]{1,0:T(8,128)(2,1)}, u32[]{:S(2)}, u32[]{:S(2)}) collective-permute-start(bf16[128,1152]{1,0:T(8,128)(2,1)S(1)} %shard_map.86.refs_2_), channel_id=1, source_target_pairs={{0,4},{1,5},{2,0},{3,1},{4,6},{5,7},{6,2},{7,3},{8,12},{9,13},{10,... | collective-permute-start | bytes 884744 | tf_op jit(solution)/shard_map/ppermute | solution.py:215
  30.6 2.3 %copy-start.5 = (bf16[128,1152]{1,0:T(8,128)(2,1)}, bf16[128,1152]{1,0:T(8,128)(2,1)S(1)}, u32[]{:S(2)}) copy-start(bf16[128,1152]{1,0:T(8,128)(2,1)S(1)} %collective-permute-done.10.refs_3_) | copy-start | bytes 884740
  30.6 1.6 %collective-permute-start.22 = (bf16[128,1152]{1,0:T(8,128)(2,1)S(1)}, bf16[128,1152]{1,0:T(8,128)(2,1)S(1)}, u32[]{:S(2)}, u32[]{:S(2)}) collective-permute-start(bf16[128,1152]{1,0:T(8,128)(2,1)S(1)} %collective-permute-done.6.refs_1_.refs_4_.refs_0_), channel_id=1, source_target_pairs={{0,8},{1,9},{2,10},{3,11},{4,12},{5,13},{6,14},{7,15},{8,0},{9,1},... | collective-permute-start | bytes 884744 | tf_op jit(solution)/shard_map/ppermute | solution.py:215
  30.6 15.5 %collective-permute-start.12 = (bf16[128,1152]{1,0:T(8,128)(2,1)S(1)}, bf16[128,1152]{1,0:T(8,128)(2,1)S(1)}, u32[]{:S(2)}, u32[]{:S(2)}) collective-permute-start(bf16[128,1152]{1,0:T(8,128)(2,1)S(1)} %collective-permute-done.11.refs_4_), channel_id=1, source_target_pairs={{0,8},{1,9},{2,10},{3,11},{4,12},{5,13},{6,14},{7,15},{8,0},{9,1},... | collective-permute-start | bytes 884744 | tf_op jit(solution)/shard_map/ppermute | solution.py:215
  32.9 8.3 %collective-permute-start.27 = (bf16[64,1152]{1,0:T(8,128)(2,1)S(1)}, bf16[64,1152]{1,0:T(8,128)(2,1)}, u32[]{:S(2)}, u32[]{:S(2)}) collective-permute-start(bf16[64,1152]{1,0:T(8,128)(2,1)S(1)} %get-tuple-element.39), channel_id=1, source_target_pairs={{0,4},{1,5},{2,0},{3,1},{4,6},{5,7},{6,2},{7,3},{8,12},{9,13},{10,... | collective-permute-start | bytes 442376 | tf_op jit(solution)/shard_map/ppermute | solution.py:215
  34.5 12.3 %collective-permute-start.19 = (bf16[128,1152]{1,0:T(8,128)(2,1)S(1)}, bf16[128,1152]{1,0:T(8,128)(2,1)S(1)}, u32[]{:S(2)}, u32[]{:S(2)}) collective-permute-start(bf16[128,1152]{1,0:T(8,128)(2,1)S(1)} %collective-permute-done.18.refs_4_), channel_id=1, source_target_pairs={{0,8},{1,9},{2,10},{3,11},{4,12},{5,13},{6,14},{7,15},{8,0},{9,1},... | collective-permute-start | bytes 884744 | tf_op jit(solution)/shard_map/ppermute | solution.py:215
  34.8 0.7 copy-start.7
  35.5 0.7 copy-start.9
  36.2 8.4 %collective-permute-start.25 = (bf16[64,1152]{1,0:T(8,128)(2,1)S(1)}, bf16[64,1152]{1,0:T(8,128)(2,1)S(1)}, u32[]{:S(2)}, u32[]{:S(2)}) collective-permute-start(bf16[64,1152]{1,0:T(8,128)(2,1)S(1)} %get-tuple-element.40), channel_id=1, source_target_pairs={{0,4},{1,5},{2,0},{3,1},{4,6},{5,7},{6,2},{7,3},{8,12},{9,13},{10,... | collective-permute-start | bytes 442376 | tf_op jit(solution)/shard_map/ppermute | solution.py:215
  38.0 10.1 %collective-permute-start.8 = (bf16[128,1152]{1,0:T(8,128)(2,1)}, bf16[128,1152]{1,0:T(8,128)(2,1)}, u32[]{:S(2)}, u32[]{:S(2)}) collective-permute-start(bf16[128,1152]{1,0:T(8,128)(2,1)} %collective-permute-done.1.refs_2_), channel_id=1, source_target_pairs={{0,1},{1,0},{2,3},{3,2},{4,5},{5,4},{6,7},{7,6},{8,9},{9,8},{10,11... | collective-permute-start | bytes 884744 | tf_op jit(solution)/shard_map/ppermute | solution.py:215
  41.1 8.3 %collective-permute-start.2 = (bf16[128,1152]{1,0:T(8,128)(2,1)}, bf16[128,1152]{1,0:T(8,128)(2,1)S(1)}, u32[]{:S(2)}, u32[]{:S(2)}) collective-permute-start(bf16[128,1152]{1,0:T(8,128)(2,1)} %collective-permute-done.1.refs_2_), channel_id=1, source_target_pairs={{0,4},{1,5},{2,0},{3,1},{4,6},{5,7},{6,2},{7,3},{8,12},{9,13},{10,... | collective-permute-start | bytes 884744 | tf_op jit(solution)/shard_map/ppermute | solution.py:215
  44.6 7.4 %collective-permute-start.33 = (bf16[128,1152]{1,0:T(8,128)(2,1)S(1)}, bf16[128,1152]{1,0:T(8,128)(2,1)S(1)}, u32[]{:S(2)}, u32[]{:S(2)}) collective-permute-start(bf16[128,1152]{1,0:T(8,128)(2,1)S(1)} %collective-permute-done.24.refs_2_), channel_id=1, source_target_pairs={{0,16},{1,17},{2,18},{3,19},{4,20},{5,21},{6,22},{7,23},{8,24},{9,... | collective-permute-start | bytes 884744 | tf_op jit(solution)/shard_map/ppermute | solution.py:215
  46.1 0.7 copy-start.11
  46.9 7.6 %collective-permute-start.32 = (bf16[128,1152]{1,0:T(8,128)(2,1)S(1)}, bf16[128,1152]{1,0:T(8,128)(2,1)S(1)}, u32[]{:S(2)}, u32[]{:S(2)}) collective-permute-start(bf16[128,1152]{1,0:T(8,128)(2,1)S(1)} %collective-permute-done.24.refs_2_), channel_id=1, source_target_pairs={{0,8},{1,9},{2,10},{3,11},{4,12},{5,13},{6,14},{7,15},{8,0},{9,1},... | collective-permute-start | bytes 884744 | tf_op jit(solution)/shard_map/ppermute | solution.py:215
  46.9 0.7 copy-start.13
  47.6 3.4 %collective-permute-start.35 = (bf16[64,1152]{1,0:T(8,128)(2,1)}, bf16[64,1152]{1,0:T(8,128)(2,1)}, u32[]{:S(2)}, u32[]{:S(2)}) collective-permute-start(bf16[64,1152]{1,0:T(8,128)(2,1)} %collective-permute-done.27.refs_6_), channel_id=1, source_target_pairs={{0,8},{1,9},{2,10},{3,11},{4,12},{5,13},{6,14},{7,15},{8,0},{9,1},... | collective-permute-start | bytes 442376 | tf_op jit(solution)/shard_map/ppermute | solution.py:215
  48.1 6.6 %collective-permute-start.30 = (bf16[64,1152]{1,0:T(8,128)(2,1)S(1)}, bf16[64,1152]{1,0:T(8,128)(2,1)S(1)}, u32[]{:S(2)}, u32[]{:S(2)}) collective-permute-start(bf16[64,1152]{1,0:T(8,128)(2,1)S(1)} %collective-permute-done.25.refs_1_), channel_id=1, source_target_pairs={{0,16},{1,17},{2,18},{3,19},{4,20},{5,21},{6,22},{7,23},{8,24},{9,... | collective-permute-start | bytes 442376 | tf_op jit(solution)/shard_map/ppermute | solution.py:215
  49.4 12.9 %collective-permute-start.4 = (bf16[128,1152]{1,0:T(8,128)(2,1)S(1)}, bf16[128,1152]{1,0:T(8,128)(2,1)S(1)}, u32[]{:S(2)}, u32[]{:S(2)}) collective-permute-start(bf16[128,1152]{1,0:T(8,128)(2,1)S(1)} %collective-permute-done.2.refs_1_), channel_id=1, source_target_pairs={{0,1},{1,0},{2,3},{3,2},{4,5},{5,4},{6,7},{7,6},{8,9},{9,8},{10,11... | collective-permute-start | bytes 884744 | tf_op jit(solution)/shard_map/ppermute | solution.py:215
  50.9 5.4 %collective-permute-start.26 = (bf16[64,1152]{1,0:T(8,128)(2,1)S(1)}, bf16[64,1152]{1,0:T(8,128)(2,1)S(1)}, u32[]{:S(2)}, u32[]{:S(2)}) collective-permute-start(bf16[64,1152]{1,0:T(8,128)(2,1)S(1)} %collective-permute-done.25.refs_1_), channel_id=1, source_target_pairs={{0,8},{1,9},{2,10},{3,11},{4,12},{5,13},{6,14},{7,15},{8,0},{9,1},... | collective-permute-start | bytes 442376 | tf_op jit(solution)/shard_map/ppermute | solution.py:215
  52.0 5.7 %collective-permute-start.28 = (bf16[64,1152]{1,0:T(8,128)(2,1)}, bf16[64,1152]{1,0:T(8,128)(2,1)S(1)}, u32[]{:S(2)}, u32[]{:S(2)}) collective-permute-start(bf16[64,1152]{1,0:T(8,128)(2,1)} %collective-permute-done.27.refs_6_), channel_id=1, source_target_pairs={{0,16},{1,17},{2,18},{3,19},{4,20},{5,21},{6,22},{7,23},{8,24},{9,... | collective-permute-start | bytes 442376 | tf_op jit(solution)/shard_map/ppermute | solution.py:215
  54.4 9.1 %collective-permute-start.34 = (bf16[128,1152]{1,0:T(8,128)(2,1)S(1)}, bf16[128,1152]{1,0:T(8,128)(2,1)S(1)}, u32[]{:S(2)}, u32[]{:S(2)}) collective-permute-start(bf16[128,1152]{1,0:T(8,128)(2,1)S(1)} %collective-permute-done.33.refs_4_), channel_id=1, source_target_pairs={{0,8},{1,9},{2,10},{3,11},{4,12},{5,13},{6,14},{7,15},{8,0},{9,1},... | collective-permute-start | bytes 884744 | tf_op jit(solution)/shard_map/ppermute | solution.py:215
  54.7 7.1 %collective-permute-start.31 = (bf16[64,1152]{1,0:T(8,128)(2,1)S(1)}, bf16[64,1152]{1,0:T(8,128)(2,1)S(1)}, u32[]{:S(2)}, u32[]{:S(2)}) collective-permute-start(bf16[64,1152]{1,0:T(8,128)(2,1)S(1)} %collective-permute-done.30.refs_5_.refs_3_), channel_id=1, source_target_pairs={{0,8},{1,9},{2,10},{3,11},{4,12},{5,13},{6,14},{7,15},{8,0},{9,1},... | collective-permute-start | bytes 442376 | tf_op jit(solution)/shard_map/ppermute | solution.py:215
  56.4 16.2 %collective-permute-start.7 = (bf16[128,1152]{1,0:T(8,128)(2,1)}, bf16[128,1152]{1,0:T(8,128)(2,1)S(1)}, u32[]{:S(2)}, u32[]{:S(2)}) collective-permute-start(bf16[128,1152]{1,0:T(8,128)(2,1)} %collective-permute-done.1.refs_2_), channel_id=1, source_target_pairs={{0,8},{1,9},{2,10},{3,11},{4,12},{5,13},{6,14},{7,15},{8,0},{9,1},... | collective-permute-start | bytes 884744 | tf_op jit(solution)/shard_map/ppermute | solution.py:215
  57.8 14.8 %collective-permute-start.9 = (bf16[128,1152]{1,0:T(8,128)(2,1)}, bf16[128,1152]{1,0:T(8,128)(2,1)S(1)}, u32[]{:S(2)}, u32[]{:S(2)}) collective-permute-start(bf16[128,1152]{1,0:T(8,128)(2,1)} %collective-permute-done.8.refs_4_), channel_id=1, source_target_pairs={{0,8},{1,9},{2,10},{3,11},{4,12},{5,13},{6,14},{7,15},{8,0},{9,1},... | collective-permute-start | bytes 884744 | tf_op jit(solution)/shard_map/ppermute | solution.py:215
  58.5 1.0 copy-start.20
  59.5 1.0 copy-start.22
  60.4 2.0 %copy-start.18 = (bf16[128,1152]{1,0:T(8,128)(2,1)S(1)}, bf16[128,1152]{1,0:T(8,128)(2,1)}, u32[]{:S(2)}) copy-start(bf16[128,1152]{1,0:T(8,128)(2,1)} %copy-done.17) | copy-start | bytes 884740
  60.4 2.0 %copy-start.24 = (bf16[128,1152]{1,0:T(8,128)(2,1)S(1)}, bf16[128,1152]{1,0:T(8,128)(2,1)}, u32[]{:S(2)}) copy-start(bf16[128,1152]{1,0:T(8,128)(2,1)} %copy-done.23) | copy-start | bytes 884740
  61.7 2.3 %copy-start.4 = (bf16[128,1152]{1,0:T(8,128)(2,1)S(1)}, bf16[128,1152]{1,0:T(8,128)(2,1)}, u32[]{:S(2)}) copy-start(bf16[128,1152]{1,0:T(8,128)(2,1)} %copy-done.3) | copy-start | bytes 884740
  61.7 2.3 %copy-start.6 = (bf16[128,1152]{1,0:T(8,128)(2,1)S(1)}, bf16[128,1152]{1,0:T(8,128)(2,1)}, u32[]{:S(2)}) copy-start(bf16[128,1152]{1,0:T(8,128)(2,1)} %copy-done.5) | copy-start | bytes 884740
  61.8 2.3 %copy-start.12 = (bf16[128,1152]{1,0:T(8,128)(2,1)S(1)}, bf16[128,1152]{1,0:T(8,128)(2,1)}, u32[]{:S(2)}) copy-start(bf16[128,1152]{1,0:T(8,128)(2,1)} %copy-done.11) | copy-start | bytes 884740
  61.8 13.2 %collective-permute-start.3 = (bf16[128,1152]{1,0:T(8,128)(2,1)S(1)}, bf16[128,1152]{1,0:T(8,128)(2,1)S(1)}, u32[]{:S(2)}, u32[]{:S(2)}) collective-permute-start(bf16[128,1152]{1,0:T(8,128)(2,1)S(1)} %collective-permute-done.2.refs_1_), channel_id=1, source_target_pairs={{0,8},{1,9},{2,10},{3,11},{4,12},{5,13},{6,14},{7,15},{8,0},{9,1},... | collective-permute-start | bytes 884744 | tf_op jit(solution)/shard_map/ppermute | solution.py:215
  62.4 12.6 %collective-permute-start.5 = (bf16[128,1152]{1,0:T(8,128)(2,1)S(1)}, bf16[128,1152]{1,0:T(8,128)(2,1)S(1)}, u32[]{:S(2)}, u32[]{:S(2)}) collective-permute-start(bf16[128,1152]{1,0:T(8,128)(2,1)S(1)} %collective-permute-done.4.refs_3_), channel_id=1, source_target_pairs={{0,8},{1,9},{2,10},{3,11},{4,12},{5,13},{6,14},{7,15},{8,0},{9,1},... | collective-permute-start | bytes 884744 | tf_op jit(solution)/shard_map/ppermute | solution.py:215
  63.6 6.6 %collective-permute-start.29 = (bf16[64,1152]{1,0:T(8,128)(2,1)S(1)}, bf16[64,1152]{1,0:T(8,128)(2,1)S(1)}, u32[]{:S(2)}, u32[]{:S(2)}) collective-permute-start(bf16[64,1152]{1,0:T(8,128)(2,1)S(1)} %collective-permute-done.28.refs_3_.refs_1_), channel_id=1, source_target_pairs={{0,8},{1,9},{2,10},{3,11},{4,12},{5,13},{6,14},{7,15},{8,0},{9,1},... | collective-permute-start | bytes 442376 | tf_op jit(solution)/shard_map/ppermute | solution.py:215
  64.1 1.3 %copy-start.8 = (bf16[128,1152]{1,0:T(8,128)(2,1)S(1)}, bf16[128,1152]{1,0:T(8,128)(2,1)}, u32[]{:S(2)}) copy-start(bf16[128,1152]{1,0:T(8,128)(2,1)} %copy-done.7) | copy-start | bytes 884740
  64.1 1.4 %copy-start.10 = (bf16[128,1152]{1,0:T(8,128)(2,1)S(1)}, bf16[128,1152]{1,0:T(8,128)(2,1)}, u32[]{:S(2)}) copy-start(bf16[128,1152]{1,0:T(8,128)(2,1)} %copy-done.9) | copy-start | bytes 884740
  64.1 1.4 %copy-start.14 = (bf16[128,1152]{1,0:T(8,128)(2,1)S(1)}, bf16[128,1152]{1,0:T(8,128)(2,1)}, u32[]{:S(2)}) copy-start(bf16[128,1152]{1,0:T(8,128)(2,1)} %copy-done.13) | copy-start | bytes 884740
  71.0 33.3 %collective-permute-start.36 = (f32[128,1152]{1,0:T(8,128)S(1)}, f32[128,1152]{1,0:T(8,128)S(1)}, u32[]{:S(2)}, u32[]{:S(2)}) collective-permute-start(f32[128,1152]{1,0:T(8,128)S(1)} %shard_map.100), channel_id=1, source_target_pairs={{0,1},{1,0},{2,3},{3,2},{4,5},{5,4},{6,7},{7,6},{8,9},{9,8},{10,11... | collective-permute-start | bytes 1769480 | tf_op jit(solution)/shard_map/ppermute | solution.py:215
  75.9 29.5 %collective-permute-start.23 = (f32[128,1152]{1,0:T(8,128)S(1)}, f32[128,1152]{1,0:T(8,128)S(1)}, u32[]{:S(2)}, u32[]{:S(2)}) collective-permute-start(f32[128,1152]{1,0:T(8,128)S(1)} %shard_map.95), channel_id=1, source_target_pairs={{0,16},{1,17},{2,18},{3,19},{4,20},{5,21},{6,22},{7,23},{8,24},{9,... | collective-permute-start | bytes 1769480 | tf_op jit(solution)/shard_map/ppermute | solution.py:215
  78.0 13.4 %collective-permute-start.37 = (f32[8,128]{1,0:T(8,128)S(1)}, f32[8,128]{1,0:T(8,128)S(1)}, u32[]{:S(2)}, u32[]{:S(2)}) collective-permute-start(f32[8,128]{1,0:T(8,128)S(1)} %get-tuple-element.36), channel_id=1, source_target_pairs={{0,16},{1,17},{2,18},{3,19},{4,20},{5,21},{6,22},{7,23},{8,24},{9,... | collective-permute-start | bytes 12296 | tf_op jit(solution)/shard_map/ppermute | solution.py:215
  91.4 1.2 %collective-permute-start.38 = (f32[8,128]{1,0:T(8,128)S(1)}, f32[8,128]{1,0:T(8,128)S(1)}, u32[]{:S(2)}, u32[]{:S(2)}) collective-permute-start(f32[8,128]{1,0:T(8,128)S(1)} %add.91), channel_id=1, source_target_pairs={{0,8},{1,9},{2,10},{3,11},{4,12},{5,13},{6,14},{7,15},{8,0},{9,1},... | collective-permute-start | bytes 12296 | tf_op jit(solution)/shard_map/ppermute | solution.py:215
  92.5 3.6 %collective-permute-start.39 = (f32[8,128]{1,0:T(8,128)S(1)}, f32[8,128]{1,0:T(8,128)S(1)}, u32[]{:S(2)}, u32[]{:S(2)}) collective-permute-start(f32[8,128]{1,0:T(8,128)S(1)} %add.92), channel_id=1, source_target_pairs={{0,2},{1,3},{2,0},{3,1},{4,6},{5,7},{6,4},{7,5},{8,10},{9,11},{10,... | collective-permute-start | bytes 12296 | tf_op jit(solution)/shard_map/ppermute | solution.py:215
  96.2 4.5 %collective-permute-start.40 = (f32[8,128]{1,0:T(8,128)S(1)}, f32[8,128]{1,0:T(8,128)S(1)}, u32[]{:S(2)}, u32[]{:S(2)}) collective-permute-start(f32[8,128]{1,0:T(8,128)S(1)} %add.93), channel_id=1, source_target_pairs={{0,4},{1,5},{2,6},{3,7},{4,0},{5,1},{6,2},{7,3},{8,12},{9,13},{10,... | collective-permute-start | bytes 12296 | tf_op jit(solution)/shard_map/ppermute | solution.py:215
  100.7 3.6 %collective-permute-start.41 = (f32[8,128]{1,0:T(8,128)S(1)}, f32[8,128]{1,0:T(8,128)S(1)}, u32[]{:S(2)}, u32[]{:S(2)}) collective-permute-start(f32[8,128]{1,0:T(8,128)S(1)} %add.94.refs_2_), channel_id=1, source_target_pairs={{0,1},{1,0},{2,3},{3,2},{4,5},{5,4},{6,7},{7,6},{8,9},{9,8},{10,11... | collective-permute-start | bytes 12296 | tf_op jit(solution)/shard_map/ppermute | solution.py:215
  101.2 3.1 %copy-start.1 = (bf16[128,1152]{1,0:T(8,128)(2,1)S(1)}, bf16[128,1152]{1,0:T(8,128)(2,1)}, u32[]{:S(2)}) copy-start(bf16[128,1152]{1,0:T(8,128)(2,1)} %values.7) | copy-start | bytes 884740
  (3 other events, 2.1 us)
